TPU v7x, 32 devices: a whole 2x2x4 slice. The times are simulated.
32 devices in a mesh: dp: 4 (over y, x), segment: 2 (over core), band: 4 (over z).
Axes of the slice: x: 2, y: 2, z: 4, core: 2. Of those that a mesh axis runs over, the one named last changes fastest.
Arguments:
- fields: bfloat16 [4, 2, 32, 16, 512], P('dp', None, 'band'), may hold values from -6 to 6
- cell_mask: int32 [4, 2, 32, 16], P('dp', None, 'band'), may hold values 0 or 1
- merge_weight: bfloat16 [2, 1024, 512], P('segment', 'dp'), may hold values from -0.1875 to 0.1875
- qkv_weight: bfloat16 [2, 512, 1536], P('segment', 'dp')
- out_weight: bfloat16 [2, 512, 512], P('segment', 'dp'), may hold values from -1 to 1
- norm_gain: bfloat16 [2, 512], P('segment', 'dp'), may hold values from 0.099609375 to 1.8984375
- out_cotangent: bfloat16 [4, 2, 32, 16, 512], P('dp', None, 'band'), may hold values from -6 to 6
Outputs:
- section_out: bfloat16 [2, 4, 2, 32, 16, 512], P('segment', 'dp', None, 'band')
- merge_grad: float32 [2, 1024, 512], P('segment', 'dp')
- qkv_grad: float32 [2, 512, 1536], P('segment', 'dp')
- out_grad: float32 [2, 512, 512], P('segment', 'dp')
- gain_grad: float32 [2, 512], P('segment', 'dp')
Inputs may be any that keep to these rules, and one draw needn't show every extreme that they name: `cell_mask`: 1 marks a cell whose keys may be attended.
All inputs are finite; a program needn't handle non-finite values. No bound on the sum of `cell_mask` on one device may be relied on, other than what follows from the above.
Results may differ from a plain program's by a relative error of at most 0.03.
Values may be sent and summed in bfloat16 or wider, within the bound.
No kernel may reach another device: no remote copies, remote signals or barrier semaphores. Data moves between devices by JAX's collectives and lax.ppermute only.
A program may use at most 128 MiB of HBM per device.

v0:
```python
import jax
import jax.numpy as jnp
from jax import lax
from jax.sharding import PartitionSpec as P

HEADS = 8
WH = 8
WW = 16
SH = 4
SW = 8


EPSILON = 1e-05
MASKED = -1e30


def padded(shard, sides, width):
    for axis, dim in sides:
        size, length = (lax.axis_size(axis), shard.shape[dim])
        up = [(i, (i + 1) % size) for i in range(size - 1)]
        down = [(j, i) for i, j in up]
        last = lax.slice_in_dim(shard, length - width, length, axis=dim)
        first = lax.slice_in_dim(shard, 0, width, axis=dim)
        before = lax.ppermute(last, axis, up)
        after = lax.ppermute(first, axis, down)
        shard = jnp.concatenate([before, shard, after], axis=dim)
    return shard


def normalize(update):
    average = jnp.mean(update, axis=-1, keepdims=True)
    centered = update - average
    spread = jnp.mean(centered * centered, axis=-1, keepdims=True)
    inverse = lax.rsqrt(spread + EPSILON)
    return (centered * inverse, inverse)


def window_pattern(lon_count):
    query_index = jnp.arange(WH * lon_count, dtype=jnp.int32)
    key_index = jnp.arange(2 * WH * lon_count, dtype=jnp.int32)
    query_row = query_index // lon_count
    query_col = query_index % lon_count
    key_row = key_index // lon_count
    key_col = key_index % lon_count
    lat_same = ((query_row + SH) // WH)[:, None] == (key_row // WH)[None, :]
    lon_same = ((query_col + SW) // WW)[:, None] == ((key_col + SW) // WW)[None, :]
    self_key = ((query_row + SH)[:, None] == key_row[None, :]) & (
        query_col[:, None] == key_col[None, :]
    )
    return (lat_same & lon_same, self_key)


def attend(queries, keyvals, usable):
    row_count, lon_count, feature = queries.shape
    blocks = row_count // WH
    head_dim = feature // HEADS
    query_blocks = queries.reshape(blocks, WH * lon_count, HEADS, head_dim)
    kv_blocks = keyvals.reshape(blocks + 1, WH * lon_count, 2, HEADS, head_dim)
    key_pairs = jnp.concatenate([kv_blocks[:-1], kv_blocks[1:]], axis=1)
    use_blocks = usable.reshape(blocks + 1, WH * lon_count)
    use_pairs = jnp.concatenate([use_blocks[:-1], use_blocks[1:]], axis=1)
    inside, self_key = window_pattern(lon_count)
    allowed = inside[None] & (use_pairs[:, None, :] | self_key[None])
    scores = jnp.einsum(
        "nqhd,nkhd->nhqk", query_blocks, key_pairs[:, :, 0], preferred_element_type=jnp.float32
    ) * head_dim ** (-0.5)
    scores = jnp.where(allowed[:, None], scores, MASKED)
    highest = jnp.max(scores, axis=-1, keepdims=True)
    weights = jnp.exp(scores - highest)
    attn_prob = (weights / jnp.sum(weights, axis=-1, keepdims=True)).astype(jnp.bfloat16)
    mixture = jnp.einsum(
        "nhqk,nkhd->nqhd", attn_prob, key_pairs[:, :, 1], preferred_element_type=jnp.float32
    )
    return mixture.reshape(row_count, lon_count, feature).astype(jnp.bfloat16)


def guarded(active, function, operands):

    def skipped(values):
        return jax.tree.map(jnp.zeros_like, function(values))

    return lax.cond(active, function, skipped, operands)


def project(joined, merge_full, qkv_full, gain_full):
    update = jnp.einsum("rwj,jd->rwd", joined, merge_full, preferred_element_type=jnp.float32)
    normed, inverse = normalize(update)
    hidden = (normed * gain_full.astype(jnp.float32)).astype(jnp.bfloat16)
    projected = jnp.einsum("rwd,de->rwe", hidden, qkv_full, preferred_element_type=jnp.float32)
    feature = update.shape[-1]
    queries = projected[..., :feature].astype(jnp.bfloat16)
    keyvals = projected[..., feature:].astype(jnp.bfloat16)
    return (update, normed, inverse, hidden, queries, keyvals)


def section_forward(active, joined, usable, merge_full, qkv_full, gain_full, out_full):
    update, normed, inverse, hidden, queries, own_keys = guarded(
        active, lambda rows_own: project(rows_own, merge_full, qkv_full, gain_full), joined
    )
    keyvals = padded(own_keys, (("band", 0),), SH)

    def finish(operands):
        update_in, query_in, keyval_in, usable_in = operands
        mixture = attend(query_in, keyval_in, usable_in)
        result = (
            update_in
            + jnp.einsum("rwd,de->rwe", mixture, out_full, preferred_element_type=jnp.float32)
        ).astype(jnp.bfloat16)
        return (mixture, result)

    mixture, result = guarded(active, finish, (update, queries, keyvals, usable))
    return (result, (joined, normed, inverse, hidden, queries, keyvals, mixture))


def attend_back(out_full, operands):
    grad_out, queries, keyvals, mixture, usable = operands
    grad_mixture = jnp.einsum(
        "rwe,de->rwd", grad_out, out_full, preferred_element_type=jnp.float32
    ).astype(jnp.bfloat16)
    unused, pull_back = jax.vjp(
        lambda query_in, keyval_in: attend(query_in, keyval_in, usable), queries, keyvals
    )
    grad_query, grad_keyval = pull_back(grad_mixture)
    grad_outw = jnp.einsum("rwd,rwe->de", mixture, grad_out, preferred_element_type=jnp.float32)
    return (grad_query, grad_keyval, grad_outw)


def fold_rims(grad_keyval, row_count):
    rim_rows = jnp.concatenate([grad_keyval[:SH], grad_keyval[SH + row_count :]], axis=0)
    returned = padded(rim_rows, (("band", 0),), SH)
    own_part = grad_keyval[SH : SH + row_count].astype(jnp.float32)
    return jnp.concatenate(
        [
            own_part[:SH] + returned[:SH].astype(jnp.float32),
            own_part[SH : row_count - SH],
            own_part[row_count - SH :] + returned[3 * SH :].astype(jnp.float32),
        ],
        axis=0,
    ).astype(jnp.bfloat16)


def back_core(qkv_full, gain_full, grad_query, grad_keyown, grad_out, normed, inverse):
    grad_proj = jnp.concatenate([grad_query, grad_keyown], axis=-1)
    grad_hidden = jnp.einsum("rwe,de->rwd", grad_proj, qkv_full, preferred_element_type=jnp.float32)
    grad_normed = grad_hidden * gain_full.astype(jnp.float32)
    grad_update = (
        grad_out.astype(jnp.float32)
        + inverse
        * (
            grad_normed
            - jnp.mean(grad_normed, axis=-1, keepdims=True)
            - normed * jnp.mean(grad_normed * normed, axis=-1, keepdims=True)
        )
    ).astype(jnp.bfloat16)
    return (grad_proj, grad_hidden, grad_update)


def body(fields, cell_mask, merge_weight, qkv_weight, out_weight, norm_gain, out_cotangent):
    merge_rows, qkv_rows, out_rows, gain_rows = (
        lax.all_gather(merge_weight, "dp", axis=1, tiled=True),
        lax.all_gather(qkv_weight, "dp", axis=1, tiled=True),
        lax.all_gather(out_weight, "dp", axis=1, tiled=True),
        lax.all_gather(norm_gain, "dp", axis=1, tiled=True),
    )
    merge_full = merge_rows[0]
    qkv_full = qkv_rows[0]
    inputs = fields[0]
    cotangent = out_cotangent[0]
    micro_count, row_count, lon_count, feature = inputs.shape
    mask_ext = padded(cell_mask[0], (("band", 1),), SH)
    usable_ext = mask_ext == 1
    section_count = lax.axis_size("segment")
    half_count = section_count // 2
    section_rank = lax.axis_index("segment")
    merge_all, qkv_all, out_all, gain_all = (
        lax.all_gather(merge_rows, "segment", axis=0, tiled=True),
        lax.all_gather(qkv_rows, "segment", axis=0, tiled=True),
        lax.all_gather(out_rows, "segment", axis=0, tiled=True),
        lax.all_gather(gain_rows, "segment", axis=0, tiled=True),
    )
    local_count = micro_count // section_count
    always = jnp.array(True)
    shipped = [[] for index in range(section_count)]
    pick = section_rank * local_count + 0
    inputs_now = lax.dynamic_index_in_dim(inputs, pick, 0, keepdims=False)
    cotangent_now = lax.dynamic_index_in_dim(cotangent, pick, 0, keepdims=False)
    usable_now = lax.dynamic_index_in_dim(usable_ext, pick, 0, keepdims=False)
    outputs = []
    records = []
    for index in range(section_count):
        chain_in = inputs_now if index == 0 else outputs[index - 1]
        side_in = inputs_now if index < half_count else outputs[section_count - 1 - index]
        joined = jnp.concatenate([chain_in, side_in], axis=-1)
        result, record = section_forward(
            always,
            joined,
            usable_now,
            merge_all[index],
            qkv_all[index],
            gain_all[index],
            out_all[index],
        )
        outputs.append(result)
        records.append(record)
    flows = [None] * section_count
    for index in range(section_count - 1, -1, -1):
        grad_out = (
            cotangent_now if index == section_count - 1 else flows[index].astype(jnp.bfloat16)
        )
        joined, normed, inverse, hidden, queries, keyvals, mixture = records[index]
        grad_query, grad_keyval, unused = attend_back(
            out_all[index], (grad_out, queries, keyvals, mixture, usable_now)
        )
        grad_keyown = fold_rims(grad_keyval, row_count)
        grad_proj, unused, grad_update = back_core(
            qkv_all[index], gain_all[index], grad_query, grad_keyown, grad_out, normed, inverse
        )
        grad_joined = jnp.einsum(
            "rwd,jd->rwj", grad_update, merge_all[index], preferred_element_type=jnp.float32
        )
        grad_chain = grad_joined[..., :feature].astype(jnp.bfloat16).astype(jnp.float32)
        grad_side = grad_joined[..., feature:].astype(jnp.bfloat16).astype(jnp.float32)
        if index > 0:
            flows[index - 1] = grad_chain
        if index >= half_count:
            target = section_count - 1 - index
            flows[target] = flows[target] + grad_side
        shipped[index].append(
            (outputs[index], joined, grad_update, hidden, grad_proj, mixture, grad_out)
        )
    packed = tuple(
        (
            jnp.stack([jnp.stack([shipped[index][0][field]]) for index in range(section_count)])
            for field in range(7)
        )
    )
    home = (
        lax.all_to_all(packed[0], "segment", split_axis=0, concat_axis=1, tiled=True),
        lax.all_to_all(packed[1], "segment", split_axis=0, concat_axis=1, tiled=True),
        lax.all_to_all(packed[2], "segment", split_axis=0, concat_axis=1, tiled=True),
        lax.all_to_all(packed[3], "segment", split_axis=0, concat_axis=1, tiled=True),
        lax.all_to_all(packed[4], "segment", split_axis=0, concat_axis=1, tiled=True),
        lax.all_to_all(packed[5], "segment", split_axis=0, concat_axis=1, tiled=True),
        lax.all_to_all(packed[6], "segment", split_axis=0, concat_axis=1, tiled=True),
    )
    joined_all, grad_update_all, hidden_all, grad_proj_all, mixture_all, grad_out_all = [
        part[0] for part in home[1:]
    ]
    grad_merge = jnp.einsum(
        "mrwj,mrwd->jd", joined_all, grad_update_all, preferred_element_type=jnp.float32
    )
    grad_qkv = jnp.einsum(
        "mrwd,mrwe->de", hidden_all, grad_proj_all, preferred_element_type=jnp.float32
    )
    grad_outw = jnp.einsum(
        "mrwd,mrwe->de", mixture_all, grad_out_all, preferred_element_type=jnp.float32
    )
    update_all = jnp.einsum(
        "mrwj,jd->mrwd", joined_all, merge_full, preferred_element_type=jnp.float32
    )
    normed_all, unused = normalize(update_all)
    grad_hidden_all = jnp.einsum(
        "mrwe,de->mrwd", grad_proj_all, qkv_full, preferred_element_type=jnp.float32
    )
    grad_gain = jnp.sum(grad_hidden_all * normed_all, axis=(0, 1, 2))
    grad_sums = (grad_merge, grad_qkv, grad_outw, grad_gain)
    section_home = home[0][None]
    merge_part_sum, qkv_part_sum, out_part_sum, gain_part_sum = (
        lax.psum_scatter(
            grad_sums[0][None].astype(jnp.bfloat16), "dp", scatter_dimension=1, tiled=True
        ).astype(jnp.float32),
        lax.psum_scatter(
            grad_sums[1][None].astype(jnp.bfloat16), "dp", scatter_dimension=1, tiled=True
        ).astype(jnp.float32),
        lax.psum_scatter(
            grad_sums[2][None].astype(jnp.bfloat16), "dp", scatter_dimension=1, tiled=True
        ).astype(jnp.float32),
        lax.psum_scatter(
            grad_sums[3][None].astype(jnp.bfloat16), "dp", scatter_dimension=1, tiled=True
        ).astype(jnp.float32),
    )
    merge_grad, qkv_grad, out_grad, gain_grad = (
        lax.psum(merge_part_sum.astype(jnp.bfloat16), "band").astype(jnp.float32),
        lax.psum(qkv_part_sum.astype(jnp.bfloat16), "band").astype(jnp.float32),
        lax.psum(out_part_sum.astype(jnp.bfloat16), "band").astype(jnp.float32),
        lax.psum(gain_part_sum.astype(jnp.bfloat16), "band").astype(jnp.float32),
    )
    return (section_home, merge_grad, qkv_grad, out_grad, gain_grad)


def solution(mesh):
    return jax.shard_map(
        body,
        mesh=mesh,
        in_specs=(
            P("dp", None, "band", None, None),
            P("dp", None, "band", None),
            P("segment", "dp", None),
            P("segment", "dp", None),
            P("segment", "dp", None),
            P("segment", "dp"),
            P("dp", None, "band", None, None),
        ),
        out_specs=(
            P("segment", "dp", None, "band", None, None),
            P("segment", "dp", None),
            P("segment", "dp", None),
            P("segment", "dp", None),
            P("segment", "dp"),
        ),
        check_vma=False,
    )
```

profile of v0, /device:TPU:0, one launch (start us, length us, event | category | flops | bytes accessed | tf_op | source)
XLA Modules:
  0.0 377.2 jit_solution(2174182986141230632)
XLA Ops:
  8.8 30.4 %all-gather.7.cloned.1.call-done = bf16[1,1024,512]{2,1,0:T(8,128)(2,1)} async-done(((bf16[1,256,512]{2,1,0:T(8,128)(2,1)}), bf16[1,1024,512]{2,1,0:T(8,128)(2,1)}) %all-gather.7.cloned.1.call-update) | async-done | bytes 1048592 | tf_op jit(solution)/shard_map/all_gather | solution.py:160
  39.2 32.6 %all-gather.11.cloned.1.call-done = bf16[1,512,1536]{2,1,0:T(8,128)(2,1)} async-done(((bf16[1,128,1536]{2,1,0:T(8,128)(2,1)}), bf16[1,512,1536]{2,1,0:T(8,128)(2,1)}) %all-gather.11.cloned.1.call-update) | async-done | bytes 1572880 | tf_op jit(solution)/shard_map/all_gather | solution.py:161
  73.2 4.5 %collective-permute-start.2 = (s32[2,4,16]{2,1,0:T(4,128)S(1)}, s32[2,4,16]{2,1,0:T(4,128)S(1)}, u32[]{:S(2)}, u32[]{:S(2)}) collective-permute-start(s32[2,4,16]{2,1,0:T(4,128)S(1)} %get-tuple-element.47), channel_id=1, source_target_pairs={{0,1},{1,2},{2,3},{4,5},{5,6},{6,7},{8,9},{9,10},{10,11},{12,13},{... | collective-permute-start | bytes 1544 | tf_op jit(solution)/shard_map/ppermute | solution.py:24
  77.8 10.6 %all_gather.30 = bf16[1,512,512]{2,1,0:T(8,128)(2,1)} all-gather(bf16[1,128,512]{2,1,0:T(8,128)(2,1)S(1)} %copy-done.33), channel_id=1, replica_groups=mesh['dp'=4,'segment'=2,'band'=4] {'dp'}, dimensions={1}, use_global_device_ids=true | all-gather | bytes 655360 | tf_op jit(solution)/shard_map/all_gather | solution.py:162
  88.5 7.1 %all_gather.26 = bf16[1,512]{1,0:T(2,128)(2,1)S(1)} all-gather(bf16[1,128]{1,0:T(2,128)(2,1)S(1)} %copy-done.44), channel_id=1, replica_groups=mesh['dp'=4,'segment'=2,'band'=4] {'dp'}, dimensions={1}, use_global_device_ids=true | all-gather | bytes 1280 | tf_op jit(solution)/shard_map/all_gather | solution.py:163
  95.6 1.8 all-gather
  98.5 1.6 fusion.133
  100.4 1.8 convolution_convert_fusion.1
  102.3 3.4 collective-permute-start
  107.0 3.3 all-gather.15.cloned.1.call-done
  117.3 1.4 fusion.23
  118.7 1.6 fusion.135
  125.8 3.4 collective-permute-start.4
  129.2 1.5 collective-permute-start.5
  131.2 1.4 collective-permute-done.4
  132.7 3.8 %collective-permute-done.5 = bf16[4,16,1024]{2,1,0:T(8,128)(2,1)S(1)} collective-permute-done((bf16[4,16,1024]{2,1,0:T(8,128)(2,1)S(1)}, bf16[4,16,1024]{2,1,0:T(8,128)(2,1)S(1)}, u32[]{:S(2)}, u32[]{:S(2)}) %collective-permute-start.5) | collective-permute-done | bytes 131104 | tf_op jit(solution)/shard_map/ppermute | solution.py:25
  136.5 1.7 pad_maximum_fusion.4
  144.3 1.7 fusion.19
  146.0 1.6 fusion.28
  149.3 4.1 %all-to-all-start.5 = ((bf16[2,1,8,16,512]{4,3,2,1,0:T(8,128)(2,1)}), bf16[2,1,8,16,512]{4,3,2,1,0:T(8,128)(2,1)}, u32[]{:S(2)}, u32[]{:S(2)}) async-start(bf16[2,1,8,16,512]{4,3,2,1,0:T(8,128)(2,1)} %pad_maximum_fusion.13), calls=%async_computation.7 | async-start | bytes 524288 | tf_op jit(solution)/shard_map/all_to_all | solution.py:243
  156.7 1.8 copy.63
  158.5 1.5 reshape.688
  161.1 3.4 collective-permute-start.6
  164.4 1.5 collective-permute-start.7
  167.8 4.1 %collective-permute-done.7 = bf16[4,16,1024]{2,1,0:T(8,128)(2,1)S(1)} collective-permute-done((bf16[4,16,1024]{2,1,0:T(8,128)(2,1)S(1)}, bf16[4,16,1024]{2,1,0:T(8,128)(2,1)S(1)}, u32[]{:S(2)}, u32[]{:S(2)}) %collective-permute-start.7) | collective-permute-done | bytes 131104 | tf_op jit(solution)/shard_map/ppermute | solution.py:25
  172.0 2.3 fusion.126
  178.3 1.7 fusion.29
  183.2 3.4 collective-permute-start.8
  189.1 4.4 %collective-permute-done.9 = bf16[4,16,1024]{2,1,0:T(8,128)(2,1)S(1)} collective-permute-done((bf16[4,16,1024]{2,1,0:T(8,128)(2,1)S(1)}, bf16[4,16,1024]{2,1,0:T(8,128)(2,1)S(1)}, u32[]{:S(2)}, u32[]{:S(2)}) %collective-permute-start.9) | collective-permute-done | bytes 131104 | tf_op jit(solution)/shard_map/ppermute | solution.py:25
  193.5 2.2 fusion.125
  196.0 3.9 %all_to_all.28 = bf16[2,1,8,16,512]{4,3,2,1,0:T(8,128)(2,1)S(1)} all-to-all(bf16[2,1,8,16,512]{4,3,2,1,0:T(8,128)(2,1)S(1)} %pad_maximum_fusion.14), channel_id=1, replica_groups=mesh['dp'=4,'segment'=2,'band'=4] {'segment'}, dimensions={0} | all-to-all | bytes 524288 | tf_op jit(solution)/shard_map/all_to_all | solution.py:244
  199.9 2.1 fusion.10
  203.0 3.5 all-to-all-start.1
  206.5 1.6 all-to-all-done.1
  208.2 3.9 %all_to_all.29 = bf16[2,1,8,16,512]{4,3,2,1,0:T(8,128)(2,1)S(1)} all-to-all(bf16[2,1,8,16,512]{4,3,2,1,0:T(8,128)(2,1)S(1)} %pad_maximum_fusion.11), channel_id=1, replica_groups=mesh['dp'=4,'segment'=2,'band'=4] {'segment'}, dimensions={0} | all-to-all | bytes 524288 | tf_op jit(solution)/shard_map/all_to_all | solution.py:240
  212.1 1.5 fusion.6
  214.4 3.4 all-to-all-start.3
  220.1 4.4 %all_to_all.30 = bf16[2,1,8,16,1536]{4,3,2,1,0:T(8,128)(2,1)S(1)} all-to-all(bf16[2,1,8,16,1536]{4,3,2,1,0:T(8,128)(2,1)S(1)} %pad_maximum_fusion), channel_id=1, replica_groups=mesh['dp'=4,'segment'=2,'band'=4] {'segment'}, dimensions={0} | all-to-all | bytes 1572864 | tf_op jit(solution)/shard_map/all_to_all | solution.py:242
  224.4 2.8 fusion.1
  230.3 26.1 %reduce-scatter.7.cloned.1.call-done = bf16[1,256,512]{2,1,0:T(8,128)(2,1)} async-done(((bf16[1,1024,512]{2,1,0:T(8,128)(2,1)}), bf16[1,256,512]{2,1,0:T(8,128)(2,1)}) %reduce-scatter.7.cloned.1.call-update) | async-done | bytes 262160 | tf_op jit(solution)/shard_map/reduce_scatter | solution.py:269
  256.3 34.2 %reduce-scatter.9.cloned.1.call-done = bf16[1,128,1536]{2,1,0:T(8,128)(2,1)} async-done(((bf16[1,512,1536]{2,1,0:T(8,128)(2,1)}), bf16[1,128,1536]{2,1,0:T(8,128)(2,1)}) %reduce-scatter.9.cloned.1.call-update) | async-done | bytes 393232 | tf_op jit(solution)/shard_map/reduce_scatter | solution.py:272
  291.0 3.9 %all_to_all.31 = bf16[2,1,8,16,512]{4,3,2,1,0:T(8,128)(2,1)S(1)} all-to-all(bf16[2,1,8,16,512]{4,3,2,1,0:T(8,128)(2,1)S(1)} %pad_maximum_fusion.10), channel_id=1, replica_groups=mesh['dp'=4,'segment'=2,'band'=4] {'segment'}, dimensions={0} | all-to-all | bytes 524288 | tf_op jit(solution)/shard_map/all_to_all | solution.py:238
  295.0 23.0 %reduce-scatter.13.cloned.1.call-done = bf16[128,1]{1,0:T(8,128)(2,1)} async-done(((bf16[512,1]{1,0:T(8,128)(2,1)}), bf16[128,1]{1,0:T(8,128)(2,1)}) %reduce-scatter.13.cloned.1.call-update) | async-done | bytes 272
  318.8 11.7 %psum.31 = bf16[1,128]{1,0:T(2,128)(2,1)S(1)} all-reduce(bf16[1,128]{1,0:T(2,128)(2,1)S(1)} %copy.77), channel_id=1, replica_groups=mesh['dp'=4,'segment'=2,'band'=4] {'band'}, use_global_device_ids=true, to_apply=%region_28.29 | all-reduce | flops 128 | bytes 512 | tf_op jit(solution)/shard_map/psum | solution.py:286
  331.0 33.2 %all-reduce.11.cloned.1.call-done = (bf16[1,256,512]{2,1,0:T(8,128)(2,1)}, bf16[1,128,1536]{2,1,0:T(8,128)(2,1)}, bf16[1,128,512]{2,1,0:T(8,128)(2,1)}) async-done(((bf16[1,256,512]{2,1,0:T(8,128)(2,1)}, bf16[1,128,1536]{2,1,0:T(8,128)(2,1)}, bf16[1,128,512]{2,1,0:T(8,128)(2,1)}), (bf16[1,256,512]{2,1,0:T(8,128)(2,1)}, bf16[1,128,1536]{2,1,0:T(8,128)(2,1)}, ...) | async-done | bytes 786448 | tf_op jit(solution)/shard_map/psum | solution.py:283
  364.3 1.8 convert_element_type.336
  366.1 1.6 convert_element_type.344
  367.7 2.0 convert_element_type.339
  (244 shorter events, 51.2 us)
Async XLA Ops:
  7.2 90.8 %copy-start = (bf16[1,2,8,16,512]{4,3,2,1,0:T(8,128)(2,1)S(1)}, bf16[1,2,8,16,512]{4,3,2,1,0:T(8,128)(2,1)}, u32[]{:S(2)}) copy-start(bf16[1,2,8,16,512]{4,3,2,1,0:T(8,128)(2,1)} %param.7) | copy-start | bytes 786436
  7.2 64.7 %copy-start.35 = (s32[1,2,8,16]{3,2,1,0:T(8,128)S(1)}, s32[1,2,8,16]{3,2,1,0:T(8,128)}, u32[]{:S(2)}) copy-start(s32[1,2,8,16]{3,2,1,0:T(8,128)} %param.8) | copy-start | bytes 3076
  7.2 70.6 %copy-start.33 = (bf16[1,128,512]{2,1,0:T(8,128)(2,1)S(1)}, bf16[1,128,512]{2,1,0:T(8,128)(2,1)}, u32[]{:S(2)}) copy-start(bf16[1,128,512]{2,1,0:T(8,128)(2,1)} %param.11) | copy-start | bytes 393220
  7.2 31.9 %all-gather.7.cloned.1.call-start = ((), (), s32[]{:S(2)}) async-start(), calls=%async_computation.11 | async-start | bytes 1310720 | tf_op jit(solution)/shard_map/all_gather | solution.py:160
  7.9 80.5 %copy-start.44 = (bf16[1,128]{1,0:T(2,128)(2,1)S(1)}, bf16[1,128]{1,0:T(2,128)(2,1)}, u32[]{:S(2)}) copy-start(bf16[1,128]{1,0:T(2,128)(2,1)} %param.12) | copy-start | bytes 772
  7.9 63.9 %all-gather.11.cloned.1.call-start = ((), (), s32[]{:S(2)}) async-start(), calls=%async_computation.13 | async-start | bytes 1966080 | tf_op jit(solution)/shard_map/all_gather | solution.py:161
  8.7 89.3 %copy-start.28 = (bf16[1,2,8,16,512]{4,3,2,1,0:T(8,128)(2,1)S(1)}, bf16[1,2,8,16,512]{4,3,2,1,0:T(8,128)(2,1)}, u32[]{:S(2)}) copy-start(bf16[1,2,8,16,512]{4,3,2,1,0:T(8,128)(2,1)} %param.13) | copy-start | bytes 786436
  8.7 89.8 %all-gather.9.cloned.1.call-start = ((), (), s32[]{:S(2)}) async-start(), calls=%async_computation.12 | async-start | bytes 3145728 | tf_op jit(solution)/shard_map/all_gather | solution.py:176
  39.1 61.2 %all-gather.13.cloned.1.call-start = ((), (), s32[]{:S(2)}) async-start(), calls=%async_computation.14 | async-start | bytes 4718592 | tf_op jit(solution)/shard_map/all_gather | solution.py:177
  71.8 38.5 %all-gather.15.cloned.1.call-start = ((), (), s32[]{:S(2)}) async-start(), calls=%async_computation.15 | async-start | bytes 1572864 | tf_op jit(solution)/shard_map/all_gather | solution.py:178
  71.9 26.2 %collective-permute-start.3 = (s32[2,4,16]{2,1,0:T(4,128)S(1)}, s32[2,4,16]{2,1,0:T(4,128)S(1)}, u32[]{:S(2)}, u32[]{:S(2)}) collective-permute-start(s32[2,4,16]{2,1,0:T(4,128)S(1)} %get-tuple-element.46), channel_id=1, source_target_pairs={{1,0},{2,1},{3,2},{5,4},{6,5},{7,6},{9,8},{10,9},{11,10},{13,12},{... | collective-permute-start | bytes 1544 | tf_op jit(solution)/shard_map/ppermute | solution.py:25
  73.2 24.9 %collective-permute-start.2 = (s32[2,4,16]{2,1,0:T(4,128)S(1)}, s32[2,4,16]{2,1,0:T(4,128)S(1)}, u32[]{:S(2)}, u32[]{:S(2)}) collective-permute-start(s32[2,4,16]{2,1,0:T(4,128)S(1)} %get-tuple-element.47), channel_id=1, source_target_pairs={{0,1},{1,2},{2,3},{4,5},{5,6},{6,7},{8,9},{9,10},{10,11},{12,13},{... | collective-permute-start | bytes 1544 | tf_op jit(solution)/shard_map/ppermute | solution.py:24
  98.0 4.2 %copy-start.41 = (f32[1,1,512]{2,1,0:T(1,128)}, f32[1,1,512]{2,1,0:T(1,128)S(1)}, u32[]{:S(2)}) copy-start(f32[1,1,512]{2,1,0:T(1,128)S(1)} %get-tuple-element.49) | copy-start | bytes 6148
  98.0 4.2 %copy-start.13 = (bf16[8,16,512]{2,1,0:T(8,128)(2,1)}, bf16[8,16,512]{2,1,0:T(8,128)(2,1)S(1)}, u32[]{:S(2)}) copy-start(bf16[8,16,512]{2,1,0:T(8,128)(2,1)S(1)} %dynamic-slice_bitcast_fusion) | copy-start | bytes 393220
  98.0 12.3 %copy-start.16 = (bf16[1,1,8,16,512]{4,3,2,1,0:T(8,128)(2,1)}, bf16[1,1,8,16,512]{4,3,2,1,0:T(8,128)(2,1)S(1)}, u32[]{:S(2)}) copy-start(bf16[1,1,8,16,512]{4,3,2,1,0:T(8,128)(2,1)S(1)} %constant_dynamic-slice_fusion) | copy-start | bytes 393220
  98.5 16.0 %copy-start.25 = (pred[128,256]{1,0:T(8,128)(4,1)}, pred[128,256]{1,0:T(8,128)(4,1)S(1)}, u32[]{:S(2)}) copy-start(pred[128,256]{1,0:T(8,128)(4,1)S(1)} %or_and_fusion) | copy-start | bytes 98308
  100.1 17.2 %copy-start.6 = (f32[8,16,512]{2,1,0:T(8,128)}, f32[8,16,512]{2,1,0:T(8,128)S(1)}, u32[]{:S(2)}) copy-start(f32[8,16,512]{2,1,0:T(8,128)S(1)} %get-tuple-element.53) | copy-start | bytes 786436
  102.3 10.2 %collective-permute-start = (bf16[4,16,1024]{2,1,0:T(8,128)(2,1)S(1)}, bf16[4,16,1024]{2,1,0:T(8,128)(2,1)S(1)}, u32[]{:S(2)}, u32[]{:S(2)}) collective-permute-start(bf16[4,16,1024]{2,1,0:T(8,128)(2,1)S(1)} %get-tuple-element.35), channel_id=1, source_target_pairs={{0,1},{1,2},{2,3},{4,5},{5,6},{6,7},{8,9},{9,10},{10,11},{12,13},{... | collective-permute-start | bytes 393224 | tf_op jit(solution)/shard_map/ppermute | solution.py:24
  105.7 7.2 %collective-permute-start.1 = (bf16[4,16,1024]{2,1,0:T(8,128)(2,1)S(1)}, bf16[4,16,1024]{2,1,0:T(8,128)(2,1)S(1)}, u32[]{:S(2)}, u32[]{:S(2)}) collective-permute-start(bf16[4,16,1024]{2,1,0:T(8,128)(2,1)S(1)} %get-tuple-element.36), channel_id=1, source_target_pairs={{1,0},{2,1},{3,2},{5,4},{6,5},{7,6},{9,8},{10,9},{11,10},{13,12},{... | collective-permute-start | bytes 393224 | tf_op jit(solution)/shard_map/ppermute | solution.py:25
  117.3 3.3 copy-start.45
  118.7 3.0 copy-start.9
  120.4 4.5 %copy-start.4 = (f32[8,16,512]{2,1,0:T(8,128)}, f32[8,16,512]{2,1,0:T(8,128)S(1)}, u32[]{:S(2)}) copy-start(f32[8,16,512]{2,1,0:T(8,128)S(1)} %get-tuple-element.57) | copy-start | bytes 786436
  125.8 6.9 %collective-permute-start.4 = (bf16[4,16,1024]{2,1,0:T(8,128)(2,1)}, bf16[4,16,1024]{2,1,0:T(8,128)(2,1)S(1)}, u32[]{:S(2)}, u32[]{:S(2)}) collective-permute-start(bf16[4,16,1024]{2,1,0:T(8,128)(2,1)} %get-tuple-element.33), channel_id=1, source_target_pairs={{0,1},{1,2},{2,3},{4,5},{5,6},{6,7},{8,9},{9,10},{10,11},{12,13},{... | collective-permute-start | bytes 393224 | tf_op jit(solution)/shard_map/ppermute | solution.py:24
  129.2 7.3 %collective-permute-start.5 = (bf16[4,16,1024]{2,1,0:T(8,128)(2,1)S(1)}, bf16[4,16,1024]{2,1,0:T(8,128)(2,1)S(1)}, u32[]{:S(2)}, u32[]{:S(2)}) collective-permute-start(bf16[4,16,1024]{2,1,0:T(8,128)(2,1)S(1)} %get-tuple-element.34), channel_id=1, source_target_pairs={{1,0},{2,1},{3,2},{5,4},{6,5},{7,6},{9,8},{10,9},{11,10},{13,12},{... | collective-permute-start | bytes 393224 | tf_op jit(solution)/shard_map/ppermute | solution.py:25
  148.3 7.5 %copy-start.2 = (bf16[1,128,8,64]{3,2,1,0:T(8,128)(2,1)}, bf16[1,128,8,64]{3,2,1,0:T(8,128)(2,1)S(1)}, u32[]{:S(2)}) copy-start(bf16[1,128,8,64]{3,2,1,0:T(8,128)(2,1)S(1)} %copy.58) | copy-start | bytes 393220
  149.3 46.7 %all-to-all-start.5 = ((bf16[2,1,8,16,512]{4,3,2,1,0:T(8,128)(2,1)}), bf16[2,1,8,16,512]{4,3,2,1,0:T(8,128)(2,1)}, u32[]{:S(2)}, u32[]{:S(2)}) async-start(bf16[2,1,8,16,512]{4,3,2,1,0:T(8,128)(2,1)} %pad_maximum_fusion.13), calls=%async_computation.7 | async-start | bytes 524288 | tf_op jit(solution)/shard_map/all_to_all | solution.py:243
  153.4 76.8 %reduce-scatter.11.cloned.1.call-start = ((), (), s32[]{:S(2)}) async-start(), calls=%async_computation.18 | async-start | bytes 655360 | tf_op jit(solution)/shard_map/reduce_scatter | solution.py:275
  160.0 12.0 %copy-start.5 = (f32[8,16,512]{2,1,0:T(8,128)S(1)}, f32[8,16,512]{2,1,0:T(8,128)}, u32[]{:S(2)}) copy-start(f32[8,16,512]{2,1,0:T(8,128)} %copy-done.4) | copy-start | bytes 786436
  160.0 12.0 %copy-start.39 = (f32[8,16]{1,0:T(8,128)S(1)}, f32[8,16]{1,0:T(8,128)}, u32[]{:S(2)}) copy-start(f32[8,16]{1,0:T(8,128)} %copy-done.38) | copy-start | bytes 1540
  160.0 12.0 %copy-start.43 = (f32[1,1,512]{2,1,0:T(1,128)S(1)}, f32[1,1,512]{2,1,0:T(1,128)}, u32[]{:S(2)}) copy-start(f32[1,1,512]{2,1,0:T(1,128)} %get-tuple-element.48) | copy-start | bytes 6148
  161.1 6.7 %collective-permute-start.6 = (bf16[4,16,1024]{2,1,0:T(8,128)(2,1)S(1)}, bf16[4,16,1024]{2,1,0:T(8,128)(2,1)S(1)}, u32[]{:S(2)}, u32[]{:S(2)}) collective-permute-start(bf16[4,16,1024]{2,1,0:T(8,128)(2,1)S(1)} %get-tuple-element.29), channel_id=1, source_target_pairs={{0,1},{1,2},{2,3},{4,5},{5,6},{6,7},{8,9},{9,10},{10,11},{12,13},{... | collective-permute-start | bytes 393224 | tf_op jit(solution)/shard_map/ppermute | solution.py:24
  164.4 7.5 %collective-permute-start.7 = (bf16[4,16,1024]{2,1,0:T(8,128)(2,1)S(1)}, bf16[4,16,1024]{2,1,0:T(8,128)(2,1)S(1)}, u32[]{:S(2)}, u32[]{:S(2)}) collective-permute-start(bf16[4,16,1024]{2,1,0:T(8,128)(2,1)S(1)} %get-tuple-element.30), channel_id=1, source_target_pairs={{1,0},{2,1},{3,2},{5,4},{6,5},{7,6},{9,8},{10,9},{11,10},{13,12},{... | collective-permute-start | bytes 393224 | tf_op jit(solution)/shard_map/ppermute | solution.py:25
  167.0 7.4 %copy-start.29 = (bf16[1,2,8,16,512]{4,3,2,1,0:T(8,128)(2,1)S(1)}, bf16[1,2,8,16,512]{4,3,2,1,0:T(8,128)(2,1)}, u32[]{:S(2)}) copy-start(bf16[1,2,8,16,512]{4,3,2,1,0:T(8,128)(2,1)} %param.13) | copy-start | bytes 786436
  182.4 11.1 %copy-start.7 = (f32[8,16,512]{2,1,0:T(8,128)S(1)}, f32[8,16,512]{2,1,0:T(8,128)}, u32[]{:S(2)}) copy-start(f32[8,16,512]{2,1,0:T(8,128)} %copy-done.6) | copy-start | bytes 786436
  182.4 11.1 %copy-start.37 = (f32[8,16]{1,0:T(8,128)S(1)}, f32[8,16]{1,0:T(8,128)}, u32[]{:S(2)}) copy-start(f32[8,16]{1,0:T(8,128)} %copy-done.36) | copy-start | bytes 1540
  182.4 11.1 %copy-start.42 = (f32[1,1,512]{2,1,0:T(1,128)S(1)}, f32[1,1,512]{2,1,0:T(1,128)}, u32[]{:S(2)}) copy-start(f32[1,1,512]{2,1,0:T(1,128)} %copy-done.41) | copy-start | bytes 6148
  183.2 5.9 %collective-permute-start.8 = (bf16[4,16,1024]{2,1,0:T(8,128)(2,1)S(1)}, bf16[4,16,1024]{2,1,0:T(8,128)(2,1)S(1)}, u32[]{:S(2)}, u32[]{:S(2)}) collective-permute-start(bf16[4,16,1024]{2,1,0:T(8,128)(2,1)S(1)} %get-tuple-element.23), channel_id=1, source_target_pairs={{0,1},{1,2},{2,3},{4,5},{5,6},{6,7},{8,9},{9,10},{10,11},{12,13},{... | collective-permute-start | bytes 393224 | tf_op jit(solution)/shard_map/ppermute | solution.py:24
  186.6 6.9 %collective-permute-start.9 = (bf16[4,16,1024]{2,1,0:T(8,128)(2,1)S(1)}, bf16[4,16,1024]{2,1,0:T(8,128)(2,1)S(1)}, u32[]{:S(2)}, u32[]{:S(2)}) collective-permute-start(bf16[4,16,1024]{2,1,0:T(8,128)(2,1)S(1)} %get-tuple-element.24), channel_id=1, source_target_pairs={{1,0},{2,1},{3,2},{5,4},{6,5},{7,6},{9,8},{10,9},{11,10},{13,12},{... | collective-permute-start | bytes 393224 | tf_op jit(solution)/shard_map/ppermute | solution.py:25
  187.9 7.8 %copy-start.32 = (bf16[8,16,1024]{2,1,0:T(8,128)(2,1)S(1)}, bf16[8,16,1024]{2,1,0:T(8,128)(2,1)}, u32[]{:S(2)}) copy-start(bf16[8,16,1024]{2,1,0:T(8,128)(2,1)} %copy-done.31) | copy-start | bytes 786436
  203.0 5.2 %all-to-all-start.1 = ((bf16[2,1,8,16,1024]{4,3,2,1,0:T(8,128)(2,1)}), bf16[2,1,8,16,1024]{4,3,2,1,0:T(8,128)(2,1)S(1)}, u32[]{:S(2)}, u32[]{:S(2)}) async-start(bf16[2,1,8,16,1024]{4,3,2,1,0:T(8,128)(2,1)} %pad_maximum_fusion.1), calls=%async_computation.1 | async-start | bytes 1048576 | tf_op jit(solution)/shard_map/all_to_all | solution.py:239
  206.5 49.9 %reduce-scatter.7.cloned.1.call-start = ((), (), s32[]{:S(2)}) async-start(), calls=%async_computation.16 | async-start | bytes 1310720 | tf_op jit(solution)/shard_map/reduce_scatter | solution.py:269
  214.4 5.0 %all-to-all-start.3 = ((bf16[2,1,8,16,512]{4,3,2,1,0:T(8,128)(2,1)}), bf16[2,1,8,16,512]{4,3,2,1,0:T(8,128)(2,1)S(1)}, u32[]{:S(2)}, u32[]{:S(2)}) async-start(bf16[2,1,8,16,512]{4,3,2,1,0:T(8,128)(2,1)} %pad_maximum_fusion.12), calls=%async_computation.4 | async-start | bytes 524288 | tf_op jit(solution)/shard_map/all_to_all | solution.py:241
  217.8 72.7 %reduce-scatter.9.cloned.1.call-start = ((), (), s32[]{:S(2)}) async-start(), calls=%async_computation.17 | async-start | bytes 1966080 | tf_op jit(solution)/shard_map/reduce_scatter | solution.py:272
  224.4 2.9 copy-start.1
  227.3 90.7 %reduce-scatter.13.cloned.1.call-start = ((), (), s32[]{:S(2)}) async-start(), calls=%async_computation.19 | async-start | bytes 163840
  228.8 61.8 %copy-start.3 = (bf16[1,128,8,64]{3,2,1,0:T(8,128)(2,1)S(1)}, bf16[1,128,8,64]{3,2,1,0:T(8,128)(2,1)}, u32[]{:S(2)}) copy-start(bf16[1,128,8,64]{3,2,1,0:T(8,128)(2,1)} %copy-done.2) | copy-start | bytes 393220
  228.8 62.0 %copy-start.12 = (bf16[2,512,512]{2,1,0:T(8,128)(2,1)S(1)}, bf16[2,512,512]{2,1,0:T(8,128)(2,1)}, u32[]{:S(2)}) copy-start(bf16[2,512,512]{2,1,0:T(8,128)(2,1)} %all-gather.15.cloned.1.call-done) | copy-start | bytes 3145732
  230.2 134.1 %all-reduce.11.cloned.1.call-start = ((), (), s32[]{:S(2)}) async-start(), calls=%async_computation.20 | async-start | bytes 1572864 | tf_op jit(solution)/shard_map/psum | solution.py:283
  (22 other events, 38.6 us)
Sparse Core Ops, SparseCore 0:
  9.9 29.2 all-gather.6
  40.9 30.8 all-gather.10
  73.4 10.5 all-gather.8
  85.4 13.2 all-gather.12
  100.1 10.1 all-gather.14
  202.2 23.2 reduce-scatter.10
  228.3 27.9 reduce-scatter.6
  259.3 31.1 reduce-scatter.8
  293.8 24.1 reduce-scatter.12
  320.4 43.7 all-reduce.10
where the time goes:
time: 379 us; the launch traced here: 377 us
  waiting for transfers between devices  203 us (54%)
  blocking collectives  47.4 us (13%)
  starting transfers between devices  36.4 us (10%)
  matrix products  32 us (8%)
  local copies, waits for them, and re-layouts  23.7 us (6%)
  other arithmetic  18.8 us (5%)
  between operations  15.6 us (4%)
    reduce_scatter x1, waiting for transfers between devices, body(): lax.psum_scatter(grad_sums[1][None].astype(jnp.bfloat16), 'dp', scatter_d...  34.2 us
    psum x1, waiting for transfers between devices, body(): lax.psum(merge_part_sum.astype(jnp.bfloat16), 'band').astype(jnp.float32)  33.2 us
    all_gather x1, waiting for transfers between devices, body(): lax.all_gather(qkv_weight, 'dp', axis=1, tiled=True)  32.6 us
    all_gather x1, waiting for transfers between devices, body(): lax.all_gather(merge_weight, 'dp', axis=1, tiled=True)  30.4 us
    reduce_scatter x1, waiting for transfers between devices, body(): lax.psum_scatter(grad_sums[0][None].astype(jnp.bfloat16), 'dp', scatter_d...  26.1 us
    unnamed x11, waiting for transfers between devices  24.5 us
    ppermute x5, starting transfers between devices, padded(): before = lax.ppermute(last, axis, up)  18.1 us
    ppermute x5, waiting for transfers between devices, padded(): after = lax.ppermute(first, axis, down)  12.6 us
  transfers between devices with their start and end apart: 23, of which 16 were waited for; matrix products, arithmetic and copies ran while one was open for 10% of the time, Pallas kernels for 0%

commit v1 on v0

v1 whole, which is shorter than its diff:
```python
import functools

import jax
import jax.numpy as jnp
from jax import lax
from jax.experimental import pallas as pl
from jax.experimental.pallas import tpu as pltpu
from jax.sharding import PartitionSpec as P

HEADS = 8
WH = 8
WW = 16
SH = 4
SW = 8
PAD = 16

EPSILON = 1e-05
MASKED = -1e30

F32 = jnp.float32
BF16 = jnp.bfloat16


def dot(a, b):
    return lax.dot_general(a, b, (((1,), (0,)), ((), ())), preferred_element_type=F32)


def dot_nt(a, b):
    return lax.dot_general(a, b, (((1,), (1,)), ((), ())), preferred_element_type=F32)


def dot_tn(a, b):
    return lax.dot_general(a, b, (((0,), (0,)), ((), ())), preferred_element_type=F32)


class Copies:
    def __init__(self, sems):
        self.sems = sems
        self.used = 0

    def start(self, src, dst):
        copy = pltpu.make_async_copy(src, dst, self.sems.at[self.used])
        self.used += 1
        copy.start()
        return copy


def wait_all(copies):
    for copy in copies:
        copy.wait()


def layout(feature, shards):
    merge, rows = 2 * feature // shards, feature // shards
    first = {"merge": (0, merge), "q": (merge, rows), "gain": (merge + rows, PAD)}
    second = {"k": (0, rows), "v": (rows, rows), "out": (2 * rows, rows), "pad": (3 * rows, PAD)}
    return (first, second, merge + rows + PAD)


def load_weights(copies, me, pieces, names, dst, feature, shards):
    own, by_low, by_high, both_first, both_second = pieces
    first, second, half = layout(feature, shards)
    started = {}
    for name in names:
        started[name] = []
        for flip, ref in ((0, own), (1, by_low), (shards // 2, by_high), (shards - 1, None)):
            owner = me ^ flip
            base = 0
            if name in first:
                start, rows = first[name]
                source = both_first if ref is None else ref
            else:
                start, rows = second[name]
                source = both_second if ref is None else ref
                base = 0 if ref is None else half
            at = pl.multiple_of(owner * rows, rows)
            started[name].append(
                copies.start(source.at[pl.ds(base + start, rows)], dst[name].at[pl.ds(at, rows)])
            )
    return started


def load_tokens(copies, moved, own, dst):
    started = []
    for m in range(moved.shape[0]):
        part = moved.shape[1]
        size = own.shape[1]
        started.append(copies.start(moved.at[m], dst.at[pl.ds(m * size, part)]))
        started.append(
            copies.start(
                own.at[m, pl.ds(0, size - part)], dst.at[pl.ds(m * size + part, size - part)]
            )
        )
    return started


def full_gain(gain, shards):
    feature = gain.shape[1]
    rows = feature // shards
    parts = [gain[i * PAD : i * PAD + 1, :rows] for i in range(shards)]
    return jnp.concatenate(parts, axis=1).astype(F32)


def window_allowed(mask_row, first_band, lon_count):
    cells = mask_row.shape[1]
    query = lax.broadcasted_iota(jnp.int32, (cells, cells), 0)
    key = lax.broadcasted_iota(jnp.int32, (cells, cells), 1)
    lon_same = (query % lon_count + SW) // WW == (key % lon_count + SW) // WW
    lat_same = (query // lon_count) // SH == (key // lon_count) // SH
    inside = lon_same & (lat_same | jnp.logical_not(first_band))
    usable = jnp.broadcast_to(mask_row, (cells, cells)) == 1
    return inside & (usable | (query == key))


def stacked_heads(pair, head_dim):
    lane = lax.broadcasted_iota(jnp.int32, pair.shape, 1)
    zero = jnp.zeros_like(pair)
    return jnp.concatenate(
        [jnp.where(lane < head_dim, pair, zero), jnp.where(lane < head_dim, zero, pair)], axis=0
    )


def unstacked_heads(stacked, head_dim):
    cells = stacked.shape[0] // 2
    low, high = stacked[:cells], stacked[cells:]
    lane = lax.broadcasted_iota(jnp.int32, low.shape, 1)
    return jnp.where(lane < head_dim, low, high)


def probabilities(q_stack, k, allowed2, head_dim):
    scores = dot_nt(q_stack, k) * head_dim ** (-0.5)
    scores = jnp.where(allowed2, scores, MASKED)
    weights = jnp.exp(scores - jnp.max(scores, axis=-1, keepdims=True))
    return weights / jnp.sum(weights, axis=-1, keepdims=True)


def masks(mask, first_band, lon_count):
    out = []
    for m in range(mask.shape[0]):
        allowed = window_allowed(mask[m : m + 1, :], first_band, lon_count)
        out.append(jnp.concatenate([allowed, allowed], axis=0))
    return out


def pairs(mask_shape, feature):
    micro, cells = mask_shape
    lanes = 2 * (feature // HEADS)
    for m in range(micro):
        for p in range(feature // lanes):
            yield (m, slice(m * cells, (m + 1) * cells), p * lanes, lanes)


def attend(qkv, mix, allowed, mask_shape, feature):
    head_dim = feature // HEADS
    for m, rows, at, lanes in pairs(mask_shape, feature):
        q, k, v = (qkv[rows, i * feature + at : i * feature + at + lanes] for i in range(3))
        probs = probabilities(stacked_heads(q, head_dim), k, allowed[m], head_dim).astype(BF16)
        mixed = unstacked_heads(dot(probs, v), head_dim)
        mix[rows, at : at + lanes] = mixed.astype(BF16)


def attend_back(qkv, grad_mix, grad_proj, allowed, mask_shape, feature):
    head_dim = feature // HEADS
    for m, rows, at, lanes in pairs(mask_shape, feature):
        q, k, v = (qkv[rows, i * feature + at : i * feature + at + lanes] for i in range(3))
        q_stack = stacked_heads(q, head_dim)
        g_stack = stacked_heads(grad_mix[rows, at : at + lanes], head_dim)
        probs = probabilities(q_stack, k, allowed[m], head_dim)
        grad_probs = dot_nt(g_stack, v)
        inner = jnp.sum(grad_probs * probs, axis=-1, keepdims=True)
        grad_scores = (probs * (grad_probs - inner) * head_dim ** (-0.5)).astype(BF16)
        grad_q = unstacked_heads(dot(grad_scores, k), head_dim)
        grad_k = dot_tn(grad_scores, q_stack)
        grad_v = dot_tn(probs.astype(BF16), g_stack)
        for i, grad in enumerate((grad_q, grad_k, grad_v)):
            grad_proj[rows, i * feature + at : i * feature + at + lanes] = grad.astype(BF16)


def normalize(update):
    average = jnp.mean(update, axis=-1, keepdims=True)
    centered = update - average
    spread = jnp.mean(centered * centered, axis=-1, keepdims=True)
    inverse = lax.rsqrt(spread + EPSILON)
    return (centered * inverse, inverse)


def forward(x, w, waits, gain_of, allowed, mask_shape, normed_ref, inverse_ref, hidden, qkv, mix):
    feature = x.shape[1]
    wait_all(waits["merge"])
    tokens = x[...]
    update = dot(tokens, w["merge"][:feature]) + dot(tokens, w["merge"][feature:])
    normed, inverse = normalize(update)
    normed_ref[...] = normed
    inverse_ref[...] = jnp.broadcast_to(inverse, inverse_ref.shape)
    hidden[...] = (normed * gain_of()).astype(BF16)
    for i, name in enumerate(("q", "k", "v")):
        wait_all(waits[name])
        qkv[:, i * feature : (i + 1) * feature] = dot(hidden[...], w[name][...]).astype(BF16)
    attend(qkv, mix, allowed, mask_shape, feature)
    wait_all(waits["out"])
    return update + dot(mix[...], w["out"][...])


def backward(grad_out, w, gain, allowed, mask_shape, normed, inverse, qkv, grad_mix, grad_proj):
    feature = grad_out.shape[1]
    grad_mix[...] = dot_nt(grad_out[...], w["out"][...]).astype(BF16)
    attend_back(qkv, grad_mix, grad_proj, allowed, mask_shape, feature)
    grad_hidden = sum(
        dot_nt(grad_proj[:, i * feature : (i + 1) * feature], w[name][...])
        for i, name in enumerate(("q", "k", "v"))
    )
    normed = normed[...]
    grad_gain = jnp.sum(grad_hidden * normed, axis=0, keepdims=True)
    grad_normed = grad_hidden * gain
    centered = (
        grad_normed
        - jnp.mean(grad_normed, axis=-1, keepdims=True)
        - normed * jnp.mean(grad_normed * normed, axis=-1, keepdims=True)
    )
    grad_update = grad_out[...].astype(F32) + inverse[:, :1] * centered
    return (grad_update.astype(BF16), grad_gain)


def send_grads(copies, me, x, hidden, mix, grad_out, grad_proj, grad_update, grad_gain, dw, outs):
    feature = x.shape[1]
    p_keep, p_send, q_keep, q_send = outs
    shards = 2 * p_keep.shape[0]
    first, second, half = layout(feature, shards)
    low, high = me % 2, me // 2
    rows = feature // shards
    started = []

    def target(name, by_low, by_high):
        if name in first:
            start, size = first[name]
            ref = (p_send if by_high else p_keep).at[by_low]
        else:
            start, size = second[name]
            ref = (q_send if by_low else q_keep).at[by_high]
        return ref.at[pl.ds(start, size)]

    def emit(name, period):
        for by_high in range(2):
            for by_low in range(2):
                owner = (high ^ by_high) * 2 + (low ^ by_low)
                to = target(name, by_low, by_high)
                at = pl.multiple_of((owner * to.shape[0]) % period, to.shape[0])
                started.append(copies.start(dw[name].at[pl.ds(at, to.shape[0])], to))

    dw["out"][...] = dot_tn(mix[...], grad_out[...]).astype(BF16)
    emit("out", feature)
    for i, name in enumerate(("q", "k", "v")):
        part = grad_proj[:, i * feature : (i + 1) * feature]
        dw[name][...] = dot_tn(hidden[...], part).astype(BF16)
        emit(name, feature)
    for i in range(shards):
        part = grad_gain[:, i * rows : (i + 1) * rows].astype(BF16)
        dw["gain"][i * PAD : (i + 1) * PAD, :] = jnp.zeros((PAD, feature), BF16)
        dw["gain"][i * PAD : (i + 1) * PAD, :rows] = jnp.broadcast_to(part, (PAD, rows))
    emit("gain", shards * PAD)
    dw["pad"][...] = jnp.zeros_like(dw["pad"])
    emit("pad", PAD)
    dw["merge"][...] = dot_tn(x[...], grad_update).astype(BF16)
    emit("merge", feature)
    return started


def lon_of(cells):
    return cells // WH


def forward_kernel(place, mask, moved, own, w0, w1, w2, w3, w4, y, normed, inverse, hidden, qkv, mix,
                   x, wm, wq, wk, wv, wo, wg, y_s, normed_s, inverse_s, hidden_s, qkv_s, mix_s, sems):
    shards = wg.shape[0] // PAD
    feature = x.shape[1]

    @pl.when(place[0] == 0)
    def run():
        copies = Copies(sems)
        w = {"merge": wm, "q": wq, "k": wk, "v": wv, "out": wo, "gain": wg}
        tokens = load_tokens(copies, moved, own, x)
        names = ("merge", "gain", "q", "k", "v", "out")
        waits = load_weights(copies, place[1], (w0, w1, w2, w3, w4), names, w, feature, shards)
        allowed = masks(mask, place[2] == 0, lon_of(mask.shape[1]))
        wait_all(tokens)

        def gain_of():
            wait_all(waits["gain"])
            return full_gain(wg, shards)

        result = forward(x, w, waits, gain_of, allowed, mask.shape,
                         normed_s, inverse_s, hidden_s, qkv_s, mix_s)
        y_s[...] = result.astype(BF16)
        done = [
            copies.start(a, b)
            for a, b in ((y_s, y), (normed_s, normed), (inverse_s, inverse), (hidden_s, hidden),
                         (qkv_s, qkv), (mix_s, mix))
        ]
        wait_all(done)


def last_kernel(place, mask, moved, own, y0, w0, w1, w2, w3, w4, y_in, y, g0, pk, ps, qk, qs,
                x, g, wm, wq, wk, wv, wo, wg, y_s, g_s, normed_s, inverse_s, hidden_s, qkv_s, mix_s,
                gmix, gproj, dm, dq, dk, dv, do, dg, dz, sems):
    shards = wg.shape[0] // PAD
    feature = x.shape[1]

    @pl.when(place[0] == 1)
    def run():
        copies = Copies(sems)
        w = {"merge": wm, "q": wq, "k": wk, "v": wv, "out": wo, "gain": wg}
        x_in = copies.start(y0, x)
        names = ("merge", "gain", "q", "k", "v", "out")
        waits = load_weights(copies, place[1], (w0, w1, w2, w3, w4), names, w, feature, shards)
        tokens = load_tokens(copies, moved, own, g)
        allowed = masks(mask, place[2] == 0, lon_of(mask.shape[1]))
        x_in.wait()

        def gain_of():
            wait_all(waits["gain"])
            return full_gain(wg, shards)

        result = forward(x, w, waits, gain_of, allowed, mask.shape,
                         normed_s, inverse_s, hidden_s, qkv_s, mix_s)
        y_s[...] = result.astype(BF16)
        done = [copies.start(y_s, y)]
        wait_all(tokens)
        grad_update, grad_gain = backward(g, w, full_gain(wg, shards), allowed, mask.shape,
                                          normed_s, inverse_s, qkv_s, gmix, gproj)
        chain = dot_nt(grad_update, wm[:feature]).astype(BF16).astype(F32)
        side = dot_nt(grad_update, wm[feature:]).astype(BF16).astype(F32)
        g_s[...] = (chain + side).astype(BF16)
        done.append(copies.start(g_s, g0))
        dw = {"merge": dm, "q": dq, "k": dk, "v": dv, "out": do, "gain": dg, "pad": dz}
        done += send_grads(copies, place[1], x, hidden_s, mix_s, g, gproj, grad_update, grad_gain,
                           dw, (pk, ps, qk, qs))
        wait_all(done)


def first_kernel(place, mask, moved, own, g0, w0, w1, w2, w3, w4, normed, inverse, hidden, qkv, mix,
                 pk_in, ps_in, qk_in, qs_in, pk, ps, qk, qs,
                 x, g, wq, wk, wv, wo, wg, normed_s, inverse_s, hidden_s, qkv_s, mix_s,
                 gmix, gproj, dm, dq, dk, dv, do, dg, dz, sems):
    shards = wg.shape[0] // PAD
    feature = x.shape[1]

    @pl.when(place[0] == 0)
    def run():
        copies = Copies(sems)
        w = {"q": wq, "k": wk, "v": wv, "out": wo, "gain": wg}
        g_in = [copies.start(g0, g)]
        names = ("out", "q", "k", "v", "gain")
        waits = load_weights(copies, place[1], (w0, w1, w2, w3, w4), names, w, feature, shards)
        saved = [
            copies.start(a, b)
            for a, b in ((qkv, qkv_s), (normed, normed_s), (inverse, inverse_s), (hidden, hidden_s),
                         (mix, mix_s))
        ]
        tokens = load_tokens(copies, moved, own, x)
        allowed = masks(mask, place[2] == 0, lon_of(mask.shape[1]))
        wait_all(g_in + saved + tokens)
        for name in names:
            wait_all(waits[name])
        grad_update, grad_gain = backward(g, w, full_gain(wg, shards), allowed, mask.shape,
                                          normed_s, inverse_s, qkv_s, gmix, gproj)
        dw = {"merge": dm, "q": dq, "k": dk, "v": dv, "out": do, "gain": dg, "pad": dz}
        done = send_grads(copies, place[1], x, hidden_s, mix_s, g, gproj, grad_update, grad_gain,
                          dw, (pk, ps, qk, qs))
        wait_all(done)


def final_kernel(place, own, other, merge, qkv, out, gain):
    feature = own.shape[1]
    shards = 2 * feature // merge.shape[1]
    first, second, half = layout(feature, shards)
    even = place[2] % 2 == 0

    def rows(name):
        table, flip = (first, False) if name in first else (second, True)
        start, size = table[name]
        mine, theirs = own[start : start + size, :], other[start : start + size, :]
        a, b = (theirs, mine) if flip else (mine, theirs)
        return jnp.where(even, a.astype(F32), b.astype(F32))

    merge[0] = rows("merge")
    for i, name in enumerate(("q", "k", "v")):
        qkv[0, :, i * feature : (i + 1) * feature] = rows(name)
    out[0] = rows("out")
    gain[...] = rows("gain")[:1, : gain.shape[1]]


ANY = pl.BlockSpec(memory_space=pl.ANY)
SMEM = pl.BlockSpec(memory_space=pltpu.SMEM)
VMEM = pl.BlockSpec(memory_space=pltpu.VMEM)


def call(kernel, ins, outs, scratch, aliases, flops, name):
    moved = sum(a.size * a.dtype.itemsize for a in list(ins) + list(outs))
    return pl.pallas_call(
        kernel,
        out_shape=tuple(outs),
        in_specs=[SMEM, VMEM] + [ANY] * (len(ins) - 2),
        out_specs=tuple([ANY] * len(outs)),
        scratch_shapes=scratch,
        input_output_aliases=aliases,
        cost_estimate=pl.CostEstimate(flops=flops, bytes_accessed=moved, transcendentals=0),
        name=name,
    )(*ins)


def flip(value, axis, bit):
    size = lax.axis_size(axis)
    return lax.ppermute(value, axis, [(i, i ^ bit) for i in range(size)])


def body(fields, cell_mask, merge_weight, qkv_weight, out_weight, norm_gain, out_cotangent):
    _, micro, row_count, lon_count, feature = fields.shape
    shards, bands = lax.axis_size("dp"), lax.axis_size("band")
    assert lax.axis_size("segment") == 2 and row_count == WH and shards == 4
    segment, shard, band = (lax.axis_index(a) for a in ("segment", "dp", "band"))
    place = jnp.stack([segment, shard, band]).astype(jnp.int32)
    cells = row_count * lon_count
    total = micro * cells
    first, second, half = layout(feature, shards)
    rows = feature // shards

    qkv = qkv_weight[0]
    gain_rows = jnp.pad(norm_gain, ((0, PAD - 1), (0, feature - rows)))
    packed = jnp.concatenate(
        [
            merge_weight[0],
            qkv[:, :feature],
            gain_rows,
            qkv[:, feature : 2 * feature],
            qkv[:, 2 * feature :],
            out_weight[0],
            jnp.zeros((PAD, feature), BF16),
        ],
        axis=0,
    )
    by_low = flip(packed, "dp", 1)
    by_high = flip(packed, "dp", shards // 2)
    both_first = flip(by_low[:half], "dp", shards // 2)
    both_second = flip(by_high[half:], "dp", 1)
    pieces = (packed, by_low, by_high, both_first, both_second)

    down = [(i, (i + 1) % bands) for i in range(bands)]
    up = [(j, i) for i, j in down]
    flat = (micro, cells, feature)
    source = jnp.where(segment == 0, fields[0, :, row_count - SH :], out_cotangent[0, :, row_count - SH :])
    moved = lax.ppermute(source, "band", down).reshape(micro, SH * lon_count, feature)
    mask_moved = lax.ppermute(cell_mask[0, :, row_count - SH :], "band", down)
    mask = jnp.concatenate([mask_moved, cell_mask[0, :, : row_count - SH]], axis=1).reshape(micro, cells)
    own_fields = fields.reshape(flat)
    own_cotangent = out_cotangent.reshape(flat)

    def shape(*dims, dtype=BF16):
        return jax.ShapeDtypeStruct(dims, dtype)

    def room(*dims, dtype=BF16):
        return pltpu.VMEM(dims, dtype)

    square = room(feature, feature)
    tokens = room(total, feature)
    weights = [square] * 4 + [room(shards * PAD, feature)]
    merge_room = room(2 * feature, feature)
    record_rooms = [
        room(total, feature, dtype=F32), room(total, 128, dtype=F32), tokens,
        room(total, 3 * feature), tokens,
    ]
    grad_rooms = [tokens, room(total, 3 * feature)] + [square] * 5 + [room(shards * PAD, feature), room(PAD, feature)]
    sems = [pltpu.SemaphoreType.DMA((96,))]
    unit = 2 * total * feature * feature

    y, *records = call(
        forward_kernel,
        (place, mask, moved, own_fields) + pieces,
        [shape(total, feature), shape(total, feature, dtype=F32), shape(total, 128, dtype=F32),
         shape(total, feature), shape(total, 3 * feature), shape(total, feature)],
        [tokens, merge_room] + weights + [tokens] + record_rooms + sems,
        {}, 6 * unit, "fwd_first",
    )
    y0 = lax.ppermute(y, "segment", [(0, 1)])
    shard_shape = shape(2, half, feature)
    y, g_out, *grads = call(
        last_kernel,
        (place, mask, moved, own_cotangent, y0) + pieces + (y,),
        [shape(total, feature), shape(total, feature)] + [shard_shape] * 4,
        [tokens, tokens, merge_room] + weights + [tokens, tokens] + record_rooms + grad_rooms + sems,
        {10: 0}, 18 * unit, "last_section",
    )
    g0 = lax.ppermute(g_out, "segment", [(1, 0)])
    inputs = (place, mask, moved, own_fields, g0) + pieces + tuple(records)
    grads = call(
        first_kernel,
        inputs + tuple(grads),
        [shard_shape] * 4,
        [tokens, tokens] + weights + record_rooms + grad_rooms + sems,
        {len(inputs) + i: i for i in range(4)}, 12 * unit, "bwd_first",
    )

    y = y.reshape(micro, cells, feature)
    part = SH * lon_count
    back = lax.ppermute(y[:, :part], "band", up)
    section_out = jnp.concatenate([y[:, part:], back], axis=1)
    section_out = section_out.reshape(1, 1, micro, row_count, lon_count, feature)

    p_keep, p_send, q_keep, q_send = grads
    high = shards // 2
    p_sum = p_keep.astype(F32) + flip(p_send, "dp", high).astype(F32)
    q_sum = q_keep.astype(F32) + flip(q_send, "dp", 1).astype(F32)
    p_sum = p_sum[0] + flip(p_sum[1].astype(BF16), "dp", 1).astype(F32)
    q_sum = q_sum[0] + flip(q_sum[1].astype(BF16), "dp", high).astype(F32)

    even = band % 2 == 0
    mine = jnp.where(even, p_sum, q_sum)
    theirs = jnp.where(even, q_sum, p_sum).astype(BF16)
    mine = (mine + flip(theirs, "band", 1).astype(F32)).astype(BF16)
    bit = 2
    while bit < bands:
        mine = (mine.astype(F32) + flip(mine, "band", bit).astype(F32)).astype(BF16)
        bit *= 2
    theirs = flip(mine, "band", 1)
    merge_grad, qkv_grad, out_grad, gain_grad = pl.pallas_call(
        final_kernel,
        out_shape=(
            shape(1, 2 * rows, feature, dtype=F32), shape(1, rows, 3 * feature, dtype=F32),
            shape(1, rows, feature, dtype=F32), shape(1, rows, dtype=F32),
        ),
        in_specs=[SMEM, VMEM, VMEM],
        out_specs=(VMEM,) * 4,
        name="unpack",
    )(place, mine, theirs)
    return (section_out, merge_grad, qkv_grad, out_grad, gain_grad)


def solution(mesh):
    return jax.shard_map(
        body,
        mesh=mesh,
        in_specs=(
            P("dp", None, "band", None, None),
            P("dp", None, "band", None),
            P("segment", "dp", None),
            P("segment", "dp", None),
            P("segment", "dp", None),
            P("segment", "dp"),
            P("dp", None, "band", None, None),
        ),
        out_specs=(
            P("segment", "dp", None, "band", None, None),
            P("segment", "dp", None),
            P("segment", "dp", None),
            P("segment", "dp", None),
            P("segment", "dp"),
        ),
        check_vma=False,
    )
```

time: 379 us -> 148 us (0.39)
  waiting for transfers between devices: 203 us -> 80 us
  blocking collectives: 47.4 us -> 0 us
  matrix products: 32 us -> 0 us
  Pallas kernels: 0 us -> 21.5 us
  between operations: 15.6 us -> 0.81 us
  other arithmetic: 18.8 us -> 6.57 us
  local copies, waits for them, and re-layouts: 23.7 us -> 12.9 us
  starting transfers between devices: 36.4 us -> 25.8 us
    all_gather x5 -> x0, waiting for transfers between devices: 66.4 us -> none  [the longest x1 32.6 us: body(): lax.all_gather(qkv_weight, 'dp', axis=1, tiled=True)]
    ppermute x10 -> x16, waiting for transfers between devices: 16 us -> 80 us  [the longest x11 56.8 us: flip(): return lax.ppermute(value, axis, [(i, i ^ bit) for i in range(size)])]
    reduce_scatter x3 -> x0, waiting for transfers between devices: 60.3 us -> none  [the longest x1 34.2 us: body(): lax.psum_scatter(grad_sums[1][None].astype(jnp.bfloat16), 'dp', scatter_d...]
    psum x1 -> x0, waiting for transfers between devices: 33.2 us -> none  [body(): lax.psum(merge_part_sum.astype(jnp.bfloat16), 'band').astype(jnp.float32)]
    dot_general x28 -> x0, matrix products: 32 us -> none  [the longest x6 7.77 us: attend(): jnp.einsum('nqhd,nkhd->nhqk', query_blocks, key_pairs[:, :, 0], preferred...]
    unnamed x11 -> x0, waiting for transfers between devices: 24.5 us -> none
    pallas_call x0 -> x4, Pallas kernels: none -> 21.5 us  [the longest x3 19.2 us: call(): pl.pallas_call(kernel, out_shape=tuple(outs), in_specs=[SMEM, VMEM] + [AN...]
    all_gather x3 -> x0, blocking collectives: 19.5 us -> none  [the longest x1 10.6 us: body(): lax.all_gather(out_weight, 'dp', axis=1, tiled=True)]
  transfers between devices with their start and end apart: 23 -> 16, of which waited for: 16 -> 12; matrix products, arithmetic and copies ran while one was open for 10% -> 6% of each run, Pallas kernels for 0% -> 0%
where the time goes in v1:
time: 148 us
  waiting for transfers between devices  80 us (54%)
  starting transfers between devices  25.8 us (17%)
  Pallas kernels  21.5 us (15%)
  local copies, waits for them, and re-layouts  12.9 us (9%)
  other arithmetic  6.57 us (4%)
    ppermute x11, waiting for transfers between devices, flip(): return lax.ppermute(value, axis, [(i, i ^ bit) for i in range(size)])  56.8 us
    pallas_call x3, Pallas kernels, call(): pl.pallas_call(kernel, out_shape=tuple(outs), in_specs=[SMEM, VMEM] + [AN...  19.2 us
    ppermute x11, starting transfers between devices, flip(): return lax.ppermute(value, axis, [(i, i ^ bit) for i in range(size)])  17.1 us
    ppermute x1, waiting for transfers between devices, body(): g0 = lax.ppermute(g_out, 'segment', [(1, 0)])  12.6 us
    unnamed x34, local copies, waits for them, and re-layouts  8.24 us
    ppermute x1, waiting for transfers between devices, body(): back = lax.ppermute(y[:, :part], 'band', up)  5.05 us
    ppermute x1, waiting for transfers between devices, body(): lax.ppermute(source, 'band', down).reshape(micro, SH * lon_count, feature)  4.23 us
  transfers between devices with their start and end apart: 16, of which 12 were waited for; matrix products, arithmetic and copies ran while one was open for 6% of the time, Pallas kernels for 0%

profile of v1, /device:TPU:0, one launch (start us, length us, event | category | flops | bytes accessed | tf_op | source)
XLA Modules:
  0.0 147.6 jit_solution(18285612087729747251)
XLA Ops:
  0.6 1.0 bitcast_dynamic-update-slice_fusion
  1.7 0.9 slice_dynamic-update-slice_fusion.2
  3.2 0.9 slice_dynamic-update-slice_fusion.1
  4.2 0.9 slice_dynamic-update-slice_fusion
  5.1 0.9 bitcast_dynamic-update-slice_fusion.1
  6.0 3.1 %collective-permute-start.3 = (bf16[800,512]{1,0:T(8,128)(2,1)S(1)}, bf16[800,512]{1,0:T(8,128)(2,1)S(1)}, u32[]{:S(2)}, u32[]{:S(2)}) collective-permute-start(bf16[800,512]{1,0:T(8,128)(2,1)S(1)} %constant_dynamic-update-slice_fusion.w0), channel_id=1, source_target_pairs={{0,16},{8,24},{16,0},{24,8},{1,17},{9,25},{17,1},{25,9},{2,18},{10... | collective-permute-start | bytes 2457608 | tf_op jit(solution)/shard_map/ppermute | solution.py:413
  9.1 1.5 %collective-permute-start.2 = (bf16[800,512]{1,0:T(8,128)(2,1)S(1)}, bf16[800,512]{1,0:T(8,128)(2,1)S(1)}, u32[]{:S(2)}, u32[]{:S(2)}) collective-permute-start(bf16[800,512]{1,0:T(8,128)(2,1)S(1)} %constant_dynamic-update-slice_fusion.w0), channel_id=1, source_target_pairs={{0,8},{8,0},{16,24},{24,16},{1,9},{9,1},{17,25},{25,17},{2,10},{10... | collective-permute-start | bytes 2457608 | tf_op jit(solution)/shard_map/ppermute | solution.py:413
  10.6 0.8 slice_bitcast_fusion.3
  11.3 1.6 %collective-permute-start = (s32[2,4,16]{2,1,0:T(4,128)S(1)}, s32[2,4,16]{2,1,0:T(4,128)S(1)}, u32[]{:S(2)}, u32[]{:S(2)}) collective-permute-start(s32[2,4,16]{2,1,0:T(4,128)S(1)} %get-tuple-element.47), channel_id=1, source_target_pairs={{0,1},{1,2},{2,3},{3,0},{4,5},{5,6},{6,7},{7,4},{8,9},{9,10},{10,1... | collective-permute-start | bytes 1544 | tf_op jit(solution)/shard_map/ppermute | solution.py:452
  12.9 14.4 %collective-permute-done.3.w2 = bf16[800,512]{1,0:T(8,128)(2,1)S(1)} collective-permute-done((bf16[800,512]{1,0:T(8,128)(2,1)S(1)}, bf16[800,512]{1,0:T(8,128)(2,1)S(1)}, u32[]{:S(2)}, u32[]{:S(2)}) %collective-permute-start.3) | collective-permute-done | bytes 819232 | tf_op jit(solution)/shard_map/ppermute | solution.py:413
  27.3 0.8 slice.66
  28.1 1.7 %collective-permute-start.5 = (bf16[400,512]{1,0:T(8,128)(2,1)}, bf16[400,512]{1,0:T(8,128)(2,1)S(1)}, u32[]{:S(2)}, u32[]{:S(2)}) collective-permute-start(bf16[400,512]{1,0:T(8,128)(2,1)} %slice.66), channel_id=1, source_target_pairs={{0,8},{8,0},{16,24},{24,16},{1,9},{9,1},{17,25},{25,17},{2,10},{10... | collective-permute-start | bytes 1228808 | tf_op jit(solution)/shard_map/ppermute | solution.py:413
  29.9 0.8 slice.65
  30.7 1.5 %collective-permute-start.4 = (bf16[400,512]{1,0:T(8,128)(2,1)}, bf16[400,512]{1,0:T(8,128)(2,1)S(1)}, u32[]{:S(2)}, u32[]{:S(2)}) collective-permute-start(bf16[400,512]{1,0:T(8,128)(2,1)} %slice.65), channel_id=1, source_target_pairs={{0,16},{8,24},{16,0},{24,8},{1,17},{9,25},{17,1},{25,9},{2,18},{10... | collective-permute-start | bytes 1228808 | tf_op jit(solution)/shard_map/ppermute | solution.py:413
  32.2 0.7 select_bitcast_fusion
  32.9 1.6 %collective-permute-start.1 = (bf16[2,4,16,512]{3,2,1,0:T(8,128)(2,1)}, bf16[2,4,16,512]{3,2,1,0:T(8,128)(2,1)S(1)}, u32[]{:S(2)}, u32[]{:S(2)}) collective-permute-start(bf16[2,4,16,512]{3,2,1,0:T(8,128)(2,1)} %select_bitcast_fusion), channel_id=1, source_target_pairs={{0,1},{1,2},{2,3},{3,0},{4,5},{5,6},{6,7},{7,4},{8,9},{9,10},{10,1... | collective-permute-start | bytes 393224 | tf_op jit(solution)/shard_map/ppermute | solution.py:451
  35.7 4.2 %collective-permute-done.1 = bf16[2,4,16,512]{3,2,1,0:T(8,128)(2,1)S(1)} collective-permute-done((bf16[2,4,16,512]{3,2,1,0:T(8,128)(2,1)}, bf16[2,4,16,512]{3,2,1,0:T(8,128)(2,1)S(1)}, u32[]{:S(2)}, u32[]{:S(2)}) %collective-permute-start.1) | collective-permute-done | bytes 131104 | tf_op jit(solution)/shard_map/ppermute | solution.py:451
  39.9 1.1 collective-permute-done.4.w3
  41.0 0.7 copy-done.7
  41.7 6.9 %fwd_first.1 = (bf16[256,512]{1,0:T(8,128)(2,1)}, f32[256,512]{1,0:T(8,128)}, f32[256,128]{1,0:T(8,128)}, bf16[256,512]{1,0:T(8,128)(2,1)}, bf16[256,1536]{1,0:T(8,128)(2,1)}, /*index=5*/bf16[256,512]{1,0:T(8,128)(2,1)}) custom-call(s32[3]{0:T(128)} %pad_add_fusion.1.place, s32[2,128]{1,0:T(2,128)} %reshape.32.mask, bf16[2,64,512]{2,1,0:T(8,128)(2,1)} %bitcast.41, ...), custom_call_target="tpu_custom_call" | custom-call | flops 805306368 | bytes 5899276 | tf_op jit(solution)/shard_map/fwd_first/pallas_call | solution.py:399
  48.7 1.3 collective-permute-start.6
  50.0 1.3 collective-permute-done.6.y0
  51.3 0.7 copy-done.13
  52.0 1.7 %last_section.1 = (bf16[256,512]{1,0:T(8,128)(2,1)}, bf16[256,512]{1,0:T(8,128)(2,1)}, bf16[2,400,512]{2,1,0:T(8,128)(2,1)}, bf16[2,400,512]{2,1,0:T(8,128)(2,1)...) custom-call(s32[3]{0:T(128)} %pad_add_fusion.1.place, ...), custom_call_target="tpu_custom_call", output_to_operand_aliasing={{0}: (10, {})} | custom-call | flops 2415919104 | bytes 7996428 | tf_op jit(solution)/shard_map/last_section/pallas_call | solution.py:399
  53.7 1.3 collective-permute-start.8
  55.0 12.6 %collective-permute-done.8.g0 = bf16[256,512]{1,0:T(8,128)(2,1)S(1)} collective-permute-done((bf16[256,512]{1,0:T(8,128)(2,1)}, bf16[256,512]{1,0:T(8,128)(2,1)S(1)}, u32[]{:S(2)}, u32[]{:S(2)}) %collective-permute-start.8) | collective-permute-done | bytes 262176 | tf_op jit(solution)/shard_map/ppermute | solution.py:492
  67.6 0.7 copy-done.10
  68.2 10.6 %bwd_first.1 = (bf16[2,400,512]{2,1,0:T(8,128)(2,1)}, bf16[2,400,512]{2,1,0:T(8,128)(2,1)}, bf16[2,400,512]{2,1,0:T(8,128)(2,1)}, bf16[2,400,512]{2,1,0:T(8,128)(2,1)}) custom-call(s32[3]{0:T(128)} %pad_add_fusion.1.place, s32[2,128]{1,0:T(2,128)} %reshape.32.mask, ...), custom_call_target="tpu_custom_call", output_to_operand_aliasing={{0}: (15, {}), {1}: (16, {}), {2}: (17, {}), {3}: (18, {})} | custom-call | flops 1610612736 | bytes 12452876 | tf_op jit(solution)/shard_map/bwd_first/pallas_call | solution.py:399
  78.9 1.6 %collective-permute-start.9 = (bf16[2,400,512]{2,1,0:T(8,128)(2,1)}, bf16[2,400,512]{2,1,0:T(8,128)(2,1)S(1)}, u32[]{:S(2)}, u32[]{:S(2)}) collective-permute-start(bf16[2,400,512]{2,1,0:T(8,128)(2,1)} %get-tuple-element.38), channel_id=1, source_target_pairs={{0,16},{8,24},{16,0},{24,8},{1,17},{9,25},{17,1},{25,9},{2,18},{10... | collective-permute-start | bytes 2457608 | tf_op jit(solution)/shard_map/ppermute | solution.py:413
  81.0 14.0 %collective-permute-done.9 = bf16[2,400,512]{2,1,0:T(8,128)(2,1)S(1)} collective-permute-done((bf16[2,400,512]{2,1,0:T(8,128)(2,1)}, bf16[2,400,512]{2,1,0:T(8,128)(2,1)S(1)}, u32[]{:S(2)}, u32[]{:S(2)}) %collective-permute-start.9) | collective-permute-done | bytes 819232 | tf_op jit(solution)/shard_map/ppermute | solution.py:413
  95.0 1.5 convert_add_fusion.1
  96.4 0.8 fusion.2
  97.6 0.8 fusion.3
  98.4 1.4 collective-permute-start.12
  99.9 5.6 %collective-permute-done.10 = bf16[400,512]{1,0:T(8,128)(2,1)} collective-permute-done((bf16[400,512]{1,0:T(8,128)(2,1)}, bf16[400,512]{1,0:T(8,128)(2,1)}, u32[]{:S(2)}, u32[]{:S(2)}) %collective-permute-start.10) | collective-permute-done | bytes 409632 | tf_op jit(solution)/shard_map/ppermute | solution.py:413
  105.5 1.2 collective-permute-done.12
  106.7 1.4 select_convert_fusion
  108.1 1.6 %collective-permute-start.13 = (bf16[400,512]{1,0:T(8,128)(2,1)S(1)}, bf16[400,512]{1,0:T(8,128)(2,1)S(1)}, u32[]{:S(2)}, u32[]{:S(2)}) collective-permute-start(bf16[400,512]{1,0:T(8,128)(2,1)S(1)} %select_convert_fusion), channel_id=1, source_target_pairs={{0,1},{1,0},{2,3},{3,2},{4,5},{5,4},{6,7},{7,6},{8,9},{9,8},{10,11... | collective-permute-start | bytes 1228808 | tf_op jit(solution)/shard_map/ppermute | solution.py:413
  109.8 9.7 %collective-permute-done.13 = bf16[400,512]{1,0:T(8,128)(2,1)S(1)} collective-permute-done((bf16[400,512]{1,0:T(8,128)(2,1)S(1)}, bf16[400,512]{1,0:T(8,128)(2,1)S(1)}, u32[]{:S(2)}, u32[]{:S(2)}) %collective-permute-start.13) | collective-permute-done | bytes 409632 | tf_op jit(solution)/shard_map/ppermute | solution.py:413
  119.4 1.4 add_convert_fusion.1
  120.9 2.7 %collective-permute-start.14 = (bf16[400,512]{1,0:T(8,128)(2,1)S(1)}, bf16[400,512]{1,0:T(8,128)(2,1)S(1)}, u32[]{:S(2)}, u32[]{:S(2)}) collective-permute-start(bf16[400,512]{1,0:T(8,128)(2,1)S(1)} %add_convert_fusion.1), channel_id=1, source_target_pairs={{0,2},{1,3},{2,0},{3,1},{4,6},{5,7},{6,4},{7,5},{8,10},{9,11},{10,... | collective-permute-start | bytes 1228808 | tf_op jit(solution)/shard_map/ppermute | solution.py:413
  123.6 10.6 %collective-permute-done.14 = bf16[400,512]{1,0:T(8,128)(2,1)S(1)} collective-permute-done((bf16[400,512]{1,0:T(8,128)(2,1)S(1)}, bf16[400,512]{1,0:T(8,128)(2,1)S(1)}, u32[]{:S(2)}, u32[]{:S(2)}) %collective-permute-start.14) | collective-permute-done | bytes 409632 | tf_op jit(solution)/shard_map/ppermute | solution.py:413
  134.3 1.5 collective-permute-start.15
  135.8 2.9 %collective-permute-start.7 = (bf16[2,64,512]{2,1,0:T(8,128)(2,1)S(1)}, bf16[2,64,512]{2,1,0:T(8,128)(2,1)S(1)}, u32[]{:S(2)}, u32[]{:S(2)}) collective-permute-start(bf16[2,64,512]{2,1,0:T(8,128)(2,1)S(1)} %get-tuple-element.46), channel_id=1, source_target_pairs={{1,0},{2,1},{3,2},{0,3},{5,4},{6,5},{7,6},{4,7},{9,8},{10,9},{11,1... | collective-permute-start | bytes 393224 | tf_op jit(solution)/shard_map/ppermute | solution.py:504
  138.7 5.0 %collective-permute-done.7 = bf16[2,64,512]{2,1,0:T(8,128)(2,1)S(1)} collective-permute-done((bf16[2,64,512]{2,1,0:T(8,128)(2,1)S(1)}, bf16[2,64,512]{2,1,0:T(8,128)(2,1)S(1)}, u32[]{:S(2)}, u32[]{:S(2)}) %collective-permute-start.7) | collective-permute-done | bytes 131104 | tf_op jit(solution)/shard_map/ppermute | solution.py:504
  143.7 0.7 pad_maximum_fusion
  144.5 0.7 copy-done.9
  145.2 2.4 %unpack.1 = (f32[1,256,512]{2,1,0:T(8,128)}, f32[1,128,1536]{2,1,0:T(8,128)}, f32[1,128,512]{2,1,0:T(8,128)}, f32[1,128]{1,0:T(1,128)}) custom-call(s32[3]{0:T(128)} %pad_add_fusion.1.place, bf16[400,512]{1,0:T(8,128)(2,1)} %copy-done.5, bf16[400,512]{1,0:T(8,128)(2,1)} %copy-done.9), custom_call_target="tpu_custom_call" | custom-call | tf_op jit(solution)/shard_map/unpack/pallas_call | solution.py:524
  (39 shorter events, 2.9 us)
Async XLA Ops:
  0.6 31.6 %copy-start.4 = (bf16[1,2,8,16,512]{4,3,2,1,0:T(8,128)(2,1)S(1)}, bf16[1,2,8,16,512]{4,3,2,1,0:T(8,128)(2,1)}, u32[]{:S(2)}) copy-start(bf16[1,2,8,16,512]{4,3,2,1,0:T(8,128)(2,1)} %param.7) | copy-start | bytes 786436
  6.0 35.0 %copy-start.2 = (bf16[800,512]{1,0:T(8,128)(2,1)}, bf16[800,512]{1,0:T(8,128)(2,1)S(1)}, u32[]{:S(2)}) copy-start(bf16[800,512]{1,0:T(8,128)(2,1)S(1)} %constant_dynamic-update-slice_fusion.w0) | copy-start | bytes 2457604
  6.0 21.3 %collective-permute-start.3 = (bf16[800,512]{1,0:T(8,128)(2,1)S(1)}, bf16[800,512]{1,0:T(8,128)(2,1)S(1)}, u32[]{:S(2)}, u32[]{:S(2)}) collective-permute-start(bf16[800,512]{1,0:T(8,128)(2,1)S(1)} %constant_dynamic-update-slice_fusion.w0), channel_id=1, source_target_pairs={{0,16},{8,24},{16,0},{24,8},{1,17},{9,25},{17,1},{25,9},{2,18},{10... | collective-permute-start | bytes 2457608 | tf_op jit(solution)/shard_map/ppermute | solution.py:413
  9.1 20.8 %collective-permute-start.2 = (bf16[800,512]{1,0:T(8,128)(2,1)S(1)}, bf16[800,512]{1,0:T(8,128)(2,1)S(1)}, u32[]{:S(2)}, u32[]{:S(2)}) collective-permute-start(bf16[800,512]{1,0:T(8,128)(2,1)S(1)} %constant_dynamic-update-slice_fusion.w0), channel_id=1, source_target_pairs={{0,8},{8,0},{16,24},{24,16},{1,9},{9,1},{17,25},{25,17},{2,10},{10... | collective-permute-start | bytes 2457608 | tf_op jit(solution)/shard_map/ppermute | solution.py:413
  11.3 23.7 %collective-permute-start = (s32[2,4,16]{2,1,0:T(4,128)S(1)}, s32[2,4,16]{2,1,0:T(4,128)S(1)}, u32[]{:S(2)}, u32[]{:S(2)}) collective-permute-start(s32[2,4,16]{2,1,0:T(4,128)S(1)} %get-tuple-element.47), channel_id=1, source_target_pairs={{0,1},{1,2},{2,3},{3,0},{4,5},{5,6},{6,7},{7,4},{8,9},{9,10},{10,1... | collective-permute-start | bytes 1544 | tf_op jit(solution)/shard_map/ppermute | solution.py:452
  12.9 19.3 %copy-start.12 = (bf16[1,2,8,16,512]{4,3,2,1,0:T(8,128)(2,1)S(1)}, bf16[1,2,8,16,512]{4,3,2,1,0:T(8,128)(2,1)}, u32[]{:S(2)}) copy-start(bf16[1,2,8,16,512]{4,3,2,1,0:T(8,128)(2,1)} %param.13) | copy-start | bytes 786436
  27.3 13.7 %copy-start = (bf16[800,512]{1,0:T(8,128)(2,1)}, bf16[800,512]{1,0:T(8,128)(2,1)S(1)}, u32[]{:S(2)}) copy-start(bf16[800,512]{1,0:T(8,128)(2,1)S(1)} %collective-permute-done.3.w2) | copy-start | bytes 2457604
  28.1 11.7 %collective-permute-start.5 = (bf16[400,512]{1,0:T(8,128)(2,1)}, bf16[400,512]{1,0:T(8,128)(2,1)S(1)}, u32[]{:S(2)}, u32[]{:S(2)}) collective-permute-start(bf16[400,512]{1,0:T(8,128)(2,1)} %slice.66), channel_id=1, source_target_pairs={{0,8},{8,0},{16,24},{24,16},{1,9},{9,1},{17,25},{25,17},{2,10},{10... | collective-permute-start | bytes 1228808 | tf_op jit(solution)/shard_map/ppermute | solution.py:413
  29.9 11.1 %copy-start.1 = (bf16[800,512]{1,0:T(8,128)(2,1)}, bf16[800,512]{1,0:T(8,128)(2,1)S(1)}, u32[]{:S(2)}) copy-start(bf16[800,512]{1,0:T(8,128)(2,1)S(1)} %collective-permute-done.2.w1) | copy-start | bytes 2457604
  30.7 10.3 %collective-permute-start.4 = (bf16[400,512]{1,0:T(8,128)(2,1)}, bf16[400,512]{1,0:T(8,128)(2,1)S(1)}, u32[]{:S(2)}, u32[]{:S(2)}) collective-permute-start(bf16[400,512]{1,0:T(8,128)(2,1)} %slice.65), channel_id=1, source_target_pairs={{0,16},{8,24},{16,0},{24,8},{1,17},{9,25},{17,1},{25,9},{2,18},{10... | collective-permute-start | bytes 1228808 | tf_op jit(solution)/shard_map/ppermute | solution.py:413
  32.9 7.0 %collective-permute-start.1 = (bf16[2,4,16,512]{3,2,1,0:T(8,128)(2,1)}, bf16[2,4,16,512]{3,2,1,0:T(8,128)(2,1)S(1)}, u32[]{:S(2)}, u32[]{:S(2)}) collective-permute-start(bf16[2,4,16,512]{3,2,1,0:T(8,128)(2,1)} %select_bitcast_fusion), channel_id=1, source_target_pairs={{0,1},{1,2},{2,3},{3,0},{4,5},{5,6},{6,7},{7,4},{8,9},{9,10},{10,1... | collective-permute-start | bytes 393224 | tf_op jit(solution)/shard_map/ppermute | solution.py:451
  39.9 1.1 copy-start.8
  39.9 1.1 copy-start.6
  41.0 0.8 copy-start.7
  48.7 2.7 %collective-permute-start.6 = (bf16[256,512]{1,0:T(8,128)(2,1)}, bf16[256,512]{1,0:T(8,128)(2,1)S(1)}, u32[]{:S(2)}, u32[]{:S(2)}) collective-permute-start(bf16[256,512]{1,0:T(8,128)(2,1)} %get-tuple-element.25.y_in), channel_id=1, source_target_pairs={{0,4},{1,5},{2,6},{3,7},{8,12},{9,13},{10,14},{11,15},{16,20},{17,... | collective-permute-start | bytes 786440 | tf_op jit(solution)/shard_map/ppermute | solution.py:483
  51.3 0.7 copy-start.13
  53.7 13.9 %collective-permute-start.8 = (bf16[256,512]{1,0:T(8,128)(2,1)}, bf16[256,512]{1,0:T(8,128)(2,1)S(1)}, u32[]{:S(2)}, u32[]{:S(2)}) collective-permute-start(bf16[256,512]{1,0:T(8,128)(2,1)} %get-tuple-element.27), channel_id=1, source_target_pairs={{4,0},{5,1},{6,2},{7,3},{12,8},{13,9},{14,10},{15,11},{20,16},{21,... | collective-permute-start | bytes 786440 | tf_op jit(solution)/shard_map/ppermute | solution.py:492
  67.5 0.7 copy-start.10
  78.9 16.1 %collective-permute-start.9 = (bf16[2,400,512]{2,1,0:T(8,128)(2,1)}, bf16[2,400,512]{2,1,0:T(8,128)(2,1)S(1)}, u32[]{:S(2)}, u32[]{:S(2)}) collective-permute-start(bf16[2,400,512]{2,1,0:T(8,128)(2,1)} %get-tuple-element.38), channel_id=1, source_target_pairs={{0,16},{8,24},{16,0},{24,8},{1,17},{9,25},{17,1},{25,9},{2,18},{10... | collective-permute-start | bytes 2457608 | tf_op jit(solution)/shard_map/ppermute | solution.py:413
  80.5 16.9 %collective-permute-start.11 = (bf16[2,400,512]{2,1,0:T(8,128)(2,1)}, bf16[2,400,512]{2,1,0:T(8,128)(2,1)S(1)}, u32[]{:S(2)}, u32[]{:S(2)}) collective-permute-start(bf16[2,400,512]{2,1,0:T(8,128)(2,1)} %get-tuple-element.40), channel_id=1, source_target_pairs={{0,8},{8,0},{16,24},{24,16},{1,9},{9,1},{17,25},{25,17},{2,10},{10... | collective-permute-start | bytes 2457608 | tf_op jit(solution)/shard_map/ppermute | solution.py:413
  95.0 2.4 %copy-start.3 = (bf16[2,400,512]{2,1,0:T(8,128)(2,1)S(1)}, bf16[2,400,512]{2,1,0:T(8,128)(2,1)}, u32[]{:S(2)}) copy-start(bf16[2,400,512]{2,1,0:T(8,128)(2,1)} %get-tuple-element.39) | copy-start | bytes 2457604
  97.2 8.3 %collective-permute-start.10 = (bf16[400,512]{1,0:T(8,128)(2,1)}, bf16[400,512]{1,0:T(8,128)(2,1)}, u32[]{:S(2)}, u32[]{:S(2)}) collective-permute-start(bf16[400,512]{1,0:T(8,128)(2,1)} %fusion.2), channel_id=1, source_target_pairs={{0,8},{8,0},{16,24},{24,16},{1,9},{9,1},{17,25},{25,17},{2,10},{10... | collective-permute-start | bytes 1228808 | tf_op jit(solution)/shard_map/ppermute | solution.py:413
  98.4 8.3 %collective-permute-start.12 = (bf16[400,512]{1,0:T(8,128)(2,1)}, bf16[400,512]{1,0:T(8,128)(2,1)}, u32[]{:S(2)}, u32[]{:S(2)}) collective-permute-start(bf16[400,512]{1,0:T(8,128)(2,1)} %fusion.3), channel_id=1, source_target_pairs={{0,16},{8,24},{16,0},{24,8},{1,17},{9,25},{17,1},{25,9},{2,18},{10... | collective-permute-start | bytes 1228808 | tf_op jit(solution)/shard_map/ppermute | solution.py:413
  108.1 27.7 %copy-start.11 = (bf16[256,512]{1,0:T(8,128)(2,1)S(1)}, bf16[256,512]{1,0:T(8,128)(2,1)}, u32[]{:S(2)}) copy-start(bf16[256,512]{1,0:T(8,128)(2,1)} %get-tuple-element.26) | copy-start | bytes 786436
  108.1 11.3 %collective-permute-start.13 = (bf16[400,512]{1,0:T(8,128)(2,1)S(1)}, bf16[400,512]{1,0:T(8,128)(2,1)S(1)}, u32[]{:S(2)}, u32[]{:S(2)}) collective-permute-start(bf16[400,512]{1,0:T(8,128)(2,1)S(1)} %select_convert_fusion), channel_id=1, source_target_pairs={{0,1},{1,0},{2,3},{3,2},{4,5},{5,4},{6,7},{7,6},{8,9},{9,8},{10,11... | collective-permute-start | bytes 1228808 | tf_op jit(solution)/shard_map/ppermute | solution.py:413
  120.9 13.3 %collective-permute-start.14 = (bf16[400,512]{1,0:T(8,128)(2,1)S(1)}, bf16[400,512]{1,0:T(8,128)(2,1)S(1)}, u32[]{:S(2)}, u32[]{:S(2)}) collective-permute-start(bf16[400,512]{1,0:T(8,128)(2,1)S(1)} %add_convert_fusion.1), channel_id=1, source_target_pairs={{0,2},{1,3},{2,0},{3,1},{4,6},{5,7},{6,4},{7,5},{8,10},{9,11},{10,... | collective-permute-start | bytes 1228808 | tf_op jit(solution)/shard_map/ppermute | solution.py:413
  134.3 10.2 %copy-start.5 = (bf16[400,512]{1,0:T(8,128)(2,1)}, bf16[400,512]{1,0:T(8,128)(2,1)S(1)}, u32[]{:S(2)}) copy-start(bf16[400,512]{1,0:T(8,128)(2,1)S(1)} %add_convert_fusion.own) | copy-start | bytes 1228804
  134.3 10.1 %collective-permute-start.15 = (bf16[400,512]{1,0:T(8,128)(2,1)S(1)}, bf16[400,512]{1,0:T(8,128)(2,1)S(1)}, u32[]{:S(2)}, u32[]{:S(2)}) collective-permute-start(bf16[400,512]{1,0:T(8,128)(2,1)S(1)} %add_convert_fusion.own), channel_id=1, source_target_pairs={{0,1},{1,0},{2,3},{3,2},{4,5},{5,4},{6,7},{7,6},{8,9},{9,8},{10,11... | collective-permute-start | bytes 1228808 | tf_op jit(solution)/shard_map/ppermute | solution.py:413
  135.8 7.9 %collective-permute-start.7 = (bf16[2,64,512]{2,1,0:T(8,128)(2,1)S(1)}, bf16[2,64,512]{2,1,0:T(8,128)(2,1)S(1)}, u32[]{:S(2)}, u32[]{:S(2)}) collective-permute-start(bf16[2,64,512]{2,1,0:T(8,128)(2,1)S(1)} %get-tuple-element.46), channel_id=1, source_target_pairs={{1,0},{2,1},{3,2},{0,3},{5,4},{6,5},{7,6},{4,7},{9,8},{10,9},{11,1... | collective-permute-start | bytes 393224 | tf_op jit(solution)/shard_map/ppermute | solution.py:504
  144.5 0.8 copy-start.9

commit v2 on v1

--- a/solution.py
+++ b/solution.py
@@ -1,5 +1,3 @@
-import functools
-
 import jax
 import jax.numpy as jnp
 from jax import lax
@@ -7,6 +5,7 @@
 from jax.experimental.pallas import tpu as pltpu
 from jax.sharding import PartitionSpec as P
 
+
 HEADS = 8
 WH = 8
 WW = 16
@@ -17,6 +16,7 @@
 EPSILON = 1e-05
 MASKED = -1e30
 
+
 F32 = jnp.float32
 BF16 = jnp.bfloat16
 
@@ -57,27 +57,37 @@
     return (first, second, merge + rows + PAD)
 
 
-def load_weights(copies, me, pieces, names, dst, feature, shards):
-    own, by_low, by_high, both_first, both_second = pieces
-    first, second, half = layout(feature, shards)
+def load_weights(copies, pieces, names, dst):
+    me = lax.axis_index("dp")
+    shards = 4
     started = {}
     for name in names:
+        kind, column = WHERE[name]
+        arrays = pieces[kind]
         started[name] = []
-        for flip, ref in ((0, own), (1, by_low), (shards // 2, by_high), (shards - 1, None)):
-            owner = me ^ flip
-            base = 0
-            if name in first:
-                start, rows = first[name]
-                source = both_first if ref is None else ref
+        for flip, ref in zip((0, 1, shards // 2, shards - 1), arrays):
+            rows = dst[name].shape[0] // shards
+            at = pl.multiple_of((me ^ flip) * rows, rows)
+            if kind == "rest":
+                base = 0 if name == "out" else ref.shape[0] - PAD
+                source = ref.at[pl.ds(base, rows)]
+            elif kind == "qkv":
+                width = dst[name].shape[1]
+                source = ref.at[:, pl.ds(column * width, width)]
             else:
-                start, rows = second[name]
-                source = both_second if ref is None else ref
-                base = 0 if ref is None else half
-            at = pl.multiple_of(owner * rows, rows)
-            started[name].append(
-                copies.start(source.at[pl.ds(base + start, rows)], dst[name].at[pl.ds(at, rows)])
-            )
+                source = ref
+            started[name].append(copies.start(source, dst[name].at[pl.ds(at, rows)]))
     return started
+
+
+WHERE = {
+    "merge": ("merge", 0), "q": ("qkv", 0), "k": ("qkv", 1), "v": ("qkv", 2),
+    "out": ("rest", 0), "gain": ("rest", 1),
+}
+
+
+def pieces_of(refs):
+    return {"merge": refs[0:4], "qkv": refs[4:8], "rest": refs[8:12]}
 
 
 def load_tokens(copies, moved, own, dst):
@@ -221,11 +231,12 @@
     return (grad_update.astype(BF16), grad_gain)
 
 
-def send_grads(copies, me, x, hidden, mix, grad_out, grad_proj, grad_update, grad_gain, dw, outs):
+def send_grads(copies, x, hidden, mix, grad_out, grad_proj, grad_update, grad_gain, dw, outs):
     feature = x.shape[1]
     p_keep, p_send, q_keep, q_send = outs
     shards = 2 * p_keep.shape[0]
-    first, second, half = layout(feature, shards)
+    first, second, _ = layout(feature, shards)
+    me = lax.axis_index("dp")
     low, high = me % 2, me // 2
     rows = feature // shards
     started = []
@@ -260,7 +271,7 @@
     emit("gain", shards * PAD)
     dw["pad"][...] = jnp.zeros_like(dw["pad"])
     emit("pad", PAD)
-    dw["merge"][...] = dot_tn(x[...], grad_update).astype(BF16)
+    dw["merge"][...] = dot_tn(x[...], grad_update[...]).astype(BF16)
     emit("merge", feature)
     return started
 
@@ -269,19 +280,27 @@
     return cells // WH
 
 
-def forward_kernel(place, mask, moved, own, w0, w1, w2, w3, w4, y, normed, inverse, hidden, qkv, mix,
-                   x, wm, wq, wk, wv, wo, wg, y_s, normed_s, inverse_s, hidden_s, qkv_s, mix_s, sems):
-    shards = wg.shape[0] // PAD
-    feature = x.shape[1]
-
-    @pl.when(place[0] == 0)
+def role(segment):
+    return pl.when(lax.axis_index("segment") == segment)
+
+
+def forward_kernel(*refs):
+    mask_in, moved, own, *rest = refs
+    pieces, rest = rest[:12], rest[12:]
+    y, normed, inverse, hidden, qkv, mix, *rest = rest
+    mask, x, wm, wq, wk, wv, wo, wg, y_s, normed_s, inverse_s, hidden_s, qkv_s, mix_s, sems = rest
+
+    @role(0)
     def run():
+        shards = wg.shape[0] // PAD
         copies = Copies(sems)
         w = {"merge": wm, "q": wq, "k": wk, "v": wv, "out": wo, "gain": wg}
+        mask_copy = copies.start(mask_in, mask)
         tokens = load_tokens(copies, moved, own, x)
         names = ("merge", "gain", "q", "k", "v", "out")
-        waits = load_weights(copies, place[1], (w0, w1, w2, w3, w4), names, w, feature, shards)
-        allowed = masks(mask, place[2] == 0, lon_of(mask.shape[1]))
+        waits = load_weights(copies, pieces_of(pieces), names, w)
+        mask_copy.wait()
+        allowed = masks(mask, lax.axis_index("band") == 0, lon_of(mask.shape[1]))
         wait_all(tokens)
 
         def gain_of():
@@ -299,21 +318,26 @@
         wait_all(done)
 
 
-def last_kernel(place, mask, moved, own, y0, w0, w1, w2, w3, w4, y_in, y, g0, pk, ps, qk, qs,
-                x, g, wm, wq, wk, wv, wo, wg, y_s, g_s, normed_s, inverse_s, hidden_s, qkv_s, mix_s,
-                gmix, gproj, dm, dq, dk, dv, do, dg, dz, sems):
-    shards = wg.shape[0] // PAD
-    feature = x.shape[1]
-
-    @pl.when(place[0] == 1)
+def last_kernel(*refs):
+    mask_in, moved, own, y0, *rest = refs
+    pieces, rest = rest[:12], rest[14:]
+    y, g0, gain_out, g_out, hidden, mix, proj_out, update_out, *rest = rest
+    (mask, x, g, wm, wq, wk, wv, wo, wg, y_s, g_s, normed_s, inverse_s, hidden_s, qkv_s, mix_s,
+     gmix, gproj, gain_s, update_s, sems) = rest
+
+    @role(1)
     def run():
+        shards = wg.shape[0] // PAD
+        feature = x.shape[1]
         copies = Copies(sems)
         w = {"merge": wm, "q": wq, "k": wk, "v": wv, "out": wo, "gain": wg}
+        mask_copy = copies.start(mask_in, mask)
         x_in = copies.start(y0, x)
         names = ("merge", "gain", "q", "k", "v", "out")
-        waits = load_weights(copies, place[1], (w0, w1, w2, w3, w4), names, w, feature, shards)
+        waits = load_weights(copies, pieces_of(pieces), names, w)
         tokens = load_tokens(copies, moved, own, g)
-        allowed = masks(mask, place[2] == 0, lon_of(mask.shape[1]))
+        mask_copy.wait()
+        allowed = masks(mask, lax.axis_index("band") == 0, lon_of(mask.shape[1]))
         x_in.wait()
 
         def gain_of():
@@ -323,57 +347,81 @@
         result = forward(x, w, waits, gain_of, allowed, mask.shape,
                          normed_s, inverse_s, hidden_s, qkv_s, mix_s)
         y_s[...] = result.astype(BF16)
-        done = [copies.start(y_s, y)]
         wait_all(tokens)
+        done = [copies.start(y_s, y), copies.start(g, g_out), copies.start(hidden_s, hidden),
+                copies.start(mix_s, mix)]
         grad_update, grad_gain = backward(g, w, full_gain(wg, shards), allowed, mask.shape,
                                           normed_s, inverse_s, qkv_s, gmix, gproj)
+        done.append(copies.start(gproj, proj_out))
+        gain_s[...] = jnp.broadcast_to(grad_gain, gain_s.shape)
+        update_s[...] = grad_update
+        done += [copies.start(gain_s, gain_out), copies.start(update_s, update_out)]
         chain = dot_nt(grad_update, wm[:feature]).astype(BF16).astype(F32)
         side = dot_nt(grad_update, wm[feature:]).astype(BF16).astype(F32)
         g_s[...] = (chain + side).astype(BF16)
         done.append(copies.start(g_s, g0))
-        dw = {"merge": dm, "q": dq, "k": dk, "v": dv, "out": do, "gain": dg, "pad": dz}
-        done += send_grads(copies, place[1], x, hidden_s, mix_s, g, gproj, grad_update, grad_gain,
-                           dw, (pk, ps, qk, qs))
         wait_all(done)
 
 
-def first_kernel(place, mask, moved, own, g0, w0, w1, w2, w3, w4, normed, inverse, hidden, qkv, mix,
-                 pk_in, ps_in, qk_in, qs_in, pk, ps, qk, qs,
-                 x, g, wq, wk, wv, wo, wg, normed_s, inverse_s, hidden_s, qkv_s, mix_s,
-                 gmix, gproj, dm, dq, dk, dv, do, dg, dz, sems):
-    shards = wg.shape[0] // PAD
-    feature = x.shape[1]
-
-    @pl.when(place[0] == 0)
+def weight_kernel(*refs):
+    ins, outs, rest = refs[:7], refs[7:11], refs[11:]
+    scratch, dw_refs, sems = rest[:7], rest[7:14], rest[14]
+
+    @role(1)
     def run():
         copies = Copies(sems)
+        wait_all([copies.start(a, b) for a, b in zip(ins, scratch)])
+        x, gain, g, hidden, mix, gproj, update = scratch
+        dw = dict(zip(("merge", "q", "k", "v", "out", "gain", "pad"), dw_refs))
+        wait_all(send_grads(copies, x, hidden, mix, g, gproj, update, gain[:1, :], dw, outs))
+
+
+def first_kernel(*refs):
+    mask_in, moved, own, g0, *rest = refs
+    pieces, rest = rest[:12], rest[12:]
+    normed, inverse, hidden, qkv, mix, *rest = rest
+    outs, rest = rest[5:9], rest[9:]
+    (mask, x, g, wq, wk, wv, wo, wg, normed_s, inverse_s, hidden_s, qkv_s, mix_s,
+     gmix, gproj, *dw_refs, sems) = rest
+
+    @role(0)
+    def run():
+        shards = wg.shape[0] // PAD
+        copies = Copies(sems)
         w = {"q": wq, "k": wk, "v": wv, "out": wo, "gain": wg}
+        mask_copy = copies.start(mask_in, mask)
         g_in = [copies.start(g0, g)]
         names = ("out", "q", "k", "v", "gain")
-        waits = load_weights(copies, place[1], (w0, w1, w2, w3, w4), names, w, feature, shards)
+        waits = load_weights(copies, pieces_of(pieces), names, w)
         saved = [
             copies.start(a, b)
             for a, b in ((qkv, qkv_s), (normed, normed_s), (inverse, inverse_s), (hidden, hidden_s),
                          (mix, mix_s))
         ]
         tokens = load_tokens(copies, moved, own, x)
-        allowed = masks(mask, place[2] == 0, lon_of(mask.shape[1]))
+        mask_copy.wait()
+        allowed = masks(mask, lax.axis_index("band") == 0, lon_of(mask.shape[1]))
         wait_all(g_in + saved + tokens)
         for name in names:
             wait_all(waits[name])
         grad_update, grad_gain = backward(g, w, full_gain(wg, shards), allowed, mask.shape,
                                           normed_s, inverse_s, qkv_s, gmix, gproj)
-        dw = {"merge": dm, "q": dq, "k": dk, "v": dv, "out": do, "gain": dg, "pad": dz}
-        done = send_grads(copies, place[1], x, hidden_s, mix_s, g, gproj, grad_update, grad_gain,
-                          dw, (pk, ps, qk, qs))
-        wait_all(done)
-
-
-def final_kernel(place, own, other, merge, qkv, out, gain):
+        dw = dict(zip(("merge", "q", "k", "v", "out", "gain", "pad"), dw_refs))
+        wait_all(send_grads(copies, x, hidden_s, mix_s, g, gproj, grad_update, grad_gain, dw, outs))
+
+
+def rest_kernel(out, gain, packed):
+    rows, width = gain.shape[1], out.shape[1]
+    packed[: out.shape[0], :] = out[...]
+    packed[out.shape[0] :, :] = jnp.zeros((PAD, width), BF16)
+    packed[out.shape[0] :, :rows] = jnp.broadcast_to(gain[...], (PAD, rows))
+
+
+def final_kernel(own, other, merge, qkv, out, gain):
     feature = own.shape[1]
     shards = 2 * feature // merge.shape[1]
-    first, second, half = layout(feature, shards)
-    even = place[2] % 2 == 0
+    first, second, _ = layout(feature, shards)
+    even = lax.axis_index("band") % 2 == 0
 
     def rows(name):
         table, flip = (first, False) if name in first else (second, True)
@@ -390,113 +438,129 @@
 
 
 ANY = pl.BlockSpec(memory_space=pl.ANY)
-SMEM = pl.BlockSpec(memory_space=pltpu.SMEM)
 VMEM = pl.BlockSpec(memory_space=pltpu.VMEM)
 
 
-def call(kernel, ins, outs, scratch, aliases, flops, name):
+def call(kernel, ins, outs, scratch, aliases, flops):
     moved = sum(a.size * a.dtype.itemsize for a in list(ins) + list(outs))
     return pl.pallas_call(
         kernel,
         out_shape=tuple(outs),
-        in_specs=[SMEM, VMEM] + [ANY] * (len(ins) - 2),
+        in_specs=[ANY] * len(ins),
         out_specs=tuple([ANY] * len(outs)),
         scratch_shapes=scratch,
         input_output_aliases=aliases,
         cost_estimate=pl.CostEstimate(flops=flops, bytes_accessed=moved, transcendentals=0),
-        name=name,
     )(*ins)
 
 
 def flip(value, axis, bit):
     size = lax.axis_size(axis)
     return lax.ppermute(value, axis, [(i, i ^ bit) for i in range(size)])
+
+
+def flip_on(value, bit, segment):
+    shards, segments = lax.axis_size("dp"), lax.axis_size("segment")
+    pairs = [(i * segments + segment, (i ^ bit) * segments + segment) for i in range(shards)]
+    return lax.ppermute(value, ("dp", "segment"), pairs)
+
+
+def gather(merge, qkv, rest, segment):
+    high = lax.axis_size("dp") // 2
+    merge_low = flip_on(merge, 1, segment)
+    merge_high = flip_on(merge, high, segment)
+    qkv_low = flip_on(qkv, 1, segment)
+    qkv_high = flip_on(qkv, high, segment)
+    rest_low = flip_on(rest, 1, segment)
+    rest_high = flip_on(rest, high, segment)
+    merge_both = flip_on(merge_low, high, segment)
+    qkv_both = flip_on(qkv_high, 1, segment)
+    rest_both = flip_on(rest_low, high, segment)
+    return (merge, merge_low, merge_high, merge_both, qkv, qkv_low, qkv_high, qkv_both,
+            rest, rest_low, rest_high, rest_both)
 
 
 def body(fields, cell_mask, merge_weight, qkv_weight, out_weight, norm_gain, out_cotangent):
     _, micro, row_count, lon_count, feature = fields.shape
     shards, bands = lax.axis_size("dp"), lax.axis_size("band")
     assert lax.axis_size("segment") == 2 and row_count == WH and shards == 4
-    segment, shard, band = (lax.axis_index(a) for a in ("segment", "dp", "band"))
-    place = jnp.stack([segment, shard, band]).astype(jnp.int32)
+    segment, band = lax.axis_index("segment"), lax.axis_index("band")
     cells = row_count * lon_count
     total = micro * cells
-    first, second, half = layout(feature, shards)
+    _, _, half = layout(feature, shards)
     rows = feature // shards
 
-    qkv = qkv_weight[0]
-    gain_rows = jnp.pad(norm_gain, ((0, PAD - 1), (0, feature - rows)))
-    packed = jnp.concatenate(
-        [
-            merge_weight[0],
-            qkv[:, :feature],
-            gain_rows,
-            qkv[:, feature : 2 * feature],
-            qkv[:, 2 * feature :],
-            out_weight[0],
-            jnp.zeros((PAD, feature), BF16),
-        ],
-        axis=0,
-    )
-    by_low = flip(packed, "dp", 1)
-    by_high = flip(packed, "dp", shards // 2)
-    both_first = flip(by_low[:half], "dp", shards // 2)
-    both_second = flip(by_high[half:], "dp", 1)
-    pieces = (packed, by_low, by_high, both_first, both_second)
+    def shape(*dims, dtype=BF16):
+        return jax.ShapeDtypeStruct(dims, dtype)
+
+    def room(*dims, dtype=BF16):
+        return pltpu.VMEM(dims, dtype)
+
+    merge, qkv, out = merge_weight[0], qkv_weight[0], out_weight[0]
+    rest = pl.pallas_call(
+        rest_kernel,
+        out_shape=shape(rows + PAD, feature),
+        in_specs=[VMEM, VMEM],
+        out_specs=VMEM,
+        name="pack",
+    )(out, norm_gain)
+    pieces0 = gather(merge, qkv, rest, 0)
+    token = pieces0[5][:PAD, :128] + pieces0[6][:PAD, :128]
+    token = lax.ppermute(token, "segment", [(0, 1)])
+    pieces1 = gather(merge, qkv, rest, 1)
 
     down = [(i, (i + 1) % bands) for i in range(bands)]
     up = [(j, i) for i, j in down]
     flat = (micro, cells, feature)
     source = jnp.where(segment == 0, fields[0, :, row_count - SH :], out_cotangent[0, :, row_count - SH :])
-    moved = lax.ppermute(source, "band", down).reshape(micro, SH * lon_count, feature)
+    moved = lax.ppermute(source, "band", down)
+    moved = moved.reshape(micro, SH * lon_count, feature)
     mask_moved = lax.ppermute(cell_mask[0, :, row_count - SH :], "band", down)
     mask = jnp.concatenate([mask_moved, cell_mask[0, :, : row_count - SH]], axis=1).reshape(micro, cells)
     own_fields = fields.reshape(flat)
     own_cotangent = out_cotangent.reshape(flat)
 
-    def shape(*dims, dtype=BF16):
-        return jax.ShapeDtypeStruct(dims, dtype)
-
-    def room(*dims, dtype=BF16):
-        return pltpu.VMEM(dims, dtype)
-
     square = room(feature, feature)
     tokens = room(total, feature)
+    wide = room(total, 3 * feature)
+    mask_room = pltpu.VMEM((micro, cells), jnp.int32)
     weights = [square] * 4 + [room(shards * PAD, feature)]
     merge_room = room(2 * feature, feature)
     record_rooms = [
-        room(total, feature, dtype=F32), room(total, 128, dtype=F32), tokens,
-        room(total, 3 * feature), tokens,
+        room(total, feature, dtype=F32), room(total, 128, dtype=F32), tokens, wide, tokens,
     ]
-    grad_rooms = [tokens, room(total, 3 * feature)] + [square] * 5 + [room(shards * PAD, feature), room(PAD, feature)]
+    grad_rooms = [square] * 5 + [room(shards * PAD, feature), room(PAD, feature)]
     sems = [pltpu.SemaphoreType.DMA((96,))]
     unit = 2 * total * feature * feature
+    token_shape, wide_shape = shape(total, feature), shape(total, 3 * feature)
 
     y, *records = call(
         forward_kernel,
-        (place, mask, moved, own_fields) + pieces,
-        [shape(total, feature), shape(total, feature, dtype=F32), shape(total, 128, dtype=F32),
-         shape(total, feature), shape(total, 3 * feature), shape(total, feature)],
-        [tokens, merge_room] + weights + [tokens] + record_rooms + sems,
-        {}, 6 * unit, "fwd_first",
+        (mask, moved, own_fields) + pieces0,
+        [token_shape, shape(total, feature, dtype=F32), shape(total, 128, dtype=F32),
+         token_shape, wide_shape, token_shape],
+        [mask_room, tokens, merge_room] + weights + [tokens] + record_rooms + sems,
+        {}, 6 * unit,
     )
     y0 = lax.ppermute(y, "segment", [(0, 1)])
+    gain_room = room(8, feature, dtype=F32)
+    y, g_out, *operands = call(
+        last_kernel,
+        (mask, moved, own_cotangent, y0) + pieces1 + (token, y),
+        [token_shape, token_shape, shape(8, feature, dtype=F32), token_shape, token_shape, token_shape,
+         wide_shape, token_shape],
+        [mask_room, tokens, tokens, merge_room] + weights + [tokens, tokens] + record_rooms
+        + [tokens, wide, gain_room, tokens] + sems,
+        {17: 0}, 13 * unit,
+    )
+    g0 = lax.ppermute(g_out, "segment", [(1, 0)])
     shard_shape = shape(2, half, feature)
-    y, g_out, *grads = call(
-        last_kernel,
-        (place, mask, moved, own_cotangent, y0) + pieces + (y,),
-        [shape(total, feature), shape(total, feature)] + [shard_shape] * 4,
-        [tokens, tokens, merge_room] + weights + [tokens, tokens] + record_rooms + grad_rooms + sems,
-        {10: 0}, 18 * unit, "last_section",
-    )
-    g0 = lax.ppermute(g_out, "segment", [(1, 0)])
-    inputs = (place, mask, moved, own_fields, g0) + pieces + tuple(records)
     grads = call(
-        first_kernel,
-        inputs + tuple(grads),
+        weight_kernel,
+        (y0,) + tuple(operands),
         [shard_shape] * 4,
-        [tokens, tokens] + weights + record_rooms + grad_rooms + sems,
-        {len(inputs) + i: i for i in range(4)}, 12 * unit, "bwd_first",
+        [tokens, gain_room, tokens, tokens, tokens, wide, tokens] + grad_rooms + sems,
+        {}, 5 * unit,
     )
 
     y = y.reshape(micro, cells, feature)
@@ -504,6 +568,15 @@
     back = lax.ppermute(y[:, :part], "band", up)
     section_out = jnp.concatenate([y[:, part:], back], axis=1)
     section_out = section_out.reshape(1, 1, micro, row_count, lon_count, feature)
+
+    inputs = (mask, moved, own_fields, g0) + pieces0 + tuple(records) + (section_out,)
+    grads = call(
+        first_kernel,
+        inputs + tuple(grads),
+        [shard_shape] * 4,
+        [mask_room, tokens, tokens] + weights + record_rooms + [tokens, wide] + grad_rooms + sems,
+        {len(inputs) + i: i for i in range(4)}, 12 * unit,
+    )
 
     p_keep, p_send, q_keep, q_send = grads
     high = shards // 2
@@ -527,10 +600,10 @@
             shape(1, 2 * rows, feature, dtype=F32), shape(1, rows, 3 * feature, dtype=F32),
             shape(1, rows, feature, dtype=F32), shape(1, rows, dtype=F32),
         ),
-        in_specs=[SMEM, VMEM, VMEM],
+        in_specs=[VMEM, VMEM],
         out_specs=(VMEM,) * 4,
         name="unpack",
-    )(place, mine, theirs)
+    )(mine, theirs)
     return (section_out, merge_grad, qkv_grad, out_grad, gain_grad)
 
 

time: 148 us -> 162 us (1.095)
  starting transfers between devices: 25.8 us -> 53.4 us
  waiting for transfers between devices: 80 us -> 71.7 us
  local copies, waits for them, and re-layouts: 12.9 us -> 6.34 us
    ppermute x1 -> x20, starting transfers between devices: 1.58 us -> 40.1 us  [the longest x18 36.7 us: flip_on(): return lax.ppermute(value, ('dp', 'segment'), pairs)]
    ppermute x11 -> x7, starting transfers between devices: 17.1 us -> 8.32 us  [flip(): return lax.ppermute(value, axis, [(i, i ^ bit) for i in range(size)])]
    ppermute x1, waiting for transfers between devices: 12.6 us -> 4.63 us  [body(): g0 = lax.ppermute(g_out, 'segment', [(1, 0)])]
    unnamed x34 -> x42, local copies, waits for them, and re-layouts: 8.24 us -> 2.29 us
    ppermute x1, waiting for transfers between devices: 0.01 us -> 3.83 us  [body(): mask_moved = lax.ppermute(cell_mask[0, :, row_count - SH:], 'band', down)]
    ppermute x11 -> x7, waiting for transfers between devices: 56.8 us -> 53.8 us  [flip(): return lax.ppermute(value, axis, [(i, i ^ bit) for i in range(size)])]
    ppermute x1, starting transfers between devices: 2.89 us -> 0.8 us  [body(): back = lax.ppermute(y[:, :part], 'band', up)]
    ppermute x1 -> x20, waiting for transfers between devices: 4.23 us -> 6.1 us  [the longest x18 5.31 us: flip_on(): return lax.ppermute(value, ('dp', 'segment'), pairs)]
  transfers between devices with their start and end apart: 16 -> 31, of which waited for: 12 -> 11; matrix products, arithmetic and copies ran while one was open for 6% -> 5% of each run, Pallas kernels for 0% -> 4%
where the time goes in v2:
time: 162 us; the launch traced here: 161 us
  waiting for transfers between devices  71.7 us (44%)
  starting transfers between devices  53.4 us (33%)
  Pallas kernels  21.6 us (13%)
  other arithmetic  7.02 us (4%)
  local copies, waits for them, and re-layouts  6.34 us (4%)
    ppermute x7, waiting for transfers between devices, flip(): return lax.ppermute(value, axis, [(i, i ^ bit) for i in range(size)])  53.8 us
    ppermute x18, starting transfers between devices, flip_on(): return lax.ppermute(value, ('dp', 'segment'), pairs)  36.7 us
    pallas_call x4, Pallas kernels, call(): pl.pallas_call(kernel, out_shape=tuple(outs), in_specs=[ANY] * len(ins),...  17.7 us
    ppermute x7, starting transfers between devices, flip(): return lax.ppermute(value, axis, [(i, i ^ bit) for i in range(size)])  8.32 us
    ppermute x18, waiting for transfers between devices, flip_on(): return lax.ppermute(value, ('dp', 'segment'), pairs)  5.31 us
    ppermute x1, waiting for transfers between devices, body(): g0 = lax.ppermute(g_out, 'segment', [(1, 0)])  4.63 us
    ppermute x1, waiting for transfers between devices, body(): mask_moved = lax.ppermute(cell_mask[0, :, row_count - SH:], 'band', down)  3.83 us
    ppermute x1, waiting for transfers between devices, body(): back = lax.ppermute(y[:, :part], 'band', up)  3.35 us
  transfers between devices with their start and end apart: 31, of which 11 were waited for; matrix products, arithmetic and copies ran while one was open for 5% of the time, Pallas kernels for 4%

profile of v2, /device:TPU:0, one launch (start us, length us, event | category | flops | bytes accessed | tf_op | source)
XLA Modules:
  0.0 161.2 jit_solution(14578528380210216695)
XLA Ops:
  0.6 1.6 pack.1.refs_11_.refs_12_
  2.9 4.9 %collective-permute-start.9 = (bf16[144,512]{1,0:T(8,128)(2,1)}, bf16[144,512]{1,0:T(8,128)(2,1)S(1)}, u32[]{:S(2)}, u32[]{:S(2)}) collective-permute-start(bf16[144,512]{1,0:T(8,128)(2,1)} %pack.1.refs_11_.refs_12_), channel_id=1, source_target_pairs={{0,16},{8,24},{16,0},{24,8},{1,17},{9,25},{17,1},{25,9},{2,18},{10... | collective-permute-start | bytes 442376 | tf_op jit(solution)/shard_map/ppermute | solution.py:465
  7.8 1.9 %collective-permute-start.6 = (bf16[128,1536]{1,0:T(8,128)(2,1)}, bf16[128,1536]{1,0:T(8,128)(2,1)S(1)}, u32[]{:S(2)}, u32[]{:S(2)}) collective-permute-start(bf16[128,1536]{1,0:T(8,128)(2,1)} %bitcast.36), channel_id=1, source_target_pairs={{0,16},{8,24},{16,0},{24,8},{1,17},{9,25},{17,1},{25,9},{2,18},{10... | collective-permute-start | bytes 1179656 | tf_op jit(solution)/shard_map/ppermute | solution.py:465
  9.7 1.0 select_bitcast_fusion
  10.7 2.1 %collective-permute-start.1 = (bf16[2,4,16,512]{3,2,1,0:T(8,128)(2,1)S(1)}, bf16[2,4,16,512]{3,2,1,0:T(8,128)(2,1)S(1)}, u32[]{:S(2)}, u32[]{:S(2)}) collective-permute-start(bf16[2,4,16,512]{3,2,1,0:T(8,128)(2,1)S(1)} %select_bitcast_fusion), channel_id=1, source_target_pairs={{0,1},{1,2},{2,3},{3,0},{4,5},{5,6},{6,7},{7,4},{8,9},{9,10},{10,1... | collective-permute-start | bytes 393224 | tf_op jit(solution)/shard_map/ppermute | solution.py:516
  13.6 1.6 collective-permute-start
  15.2 3.8 %collective-permute-done = s32[2,4,16]{2,1,0:T(4,128)S(1)} collective-permute-done((s32[2,4,16]{2,1,0:T(4,128)S(1)}, s32[2,4,16]{2,1,0:T(4,128)S(1)}, u32[]{:S(2)}, u32[]{:S(2)}) %collective-permute-start) | collective-permute-done | bytes 544 | tf_op jit(solution)/shard_map/ppermute | solution.py:518
  19.0 3.4 %collective-permute-start.8 = (bf16[144,512]{1,0:T(8,128)(2,1)}, bf16[144,512]{1,0:T(8,128)(2,1)S(1)}, u32[]{:S(2)}, u32[]{:S(2)}) collective-permute-start(bf16[144,512]{1,0:T(8,128)(2,1)} %pack.1.refs_11_.refs_12_), channel_id=1, source_target_pairs={{0,8},{8,0},{16,24},{24,16},{1,9},{9,1},{17,25},{25,17},{2,10},{10... | collective-permute-start | bytes 442376 | tf_op jit(solution)/shard_map/ppermute | solution.py:465
  22.4 2.4 %collective-permute-start.2 = (bf16[256,512]{1,0:T(8,128)(2,1)}, bf16[256,512]{1,0:T(8,128)(2,1)S(1)}, u32[]{:S(2)}, u32[]{:S(2)}) collective-permute-start(bf16[256,512]{1,0:T(8,128)(2,1)} %bitcast.45), channel_id=1, source_target_pairs={{0,8},{8,0},{16,24},{24,16},{1,9},{9,1},{17,25},{25,17},{2,10},{10... | collective-permute-start | bytes 786440 | tf_op jit(solution)/shard_map/ppermute | solution.py:465
  24.9 3.4 %collective-permute-start.3 = (bf16[256,512]{1,0:T(8,128)(2,1)}, bf16[256,512]{1,0:T(8,128)(2,1)S(1)}, u32[]{:S(2)}, u32[]{:S(2)}) collective-permute-start(bf16[256,512]{1,0:T(8,128)(2,1)} %bitcast.46), channel_id=1, source_target_pairs={{0,16},{8,24},{16,0},{24,8},{1,17},{9,25},{17,1},{25,9},{2,18},{10... | collective-permute-start | bytes 786440 | tf_op jit(solution)/shard_map/ppermute | solution.py:465
  29.1 3.4 %collective-permute-start.5 = (bf16[128,1536]{1,0:T(8,128)(2,1)}, bf16[128,1536]{1,0:T(8,128)(2,1)S(1)}, u32[]{:S(2)}, u32[]{:S(2)}) collective-permute-start(bf16[128,1536]{1,0:T(8,128)(2,1)} %bitcast.38), channel_id=1, source_target_pairs={{0,8},{8,0},{16,24},{24,16},{1,9},{9,1},{17,25},{25,17},{2,10},{10... | collective-permute-start | bytes 1179656 | tf_op jit(solution)/shard_map/ppermute | solution.py:465
  32.5 2.4 %collective-permute-start.7 = (bf16[128,1536]{1,0:T(8,128)(2,1)S(1)}, bf16[128,1536]{1,0:T(8,128)(2,1)S(1)}, u32[]{:S(2)}, u32[]{:S(2)}) collective-permute-start(bf16[128,1536]{1,0:T(8,128)(2,1)S(1)} %collective-permute-done.6.refs_9_.refs_10_), channel_id=1, source_target_pairs={{0,8},{8,0},{16,24},{24,16},{1,9},{9,1},{17,25},{25,17},{2,10},{10... | collective-permute-start | bytes 1179656 | tf_op jit(solution)/shard_map/ppermute | solution.py:465
  35.0 2.4 %collective-permute-start.4 = (bf16[256,512]{1,0:T(8,128)(2,1)S(1)}, bf16[256,512]{1,0:T(8,128)(2,1)S(1)}, u32[]{:S(2)}, u32[]{:S(2)}) collective-permute-start(bf16[256,512]{1,0:T(8,128)(2,1)S(1)} %collective-permute-done.2.refs_4_.refs_5_), channel_id=1, source_target_pairs={{0,16},{8,24},{16,0},{24,8},{1,17},{9,25},{17,1},{25,9},{2,18},{10... | collective-permute-start | bytes 786440 | tf_op jit(solution)/shard_map/ppermute | solution.py:465
  37.4 3.4 %collective-permute-start.10 = (bf16[144,512]{1,0:T(8,128)(2,1)S(1)}, bf16[144,512]{1,0:T(8,128)(2,1)S(1)}, u32[]{:S(2)}, u32[]{:S(2)}) collective-permute-start(bf16[144,512]{1,0:T(8,128)(2,1)S(1)} %collective-permute-done.8.refs_12_.refs_13_), channel_id=1, source_target_pairs={{0,16},{8,24},{16,0},{24,8},{1,17},{9,25},{17,1},{25,9},{2,18},{10... | collective-permute-start | bytes 442376 | tf_op jit(solution)/shard_map/ppermute | solution.py:465
  40.9 5.3 %collective-permute-done.10.refs_14_.refs_15_ = bf16[144,512]{1,0:T(8,128)(2,1)S(1)} collective-permute-done((bf16[144,512]{1,0:T(8,128)(2,1)S(1)}, bf16[144,512]{1,0:T(8,128)(2,1)S(1)}, u32[]{:S(2)}, u32[]{:S(2)}) %collective-permute-start.10) | collective-permute-done | bytes 147488 | tf_op jit(solution)/shard_map/ppermute | solution.py:465
  46.1 1.4 collective-permute-start.12
  47.5 1.4 collective-permute-start.13
  48.9 1.3 collective-permute-start.18
  50.9 1.4 collective-permute-start.17
  53.1 6.2 %shard_map.110 = (bf16[256,512]{1,0:T(8,128)(2,1)}, f32[256,512]{1,0:T(8,128)}, f32[256,128]{1,0:T(8,128)}, bf16[256,512]{1,0:T(8,128)(2,1)}, bf16[256,1536]{1,0:T(8,128)(2,1)}, /*index=5*/bf16[256,512]{1,0:T(8,128)(2,1)}) custom-call(s32[2,128]{1,0:T(2,128)} %reshape.32.refs_0_, bf16[2,64,512]{2,1,0:T(8,128)(2,1)} %bitcast.52, ...), custom_call_target="tpu_custom_call" | custom-call | flops 805306368 | bytes 5833728 | tf_op jit(solution)/shard_map/pallas_call | solution.py:446
  60.1 1.3 collective-permute-start.11
  62.8 1.3 collective-permute-start.21
  64.1 0.8 collective-permute-done.21.refs_16_
  65.7 0.9 shard_map.111
  66.6 1.3 collective-permute-start.23
  67.9 1.0 fusion.4
  68.9 0.8 collective-permute-start.22
  69.7 0.9 shard_map.112
  70.5 3.4 %collective-permute-done.22 = bf16[2,64,512]{2,1,0:T(8,128)(2,1)S(1)} collective-permute-done((bf16[2,64,512]{2,1,0:T(8,128)(2,1)S(1)}, bf16[2,64,512]{2,1,0:T(8,128)(2,1)S(1)}, u32[]{:S(2)}, u32[]{:S(2)}) %collective-permute-start.22) | collective-permute-done | bytes 131104 | tf_op jit(solution)/shard_map/ppermute | solution.py:568
  74.6 4.6 %collective-permute-done.23.refs_3_ = bf16[256,512]{1,0:T(8,128)(2,1)S(1)} collective-permute-done((bf16[256,512]{1,0:T(8,128)(2,1)}, bf16[256,512]{1,0:T(8,128)(2,1)S(1)}, u32[]{:S(2)}, u32[]{:S(2)}) %collective-permute-start.23) | collective-permute-done | bytes 262176 | tf_op jit(solution)/shard_map/ppermute | solution.py:556
  79.9 9.7 %shard_map.113 = (bf16[2,400,512]{2,1,0:T(8,128)(2,1)}, bf16[2,400,512]{2,1,0:T(8,128)(2,1)}, bf16[2,400,512]{2,1,0:T(8,128)(2,1)}, bf16[2,400,512]{2,1,0:T(8,128)(2,1)}) custom-call(s32[2,128]{1,0:T(2,128)} %reshape.32.refs_0_, bf16[2,64,512]{2,1,0:T(8,128)(2,1)} %bitcast.54, ...), custom_call_target="tpu_custom_call", output_to_operand_aliasing={{0}: (22, {}), {1}: (23, {}), {2}: (24, {}), {3}: (25, {})} | custom-call | flops 1610612736 | bytes 12649472 | tf_op jit(solution)/shard_map/pallas_call | solution.py:446
  89.7 1.0 collective-permute-start.24
  90.7 2.0 %collective-permute-start.26 = (bf16[2,400,512]{2,1,0:T(8,128)(2,1)}, bf16[2,400,512]{2,1,0:T(8,128)(2,1)S(1)}, u32[]{:S(2)}, u32[]{:S(2)}) collective-permute-start(bf16[2,400,512]{2,1,0:T(8,128)(2,1)} %get-tuple-element.52), channel_id=1, source_target_pairs={{0,8},{8,0},{16,24},{24,16},{1,9},{9,1},{17,25},{25,17},{2,10},{10... | collective-permute-start | bytes 2457608 | tf_op jit(solution)/shard_map/ppermute | solution.py:459
  92.6 14.0 %collective-permute-done.24 = bf16[2,400,512]{2,1,0:T(8,128)(2,1)S(1)} collective-permute-done((bf16[2,400,512]{2,1,0:T(8,128)(2,1)}, bf16[2,400,512]{2,1,0:T(8,128)(2,1)S(1)}, u32[]{:S(2)}, u32[]{:S(2)}) %collective-permute-start.24) | collective-permute-done | bytes 819232 | tf_op jit(solution)/shard_map/ppermute | solution.py:459
  106.7 1.5 convert_add_fusion.1
  108.1 0.8 fusion.2
  109.0 2.1 %collective-permute-start.25 = (bf16[400,512]{1,0:T(8,128)(2,1)}, bf16[400,512]{1,0:T(8,128)(2,1)}, u32[]{:S(2)}, u32[]{:S(2)}) collective-permute-start(bf16[400,512]{1,0:T(8,128)(2,1)} %fusion.2), channel_id=1, source_target_pairs={{0,8},{8,0},{16,24},{24,16},{1,9},{9,1},{17,25},{25,17},{2,10},{10... | collective-permute-start | bytes 1228808 | tf_op jit(solution)/shard_map/ppermute | solution.py:459
  111.3 0.8 fusion.3
  112.1 0.9 collective-permute-start.27
  113.0 4.3 %collective-permute-done.25 = bf16[400,512]{1,0:T(8,128)(2,1)} collective-permute-done((bf16[400,512]{1,0:T(8,128)(2,1)}, bf16[400,512]{1,0:T(8,128)(2,1)}, u32[]{:S(2)}, u32[]{:S(2)}) %collective-permute-start.25) | collective-permute-done | bytes 409632 | tf_op jit(solution)/shard_map/ppermute | solution.py:459
  117.3 3.1 %collective-permute-done.27 = bf16[400,512]{1,0:T(8,128)(2,1)} collective-permute-done((bf16[400,512]{1,0:T(8,128)(2,1)}, bf16[400,512]{1,0:T(8,128)(2,1)}, u32[]{:S(2)}, u32[]{:S(2)}) %collective-permute-start.27) | collective-permute-done | bytes 409632 | tf_op jit(solution)/shard_map/ppermute | solution.py:459
  120.4 1.4 select_convert_fusion
  121.8 2.2 %collective-permute-start.28 = (bf16[400,512]{1,0:T(8,128)(2,1)S(1)}, bf16[400,512]{1,0:T(8,128)(2,1)S(1)}, u32[]{:S(2)}, u32[]{:S(2)}) collective-permute-start(bf16[400,512]{1,0:T(8,128)(2,1)S(1)} %select_convert_fusion), channel_id=1, source_target_pairs={{0,1},{1,0},{2,3},{3,2},{4,5},{5,4},{6,7},{7,6},{8,9},{9,8},{10,11... | collective-permute-start | bytes 1228808 | tf_op jit(solution)/shard_map/ppermute | solution.py:459
  124.0 7.2 %collective-permute-done.28 = bf16[400,512]{1,0:T(8,128)(2,1)S(1)} collective-permute-done((bf16[400,512]{1,0:T(8,128)(2,1)S(1)}, bf16[400,512]{1,0:T(8,128)(2,1)S(1)}, u32[]{:S(2)}, u32[]{:S(2)}) %collective-permute-start.28) | collective-permute-done | bytes 409632 | tf_op jit(solution)/shard_map/ppermute | solution.py:459
  131.2 1.4 add_convert_fusion.1
  132.7 15.7 %collective-permute-done.29 = bf16[400,512]{1,0:T(8,128)(2,1)S(1)} collective-permute-done((bf16[400,512]{1,0:T(8,128)(2,1)S(1)}, bf16[400,512]{1,0:T(8,128)(2,1)S(1)}, u32[]{:S(2)}, u32[]{:S(2)}) %collective-permute-start.29) | collective-permute-done | bytes 409632 | tf_op jit(solution)/shard_map/ppermute | solution.py:459
  148.5 9.5 %collective-permute-done.30.other = bf16[400,512]{1,0:T(8,128)(2,1)S(1)} collective-permute-done((bf16[400,512]{1,0:T(8,128)(2,1)S(1)}, bf16[400,512]{1,0:T(8,128)(2,1)S(1)}, u32[]{:S(2)}, u32[]{:S(2)}) %collective-permute-start.30) | collective-permute-done | bytes 409632 | tf_op jit(solution)/shard_map/ppermute | solution.py:459
  158.8 2.3 %unpack.1 = (f32[1,256,512]{2,1,0:T(8,128)}, f32[1,128,1536]{2,1,0:T(8,128)}, f32[1,128,512]{2,1,0:T(8,128)}, f32[1,128]{1,0:T(1,128)}) custom-call(bf16[400,512]{1,0:T(8,128)(2,1)} %copy-done.1, bf16[400,512]{1,0:T(8,128)(2,1)} %copy-done.12), custom_call_target="tpu_custom_call" | custom-call | tf_op jit(solution)/shard_map/unpack/pallas_call | solution.py:597
  (76 shorter events, 9.0 us)
Async XLA Ops:
  2.2 22.7 %collective-permute-start.19 = (bf16[144,512]{1,0:T(8,128)(2,1)}, bf16[144,512]{1,0:T(8,128)(2,1)S(1)}, u32[]{:S(2)}, u32[]{:S(2)}) collective-permute-start(bf16[144,512]{1,0:T(8,128)(2,1)} %pack.1.refs_11_.refs_12_), channel_id=1, source_target_pairs={{4,20},{12,28},{20,4},{28,12},{5,21},{13,29},{21,5},{29,13},{6,22}... | collective-permute-start | bytes 442376 | tf_op jit(solution)/shard_map/ppermute | solution.py:465
  2.9 25.5 %collective-permute-start.9 = (bf16[144,512]{1,0:T(8,128)(2,1)}, bf16[144,512]{1,0:T(8,128)(2,1)S(1)}, u32[]{:S(2)}, u32[]{:S(2)}) collective-permute-start(bf16[144,512]{1,0:T(8,128)(2,1)} %pack.1.refs_11_.refs_12_), channel_id=1, source_target_pairs={{0,16},{8,24},{16,0},{24,8},{1,17},{9,25},{17,1},{25,9},{2,18},{10... | collective-permute-start | bytes 442376 | tf_op jit(solution)/shard_map/ppermute | solution.py:465
  7.8 24.7 %collective-permute-start.6 = (bf16[128,1536]{1,0:T(8,128)(2,1)}, bf16[128,1536]{1,0:T(8,128)(2,1)S(1)}, u32[]{:S(2)}, u32[]{:S(2)}) collective-permute-start(bf16[128,1536]{1,0:T(8,128)(2,1)} %bitcast.36), channel_id=1, source_target_pairs={{0,16},{8,24},{16,0},{24,8},{1,17},{9,25},{17,1},{25,9},{2,18},{10... | collective-permute-start | bytes 1179656 | tf_op jit(solution)/shard_map/ppermute | solution.py:465
  10.7 11.7 %collective-permute-start.1 = (bf16[2,4,16,512]{3,2,1,0:T(8,128)(2,1)S(1)}, bf16[2,4,16,512]{3,2,1,0:T(8,128)(2,1)S(1)}, u32[]{:S(2)}, u32[]{:S(2)}) collective-permute-start(bf16[2,4,16,512]{3,2,1,0:T(8,128)(2,1)S(1)} %select_bitcast_fusion), channel_id=1, source_target_pairs={{0,1},{1,2},{2,3},{3,0},{4,5},{5,6},{6,7},{7,4},{8,9},{9,10},{10,1... | collective-permute-start | bytes 393224 | tf_op jit(solution)/shard_map/ppermute | solution.py:516
  13.6 5.4 %collective-permute-start = (s32[2,4,16]{2,1,0:T(4,128)S(1)}, s32[2,4,16]{2,1,0:T(4,128)S(1)}, u32[]{:S(2)}, u32[]{:S(2)}) collective-permute-start(s32[2,4,16]{2,1,0:T(4,128)S(1)} %get-tuple-element.59), channel_id=1, source_target_pairs={{0,1},{1,2},{2,3},{3,0},{4,5},{5,6},{6,7},{7,4},{8,9},{9,10},{10,1... | collective-permute-start | bytes 1544 | tf_op jit(solution)/shard_map/ppermute | solution.py:518
  19.0 10.0 %collective-permute-start.8 = (bf16[144,512]{1,0:T(8,128)(2,1)}, bf16[144,512]{1,0:T(8,128)(2,1)S(1)}, u32[]{:S(2)}, u32[]{:S(2)}) collective-permute-start(bf16[144,512]{1,0:T(8,128)(2,1)} %pack.1.refs_11_.refs_12_), channel_id=1, source_target_pairs={{0,8},{8,0},{16,24},{24,16},{1,9},{9,1},{17,25},{25,17},{2,10},{10... | collective-permute-start | bytes 442376 | tf_op jit(solution)/shard_map/ppermute | solution.py:465
  22.4 30.6 %copy-start.11 = (bf16[2,4,16,512]{3,2,1,0:T(8,128)(2,1)}, bf16[2,4,16,512]{3,2,1,0:T(8,128)(2,1)S(1)}, u32[]{:S(2)}) copy-start(bf16[2,4,16,512]{3,2,1,0:T(8,128)(2,1)S(1)} %collective-permute-done.1) | copy-start | bytes 393220
  22.4 12.5 %collective-permute-start.2 = (bf16[256,512]{1,0:T(8,128)(2,1)}, bf16[256,512]{1,0:T(8,128)(2,1)S(1)}, u32[]{:S(2)}, u32[]{:S(2)}) collective-permute-start(bf16[256,512]{1,0:T(8,128)(2,1)} %bitcast.45), channel_id=1, source_target_pairs={{0,8},{8,0},{16,24},{24,16},{1,9},{9,1},{17,25},{25,17},{2,10},{10... | collective-permute-start | bytes 786440 | tf_op jit(solution)/shard_map/ppermute | solution.py:465
  24.9 40.0 %copy-start.18 = (bf16[144,512]{1,0:T(8,128)(2,1)}, bf16[144,512]{1,0:T(8,128)(2,1)S(1)}, u32[]{:S(2)}) copy-start(bf16[144,512]{1,0:T(8,128)(2,1)S(1)} %collective-permute-done.19.refs_14_) | copy-start | bytes 442372
  24.9 12.5 %collective-permute-start.3 = (bf16[256,512]{1,0:T(8,128)(2,1)}, bf16[256,512]{1,0:T(8,128)(2,1)S(1)}, u32[]{:S(2)}, u32[]{:S(2)}) collective-permute-start(bf16[256,512]{1,0:T(8,128)(2,1)} %bitcast.46), channel_id=1, source_target_pairs={{0,16},{8,24},{16,0},{24,8},{1,17},{9,25},{17,1},{25,9},{2,18},{10... | collective-permute-start | bytes 786440 | tf_op jit(solution)/shard_map/ppermute | solution.py:465
  28.4 24.7 %copy-start.8 = (bf16[144,512]{1,0:T(8,128)(2,1)}, bf16[144,512]{1,0:T(8,128)(2,1)S(1)}, u32[]{:S(2)}) copy-start(bf16[144,512]{1,0:T(8,128)(2,1)S(1)} %collective-permute-done.9.refs_13_.refs_14_) | copy-start | bytes 442372
  28.4 19.1 %collective-permute-start.16 = (bf16[128,1536]{1,0:T(8,128)(2,1)}, bf16[128,1536]{1,0:T(8,128)(2,1)S(1)}, u32[]{:S(2)}, u32[]{:S(2)}) collective-permute-start(bf16[128,1536]{1,0:T(8,128)(2,1)} %bitcast.37), channel_id=1, source_target_pairs={{4,20},{12,28},{20,4},{28,12},{5,21},{13,29},{21,5},{29,13},{6,22}... | collective-permute-start | bytes 1179656 | tf_op jit(solution)/shard_map/ppermute | solution.py:465
  29.1 24.0 %copy-start.9 = (bf16[144,512]{1,0:T(8,128)(2,1)}, bf16[144,512]{1,0:T(8,128)(2,1)S(1)}, u32[]{:S(2)}) copy-start(bf16[144,512]{1,0:T(8,128)(2,1)S(1)} %collective-permute-done.8.refs_12_.refs_13_) | copy-start | bytes 442372
  29.1 19.8 %collective-permute-start.5 = (bf16[128,1536]{1,0:T(8,128)(2,1)}, bf16[128,1536]{1,0:T(8,128)(2,1)S(1)}, u32[]{:S(2)}, u32[]{:S(2)}) collective-permute-start(bf16[128,1536]{1,0:T(8,128)(2,1)} %bitcast.38), channel_id=1, source_target_pairs={{0,8},{8,0},{16,24},{24,16},{1,9},{9,1},{17,25},{25,17},{2,10},{10... | collective-permute-start | bytes 1179656 | tf_op jit(solution)/shard_map/ppermute | solution.py:465
  32.5 20.6 %copy-start.2 = (bf16[128,1536]{1,0:T(8,128)(2,1)}, bf16[128,1536]{1,0:T(8,128)(2,1)S(1)}, u32[]{:S(2)}) copy-start(bf16[128,1536]{1,0:T(8,128)(2,1)S(1)} %collective-permute-done.6.refs_9_.refs_10_) | copy-start | bytes 1179652
  32.5 18.4 %collective-permute-start.7 = (bf16[128,1536]{1,0:T(8,128)(2,1)S(1)}, bf16[128,1536]{1,0:T(8,128)(2,1)S(1)}, u32[]{:S(2)}, u32[]{:S(2)}) collective-permute-start(bf16[128,1536]{1,0:T(8,128)(2,1)S(1)} %collective-permute-done.6.refs_9_.refs_10_), channel_id=1, source_target_pairs={{0,8},{8,0},{16,24},{24,16},{1,9},{9,1},{17,25},{25,17},{2,10},{10... | collective-permute-start | bytes 1179656 | tf_op jit(solution)/shard_map/ppermute | solution.py:465
  35.0 18.1 %copy-start.5 = (bf16[256,512]{1,0:T(8,128)(2,1)}, bf16[256,512]{1,0:T(8,128)(2,1)S(1)}, u32[]{:S(2)}) copy-start(bf16[256,512]{1,0:T(8,128)(2,1)S(1)} %collective-permute-done.2.refs_4_.refs_5_) | copy-start | bytes 786436
  35.0 15.2 %collective-permute-start.4 = (bf16[256,512]{1,0:T(8,128)(2,1)S(1)}, bf16[256,512]{1,0:T(8,128)(2,1)S(1)}, u32[]{:S(2)}, u32[]{:S(2)}) collective-permute-start(bf16[256,512]{1,0:T(8,128)(2,1)S(1)} %collective-permute-done.2.refs_4_.refs_5_), channel_id=1, source_target_pairs={{0,16},{8,24},{16,0},{24,8},{1,17},{9,25},{17,1},{25,9},{2,18},{10... | collective-permute-start | bytes 786440 | tf_op jit(solution)/shard_map/ppermute | solution.py:465
  37.4 15.7 %copy-start.6 = (bf16[256,512]{1,0:T(8,128)(2,1)}, bf16[256,512]{1,0:T(8,128)(2,1)S(1)}, u32[]{:S(2)}) copy-start(bf16[256,512]{1,0:T(8,128)(2,1)S(1)} %collective-permute-done.3.refs_5_.refs_6_) | copy-start | bytes 786436
  37.4 8.7 %collective-permute-start.10 = (bf16[144,512]{1,0:T(8,128)(2,1)S(1)}, bf16[144,512]{1,0:T(8,128)(2,1)S(1)}, u32[]{:S(2)}, u32[]{:S(2)}) collective-permute-start(bf16[144,512]{1,0:T(8,128)(2,1)S(1)} %collective-permute-done.8.refs_12_.refs_13_), channel_id=1, source_target_pairs={{0,16},{8,24},{16,0},{24,8},{1,17},{9,25},{17,1},{25,9},{2,18},{10... | collective-permute-start | bytes 442376 | tf_op jit(solution)/shard_map/ppermute | solution.py:465
  46.1 7.0 %copy-start.10 = (bf16[144,512]{1,0:T(8,128)(2,1)}, bf16[144,512]{1,0:T(8,128)(2,1)S(1)}, u32[]{:S(2)}) copy-start(bf16[144,512]{1,0:T(8,128)(2,1)S(1)} %collective-permute-done.10.refs_14_.refs_15_) | copy-start | bytes 442372
  46.1 13.2 %collective-permute-start.12 = (bf16[256,512]{1,0:T(8,128)(2,1)}, bf16[256,512]{1,0:T(8,128)(2,1)}, u32[]{:S(2)}, u32[]{:S(2)}) collective-permute-start(bf16[256,512]{1,0:T(8,128)(2,1)} %bitcast.47), channel_id=1, source_target_pairs={{4,12},{12,4},{20,28},{28,20},{5,13},{13,5},{21,29},{29,21},{6,14}... | collective-permute-start | bytes 786440 | tf_op jit(solution)/shard_map/ppermute | solution.py:465
  47.5 17.4 %copy-start.14 = (bf16[128,1536]{1,0:T(8,128)(2,1)}, bf16[128,1536]{1,0:T(8,128)(2,1)S(1)}, u32[]{:S(2)}) copy-start(bf16[128,1536]{1,0:T(8,128)(2,1)S(1)} %collective-permute-done.16.refs_10_) | copy-start | bytes 1179652
  47.5 13.9 %collective-permute-start.13 = (bf16[256,512]{1,0:T(8,128)(2,1)}, bf16[256,512]{1,0:T(8,128)(2,1)}, u32[]{:S(2)}, u32[]{:S(2)}) collective-permute-start(bf16[256,512]{1,0:T(8,128)(2,1)} %bitcast.48), channel_id=1, source_target_pairs={{4,20},{12,28},{20,4},{28,12},{5,21},{13,29},{21,5},{29,13},{6,22}... | collective-permute-start | bytes 786440 | tf_op jit(solution)/shard_map/ppermute | solution.py:465
  48.9 4.2 %copy-start.3 = (bf16[128,1536]{1,0:T(8,128)(2,1)}, bf16[128,1536]{1,0:T(8,128)(2,1)S(1)}, u32[]{:S(2)}) copy-start(bf16[128,1536]{1,0:T(8,128)(2,1)S(1)} %collective-permute-done.5.refs_8_.refs_9_) | copy-start | bytes 1179652
  48.9 11.2 %collective-permute-start.18 = (bf16[144,512]{1,0:T(8,128)(2,1)}, bf16[144,512]{1,0:T(8,128)(2,1)}, u32[]{:S(2)}, u32[]{:S(2)}) collective-permute-start(bf16[144,512]{1,0:T(8,128)(2,1)} %pack.1.refs_11_.refs_12_), channel_id=1, source_target_pairs={{4,12},{12,4},{20,28},{28,20},{5,13},{13,5},{21,29},{29,21},{6,14}... | collective-permute-start | bytes 442376 | tf_op jit(solution)/shard_map/ppermute | solution.py:465
  50.2 2.9 %copy-start.7 = (bf16[256,512]{1,0:T(8,128)(2,1)}, bf16[256,512]{1,0:T(8,128)(2,1)S(1)}, u32[]{:S(2)}) copy-start(bf16[256,512]{1,0:T(8,128)(2,1)S(1)} %collective-permute-done.4.refs_6_.refs_7_) | copy-start | bytes 786436
  50.2 13.8 %collective-permute-start.15 = (bf16[128,1536]{1,0:T(8,128)(2,1)}, bf16[128,1536]{1,0:T(8,128)(2,1)S(1)}, u32[]{:S(2)}, u32[]{:S(2)}) collective-permute-start(bf16[128,1536]{1,0:T(8,128)(2,1)} %bitcast.39), channel_id=1, source_target_pairs={{4,12},{12,4},{20,28},{28,20},{5,13},{13,5},{21,29},{29,21},{6,14}... | collective-permute-start | bytes 1179656 | tf_op jit(solution)/shard_map/ppermute | solution.py:465
  50.9 2.2 %copy-start.4 = (bf16[128,1536]{1,0:T(8,128)(2,1)}, bf16[128,1536]{1,0:T(8,128)(2,1)S(1)}, u32[]{:S(2)}) copy-start(bf16[128,1536]{1,0:T(8,128)(2,1)S(1)} %collective-permute-done.7.refs_10_.refs_11_) | copy-start | bytes 1179652
  50.9 14.0 %collective-permute-start.17 = (bf16[128,1536]{1,0:T(8,128)(2,1)S(1)}, bf16[128,1536]{1,0:T(8,128)(2,1)}, u32[]{:S(2)}, u32[]{:S(2)}) collective-permute-start(bf16[128,1536]{1,0:T(8,128)(2,1)S(1)} %collective-permute-done.16.refs_10_), channel_id=1, source_target_pairs={{4,12},{12,4},{20,28},{28,20},{5,13},{13,5},{21,29},{29,21},{6,14}... | collective-permute-start | bytes 1179656 | tf_op jit(solution)/shard_map/ppermute | solution.py:465
  59.4 5.5 %collective-permute-start.14 = (bf16[256,512]{1,0:T(8,128)(2,1)}, bf16[256,512]{1,0:T(8,128)(2,1)S(1)}, u32[]{:S(2)}, u32[]{:S(2)}) collective-permute-start(bf16[256,512]{1,0:T(8,128)(2,1)} %collective-permute-done.12.refs_5_), channel_id=1, source_target_pairs={{4,20},{12,28},{20,4},{28,12},{5,21},{13,29},{21,5},{29,13},{6,22}... | collective-permute-start | bytes 786440 | tf_op jit(solution)/shard_map/ppermute | solution.py:465
  60.1 4.8 %collective-permute-start.11 = (bf16[256,512]{1,0:T(8,128)(2,1)}, bf16[256,512]{1,0:T(8,128)(2,1)S(1)}, u32[]{:S(2)}, u32[]{:S(2)}) collective-permute-start(bf16[256,512]{1,0:T(8,128)(2,1)} %get-tuple-element.31.refs_17_), channel_id=1, source_target_pairs={{0,4},{1,5},{2,6},{3,7},{8,12},{9,13},{10,14},{11,15},{16,20},{17,... | collective-permute-start | bytes 786440 | tf_op jit(solution)/shard_map/ppermute | solution.py:545
  61.4 1.4 collective-permute-start.20
  62.8 2.2 %copy-start.19 = (bf16[144,512]{1,0:T(8,128)(2,1)}, bf16[144,512]{1,0:T(8,128)(2,1)S(1)}, u32[]{:S(2)}) copy-start(bf16[144,512]{1,0:T(8,128)(2,1)S(1)} %collective-permute-done.20.refs_15_) | copy-start | bytes 442372
  62.8 2.1 %collective-permute-start.21 = (bf16[16,128]{1,0:T(8,128)(2,1)S(1)}, bf16[16,128]{1,0:T(8,128)(2,1)S(1)}, u32[]{:S(2)}, u32[]{:S(2)}) collective-permute-start(bf16[16,128]{1,0:T(8,128)(2,1)S(1)} %slice_add_fusion), channel_id=1, source_target_pairs={{0,4},{1,5},{2,6},{3,7},{8,12},{9,13},{10,14},{11,15},{16,20},{17,... | collective-permute-start | bytes 12296 | tf_op jit(solution)/shard_map/ppermute | solution.py:509
  64.1 0.9 copy-start.15
  64.9 0.8 copy-start.16
  66.6 12.7 %collective-permute-start.23 = (bf16[256,512]{1,0:T(8,128)(2,1)}, bf16[256,512]{1,0:T(8,128)(2,1)S(1)}, u32[]{:S(2)}, u32[]{:S(2)}) collective-permute-start(bf16[256,512]{1,0:T(8,128)(2,1)} %get-tuple-element.33), channel_id=1, source_target_pairs={{4,0},{5,1},{6,2},{7,3},{12,8},{13,9},{14,10},{15,11},{20,16},{21,... | collective-permute-start | bytes 786440 | tf_op jit(solution)/shard_map/ppermute | solution.py:556
  68.9 5.0 %collective-permute-start.22 = (bf16[2,64,512]{2,1,0:T(8,128)(2,1)S(1)}, bf16[2,64,512]{2,1,0:T(8,128)(2,1)S(1)}, u32[]{:S(2)}, u32[]{:S(2)}) collective-permute-start(bf16[2,64,512]{2,1,0:T(8,128)(2,1)S(1)} %get-tuple-element.58), channel_id=1, source_target_pairs={{1,0},{2,1},{3,2},{0,3},{5,4},{6,5},{7,6},{4,7},{9,8},{10,9},{11,1... | collective-permute-start | bytes 393224 | tf_op jit(solution)/shard_map/ppermute | solution.py:568
  89.7 17.0 %collective-permute-start.24 = (bf16[2,400,512]{2,1,0:T(8,128)(2,1)}, bf16[2,400,512]{2,1,0:T(8,128)(2,1)S(1)}, u32[]{:S(2)}, u32[]{:S(2)}) collective-permute-start(bf16[2,400,512]{2,1,0:T(8,128)(2,1)} %get-tuple-element.50), channel_id=1, source_target_pairs={{0,16},{8,24},{16,0},{24,8},{1,17},{9,25},{17,1},{25,9},{2,18},{10... | collective-permute-start | bytes 2457608 | tf_op jit(solution)/shard_map/ppermute | solution.py:459
  90.7 20.4 %collective-permute-start.26 = (bf16[2,400,512]{2,1,0:T(8,128)(2,1)}, bf16[2,400,512]{2,1,0:T(8,128)(2,1)S(1)}, u32[]{:S(2)}, u32[]{:S(2)}) collective-permute-start(bf16[2,400,512]{2,1,0:T(8,128)(2,1)} %get-tuple-element.52), channel_id=1, source_target_pairs={{0,8},{8,0},{16,24},{24,16},{1,9},{9,1},{17,25},{25,17},{2,10},{10... | collective-permute-start | bytes 2457608 | tf_op jit(solution)/shard_map/ppermute | solution.py:459
  106.7 4.4 %copy-start = (bf16[2,400,512]{2,1,0:T(8,128)(2,1)S(1)}, bf16[2,400,512]{2,1,0:T(8,128)(2,1)}, u32[]{:S(2)}) copy-start(bf16[2,400,512]{2,1,0:T(8,128)(2,1)} %get-tuple-element.51) | copy-start | bytes 2457604
  109.0 8.4 %collective-permute-start.25 = (bf16[400,512]{1,0:T(8,128)(2,1)}, bf16[400,512]{1,0:T(8,128)(2,1)}, u32[]{:S(2)}, u32[]{:S(2)}) collective-permute-start(bf16[400,512]{1,0:T(8,128)(2,1)} %fusion.2), channel_id=1, source_target_pairs={{0,8},{8,0},{16,24},{24,16},{1,9},{9,1},{17,25},{25,17},{2,10},{10... | collective-permute-start | bytes 1228808 | tf_op jit(solution)/shard_map/ppermute | solution.py:459
  112.1 8.3 %collective-permute-start.27 = (bf16[400,512]{1,0:T(8,128)(2,1)}, bf16[400,512]{1,0:T(8,128)(2,1)}, u32[]{:S(2)}, u32[]{:S(2)}) collective-permute-start(bf16[400,512]{1,0:T(8,128)(2,1)} %fusion.3), channel_id=1, source_target_pairs={{0,16},{8,24},{16,0},{24,8},{1,17},{9,25},{17,1},{25,9},{2,18},{10... | collective-permute-start | bytes 1228808 | tf_op jit(solution)/shard_map/ppermute | solution.py:459
  121.8 9.4 %collective-permute-start.28 = (bf16[400,512]{1,0:T(8,128)(2,1)S(1)}, bf16[400,512]{1,0:T(8,128)(2,1)S(1)}, u32[]{:S(2)}, u32[]{:S(2)}) collective-permute-start(bf16[400,512]{1,0:T(8,128)(2,1)S(1)} %select_convert_fusion), channel_id=1, source_target_pairs={{0,1},{1,0},{2,3},{3,2},{4,5},{5,4},{6,7},{7,6},{8,9},{9,8},{10,11... | collective-permute-start | bytes 1228808 | tf_op jit(solution)/shard_map/ppermute | solution.py:459
  132.6 15.8 %collective-permute-start.29 = (bf16[400,512]{1,0:T(8,128)(2,1)S(1)}, bf16[400,512]{1,0:T(8,128)(2,1)S(1)}, u32[]{:S(2)}, u32[]{:S(2)}) collective-permute-start(bf16[400,512]{1,0:T(8,128)(2,1)S(1)} %add_convert_fusion.1), channel_id=1, source_target_pairs={{0,2},{1,3},{2,0},{3,1},{4,6},{5,7},{6,4},{7,5},{8,10},{9,11},{10,... | collective-permute-start | bytes 1228808 | tf_op jit(solution)/shard_map/ppermute | solution.py:459
  148.5 9.6 %copy-start.1 = (bf16[400,512]{1,0:T(8,128)(2,1)}, bf16[400,512]{1,0:T(8,128)(2,1)S(1)}, u32[]{:S(2)}) copy-start(bf16[400,512]{1,0:T(8,128)(2,1)S(1)} %add_convert_fusion.own) | copy-start | bytes 1228804
  148.5 9.6 %collective-permute-start.30 = (bf16[400,512]{1,0:T(8,128)(2,1)S(1)}, bf16[400,512]{1,0:T(8,128)(2,1)S(1)}, u32[]{:S(2)}, u32[]{:S(2)}) collective-permute-start(bf16[400,512]{1,0:T(8,128)(2,1)S(1)} %add_convert_fusion.own), channel_id=1, source_target_pairs={{0,1},{1,0},{2,3},{3,2},{4,5},{5,4},{6,7},{7,6},{8,9},{9,8},{10,11... | collective-permute-start | bytes 1228808 | tf_op jit(solution)/shard_map/ppermute | solution.py:459
  (4 other events, 2.7 us)

commit v3 on v2

--- a/solution.py
+++ b/solution.py
@@ -12,6 +12,7 @@
 SH = 4
 SW = 8
 PAD = 16
+CHUNKS = 2
 
 EPSILON = 1e-05
 MASKED = -1e30
@@ -233,15 +234,16 @@
 
 def send_grads(copies, x, hidden, mix, grad_out, grad_proj, grad_update, grad_gain, dw, outs):
     feature = x.shape[1]
-    p_keep, p_send, q_keep, q_send = outs
-    shards = 2 * p_keep.shape[0]
+    shards = 2 * outs[0].shape[0]
     first, second, _ = layout(feature, shards)
     me = lax.axis_index("dp")
     low, high = me % 2, me // 2
     rows = feature // shards
+    width = feature // CHUNKS
     started = []
 
-    def target(name, by_low, by_high):
+    def target(name, chunk, by_low, by_high):
+        p_keep, p_send, q_keep, q_send = outs[4 * chunk : 4 * chunk + 4]
         if name in first:
             start, size = first[name]
             ref = (p_send if by_high else p_keep).at[by_low]
@@ -251,12 +253,14 @@
         return ref.at[pl.ds(start, size)]
 
     def emit(name, period):
-        for by_high in range(2):
-            for by_low in range(2):
-                owner = (high ^ by_high) * 2 + (low ^ by_low)
-                to = target(name, by_low, by_high)
-                at = pl.multiple_of((owner * to.shape[0]) % period, to.shape[0])
-                started.append(copies.start(dw[name].at[pl.ds(at, to.shape[0])], to))
+        for chunk in range(CHUNKS):
+            for by_high in range(2):
+                for by_low in range(2):
+                    owner = (high ^ by_high) * 2 + (low ^ by_low)
+                    to = target(name, chunk, by_low, by_high)
+                    at = pl.multiple_of((owner * to.shape[0]) % period, to.shape[0])
+                    part = dw[name].at[pl.ds(at, to.shape[0]), pl.ds(chunk * width, width)]
+                    started.append(copies.start(part, to))
 
     dw["out"][...] = dot_tn(mix[...], grad_out[...]).astype(BF16)
     emit("out", feature)
@@ -320,7 +324,7 @@
 
 def last_kernel(*refs):
     mask_in, moved, own, y0, *rest = refs
-    pieces, rest = rest[:12], rest[14:]
+    pieces, rest = rest[:12], rest[13:]
     y, g0, gain_out, g_out, hidden, mix, proj_out, update_out, *rest = rest
     (mask, x, g, wm, wq, wk, wv, wo, wg, y_s, g_s, normed_s, inverse_s, hidden_s, qkv_s, mix_s,
      gmix, gproj, gain_s, update_s, sems) = rest
@@ -364,7 +368,7 @@
 
 
 def weight_kernel(*refs):
-    ins, outs, rest = refs[:7], refs[7:11], refs[11:]
+    ins, outs, rest = refs[:7], refs[7 : 7 + 4 * CHUNKS], refs[7 + 4 * CHUNKS :]
     scratch, dw_refs, sems = rest[:7], rest[7:14], rest[14]
 
     @role(1)
@@ -380,7 +384,8 @@
     mask_in, moved, own, g0, *rest = refs
     pieces, rest = rest[:12], rest[12:]
     normed, inverse, hidden, qkv, mix, *rest = rest
-    outs, rest = rest[5:9], rest[9:]
+    skip, count = 1 + 4 * CHUNKS, 4 * CHUNKS
+    outs, rest = rest[skip : skip + count], rest[skip + count :]
     (mask, x, g, wq, wk, wv, wo, wg, normed_s, inverse_s, hidden_s, qkv_s, mix_s,
      gmix, gproj, *dw_refs, sems) = rest
 
@@ -417,24 +422,29 @@
     packed[out.shape[0] :, :rows] = jnp.broadcast_to(gain[...], (PAD, rows))
 
 
-def final_kernel(own, other, merge, qkv, out, gain):
-    feature = own.shape[1]
+def final_kernel(*refs):
+    halves, (merge, qkv, out, gain) = refs[: 2 * CHUNKS], refs[2 * CHUNKS :]
+    feature = merge.shape[2]
     shards = 2 * feature // merge.shape[1]
     first, second, _ = layout(feature, shards)
     even = lax.axis_index("band") % 2 == 0
-
-    def rows(name):
+    width = feature // CHUNKS
+
+    def rows(name, chunk):
+        own, other = halves[2 * chunk], halves[2 * chunk + 1]
         table, flip = (first, False) if name in first else (second, True)
         start, size = table[name]
         mine, theirs = own[start : start + size, :], other[start : start + size, :]
         a, b = (theirs, mine) if flip else (mine, theirs)
         return jnp.where(even, a.astype(F32), b.astype(F32))
 
-    merge[0] = rows("merge")
-    for i, name in enumerate(("q", "k", "v")):
-        qkv[0, :, i * feature : (i + 1) * feature] = rows(name)
-    out[0] = rows("out")
-    gain[...] = rows("gain")[:1, : gain.shape[1]]
+    for chunk in range(CHUNKS):
+        at = chunk * width
+        merge[0, :, at : at + width] = rows("merge", chunk)
+        for i, name in enumerate(("q", "k", "v")):
+            qkv[0, :, i * feature + at : i * feature + at + width] = rows(name, chunk)
+        out[0, :, at : at + width] = rows("out", chunk)
+    gain[...] = rows("gain", 0)[:1, : gain.shape[1]]
 
 
 ANY = pl.BlockSpec(memory_space=pl.ANY)
@@ -459,23 +469,18 @@
     return lax.ppermute(value, axis, [(i, i ^ bit) for i in range(size)])
 
 
-def flip_on(value, bit, segment):
-    shards, segments = lax.axis_size("dp"), lax.axis_size("segment")
-    pairs = [(i * segments + segment, (i ^ bit) * segments + segment) for i in range(shards)]
-    return lax.ppermute(value, ("dp", "segment"), pairs)
-
-
-def gather(merge, qkv, rest, segment):
+def gather(merge, qkv, rest):
     high = lax.axis_size("dp") // 2
-    merge_low = flip_on(merge, 1, segment)
-    merge_high = flip_on(merge, high, segment)
-    qkv_low = flip_on(qkv, 1, segment)
-    qkv_high = flip_on(qkv, high, segment)
-    rest_low = flip_on(rest, 1, segment)
-    rest_high = flip_on(rest, high, segment)
-    merge_both = flip_on(merge_low, high, segment)
-    qkv_both = flip_on(qkv_high, 1, segment)
-    rest_both = flip_on(rest_low, high, segment)
+
+    def named(value, bit):
+        return flip(value, "dp", bit)
+
+    merge_low, merge_high = named(merge, 1), named(merge, high)
+    qkv_low, qkv_high = named(qkv, 1), named(qkv, high)
+    rest_low, rest_high = named(rest, 1), named(rest, high)
+    merge_both = named(merge_low, high)
+    qkv_both = named(qkv_high, 1)
+    rest_both = named(rest_low, high)
     return (merge, merge_low, merge_high, merge_both, qkv, qkv_low, qkv_high, qkv_both,
             rest, rest_low, rest_high, rest_both)
 
@@ -504,10 +509,7 @@
         out_specs=VMEM,
         name="pack",
     )(out, norm_gain)
-    pieces0 = gather(merge, qkv, rest, 0)
-    token = pieces0[5][:PAD, :128] + pieces0[6][:PAD, :128]
-    token = lax.ppermute(token, "segment", [(0, 1)])
-    pieces1 = gather(merge, qkv, rest, 1)
+    pieces = gather(merge, qkv, rest)
 
     down = [(i, (i + 1) % bands) for i in range(bands)]
     up = [(j, i) for i, j in down]
@@ -530,13 +532,13 @@
         room(total, feature, dtype=F32), room(total, 128, dtype=F32), tokens, wide, tokens,
     ]
     grad_rooms = [square] * 5 + [room(shards * PAD, feature), room(PAD, feature)]
-    sems = [pltpu.SemaphoreType.DMA((96,))]
+    sems = [pltpu.SemaphoreType.DMA((128,))]
     unit = 2 * total * feature * feature
     token_shape, wide_shape = shape(total, feature), shape(total, 3 * feature)
 
     y, *records = call(
         forward_kernel,
-        (mask, moved, own_fields) + pieces0,
+        (mask, moved, own_fields) + pieces,
         [token_shape, shape(total, feature, dtype=F32), shape(total, 128, dtype=F32),
          token_shape, wide_shape, token_shape],
         [mask_room, tokens, merge_room] + weights + [tokens] + record_rooms + sems,
@@ -546,19 +548,19 @@
     gain_room = room(8, feature, dtype=F32)
     y, g_out, *operands = call(
         last_kernel,
-        (mask, moved, own_cotangent, y0) + pieces1 + (token, y),
+        (mask, moved, own_cotangent, y0) + pieces + (y,),
         [token_shape, token_shape, shape(8, feature, dtype=F32), token_shape, token_shape, token_shape,
          wide_shape, token_shape],
         [mask_room, tokens, tokens, merge_room] + weights + [tokens, tokens] + record_rooms
         + [tokens, wide, gain_room, tokens] + sems,
-        {17: 0}, 13 * unit,
+        {16: 0}, 13 * unit,
     )
     g0 = lax.ppermute(g_out, "segment", [(1, 0)])
-    shard_shape = shape(2, half, feature)
+    shard_shapes = [shape(2, half, feature // CHUNKS)] * (4 * CHUNKS)
     grads = call(
         weight_kernel,
         (y0,) + tuple(operands),
-        [shard_shape] * 4,
+        shard_shapes,
         [tokens, gain_room, tokens, tokens, tokens, wide, tokens] + grad_rooms + sems,
         {}, 5 * unit,
     )
@@ -569,41 +571,48 @@
     section_out = jnp.concatenate([y[:, part:], back], axis=1)
     section_out = section_out.reshape(1, 1, micro, row_count, lon_count, feature)
 
-    inputs = (mask, moved, own_fields, g0) + pieces0 + tuple(records) + (section_out,)
+    inputs = (mask, moved, own_fields, g0) + pieces + tuple(records) + (section_out,)
     grads = call(
         first_kernel,
         inputs + tuple(grads),
-        [shard_shape] * 4,
+        shard_shapes,
         [mask_room, tokens, tokens] + weights + record_rooms + [tokens, wide] + grad_rooms + sems,
-        {len(inputs) + i: i for i in range(4)}, 12 * unit,
-    )
-
-    p_keep, p_send, q_keep, q_send = grads
+        {len(inputs) + i: i for i in range(4 * CHUNKS)}, 12 * unit,
+    )
+
     high = shards // 2
-    p_sum = p_keep.astype(F32) + flip(p_send, "dp", high).astype(F32)
-    q_sum = q_keep.astype(F32) + flip(q_send, "dp", 1).astype(F32)
-    p_sum = p_sum[0] + flip(p_sum[1].astype(BF16), "dp", 1).astype(F32)
-    q_sum = q_sum[0] + flip(q_sum[1].astype(BF16), "dp", high).astype(F32)
-
     even = band % 2 == 0
-    mine = jnp.where(even, p_sum, q_sum)
-    theirs = jnp.where(even, q_sum, p_sum).astype(BF16)
-    mine = (mine + flip(theirs, "band", 1).astype(F32)).astype(BF16)
-    bit = 2
-    while bit < bands:
-        mine = (mine.astype(F32) + flip(mine, "band", bit).astype(F32)).astype(BF16)
-        bit *= 2
-    theirs = flip(mine, "band", 1)
+    halves = []
+
+    def named(value, axis, bit):
+        return flip(value, axis, bit).astype(F32)
+
+    for chunk in range(CHUNKS):
+        p_keep, p_send, q_keep, q_send = grads[4 * chunk : 4 * chunk + 4]
+        p_in = named(p_send, "dp", high)
+        q_in = named(q_send, "dp", 1)
+        p_pass = (p_keep[1].astype(F32) + p_in[1]).astype(BF16)
+        q_pass = (q_keep[1].astype(F32) + q_in[1]).astype(BF16)
+        p_sum = p_keep[0].astype(F32) + p_in[0] + named(p_pass, "dp", 1)
+        q_sum = q_keep[0].astype(F32) + q_in[0] + named(q_pass, "dp", high)
+        mine = jnp.where(even, p_sum, q_sum)
+        theirs = jnp.where(even, q_sum, p_sum).astype(BF16)
+        mine = (mine + named(theirs, "band", 1)).astype(BF16)
+        bit = 2
+        while bit < bands:
+            mine = (mine.astype(F32) + named(mine, "band", bit)).astype(BF16)
+            bit *= 2
+        halves += [mine, flip(mine, "band", 1)]
     merge_grad, qkv_grad, out_grad, gain_grad = pl.pallas_call(
         final_kernel,
         out_shape=(
             shape(1, 2 * rows, feature, dtype=F32), shape(1, rows, 3 * feature, dtype=F32),
             shape(1, rows, feature, dtype=F32), shape(1, rows, dtype=F32),
         ),
-        in_specs=[VMEM, VMEM],
+        in_specs=[VMEM] * len(halves),
         out_specs=(VMEM,) * 4,
         name="unpack",
-    )(mine, theirs)
+    )(*halves)
     return (section_out, merge_grad, qkv_grad, out_grad, gain_grad)
 
 

time: 162 us -> 136 us (0.84)
  starting transfers between devices: 53.4 us -> 31.8 us
  other arithmetic: 7.02 us -> 2.93 us
  local copies, waits for them, and re-layouts: 6.34 us -> 4.7 us
    ppermute x19 -> x0, starting transfers between devices: 37.9 us -> none  [the longest x18 36.7 us: flip_on(): return lax.ppermute(value, ('dp', 'segment'), pairs)]
    ppermute x7 -> x23, starting transfers between devices: 8.32 us -> 23.6 us  [flip(): return lax.ppermute(value, axis, [(i, i ^ bit) for i in range(size)])]
    ppermute x7 -> x23, waiting for transfers between devices: 53.8 us -> 61.5 us  [flip(): return lax.ppermute(value, axis, [(i, i ^ bit) for i in range(size)])]
    ppermute x19 -> x0, waiting for transfers between devices: 6.1 us -> none  [the longest x18 5.31 us: flip_on(): return lax.ppermute(value, ('dp', 'segment'), pairs)]
    add x3 -> x0, other arithmetic: 2.37 us -> none  [the longest x1 1.45 us: body(): p_sum = p_keep.astype(F32) + flip(p_send, 'dp', high).astype(F32)]
    ppermute x1, waiting for transfers between devices: 3.35 us -> 1.49 us  [body(): back = lax.ppermute(y[:, :part], 'band', up)]
  transfers between devices with their start and end apart: 31 -> 28, of which waited for: 11 -> 17; matrix products, arithmetic and copies ran while one was open for 5% -> 3% of each run, Pallas kernels for 4% -> 2%
where the time goes in v3:
time: 136 us
  waiting for transfers between devices  72.8 us (54%)
  starting transfers between devices  31.8 us (23%)
  Pallas kernels  22.9 us (17%)
  local copies, waits for them, and re-layouts  4.7 us (3%)
  other arithmetic  2.93 us (2%)
    ppermute x23, waiting for transfers between devices, flip(): return lax.ppermute(value, axis, [(i, i ^ bit) for i in range(size)])  61.5 us
    ppermute x23, starting transfers between devices, flip(): return lax.ppermute(value, axis, [(i, i ^ bit) for i in range(size)])  23.6 us
    pallas_call x4, Pallas kernels, call(): pl.pallas_call(kernel, out_shape=tuple(outs), in_specs=[ANY] * len(ins),...  18.9 us
    ppermute x1, waiting for transfers between devices, body(): g0 = lax.ppermute(g_out, 'segment', [(1, 0)])  4.66 us
    ppermute x1, waiting for transfers between devices, body(): mask_moved = lax.ppermute(cell_mask[0, :, row_count - SH:], 'band', down)  3.83 us
    unnamed x46, local copies, waits for them, and re-layouts  3.08 us
  transfers between devices with their start and end apart: 28, of which 17 were waited for; matrix products, arithmetic and copies ran while one was open for 3% of the time, Pallas kernels for 2%

profile of v3, /device:TPU:0, one launch (start us, length us, event | category | flops | bytes accessed | tf_op | source)
XLA Modules:
  0.0 136.2 jit_solution(18275852085686302245)
XLA Ops:
  0.6 3.1 %collective-permute-start.6 = (bf16[128,1536]{1,0:T(8,128)(2,1)}, bf16[128,1536]{1,0:T(8,128)(2,1)S(1)}, u32[]{:S(2)}, u32[]{:S(2)}) collective-permute-start(bf16[128,1536]{1,0:T(8,128)(2,1)} %bitcast.56), channel_id=1, source_target_pairs={{0,16},{8,24},{16,0},{24,8},{1,17},{9,25},{17,1},{25,9},{2,18},{10... | collective-permute-start | bytes 1179656 | tf_op jit(solution)/shard_map/ppermute | solution.py:469
  3.7 1.0 select_bitcast_fusion
  4.7 1.6 %collective-permute-start.1 = (bf16[2,4,16,512]{3,2,1,0:T(8,128)(2,1)S(1)}, bf16[2,4,16,512]{3,2,1,0:T(8,128)(2,1)S(1)}, u32[]{:S(2)}, u32[]{:S(2)}) collective-permute-start(bf16[2,4,16,512]{3,2,1,0:T(8,128)(2,1)S(1)} %select_bitcast_fusion), channel_id=1, source_target_pairs={{0,1},{1,2},{2,3},{3,0},{4,5},{5,6},{6,7},{7,4},{8,9},{9,10},{10,1... | collective-permute-start | bytes 393224 | tf_op jit(solution)/shard_map/ppermute | solution.py:518
  6.4 1.6 %pack.1.refs_11_.refs_12_ = bf16[144,512]{1,0:T(8,128)(2,1)} custom-call(bf16[128,512]{1,0:T(8,128)(2,1)} %bitcast.72, bf16[1,128]{1,0:T(2,128)(2,1)} %gain.1), custom_call_target="tpu_custom_call" | custom-call | tf_op jit(solution)/shard_map/pack/pallas_call | solution.py:505
  8.5 1.5 %collective-permute-start.2 = (bf16[256,512]{1,0:T(8,128)(2,1)S(1)}, bf16[256,512]{1,0:T(8,128)(2,1)S(1)}, u32[]{:S(2)}, u32[]{:S(2)}) collective-permute-start(bf16[256,512]{1,0:T(8,128)(2,1)S(1)} %bitcast.66), channel_id=1, source_target_pairs={{0,8},{8,0},{16,24},{24,16},{1,9},{9,1},{17,25},{25,17},{2,10},{10... | collective-permute-start | bytes 786440 | tf_op jit(solution)/shard_map/ppermute | solution.py:469
  10.0 1.6 %collective-permute-start = (s32[2,4,16]{2,1,0:T(4,128)S(1)}, s32[2,4,16]{2,1,0:T(4,128)S(1)}, u32[]{:S(2)}, u32[]{:S(2)}) collective-permute-start(s32[2,4,16]{2,1,0:T(4,128)S(1)} %get-tuple-element.75), channel_id=1, source_target_pairs={{0,1},{1,2},{2,3},{3,0},{4,5},{5,6},{6,7},{7,4},{8,9},{9,10},{10,1... | collective-permute-start | bytes 1544 | tf_op jit(solution)/shard_map/ppermute | solution.py:520
  11.5 3.8 %collective-permute-done = s32[2,4,16]{2,1,0:T(4,128)S(1)} collective-permute-done((s32[2,4,16]{2,1,0:T(4,128)S(1)}, s32[2,4,16]{2,1,0:T(4,128)S(1)}, u32[]{:S(2)}, u32[]{:S(2)}) %collective-permute-start) | collective-permute-done | bytes 544 | tf_op jit(solution)/shard_map/ppermute | solution.py:520
  15.9 1.5 %collective-permute-start.7 = (bf16[128,1536]{1,0:T(8,128)(2,1)S(1)}, bf16[128,1536]{1,0:T(8,128)(2,1)S(1)}, u32[]{:S(2)}, u32[]{:S(2)}) collective-permute-start(bf16[128,1536]{1,0:T(8,128)(2,1)S(1)} %collective-permute-done.6.refs_9_.refs_10_), channel_id=1, source_target_pairs={{0,8},{8,0},{16,24},{24,16},{1,9},{9,1},{17,25},{25,17},{2,10},{10... | collective-permute-start | bytes 1179656 | tf_op jit(solution)/shard_map/ppermute | solution.py:469
  18.0 1.5 %collective-permute-start.3 = (bf16[256,512]{1,0:T(8,128)(2,1)S(1)}, bf16[256,512]{1,0:T(8,128)(2,1)S(1)}, u32[]{:S(2)}, u32[]{:S(2)}) collective-permute-start(bf16[256,512]{1,0:T(8,128)(2,1)S(1)} %bitcast.67), channel_id=1, source_target_pairs={{0,16},{8,24},{16,0},{24,8},{1,17},{9,25},{17,1},{25,9},{2,18},{10... | collective-permute-start | bytes 786440 | tf_op jit(solution)/shard_map/ppermute | solution.py:469
  20.0 15.7 %collective-permute-done.8.refs_12_.refs_13_ = bf16[144,512]{1,0:T(8,128)(2,1)S(1)} collective-permute-done((bf16[144,512]{1,0:T(8,128)(2,1)}, bf16[144,512]{1,0:T(8,128)(2,1)S(1)}, u32[]{:S(2)}, u32[]{:S(2)}) %collective-permute-start.8) | collective-permute-done | bytes 147488 | tf_op jit(solution)/shard_map/ppermute | solution.py:469
  35.7 1.5 %collective-permute-start.10 = (bf16[144,512]{1,0:T(8,128)(2,1)S(1)}, bf16[144,512]{1,0:T(8,128)(2,1)S(1)}, u32[]{:S(2)}, u32[]{:S(2)}) collective-permute-start(bf16[144,512]{1,0:T(8,128)(2,1)S(1)} %collective-permute-done.8.refs_12_.refs_13_), channel_id=1, source_target_pairs={{0,16},{8,24},{16,0},{24,8},{1,17},{9,25},{17,1},{25,9},{2,18},{10... | collective-permute-start | bytes 442376 | tf_op jit(solution)/shard_map/ppermute | solution.py:469
  37.2 0.6 reshape.50.refs_0_
  37.8 3.0 %collective-permute-done.10.refs_14_.refs_15_ = bf16[144,512]{1,0:T(8,128)(2,1)S(1)} collective-permute-done((bf16[144,512]{1,0:T(8,128)(2,1)S(1)}, bf16[144,512]{1,0:T(8,128)(2,1)S(1)}, u32[]{:S(2)}, u32[]{:S(2)}) %collective-permute-start.10) | collective-permute-done | bytes 147488 | tf_op jit(solution)/shard_map/ppermute | solution.py:469
  40.9 0.6 copy-done.16
  41.9 6.5 %shard_map.110 = (bf16[256,512]{1,0:T(8,128)(2,1)}, f32[256,512]{1,0:T(8,128)}, f32[256,128]{1,0:T(8,128)}, bf16[256,512]{1,0:T(8,128)(2,1)}, bf16[256,1536]{1,0:T(8,128)(2,1)}, /*index=5*/bf16[256,512]{1,0:T(8,128)(2,1)}) custom-call(s32[2,128]{1,0:T(2,128)} %reshape.50.refs_0_, bf16[2,64,512]{2,1,0:T(8,128)(2,1)} %bitcast.68, ...), custom_call_target="tpu_custom_call" | custom-call | flops 805306368 | bytes 5833728 | tf_op jit(solution)/shard_map/pallas_call | solution.py:456
  48.4 1.3 collective-permute-start.11
  49.7 1.3 collective-permute-done.11.refs_3_.refs_0_
  51.0 0.7 copy-done.22
  51.7 1.1 shard_map.111
  52.9 1.3 collective-permute-start.13
  54.2 1.0 fusion.16
  55.2 2.4 %collective-permute-start.12 = (bf16[2,64,512]{2,1,0:T(8,128)(2,1)S(1)}, bf16[2,64,512]{2,1,0:T(8,128)(2,1)S(1)}, u32[]{:S(2)}, u32[]{:S(2)}) collective-permute-start(bf16[2,64,512]{2,1,0:T(8,128)(2,1)S(1)} %get-tuple-element.74), channel_id=1, source_target_pairs={{1,0},{2,1},{3,2},{0,3},{5,4},{6,5},{7,6},{4,7},{9,8},{10,9},{11,1... | collective-permute-start | bytes 393224 | tf_op jit(solution)/shard_map/ppermute | solution.py:570
  57.6 1.1 shard_map.112
  58.7 1.5 %collective-permute-done.12 = bf16[2,64,512]{2,1,0:T(8,128)(2,1)S(1)} collective-permute-done((bf16[2,64,512]{2,1,0:T(8,128)(2,1)S(1)}, bf16[2,64,512]{2,1,0:T(8,128)(2,1)S(1)}, u32[]{:S(2)}, u32[]{:S(2)}) %collective-permute-start.12) | collective-permute-done | bytes 131104 | tf_op jit(solution)/shard_map/ppermute | solution.py:570
  60.2 0.7 pad_maximum_fusion
  60.9 4.7 %collective-permute-done.13.refs_3_ = bf16[256,512]{1,0:T(8,128)(2,1)S(1)} collective-permute-done((bf16[256,512]{1,0:T(8,128)(2,1)}, bf16[256,512]{1,0:T(8,128)(2,1)S(1)}, u32[]{:S(2)}, u32[]{:S(2)}) %collective-permute-start.13) | collective-permute-done | bytes 262176 | tf_op jit(solution)/shard_map/ppermute | solution.py:558
  65.6 0.7 copy-done.18
  66.3 10.1 %shard_map.113 = (bf16[2,400,256]{2,1,0:T(8,128)(2,1)}, bf16[2,400,256]{2,1,0:T(8,128)(2,1)}, bf16[2,400,256]{2,1,0:T(8,128)(2,1)}, bf16[2,400,256]{2,1,0:T(8,12...) custom-call(s32[2,128]{1,0:T(2,128)} %reshape.50.refs_0_, ...), custom_call_target="tpu_custom_call", output_to_operand_aliasing={{0}: (22, {}), {1}: (23, {}), {2}: (24, {}), {3}: (25, {}),... | custom-call | flops 1610612736 | bytes 12649472 | tf_op jit(solution)/shard_map/pallas_call | solution.py:456
  76.4 1.6 %collective-permute-start.14 = (bf16[2,400,256]{2,1,0:T(8,128)(2,1)}, bf16[2,400,256]{2,1,0:T(8,128)(2,1)S(1)}, u32[]{:S(2)}, u32[]{:S(2)}) collective-permute-start(bf16[2,400,256]{2,1,0:T(8,128)(2,1)} %get-tuple-element.62), channel_id=1, source_target_pairs={{0,16},{8,24},{16,0},{24,8},{1,17},{9,25},{17,1},{25,9},{2,18},{10... | collective-permute-start | bytes 1228808 | tf_op jit(solution)/shard_map/ppermute | solution.py:469
  78.0 1.5 %collective-permute-start.16 = (bf16[2,400,256]{2,1,0:T(8,128)(2,1)}, bf16[2,400,256]{2,1,0:T(8,128)(2,1)S(1)}, u32[]{:S(2)}, u32[]{:S(2)}) collective-permute-start(bf16[2,400,256]{2,1,0:T(8,128)(2,1)} %get-tuple-element.64), channel_id=1, source_target_pairs={{0,8},{8,0},{16,24},{24,16},{1,9},{9,1},{17,25},{25,17},{2,10},{10... | collective-permute-start | bytes 1228808 | tf_op jit(solution)/shard_map/ppermute | solution.py:469
  80.0 0.5 collective-permute-start.23
  80.5 8.5 %collective-permute-done.14 = bf16[2,400,256]{2,1,0:T(8,128)(2,1)S(1)} collective-permute-done((bf16[2,400,256]{2,1,0:T(8,128)(2,1)}, bf16[2,400,256]{2,1,0:T(8,128)(2,1)S(1)}, u32[]{:S(2)}, u32[]{:S(2)}) %collective-permute-start.14) | collective-permute-done | bytes 409632 | tf_op jit(solution)/shard_map/ppermute | solution.py:469
  89.1 1.6 %collective-permute-start.15 = (bf16[400,256]{1,0:T(8,128)(2,1)S(1)}, bf16[400,256]{1,0:T(8,128)(2,1)S(1)}, u32[]{:S(2)}, u32[]{:S(2)}) collective-permute-start(bf16[400,256]{1,0:T(8,128)(2,1)S(1)} %fusion.12), channel_id=1, source_target_pairs={{0,8},{8,0},{16,24},{24,16},{1,9},{9,1},{17,25},{25,17},{2,10},{10... | collective-permute-start | bytes 614408 | tf_op jit(solution)/shard_map/ppermute | solution.py:469
  90.8 1.6 %collective-permute-start.17 = (bf16[400,256]{1,0:T(8,128)(2,1)S(1)}, bf16[400,256]{1,0:T(8,128)(2,1)S(1)}, u32[]{:S(2)}, u32[]{:S(2)}) collective-permute-start(bf16[400,256]{1,0:T(8,128)(2,1)S(1)} %fusion.13), channel_id=1, source_target_pairs={{0,16},{8,24},{16,0},{24,8},{1,17},{9,25},{17,1},{25,9},{2,18},{10... | collective-permute-start | bytes 614408 | tf_op jit(solution)/shard_map/ppermute | solution.py:469
  92.4 5.4 %collective-permute-done.21 = bf16[2,400,256]{2,1,0:T(8,128)(2,1)S(1)} collective-permute-done((bf16[2,400,256]{2,1,0:T(8,128)(2,1)}, bf16[2,400,256]{2,1,0:T(8,128)(2,1)S(1)}, u32[]{:S(2)}, u32[]{:S(2)}) %collective-permute-start.21) | collective-permute-done | bytes 409632 | tf_op jit(solution)/shard_map/ppermute | solution.py:469
  97.9 1.6 %collective-permute-start.22 = (bf16[400,256]{1,0:T(8,128)(2,1)S(1)}, bf16[400,256]{1,0:T(8,128)(2,1)S(1)}, u32[]{:S(2)}, u32[]{:S(2)}) collective-permute-start(bf16[400,256]{1,0:T(8,128)(2,1)S(1)} %fusion.14), channel_id=1, source_target_pairs={{0,8},{8,0},{16,24},{24,16},{1,9},{9,1},{17,25},{25,17},{2,10},{10... | collective-permute-start | bytes 614408 | tf_op jit(solution)/shard_map/ppermute | solution.py:469
  99.6 1.6 %collective-permute-start.24 = (bf16[400,256]{1,0:T(8,128)(2,1)S(1)}, bf16[400,256]{1,0:T(8,128)(2,1)S(1)}, u32[]{:S(2)}, u32[]{:S(2)}) collective-permute-start(bf16[400,256]{1,0:T(8,128)(2,1)S(1)} %fusion.15), channel_id=1, source_target_pairs={{0,16},{8,24},{16,0},{24,8},{1,17},{9,25},{17,1},{25,9},{2,18},{10... | collective-permute-start | bytes 614408 | tf_op jit(solution)/shard_map/ppermute | solution.py:469
  101.2 1.9 %collective-permute-done.15 = bf16[400,256]{1,0:T(8,128)(2,1)S(1)} collective-permute-done((bf16[400,256]{1,0:T(8,128)(2,1)S(1)}, bf16[400,256]{1,0:T(8,128)(2,1)S(1)}, u32[]{:S(2)}, u32[]{:S(2)}) %collective-permute-start.15) | collective-permute-done | bytes 204832 | tf_op jit(solution)/shard_map/ppermute | solution.py:469
  103.4 1.9 %collective-permute-done.22 = bf16[400,256]{1,0:T(8,128)(2,1)S(1)} collective-permute-done((bf16[400,256]{1,0:T(8,128)(2,1)S(1)}, bf16[400,256]{1,0:T(8,128)(2,1)S(1)}, u32[]{:S(2)}, u32[]{:S(2)}) %collective-permute-start.22) | collective-permute-done | bytes 204832 | tf_op jit(solution)/shard_map/ppermute | solution.py:469
  105.6 1.6 %collective-permute-start.25 = (bf16[400,256]{1,0:T(8,128)(2,1)S(1)}, bf16[400,256]{1,0:T(8,128)(2,1)S(1)}, u32[]{:S(2)}, u32[]{:S(2)}) collective-permute-start(bf16[400,256]{1,0:T(8,128)(2,1)S(1)} %select_convert_fusion), channel_id=1, source_target_pairs={{0,1},{1,0},{2,3},{3,2},{4,5},{5,4},{6,7},{7,6},{8,9},{9,8},{10,11... | collective-permute-start | bytes 614408 | tf_op jit(solution)/shard_map/ppermute | solution.py:469
  107.2 4.8 %collective-permute-done.18 = bf16[400,256]{1,0:T(8,128)(2,1)S(1)} collective-permute-done((bf16[400,256]{1,0:T(8,128)(2,1)S(1)}, bf16[400,256]{1,0:T(8,128)(2,1)S(1)}, u32[]{:S(2)}, u32[]{:S(2)}) %collective-permute-start.18) | collective-permute-done | bytes 204832 | tf_op jit(solution)/shard_map/ppermute | solution.py:469
  112.3 2.9 %collective-permute-done.25 = bf16[400,256]{1,0:T(8,128)(2,1)S(1)} collective-permute-done((bf16[400,256]{1,0:T(8,128)(2,1)S(1)}, bf16[400,256]{1,0:T(8,128)(2,1)S(1)}, u32[]{:S(2)}, u32[]{:S(2)}) %collective-permute-start.25) | collective-permute-done | bytes 204832 | tf_op jit(solution)/shard_map/ppermute | solution.py:469
  115.5 8.7 %collective-permute-done.19 = bf16[400,256]{1,0:T(8,128)(2,1)S(1)} collective-permute-done((bf16[400,256]{1,0:T(8,128)(2,1)S(1)}, bf16[400,256]{1,0:T(8,128)(2,1)S(1)}, u32[]{:S(2)}, u32[]{:S(2)}) %collective-permute-start.19) | collective-permute-done | bytes 204832 | tf_op jit(solution)/shard_map/ppermute | solution.py:469
  124.4 2.0 %collective-permute-done.26 = bf16[400,256]{1,0:T(8,128)(2,1)S(1)} collective-permute-done((bf16[400,256]{1,0:T(8,128)(2,1)S(1)}, bf16[400,256]{1,0:T(8,128)(2,1)S(1)}, u32[]{:S(2)}, u32[]{:S(2)}) %collective-permute-start.26) | collective-permute-done | bytes 204832 | tf_op jit(solution)/shard_map/ppermute | solution.py:469
  126.6 4.2 %collective-permute-done.20.refs_1_ = bf16[400,256]{1,0:T(8,128)(2,1)S(1)} collective-permute-done((bf16[400,256]{1,0:T(8,128)(2,1)S(1)}, bf16[400,256]{1,0:T(8,128)(2,1)S(1)}, u32[]{:S(2)}, u32[]{:S(2)}) %collective-permute-start.20) | collective-permute-done | bytes 204832 | tf_op jit(solution)/shard_map/ppermute | solution.py:469
  130.8 2.2 %collective-permute-done.27.refs_3_ = bf16[400,256]{1,0:T(8,128)(2,1)S(1)} collective-permute-done((bf16[400,256]{1,0:T(8,128)(2,1)S(1)}, bf16[400,256]{1,0:T(8,128)(2,1)S(1)}, u32[]{:S(2)}, u32[]{:S(2)}) %collective-permute-start.27) | collective-permute-done | bytes 204832 | tf_op jit(solution)/shard_map/ppermute | solution.py:469
  133.0 0.7 copy-done.20
  133.7 2.5 %unpack.1 = (f32[1,256,512]{2,1,0:T(8,128)}, f32[1,128,1536]{2,1,0:T(8,128)}, f32[1,128,512]{2,1,0:T(8,128)}, f32[1,128]{1,0:T(1,128)}) custom-call(bf16[400,256]{1,0:T(8,128)(2,1)} %copy-done.12, bf16[400,256]{1,0:T(8,128)(2,1)} %copy-done.19, bf16[400,256]{1,0:T(8,128)(2,1)} %copy-done.13, bf16[400,256]{1,0:T(8,128)(2,1)} %copy-done.20), custom_call_target="tpu_custom_call" | custom-call | tf_op jit(solution)/shard_map/unpack/pallas_call | solution.py:606
  (80 shorter events, 4.8 us)
Async XLA Ops:
  0.6 14.7 %copy-start.4 = (bf16[1,128,1536]{2,1,0:T(8,128)(2,1)S(1)}, bf16[1,128,1536]{2,1,0:T(8,128)(2,1)}, u32[]{:S(2)}) copy-start(bf16[1,128,1536]{2,1,0:T(8,128)(2,1)} %param.10) | copy-start | bytes 1179652
  0.6 15.3 %collective-permute-start.6 = (bf16[128,1536]{1,0:T(8,128)(2,1)}, bf16[128,1536]{1,0:T(8,128)(2,1)S(1)}, u32[]{:S(2)}, u32[]{:S(2)}) collective-permute-start(bf16[128,1536]{1,0:T(8,128)(2,1)} %bitcast.56), channel_id=1, source_target_pairs={{0,16},{8,24},{16,0},{24,8},{1,17},{9,25},{17,1},{25,9},{2,18},{10... | collective-permute-start | bytes 1179656 | tf_op jit(solution)/shard_map/ppermute | solution.py:469
  3.7 4.8 %copy-start.8 = (bf16[1,256,512]{2,1,0:T(8,128)(2,1)S(1)}, bf16[1,256,512]{2,1,0:T(8,128)(2,1)}, u32[]{:S(2)}) copy-start(bf16[1,256,512]{2,1,0:T(8,128)(2,1)} %param.9) | copy-start | bytes 786436
  4.7 12.7 %collective-permute-start.1 = (bf16[2,4,16,512]{3,2,1,0:T(8,128)(2,1)S(1)}, bf16[2,4,16,512]{3,2,1,0:T(8,128)(2,1)S(1)}, u32[]{:S(2)}, u32[]{:S(2)}) collective-permute-start(bf16[2,4,16,512]{3,2,1,0:T(8,128)(2,1)S(1)} %select_bitcast_fusion), channel_id=1, source_target_pairs={{0,1},{1,2},{2,3},{3,0},{4,5},{5,6},{6,7},{7,4},{8,9},{9,10},{10,1... | collective-permute-start | bytes 393224 | tf_op jit(solution)/shard_map/ppermute | solution.py:518
  6.4 3.6 %copy-start.21 = (s32[1,2,8,16]{3,2,1,0:T(8,128)S(1)}, s32[1,2,8,16]{3,2,1,0:T(8,128)}, u32[]{:S(2)}) copy-start(s32[1,2,8,16]{3,2,1,0:T(8,128)} %param.8) | copy-start | bytes 3076
  8.0 10.0 %collective-permute-start.9 = (bf16[144,512]{1,0:T(8,128)(2,1)}, bf16[144,512]{1,0:T(8,128)(2,1)S(1)}, u32[]{:S(2)}, u32[]{:S(2)}) collective-permute-start(bf16[144,512]{1,0:T(8,128)(2,1)} %pack.1.refs_11_.refs_12_), channel_id=1, source_target_pairs={{0,16},{8,24},{16,0},{24,8},{1,17},{9,25},{17,1},{25,9},{2,18},{10... | collective-permute-start | bytes 442376 | tf_op jit(solution)/shard_map/ppermute | solution.py:469
  8.5 11.0 %collective-permute-start.2 = (bf16[256,512]{1,0:T(8,128)(2,1)S(1)}, bf16[256,512]{1,0:T(8,128)(2,1)S(1)}, u32[]{:S(2)}, u32[]{:S(2)}) collective-permute-start(bf16[256,512]{1,0:T(8,128)(2,1)S(1)} %bitcast.66), channel_id=1, source_target_pairs={{0,8},{8,0},{16,24},{24,16},{1,9},{9,1},{17,25},{25,17},{2,10},{10... | collective-permute-start | bytes 786440 | tf_op jit(solution)/shard_map/ppermute | solution.py:469
  10.0 5.4 %collective-permute-start = (s32[2,4,16]{2,1,0:T(4,128)S(1)}, s32[2,4,16]{2,1,0:T(4,128)S(1)}, u32[]{:S(2)}, u32[]{:S(2)}) collective-permute-start(s32[2,4,16]{2,1,0:T(4,128)S(1)} %get-tuple-element.75), channel_id=1, source_target_pairs={{0,1},{1,2},{2,3},{3,0},{4,5},{5,6},{6,7},{7,4},{8,9},{9,10},{10,1... | collective-permute-start | bytes 1544 | tf_op jit(solution)/shard_map/ppermute | solution.py:520
  15.4 25.5 %collective-permute-start.5 = (bf16[128,1536]{1,0:T(8,128)(2,1)S(1)}, bf16[128,1536]{1,0:T(8,128)(2,1)S(1)}, u32[]{:S(2)}, u32[]{:S(2)}) collective-permute-start(bf16[128,1536]{1,0:T(8,128)(2,1)S(1)} %bitcast.60), channel_id=1, source_target_pairs={{0,8},{8,0},{16,24},{24,16},{1,9},{9,1},{17,25},{25,17},{2,10},{10... | collective-permute-start | bytes 1179656 | tf_op jit(solution)/shard_map/ppermute | solution.py:469
  15.9 25.0 %copy-start.5 = (bf16[128,1536]{1,0:T(8,128)(2,1)}, bf16[128,1536]{1,0:T(8,128)(2,1)S(1)}, u32[]{:S(2)}) copy-start(bf16[128,1536]{1,0:T(8,128)(2,1)S(1)} %collective-permute-done.6.refs_9_.refs_10_) | copy-start | bytes 1179652
  15.9 24.9 %collective-permute-start.7 = (bf16[128,1536]{1,0:T(8,128)(2,1)S(1)}, bf16[128,1536]{1,0:T(8,128)(2,1)S(1)}, u32[]{:S(2)}, u32[]{:S(2)}) collective-permute-start(bf16[128,1536]{1,0:T(8,128)(2,1)S(1)} %collective-permute-done.6.refs_9_.refs_10_), channel_id=1, source_target_pairs={{0,8},{8,0},{16,24},{24,16},{1,9},{9,1},{17,25},{25,17},{2,10},{10... | collective-permute-start | bytes 1179656 | tf_op jit(solution)/shard_map/ppermute | solution.py:469
  17.4 23.5 %copy-start.17 = (bf16[2,4,16,512]{3,2,1,0:T(8,128)(2,1)}, bf16[2,4,16,512]{3,2,1,0:T(8,128)(2,1)S(1)}, u32[]{:S(2)}) copy-start(bf16[2,4,16,512]{3,2,1,0:T(8,128)(2,1)S(1)} %collective-permute-done.1) | copy-start | bytes 393220
  17.4 18.3 %collective-permute-start.8 = (bf16[144,512]{1,0:T(8,128)(2,1)}, bf16[144,512]{1,0:T(8,128)(2,1)S(1)}, u32[]{:S(2)}, u32[]{:S(2)}) collective-permute-start(bf16[144,512]{1,0:T(8,128)(2,1)} %pack.1.refs_11_.refs_12_), channel_id=1, source_target_pairs={{0,8},{8,0},{16,24},{24,16},{1,9},{9,1},{17,25},{25,17},{2,10},{10... | collective-permute-start | bytes 442376 | tf_op jit(solution)/shard_map/ppermute | solution.py:469
  18.0 22.9 %copy-start.14 = (bf16[144,512]{1,0:T(8,128)(2,1)}, bf16[144,512]{1,0:T(8,128)(2,1)S(1)}, u32[]{:S(2)}) copy-start(bf16[144,512]{1,0:T(8,128)(2,1)S(1)} %collective-permute-done.9.refs_13_.refs_14_) | copy-start | bytes 442372
  18.0 19.9 %collective-permute-start.3 = (bf16[256,512]{1,0:T(8,128)(2,1)S(1)}, bf16[256,512]{1,0:T(8,128)(2,1)S(1)}, u32[]{:S(2)}, u32[]{:S(2)}) collective-permute-start(bf16[256,512]{1,0:T(8,128)(2,1)S(1)} %bitcast.67), channel_id=1, source_target_pairs={{0,16},{8,24},{16,0},{24,8},{1,17},{9,25},{17,1},{25,9},{2,18},{10... | collective-permute-start | bytes 786440 | tf_op jit(solution)/shard_map/ppermute | solution.py:469
  19.5 21.4 %copy-start.9 = (bf16[256,512]{1,0:T(8,128)(2,1)}, bf16[256,512]{1,0:T(8,128)(2,1)S(1)}, u32[]{:S(2)}) copy-start(bf16[256,512]{1,0:T(8,128)(2,1)S(1)} %collective-permute-done.2.refs_4_.refs_5_) | copy-start | bytes 786436
  19.5 21.4 %collective-permute-start.4 = (bf16[256,512]{1,0:T(8,128)(2,1)S(1)}, bf16[256,512]{1,0:T(8,128)(2,1)S(1)}, u32[]{:S(2)}, u32[]{:S(2)}) collective-permute-start(bf16[256,512]{1,0:T(8,128)(2,1)S(1)} %collective-permute-done.2.refs_4_.refs_5_), channel_id=1, source_target_pairs={{0,16},{8,24},{16,0},{24,8},{1,17},{9,25},{17,1},{25,9},{2,18},{10... | collective-permute-start | bytes 786440 | tf_op jit(solution)/shard_map/ppermute | solution.py:469
  35.7 5.2 %copy-start.15 = (bf16[144,512]{1,0:T(8,128)(2,1)}, bf16[144,512]{1,0:T(8,128)(2,1)S(1)}, u32[]{:S(2)}) copy-start(bf16[144,512]{1,0:T(8,128)(2,1)S(1)} %collective-permute-done.8.refs_12_.refs_13_) | copy-start | bytes 442372
  35.7 5.1 %collective-permute-start.10 = (bf16[144,512]{1,0:T(8,128)(2,1)S(1)}, bf16[144,512]{1,0:T(8,128)(2,1)S(1)}, u32[]{:S(2)}, u32[]{:S(2)}) collective-permute-start(bf16[144,512]{1,0:T(8,128)(2,1)S(1)} %collective-permute-done.8.refs_12_.refs_13_), channel_id=1, source_target_pairs={{0,16},{8,24},{16,0},{24,8},{1,17},{9,25},{17,1},{25,9},{2,18},{10... | collective-permute-start | bytes 442376 | tf_op jit(solution)/shard_map/ppermute | solution.py:469
  37.8 3.1 %copy-start.10 = (bf16[256,512]{1,0:T(8,128)(2,1)}, bf16[256,512]{1,0:T(8,128)(2,1)S(1)}, u32[]{:S(2)}) copy-start(bf16[256,512]{1,0:T(8,128)(2,1)S(1)} %collective-permute-done.3.refs_5_.refs_6_) | copy-start | bytes 786436
  40.8 0.8 copy-start.6
  40.8 0.9 copy-start.11
  40.9 1.0 copy-start.7
  48.4 2.7 %collective-permute-start.11 = (bf16[256,512]{1,0:T(8,128)(2,1)}, bf16[256,512]{1,0:T(8,128)(2,1)S(1)}, u32[]{:S(2)}, u32[]{:S(2)}) collective-permute-start(bf16[256,512]{1,0:T(8,128)(2,1)} %get-tuple-element.39.refs_16_), channel_id=1, source_target_pairs={{0,4},{1,5},{2,6},{3,7},{8,12},{9,13},{10,14},{11,15},{16,20},{17,... | collective-permute-start | bytes 786440 | tf_op jit(solution)/shard_map/ppermute | solution.py:547
  51.0 0.7 copy-start.22
  52.9 12.7 %collective-permute-start.13 = (bf16[256,512]{1,0:T(8,128)(2,1)}, bf16[256,512]{1,0:T(8,128)(2,1)S(1)}, u32[]{:S(2)}, u32[]{:S(2)}) collective-permute-start(bf16[256,512]{1,0:T(8,128)(2,1)} %get-tuple-element.41), channel_id=1, source_target_pairs={{4,0},{5,1},{6,2},{7,3},{12,8},{13,9},{14,10},{15,11},{20,16},{21,... | collective-permute-start | bytes 786440 | tf_op jit(solution)/shard_map/ppermute | solution.py:558
  55.2 5.0 %collective-permute-start.12 = (bf16[2,64,512]{2,1,0:T(8,128)(2,1)S(1)}, bf16[2,64,512]{2,1,0:T(8,128)(2,1)S(1)}, u32[]{:S(2)}, u32[]{:S(2)}) collective-permute-start(bf16[2,64,512]{2,1,0:T(8,128)(2,1)S(1)} %get-tuple-element.74), channel_id=1, source_target_pairs={{1,0},{2,1},{3,2},{0,3},{5,4},{6,5},{7,6},{4,7},{9,8},{10,9},{11,1... | collective-permute-start | bytes 393224 | tf_op jit(solution)/shard_map/ppermute | solution.py:570
  76.4 12.6 %collective-permute-start.14 = (bf16[2,400,256]{2,1,0:T(8,128)(2,1)}, bf16[2,400,256]{2,1,0:T(8,128)(2,1)S(1)}, u32[]{:S(2)}, u32[]{:S(2)}) collective-permute-start(bf16[2,400,256]{2,1,0:T(8,128)(2,1)} %get-tuple-element.62), channel_id=1, source_target_pairs={{0,16},{8,24},{16,0},{24,8},{1,17},{9,25},{17,1},{25,9},{2,18},{10... | collective-permute-start | bytes 1228808 | tf_op jit(solution)/shard_map/ppermute | solution.py:469
  78.0 12.7 %collective-permute-start.16 = (bf16[2,400,256]{2,1,0:T(8,128)(2,1)}, bf16[2,400,256]{2,1,0:T(8,128)(2,1)S(1)}, u32[]{:S(2)}, u32[]{:S(2)}) collective-permute-start(bf16[2,400,256]{2,1,0:T(8,128)(2,1)} %get-tuple-element.64), channel_id=1, source_target_pairs={{0,8},{8,0},{16,24},{24,16},{1,9},{9,1},{17,25},{25,17},{2,10},{10... | collective-permute-start | bytes 1228808 | tf_op jit(solution)/shard_map/ppermute | solution.py:469
  79.5 18.3 %collective-permute-start.21 = (bf16[2,400,256]{2,1,0:T(8,128)(2,1)}, bf16[2,400,256]{2,1,0:T(8,128)(2,1)S(1)}, u32[]{:S(2)}, u32[]{:S(2)}) collective-permute-start(bf16[2,400,256]{2,1,0:T(8,128)(2,1)} %get-tuple-element.66), channel_id=1, source_target_pairs={{0,16},{8,24},{16,0},{24,8},{1,17},{9,25},{17,1},{25,9},{2,18},{10... | collective-permute-start | bytes 1228808 | tf_op jit(solution)/shard_map/ppermute | solution.py:469
  80.0 9.1 %copy-start = (bf16[2,400,256]{2,1,0:T(8,128)(2,1)S(1)}, bf16[2,400,256]{2,1,0:T(8,128)(2,1)}, u32[]{:S(2)}) copy-start(bf16[2,400,256]{2,1,0:T(8,128)(2,1)} %get-tuple-element.61) | copy-start | bytes 1228804
  80.0 19.5 %collective-permute-start.23 = (bf16[2,400,256]{2,1,0:T(8,128)(2,1)}, bf16[2,400,256]{2,1,0:T(8,128)(2,1)S(1)}, u32[]{:S(2)}, u32[]{:S(2)}) collective-permute-start(bf16[2,400,256]{2,1,0:T(8,128)(2,1)} %get-tuple-element.68), channel_id=1, source_target_pairs={{0,8},{8,0},{16,24},{24,16},{1,9},{9,1},{17,25},{25,17},{2,10},{10... | collective-permute-start | bytes 1228808 | tf_op jit(solution)/shard_map/ppermute | solution.py:469
  89.1 1.6 %copy-start.1 = (bf16[2,400,256]{2,1,0:T(8,128)(2,1)S(1)}, bf16[2,400,256]{2,1,0:T(8,128)(2,1)}, u32[]{:S(2)}) copy-start(bf16[2,400,256]{2,1,0:T(8,128)(2,1)} %get-tuple-element.63) | copy-start | bytes 1228804
  89.1 14.0 %collective-permute-start.15 = (bf16[400,256]{1,0:T(8,128)(2,1)S(1)}, bf16[400,256]{1,0:T(8,128)(2,1)S(1)}, u32[]{:S(2)}, u32[]{:S(2)}) collective-permute-start(bf16[400,256]{1,0:T(8,128)(2,1)S(1)} %fusion.12), channel_id=1, source_target_pairs={{0,8},{8,0},{16,24},{24,16},{1,9},{9,1},{17,25},{25,17},{2,10},{10... | collective-permute-start | bytes 614408 | tf_op jit(solution)/shard_map/ppermute | solution.py:469
  90.8 7.0 %copy-start.2 = (bf16[2,400,256]{2,1,0:T(8,128)(2,1)S(1)}, bf16[2,400,256]{2,1,0:T(8,128)(2,1)}, u32[]{:S(2)}) copy-start(bf16[2,400,256]{2,1,0:T(8,128)(2,1)} %get-tuple-element.65) | copy-start | bytes 1228804
  90.8 12.3 %collective-permute-start.17 = (bf16[400,256]{1,0:T(8,128)(2,1)S(1)}, bf16[400,256]{1,0:T(8,128)(2,1)S(1)}, u32[]{:S(2)}, u32[]{:S(2)}) collective-permute-start(bf16[400,256]{1,0:T(8,128)(2,1)S(1)} %fusion.13), channel_id=1, source_target_pairs={{0,16},{8,24},{16,0},{24,8},{1,17},{9,25},{17,1},{25,9},{2,18},{10... | collective-permute-start | bytes 614408 | tf_op jit(solution)/shard_map/ppermute | solution.py:469
  97.9 1.6 %copy-start.3 = (bf16[2,400,256]{2,1,0:T(8,128)(2,1)S(1)}, bf16[2,400,256]{2,1,0:T(8,128)(2,1)}, u32[]{:S(2)}) copy-start(bf16[2,400,256]{2,1,0:T(8,128)(2,1)} %get-tuple-element.67) | copy-start | bytes 1228804
  97.9 7.4 %collective-permute-start.22 = (bf16[400,256]{1,0:T(8,128)(2,1)S(1)}, bf16[400,256]{1,0:T(8,128)(2,1)S(1)}, u32[]{:S(2)}, u32[]{:S(2)}) collective-permute-start(bf16[400,256]{1,0:T(8,128)(2,1)S(1)} %fusion.14), channel_id=1, source_target_pairs={{0,8},{8,0},{16,24},{24,16},{1,9},{9,1},{17,25},{25,17},{2,10},{10... | collective-permute-start | bytes 614408 | tf_op jit(solution)/shard_map/ppermute | solution.py:469
  99.6 5.8 %collective-permute-start.24 = (bf16[400,256]{1,0:T(8,128)(2,1)S(1)}, bf16[400,256]{1,0:T(8,128)(2,1)S(1)}, u32[]{:S(2)}, u32[]{:S(2)}) collective-permute-start(bf16[400,256]{1,0:T(8,128)(2,1)S(1)} %fusion.15), channel_id=1, source_target_pairs={{0,16},{8,24},{16,0},{24,8},{1,17},{9,25},{17,1},{25,9},{2,18},{10... | collective-permute-start | bytes 614408 | tf_op jit(solution)/shard_map/ppermute | solution.py:469
  103.3 8.7 %collective-permute-start.18 = (bf16[400,256]{1,0:T(8,128)(2,1)S(1)}, bf16[400,256]{1,0:T(8,128)(2,1)S(1)}, u32[]{:S(2)}, u32[]{:S(2)}) collective-permute-start(bf16[400,256]{1,0:T(8,128)(2,1)S(1)} %select_convert_fusion.1), channel_id=1, source_target_pairs={{0,1},{1,0},{2,3},{3,2},{4,5},{5,4},{6,7},{7,6},{8,9},{9,8},{10,11... | collective-permute-start | bytes 614408 | tf_op jit(solution)/shard_map/ppermute | solution.py:469
  105.6 9.7 %collective-permute-start.25 = (bf16[400,256]{1,0:T(8,128)(2,1)S(1)}, bf16[400,256]{1,0:T(8,128)(2,1)S(1)}, u32[]{:S(2)}, u32[]{:S(2)}) collective-permute-start(bf16[400,256]{1,0:T(8,128)(2,1)S(1)} %select_convert_fusion), channel_id=1, source_target_pairs={{0,1},{1,0},{2,3},{3,2},{4,5},{5,4},{6,7},{7,6},{8,9},{9,8},{10,11... | collective-permute-start | bytes 614408 | tf_op jit(solution)/shard_map/ppermute | solution.py:469
  112.2 12.0 %collective-permute-start.19 = (bf16[400,256]{1,0:T(8,128)(2,1)S(1)}, bf16[400,256]{1,0:T(8,128)(2,1)S(1)}, u32[]{:S(2)}, u32[]{:S(2)}) collective-permute-start(bf16[400,256]{1,0:T(8,128)(2,1)S(1)} %add_convert_fusion.3), channel_id=1, source_target_pairs={{0,2},{1,3},{2,0},{3,1},{4,6},{5,7},{6,4},{7,5},{8,10},{9,11},{10,... | collective-permute-start | bytes 614408 | tf_op jit(solution)/shard_map/ppermute | solution.py:469
  115.4 11.1 %collective-permute-start.26 = (bf16[400,256]{1,0:T(8,128)(2,1)S(1)}, bf16[400,256]{1,0:T(8,128)(2,1)S(1)}, u32[]{:S(2)}, u32[]{:S(2)}) collective-permute-start(bf16[400,256]{1,0:T(8,128)(2,1)S(1)} %add_convert_fusion.1), channel_id=1, source_target_pairs={{0,2},{1,3},{2,0},{3,1},{4,6},{5,7},{6,4},{7,5},{8,10},{9,11},{10,... | collective-permute-start | bytes 614408 | tf_op jit(solution)/shard_map/ppermute | solution.py:469
  124.3 2.2 %copy-start.12 = (bf16[400,256]{1,0:T(8,128)(2,1)}, bf16[400,256]{1,0:T(8,128)(2,1)S(1)}, u32[]{:S(2)}) copy-start(bf16[400,256]{1,0:T(8,128)(2,1)S(1)} %add_convert_fusion.2.refs_0_) | copy-start | bytes 614404
  124.3 6.5 %collective-permute-start.20 = (bf16[400,256]{1,0:T(8,128)(2,1)S(1)}, bf16[400,256]{1,0:T(8,128)(2,1)S(1)}, u32[]{:S(2)}, u32[]{:S(2)}) collective-permute-start(bf16[400,256]{1,0:T(8,128)(2,1)S(1)} %add_convert_fusion.2.refs_0_), channel_id=1, source_target_pairs={{0,1},{1,0},{2,3},{3,2},{4,5},{5,4},{6,7},{7,6},{8,9},{9,8},{10,11... | collective-permute-start | bytes 614408 | tf_op jit(solution)/shard_map/ppermute | solution.py:469
  126.5 6.5 %copy-start.13 = (bf16[400,256]{1,0:T(8,128)(2,1)}, bf16[400,256]{1,0:T(8,128)(2,1)S(1)}, u32[]{:S(2)}) copy-start(bf16[400,256]{1,0:T(8,128)(2,1)S(1)} %add_convert_fusion.refs_2_) | copy-start | bytes 614404
  126.5 6.5 %collective-permute-start.27 = (bf16[400,256]{1,0:T(8,128)(2,1)S(1)}, bf16[400,256]{1,0:T(8,128)(2,1)S(1)}, u32[]{:S(2)}, u32[]{:S(2)}) collective-permute-start(bf16[400,256]{1,0:T(8,128)(2,1)S(1)} %add_convert_fusion.refs_2_), channel_id=1, source_target_pairs={{0,1},{1,0},{2,3},{3,2},{4,5},{5,4},{6,7},{7,6},{8,9},{9,8},{10,11... | collective-permute-start | bytes 614408 | tf_op jit(solution)/shard_map/ppermute | solution.py:469
  130.8 2.2 %copy-start.19 = (bf16[400,256]{1,0:T(8,128)(2,1)}, bf16[400,256]{1,0:T(8,128)(2,1)S(1)}, u32[]{:S(2)}) copy-start(bf16[400,256]{1,0:T(8,128)(2,1)S(1)} %collective-permute-done.20.refs_1_) | copy-start | bytes 614404
  (3 other events, 2.0 us)

commit v4 on v3

--- a/solution.py
+++ b/solution.py
@@ -12,7 +12,7 @@
 SH = 4
 SW = 8
 PAD = 16
-CHUNKS = 2
+CHUNKS = 4
 
 EPSILON = 1e-05
 MASKED = -1e30
@@ -138,11 +138,10 @@
     return jnp.where(lane < head_dim, low, high)
 
 
-def probabilities(q_stack, k, allowed2, head_dim):
-    scores = dot_nt(q_stack, k) * head_dim ** (-0.5)
-    scores = jnp.where(allowed2, scores, MASKED)
+def probabilities(scores, allowed2, head_dim):
+    scores = jnp.where(allowed2, scores * head_dim ** (-0.5), MASKED)
     weights = jnp.exp(scores - jnp.max(scores, axis=-1, keepdims=True))
-    return weights / jnp.sum(weights, axis=-1, keepdims=True)
+    return weights * (1.0 / jnp.sum(weights, axis=-1, keepdims=True))
 
 
 def masks(mask, first_band, lon_count):
@@ -153,38 +152,55 @@
     return out
 
 
-def pairs(mask_shape, feature):
-    micro, cells = mask_shape
+def pairs(micro, cells, feature):
     lanes = 2 * (feature // HEADS)
-    for m in range(micro):
-        for p in range(feature // lanes):
-            yield (m, slice(m * cells, (m + 1) * cells), p * lanes, lanes)
-
-
-def attend(qkv, mix, allowed, mask_shape, feature):
+    count = feature // lanes
+    rows = slice(micro * cells, (micro + 1) * cells)
+    return [(micro * count + p, rows, p * lanes, lanes) for p in range(count)]
+
+
+def part_of(qkv, which, rows, at, lanes):
+    feature = qkv.shape[1] // 3
+    return qkv[rows, which * feature + at : which * feature + at + lanes]
+
+
+def attend(qkv, mix, probs, allowed, mask_shape, feature):
     head_dim = feature // HEADS
-    for m, rows, at, lanes in pairs(mask_shape, feature):
-        q, k, v = (qkv[rows, i * feature + at : i * feature + at + lanes] for i in range(3))
-        probs = probabilities(stacked_heads(q, head_dim), k, allowed[m], head_dim).astype(BF16)
-        mixed = unstacked_heads(dot(probs, v), head_dim)
-        mix[rows, at : at + lanes] = mixed.astype(BF16)
-
-
-def attend_back(qkv, grad_mix, grad_proj, allowed, mask_shape, feature):
+    for m in range(mask_shape[0]):
+        group = pairs(m, mask_shape[1], feature)
+        scores = [
+            dot_nt(stacked_heads(part_of(qkv, 0, *where), head_dim), part_of(qkv, 1, *where))
+            for _, *where in group
+        ]
+        for (n, *_), score in zip(group, scores):
+            probs[n] = probabilities(score, allowed[m], head_dim).astype(BF16)
+        for n, rows, at, lanes in group:
+            mixed = dot(probs[n], part_of(qkv, 2, rows, at, lanes))
+            mix[rows, at : at + lanes] = unstacked_heads(mixed, head_dim).astype(BF16)
+
+
+def attend_back(qkv, probs, grad_mix, grad_proj, mask_shape, feature):
     head_dim = feature // HEADS
-    for m, rows, at, lanes in pairs(mask_shape, feature):
-        q, k, v = (qkv[rows, i * feature + at : i * feature + at + lanes] for i in range(3))
-        q_stack = stacked_heads(q, head_dim)
-        g_stack = stacked_heads(grad_mix[rows, at : at + lanes], head_dim)
-        probs = probabilities(q_stack, k, allowed[m], head_dim)
-        grad_probs = dot_nt(g_stack, v)
-        inner = jnp.sum(grad_probs * probs, axis=-1, keepdims=True)
-        grad_scores = (probs * (grad_probs - inner) * head_dim ** (-0.5)).astype(BF16)
-        grad_q = unstacked_heads(dot(grad_scores, k), head_dim)
-        grad_k = dot_tn(grad_scores, q_stack)
-        grad_v = dot_tn(probs.astype(BF16), g_stack)
-        for i, grad in enumerate((grad_q, grad_k, grad_v)):
-            grad_proj[rows, i * feature + at : i * feature + at + lanes] = grad.astype(BF16)
+
+    def put(which, grad, rows, at, lanes):
+        grad_proj[rows, which * feature + at : which * feature + at + lanes] = grad.astype(BF16)
+
+    for m in range(mask_shape[0]):
+        group = pairs(m, mask_shape[1], feature)
+        grad_probs = []
+        for n, rows, at, lanes in group:
+            g_stack = stacked_heads(grad_mix[rows, at : at + lanes], head_dim)
+            grad_probs.append(dot_nt(g_stack, part_of(qkv, 2, rows, at, lanes)))
+            put(2, dot_tn(probs[n], g_stack), rows, at, lanes)
+        grad_scores = []
+        for (n, *_), grad in zip(group, grad_probs):
+            prob = probs[n].astype(F32)
+            inner = jnp.sum(grad * prob, axis=-1, keepdims=True)
+            grad_scores.append((prob * (grad - inner) * head_dim ** (-0.5)).astype(BF16))
+        for (n, rows, at, lanes), grad in zip(group, grad_scores):
+            q_stack = stacked_heads(part_of(qkv, 0, rows, at, lanes), head_dim)
+            put(0, unstacked_heads(dot(grad, part_of(qkv, 1, rows, at, lanes)), head_dim), rows, at, lanes)
+            put(1, dot_tn(grad, q_stack), rows, at, lanes)
 
 
 def normalize(update):
@@ -195,32 +211,42 @@
     return (centered * inverse, inverse)
 
 
-def forward(x, w, waits, gain_of, allowed, mask_shape, normed_ref, inverse_ref, hidden, qkv, mix):
+def forward(x, w, waits, gain_of, allowed, mask_shape, room, kept):
     feature = x.shape[1]
     wait_all(waits["merge"])
     tokens = x[...]
     update = dot(tokens, w["merge"][:feature]) + dot(tokens, w["merge"][feature:])
     normed, inverse = normalize(update)
-    normed_ref[...] = normed
-    inverse_ref[...] = jnp.broadcast_to(inverse, inverse_ref.shape)
+    room["normed"][...] = normed
+    kept("normed")
+    room["inverse"][...] = jnp.broadcast_to(inverse, room["inverse"].shape)
+    kept("inverse")
+    hidden, qkv, mix = room["hidden"], room["qkv"], room["mix"]
     hidden[...] = (normed * gain_of()).astype(BF16)
+    kept("hidden")
     for i, name in enumerate(("q", "k", "v")):
         wait_all(waits[name])
         qkv[:, i * feature : (i + 1) * feature] = dot(hidden[...], w[name][...]).astype(BF16)
-    attend(qkv, mix, allowed, mask_shape, feature)
+    kept("qkv")
+    attend(qkv, mix, room["probs"], allowed, mask_shape, feature)
+    kept("probs")
+    kept("mix")
     wait_all(waits["out"])
     return update + dot(mix[...], w["out"][...])
 
 
-def backward(grad_out, w, gain, allowed, mask_shape, normed, inverse, qkv, grad_mix, grad_proj):
+RECORDS = ("normed", "inverse", "hidden", "qkv", "mix", "probs")
+
+
+def backward(grad_out, w, gain, mask_shape, room, grad_mix, grad_proj):
     feature = grad_out.shape[1]
     grad_mix[...] = dot_nt(grad_out[...], w["out"][...]).astype(BF16)
-    attend_back(qkv, grad_mix, grad_proj, allowed, mask_shape, feature)
+    attend_back(room["qkv"], room["probs"], grad_mix, grad_proj, mask_shape, feature)
     grad_hidden = sum(
         dot_nt(grad_proj[:, i * feature : (i + 1) * feature], w[name][...])
         for i, name in enumerate(("q", "k", "v"))
     )
-    normed = normed[...]
+    normed, inverse = room["normed"][...], room["inverse"]
     grad_gain = jnp.sum(grad_hidden * normed, axis=0, keepdims=True)
     grad_normed = grad_hidden * gain
     centered = (
@@ -235,48 +261,50 @@
 def send_grads(copies, x, hidden, mix, grad_out, grad_proj, grad_update, grad_gain, dw, outs):
     feature = x.shape[1]
     shards = 2 * outs[0].shape[0]
-    first, second, _ = layout(feature, shards)
+    first, second, half = layout(feature, shards)
     me = lax.axis_index("dp")
     low, high = me % 2, me // 2
     rows = feature // shards
     width = feature // CHUNKS
+    dw_first, dw_second = dw
     started = []
 
-    def target(name, chunk, by_low, by_high):
-        p_keep, p_send, q_keep, q_send = outs[4 * chunk : 4 * chunk + 4]
-        if name in first:
-            start, size = first[name]
-            ref = (p_send if by_high else p_keep).at[by_low]
-        else:
-            start, size = second[name]
-            ref = (q_send if by_low else q_keep).at[by_high]
-        return ref.at[pl.ds(start, size)]
-
-    def emit(name, period):
+    def put(name, value):
+        block = dw_first if name in first else dw_second
+        start, size = first[name] if name in first else second[name]
+        value = value.astype(BF16)
+        for i in range(shards):
+            at = (i * size) % feature
+            block[i, start : start + size, :] = value[at : at + size]
+
+    def emit(which, start, size):
+        block = (dw_first, dw_second)[which]
         for chunk in range(CHUNKS):
+            p_keep, p_send, q_keep, q_send = outs[4 * chunk : 4 * chunk + 4]
             for by_high in range(2):
                 for by_low in range(2):
                     owner = (high ^ by_high) * 2 + (low ^ by_low)
-                    to = target(name, chunk, by_low, by_high)
-                    at = pl.multiple_of((owner * to.shape[0]) % period, to.shape[0])
-                    part = dw[name].at[pl.ds(at, to.shape[0]), pl.ds(chunk * width, width)]
-                    started.append(copies.start(part, to))
-
-    dw["out"][...] = dot_tn(mix[...], grad_out[...]).astype(BF16)
-    emit("out", feature)
-    for i, name in enumerate(("q", "k", "v")):
-        part = grad_proj[:, i * feature : (i + 1) * feature]
-        dw[name][...] = dot_tn(hidden[...], part).astype(BF16)
-        emit(name, feature)
+                    if which:
+                        ref = (q_send if by_low else q_keep).at[by_high]
+                    else:
+                        ref = (p_send if by_high else p_keep).at[by_low]
+                    part = block.at[owner, pl.ds(start, size), pl.ds(chunk * width, width)]
+                    started.append(copies.start(part, ref.at[pl.ds(start, size)]))
+
+    put("out", dot_tn(mix[...], grad_out[...]))
+    for i, name in ((1, "k"), (2, "v")):
+        put(name, dot_tn(hidden[...], grad_proj[:, i * feature : (i + 1) * feature]))
+    dw_second[:, 3 * rows :, :] = jnp.zeros((shards, PAD, feature), BF16)
+    emit(1, 0, half)
+    put("q", dot_tn(hidden[...], grad_proj[:, :feature]))
+    start = first["gain"][0]
     for i in range(shards):
         part = grad_gain[:, i * rows : (i + 1) * rows].astype(BF16)
-        dw["gain"][i * PAD : (i + 1) * PAD, :] = jnp.zeros((PAD, feature), BF16)
-        dw["gain"][i * PAD : (i + 1) * PAD, :rows] = jnp.broadcast_to(part, (PAD, rows))
-    emit("gain", shards * PAD)
-    dw["pad"][...] = jnp.zeros_like(dw["pad"])
-    emit("pad", PAD)
-    dw["merge"][...] = dot_tn(x[...], grad_update[...]).astype(BF16)
-    emit("merge", feature)
+        dw_first[i, start:, :] = jnp.zeros((PAD, feature), BF16)
+        dw_first[i, start:, :rows] = jnp.broadcast_to(part, (PAD, rows))
+    emit(0, first["q"][0], half - first["q"][0])
+    put("merge", dot_tn(x[...], grad_update[...]))
+    emit(0, 0, first["merge"][1])
     return started
 
 
@@ -291,8 +319,10 @@
 def forward_kernel(*refs):
     mask_in, moved, own, *rest = refs
     pieces, rest = rest[:12], rest[12:]
-    y, normed, inverse, hidden, qkv, mix, *rest = rest
-    mask, x, wm, wq, wk, wv, wo, wg, y_s, normed_s, inverse_s, hidden_s, qkv_s, mix_s, sems = rest
+    y, rest = rest[0], rest[1:]
+    saved, rest = dict(zip(RECORDS, rest)), rest[len(RECORDS) :]
+    mask, x, wm, wq, wk, wv, wo, wg, y_s, *rest = rest
+    room, sems = dict(zip(RECORDS, rest)), rest[-1]
 
     @role(0)
     def run():
@@ -311,14 +341,14 @@
             wait_all(waits["gain"])
             return full_gain(wg, shards)
 
-        result = forward(x, w, waits, gain_of, allowed, mask.shape,
-                         normed_s, inverse_s, hidden_s, qkv_s, mix_s)
+        done = []
+
+        def kept(name):
+            done.append(copies.start(room[name], saved[name]))
+
+        result = forward(x, w, waits, gain_of, allowed, mask.shape, room, kept)
         y_s[...] = result.astype(BF16)
-        done = [
-            copies.start(a, b)
-            for a, b in ((y_s, y), (normed_s, normed), (inverse_s, inverse), (hidden_s, hidden),
-                         (qkv_s, qkv), (mix_s, mix))
-        ]
+        done.append(copies.start(y_s, y))
         wait_all(done)
 
 
@@ -326,8 +356,9 @@
     mask_in, moved, own, y0, *rest = refs
     pieces, rest = rest[:12], rest[13:]
     y, g0, gain_out, g_out, hidden, mix, proj_out, update_out, *rest = rest
-    (mask, x, g, wm, wq, wk, wv, wo, wg, y_s, g_s, normed_s, inverse_s, hidden_s, qkv_s, mix_s,
-     gmix, gproj, gain_s, update_s, sems) = rest
+    mask, x, g, wm, wq, wk, wv, wo, wg, y_s, g_s, *rest = rest
+    room, rest = dict(zip(RECORDS, rest)), rest[len(RECORDS) :]
+    gmix, gproj, gain_s, update_s, sems = rest
 
     @role(1)
     def run():
@@ -348,14 +379,17 @@
             wait_all(waits["gain"])
             return full_gain(wg, shards)
 
-        result = forward(x, w, waits, gain_of, allowed, mask.shape,
-                         normed_s, inverse_s, hidden_s, qkv_s, mix_s)
+        done = []
+
+        def kept(name):
+            if name in ("hidden", "mix"):
+                done.append(copies.start(room[name], hidden if name == "hidden" else mix))
+
+        result = forward(x, w, waits, gain_of, allowed, mask.shape, room, kept)
         y_s[...] = result.astype(BF16)
         wait_all(tokens)
-        done = [copies.start(y_s, y), copies.start(g, g_out), copies.start(hidden_s, hidden),
-                copies.start(mix_s, mix)]
-        grad_update, grad_gain = backward(g, w, full_gain(wg, shards), allowed, mask.shape,
-                                          normed_s, inverse_s, qkv_s, gmix, gproj)
+        done += [copies.start(y_s, y), copies.start(g, g_out)]
+        grad_update, grad_gain = backward(g, w, full_gain(wg, shards), mask.shape, room, gmix, gproj)
         done.append(copies.start(gproj, proj_out))
         gain_s[...] = jnp.broadcast_to(grad_gain, gain_s.shape)
         update_s[...] = grad_update
@@ -369,50 +403,44 @@
 
 def weight_kernel(*refs):
     ins, outs, rest = refs[:7], refs[7 : 7 + 4 * CHUNKS], refs[7 + 4 * CHUNKS :]
-    scratch, dw_refs, sems = rest[:7], rest[7:14], rest[14]
+    scratch, dw, sems = rest[:7], rest[7:9], rest[9]
 
     @role(1)
     def run():
         copies = Copies(sems)
         wait_all([copies.start(a, b) for a, b in zip(ins, scratch)])
         x, gain, g, hidden, mix, gproj, update = scratch
-        dw = dict(zip(("merge", "q", "k", "v", "out", "gain", "pad"), dw_refs))
         wait_all(send_grads(copies, x, hidden, mix, g, gproj, update, gain[:1, :], dw, outs))
 
 
 def first_kernel(*refs):
-    mask_in, moved, own, g0, *rest = refs
+    cells, moved, own, g0, *rest = refs
     pieces, rest = rest[:12], rest[12:]
-    normed, inverse, hidden, qkv, mix, *rest = rest
-    skip, count = 1 + 4 * CHUNKS, 4 * CHUNKS
+    saved, rest = rest[: len(RECORDS)], rest[len(RECORDS) :]
+    skip = count = 4 * CHUNKS
     outs, rest = rest[skip : skip + count], rest[skip + count :]
-    (mask, x, g, wq, wk, wv, wo, wg, normed_s, inverse_s, hidden_s, qkv_s, mix_s,
-     gmix, gproj, *dw_refs, sems) = rest
+    x, g, wq, wk, wv, wo, wg, *rest = rest
+    rooms, rest = rest[: len(RECORDS)], rest[len(RECORDS) :]
+    gmix, gproj, dw_first, dw_second, sems = rest
 
     @role(0)
     def run():
         shards = wg.shape[0] // PAD
+        micro, size = own.shape[:2]
         copies = Copies(sems)
         w = {"q": wq, "k": wk, "v": wv, "out": wo, "gain": wg}
-        mask_copy = copies.start(mask_in, mask)
-        g_in = [copies.start(g0, g)]
+        early = [copies.start(g0, g)]
         names = ("out", "q", "k", "v", "gain")
         waits = load_weights(copies, pieces_of(pieces), names, w)
-        saved = [
-            copies.start(a, b)
-            for a, b in ((qkv, qkv_s), (normed, normed_s), (inverse, inverse_s), (hidden, hidden_s),
-                         (mix, mix_s))
-        ]
-        tokens = load_tokens(copies, moved, own, x)
-        mask_copy.wait()
-        allowed = masks(mask, lax.axis_index("band") == 0, lon_of(mask.shape[1]))
-        wait_all(g_in + saved + tokens)
+        early += [copies.start(a, b) for a, b in zip(saved, rooms)]
+        early += load_tokens(copies, moved, own, x)
+        wait_all(early)
         for name in names:
             wait_all(waits[name])
-        grad_update, grad_gain = backward(g, w, full_gain(wg, shards), allowed, mask.shape,
-                                          normed_s, inverse_s, qkv_s, gmix, gproj)
-        dw = dict(zip(("merge", "q", "k", "v", "out", "gain", "pad"), dw_refs))
-        wait_all(send_grads(copies, x, hidden_s, mix_s, g, gproj, grad_update, grad_gain, dw, outs))
+        room = dict(zip(RECORDS, rooms))
+        grad_update, grad_gain = backward(g, w, full_gain(wg, shards), (micro, size), room, gmix, gproj)
+        wait_all(send_grads(copies, x, room["hidden"], room["mix"], g, gproj, grad_update, grad_gain,
+                            (dw_first, dw_second), outs))
 
 
 def rest_kernel(out, gain, packed):
@@ -530,8 +558,9 @@
     merge_room = room(2 * feature, feature)
     record_rooms = [
         room(total, feature, dtype=F32), room(total, 128, dtype=F32), tokens, wide, tokens,
+        room(micro * HEADS // 2, 2 * cells, cells),
     ]
-    grad_rooms = [square] * 5 + [room(shards * PAD, feature), room(PAD, feature)]
+    grad_rooms = [room(shards, half, feature)] * 2
     sems = [pltpu.SemaphoreType.DMA((128,))]
     unit = 2 * total * feature * feature
     token_shape, wide_shape = shape(total, feature), shape(total, 3 * feature)
@@ -540,7 +569,7 @@
         forward_kernel,
         (mask, moved, own_fields) + pieces,
         [token_shape, shape(total, feature, dtype=F32), shape(total, 128, dtype=F32),
-         token_shape, wide_shape, token_shape],
+         token_shape, wide_shape, token_shape, shape(micro * HEADS // 2, 2 * cells, cells)],
         [mask_room, tokens, merge_room] + weights + [tokens] + record_rooms + sems,
         {}, 6 * unit,
     )
@@ -571,12 +600,12 @@
     section_out = jnp.concatenate([y[:, part:], back], axis=1)
     section_out = section_out.reshape(1, 1, micro, row_count, lon_count, feature)
 
-    inputs = (mask, moved, own_fields, g0) + pieces + tuple(records) + (section_out,)
+    inputs = (mask, moved, own_fields, g0) + pieces + tuple(records)
     grads = call(
         first_kernel,
         inputs + tuple(grads),
         shard_shapes,
-        [mask_room, tokens, tokens] + weights + record_rooms + [tokens, wide] + grad_rooms + sems,
+        [tokens, tokens] + weights + record_rooms + [tokens, wide] + grad_rooms + sems,
         {len(inputs) + i: i for i in range(4 * CHUNKS)}, 12 * unit,
     )
 

time: 136 us -> 133 us (0.978)
  waiting for transfers between devices: 72.8 us -> 57.8 us
  starting transfers between devices: 31.8 us -> 45.4 us
  Pallas kernels: 22.9 us -> 20.2 us
    ppermute x23 -> x37, waiting for transfers between devices: 61.5 us -> 44.9 us  [flip(): return lax.ppermute(value, axis, [(i, i ^ bit) for i in range(size)])]
    ppermute x23 -> x37, starting transfers between devices: 23.6 us -> 37.2 us  [flip(): return lax.ppermute(value, axis, [(i, i ^ bit) for i in range(size)])]
    ppermute x1, waiting for transfers between devices: 4.66 us -> 7.64 us  [body(): g0 = lax.ppermute(g_out, 'segment', [(1, 0)])]
    pallas_call x4, Pallas kernels: 18.9 us -> 16.1 us  [call(): pl.pallas_call(kernel, out_shape=tuple(outs), in_specs=[ANY] * len(ins),...]
    ppermute x1, waiting for transfers between devices: 1.49 us -> 0.01 us  [body(): back = lax.ppermute(y[:, :part], 'band', up)]
    unnamed x46 -> x74, local copies, waits for them, and re-layouts: 3.08 us -> 4.24 us
  transfers between devices with their start and end apart: 28 -> 42, of which waited for: 17 -> 25; matrix products, arithmetic and copies ran while one was open for 3% -> 3% of each run, Pallas kernels for 2% -> 2%
where the time goes in v4:
time: 133 us; the launch traced here: 132 us
  waiting for transfers between devices  57.8 us (43%)
  starting transfers between devices  45.4 us (34%)
  Pallas kernels  20.2 us (15%)
  local copies, waits for them, and re-layouts  4.91 us (4%)
  other arithmetic  3.05 us (2%)
    ppermute x37, waiting for transfers between devices, flip(): return lax.ppermute(value, axis, [(i, i ^ bit) for i in range(size)])  44.9 us
    ppermute x37, starting transfers between devices, flip(): return lax.ppermute(value, axis, [(i, i ^ bit) for i in range(size)])  37.2 us
    pallas_call x4, Pallas kernels, call(): pl.pallas_call(kernel, out_shape=tuple(outs), in_specs=[ANY] * len(ins),...  16.1 us
    ppermute x1, waiting for transfers between devices, body(): g0 = lax.ppermute(g_out, 'segment', [(1, 0)])  7.64 us
    unnamed x74, local copies, waits for them, and re-layouts  4.24 us
    ppermute x1, waiting for transfers between devices, body(): mask_moved = lax.ppermute(cell_mask[0, :, row_count - SH:], 'band', down)  3.83 us
  transfers between devices with their start and end apart: 42, of which 25 were waited for; matrix products, arithmetic and copies ran while one was open for 3% of the time, Pallas kernels for 2%

profile of v4, /device:TPU:0, one launch (start us, length us, event | category | flops | bytes accessed | tf_op | source)
XLA Modules:
  0.0 132.4 jit_solution(10215067070980076368)
XLA Ops:
  0.6 3.1 %collective-permute-start.6 = (bf16[128,1536]{1,0:T(8,128)(2,1)}, bf16[128,1536]{1,0:T(8,128)(2,1)S(1)}, u32[]{:S(2)}, u32[]{:S(2)}) collective-permute-start(bf16[128,1536]{1,0:T(8,128)(2,1)} %bitcast.96), channel_id=1, source_target_pairs={{0,16},{8,24},{16,0},{24,8},{1,17},{9,25},{17,1},{25,9},{2,18},{10... | collective-permute-start | bytes 1179656 | tf_op jit(solution)/shard_map/ppermute | solution.py:497
  3.7 1.0 select_bitcast_fusion
  4.7 1.6 %collective-permute-start.1 = (bf16[2,4,16,512]{3,2,1,0:T(8,128)(2,1)S(1)}, bf16[2,4,16,512]{3,2,1,0:T(8,128)(2,1)S(1)}, u32[]{:S(2)}, u32[]{:S(2)}) collective-permute-start(bf16[2,4,16,512]{3,2,1,0:T(8,128)(2,1)S(1)} %select_bitcast_fusion), channel_id=1, source_target_pairs={{0,1},{1,2},{2,3},{3,0},{4,5},{5,6},{6,7},{7,4},{8,9},{9,10},{10,1... | collective-permute-start | bytes 393224 | tf_op jit(solution)/shard_map/ppermute | solution.py:546
  6.4 1.6 %pack.1.refs_11_.refs_12_ = bf16[144,512]{1,0:T(8,128)(2,1)} custom-call(bf16[128,512]{1,0:T(8,128)(2,1)} %bitcast.111, bf16[1,128]{1,0:T(2,128)(2,1)} %gain.1), custom_call_target="tpu_custom_call" | custom-call | tf_op jit(solution)/shard_map/pack/pallas_call | solution.py:533
  8.5 1.5 %collective-permute-start.2 = (bf16[256,512]{1,0:T(8,128)(2,1)S(1)}, bf16[256,512]{1,0:T(8,128)(2,1)S(1)}, u32[]{:S(2)}, u32[]{:S(2)}) collective-permute-start(bf16[256,512]{1,0:T(8,128)(2,1)S(1)} %bitcast.104), channel_id=1, source_target_pairs={{0,8},{8,0},{16,24},{24,16},{1,9},{9,1},{17,25},{25,17},{2,10},{10... | collective-permute-start | bytes 786440 | tf_op jit(solution)/shard_map/ppermute | solution.py:497
  10.0 1.6 %collective-permute-start = (s32[2,4,16]{2,1,0:T(4,128)S(1)}, s32[2,4,16]{2,1,0:T(4,128)S(1)}, u32[]{:S(2)}, u32[]{:S(2)}) collective-permute-start(s32[2,4,16]{2,1,0:T(4,128)S(1)} %get-tuple-element.109), channel_id=1, source_target_pairs={{0,1},{1,2},{2,3},{3,0},{4,5},{5,6},{6,7},{7,4},{8,9},{9,10},{10,1... | collective-permute-start | bytes 1544 | tf_op jit(solution)/shard_map/ppermute | solution.py:548
  11.5 3.8 %collective-permute-done = s32[2,4,16]{2,1,0:T(4,128)S(1)} collective-permute-done((s32[2,4,16]{2,1,0:T(4,128)S(1)}, s32[2,4,16]{2,1,0:T(4,128)S(1)}, u32[]{:S(2)}, u32[]{:S(2)}) %collective-permute-start) | collective-permute-done | bytes 544 | tf_op jit(solution)/shard_map/ppermute | solution.py:548
  15.9 1.5 %collective-permute-start.7 = (bf16[128,1536]{1,0:T(8,128)(2,1)S(1)}, bf16[128,1536]{1,0:T(8,128)(2,1)S(1)}, u32[]{:S(2)}, u32[]{:S(2)}) collective-permute-start(bf16[128,1536]{1,0:T(8,128)(2,1)S(1)} %collective-permute-done.6.refs_9_.refs_10_), channel_id=1, source_target_pairs={{0,8},{8,0},{16,24},{24,16},{1,9},{9,1},{17,25},{25,17},{2,10},{10... | collective-permute-start | bytes 1179656 | tf_op jit(solution)/shard_map/ppermute | solution.py:497
  17.9 1.5 %collective-permute-start.3 = (bf16[256,512]{1,0:T(8,128)(2,1)S(1)}, bf16[256,512]{1,0:T(8,128)(2,1)S(1)}, u32[]{:S(2)}, u32[]{:S(2)}) collective-permute-start(bf16[256,512]{1,0:T(8,128)(2,1)S(1)} %bitcast.105), channel_id=1, source_target_pairs={{0,16},{8,24},{16,0},{24,8},{1,17},{9,25},{17,1},{25,9},{2,18},{10... | collective-permute-start | bytes 786440 | tf_op jit(solution)/shard_map/ppermute | solution.py:497
  20.0 15.7 %collective-permute-done.8.refs_12_.refs_13_ = bf16[144,512]{1,0:T(8,128)(2,1)S(1)} collective-permute-done((bf16[144,512]{1,0:T(8,128)(2,1)}, bf16[144,512]{1,0:T(8,128)(2,1)S(1)}, u32[]{:S(2)}, u32[]{:S(2)}) %collective-permute-start.8) | collective-permute-done | bytes 147488 | tf_op jit(solution)/shard_map/ppermute | solution.py:497
  35.7 1.5 %collective-permute-start.10 = (bf16[144,512]{1,0:T(8,128)(2,1)S(1)}, bf16[144,512]{1,0:T(8,128)(2,1)S(1)}, u32[]{:S(2)}, u32[]{:S(2)}) collective-permute-start(bf16[144,512]{1,0:T(8,128)(2,1)S(1)} %collective-permute-done.8.refs_12_.refs_13_), channel_id=1, source_target_pairs={{0,16},{8,24},{16,0},{24,8},{1,17},{9,25},{17,1},{25,9},{2,18},{10... | collective-permute-start | bytes 442376 | tf_op jit(solution)/shard_map/ppermute | solution.py:497
  37.9 3.0 %collective-permute-done.10.refs_14_.refs_15_ = bf16[144,512]{1,0:T(8,128)(2,1)S(1)} collective-permute-done((bf16[144,512]{1,0:T(8,128)(2,1)S(1)}, bf16[144,512]{1,0:T(8,128)(2,1)S(1)}, u32[]{:S(2)}, u32[]{:S(2)}) %collective-permute-start.10) | collective-permute-done | bytes 147488 | tf_op jit(solution)/shard_map/ppermute | solution.py:497
  41.9 6.1 %shard_map.110 = (bf16[256,512]{1,0:T(8,128)(2,1)}, f32[256,512]{1,0:T(8,128)}, f32[256,128]{1,0:T(8,128)}, bf16[256,512]{1,0:T(8,128)(2,1)}, bf16[256,1536]{1,0...) custom-call(s32[2,128]{1,0:T(2,128)} %reshape.70.refs_0_, bf16[2,64,512]{2,1,0:T(8,128)(2,1)} %bitcast.106, ...), custom_call_target="tpu_custom_call" | custom-call | flops 805306368 | bytes 6358016 | tf_op jit(solution)/shard_map/pallas_call | solution.py:484
  48.0 1.3 collective-permute-start.11
  49.3 1.3 %collective-permute-done.11.refs_3_.refs_0_ = bf16[256,512]{1,0:T(8,128)(2,1)S(1)} collective-permute-done((bf16[256,512]{1,0:T(8,128)(2,1)}, bf16[256,512]{1,0:T(8,128)(2,1)S(1)}, u32[]{:S(2)}, u32[]{:S(2)}) %collective-permute-start.11) | collective-permute-done | bytes 262176 | tf_op jit(solution)/shard_map/ppermute | solution.py:576
  51.3 1.1 shard_map.111
  52.5 1.3 collective-permute-start.13
  53.8 1.2 shard_map.112
  55.0 7.6 %collective-permute-done.13.refs_3_ = bf16[256,512]{1,0:T(8,128)(2,1)S(1)} collective-permute-done((bf16[256,512]{1,0:T(8,128)(2,1)}, bf16[256,512]{1,0:T(8,128)(2,1)S(1)}, u32[]{:S(2)}, u32[]{:S(2)}) %collective-permute-start.13) | collective-permute-done | bytes 262176 | tf_op jit(solution)/shard_map/ppermute | solution.py:587
  63.3 7.7 %shard_map.113 = (bf16[2,400,128]{2,1,0:T(8,128)(2,1)}, bf16[2,400,128]{2,1,0:T(8,128)(2,1)}, bf16[2,400,128]{2,1,0:T(8,128)(2,1)}, bf16[2,400,128]{2,1,0:T(8,12...) custom-call(s32[2,128]{1,0:T(2,128)} %reshape.70.refs_0_, ...), custom_call_target="tpu_custom_call", output_to_operand_aliasing={{0}: (22, {}), {1}: (23, {}), {2}: (24, {}), {3}: (25, {}),... | custom-call | flops 1610612736 | bytes 12911616 | tf_op jit(solution)/shard_map/pallas_call | solution.py:484
  71.0 1.6 %collective-permute-start.14 = (bf16[2,400,128]{2,1,0:T(8,128)(2,1)}, bf16[2,400,128]{2,1,0:T(8,128)(2,1)S(1)}, u32[]{:S(2)}, u32[]{:S(2)}) collective-permute-start(bf16[2,400,128]{2,1,0:T(8,128)(2,1)} %get-tuple-element.88), channel_id=1, source_target_pairs={{0,16},{8,24},{16,0},{24,8},{1,17},{9,25},{17,1},{25,9},{2,18},{10... | collective-permute-start | bytes 614408 | tf_op jit(solution)/shard_map/ppermute | solution.py:497
  72.7 2.4 %collective-permute-start.12 = (bf16[2,64,512]{2,1,0:T(8,128)(2,1)S(1)}, bf16[2,64,512]{2,1,0:T(8,128)(2,1)S(1)}, u32[]{:S(2)}, u32[]{:S(2)}) collective-permute-start(bf16[2,64,512]{2,1,0:T(8,128)(2,1)S(1)} %get-tuple-element.108), channel_id=1, source_target_pairs={{1,0},{2,1},{3,2},{0,3},{5,4},{6,5},{7,6},{4,7},{9,8},{10,9},{11,1... | collective-permute-start | bytes 393224 | tf_op jit(solution)/shard_map/ppermute | solution.py:599
  75.0 1.5 %collective-permute-start.16 = (bf16[2,400,128]{2,1,0:T(8,128)(2,1)S(1)}, bf16[2,400,128]{2,1,0:T(8,128)(2,1)S(1)}, u32[]{:S(2)}, u32[]{:S(2)}) collective-permute-start(bf16[2,400,128]{2,1,0:T(8,128)(2,1)S(1)} %copy-done.26), channel_id=1, source_target_pairs={{0,8},{8,0},{16,24},{24,16},{1,9},{9,1},{17,25},{25,17},{2,10},{10... | collective-permute-start | bytes 614408 | tf_op jit(solution)/shard_map/ppermute | solution.py:497
  77.6 0.9 collective-permute-done.14
  78.5 2.3 %collective-permute-start.28 = (bf16[2,400,128]{2,1,0:T(8,128)(2,1)}, bf16[2,400,128]{2,1,0:T(8,128)(2,1)S(1)}, u32[]{:S(2)}, u32[]{:S(2)}) collective-permute-start(bf16[2,400,128]{2,1,0:T(8,128)(2,1)} %get-tuple-element.96), channel_id=1, source_target_pairs={{0,16},{8,24},{16,0},{24,8},{1,17},{9,25},{17,1},{25,9},{2,18},{10... | collective-permute-start | bytes 614408 | tf_op jit(solution)/shard_map/ppermute | solution.py:497
  80.9 1.8 %collective-permute-done.16 = bf16[2,400,128]{2,1,0:T(8,128)(2,1)S(1)} collective-permute-done((bf16[2,400,128]{2,1,0:T(8,128)(2,1)S(1)}, bf16[2,400,128]{2,1,0:T(8,128)(2,1)S(1)}, u32[]{:S(2)}, u32[]{:S(2)}) %collective-permute-start.16) | collective-permute-done | bytes 204832 | tf_op jit(solution)/shard_map/ppermute | solution.py:497
  82.7 1.5 %collective-permute-start.30 = (bf16[2,400,128]{2,1,0:T(8,128)(2,1)S(1)}, bf16[2,400,128]{2,1,0:T(8,128)(2,1)S(1)}, u32[]{:S(2)}, u32[]{:S(2)}) collective-permute-start(bf16[2,400,128]{2,1,0:T(8,128)(2,1)S(1)} %copy-done.28), channel_id=1, source_target_pairs={{0,8},{8,0},{16,24},{24,16},{1,9},{9,1},{17,25},{25,17},{2,10},{10... | collective-permute-start | bytes 614408 | tf_op jit(solution)/shard_map/ppermute | solution.py:497
  87.0 1.6 %collective-permute-start.37 = (bf16[2,400,128]{2,1,0:T(8,128)(2,1)S(1)}, bf16[2,400,128]{2,1,0:T(8,128)(2,1)S(1)}, u32[]{:S(2)}, u32[]{:S(2)}) collective-permute-start(bf16[2,400,128]{2,1,0:T(8,128)(2,1)S(1)} %copy-done.30), channel_id=1, source_target_pairs={{0,8},{8,0},{16,24},{24,16},{1,9},{9,1},{17,25},{25,17},{2,10},{10... | collective-permute-start | bytes 614408 | tf_op jit(solution)/shard_map/ppermute | solution.py:497
  89.7 1.6 %collective-permute-done.30 = bf16[2,400,128]{2,1,0:T(8,128)(2,1)S(1)} collective-permute-done((bf16[2,400,128]{2,1,0:T(8,128)(2,1)S(1)}, bf16[2,400,128]{2,1,0:T(8,128)(2,1)S(1)}, u32[]{:S(2)}, u32[]{:S(2)}) %collective-permute-start.30) | collective-permute-done | bytes 204832 | tf_op jit(solution)/shard_map/ppermute | solution.py:497
  92.1 1.5 %collective-permute-start.22 = (bf16[400,128]{1,0:T(8,128)(2,1)S(1)}, bf16[400,128]{1,0:T(8,128)(2,1)S(1)}, u32[]{:S(2)}, u32[]{:S(2)}) collective-permute-start(bf16[400,128]{1,0:T(8,128)(2,1)S(1)} %fusion.26), channel_id=1, source_target_pairs={{0,8},{8,0},{16,24},{24,16},{1,9},{9,1},{17,25},{25,17},{2,10},{10... | collective-permute-start | bytes 307208 | tf_op jit(solution)/shard_map/ppermute | solution.py:497
  93.7 1.5 %collective-permute-done.37 = bf16[2,400,128]{2,1,0:T(8,128)(2,1)S(1)} collective-permute-done((bf16[2,400,128]{2,1,0:T(8,128)(2,1)S(1)}, bf16[2,400,128]{2,1,0:T(8,128)(2,1)S(1)}, u32[]{:S(2)}, u32[]{:S(2)}) %collective-permute-start.37) | collective-permute-done | bytes 204832 | tf_op jit(solution)/shard_map/ppermute | solution.py:497
  95.1 1.0 collective-permute-start.24
  96.2 1.1 collective-permute-done.15
  97.3 1.6 %collective-permute-start.29 = (bf16[400,128]{1,0:T(8,128)(2,1)S(1)}, bf16[400,128]{1,0:T(8,128)(2,1)S(1)}, u32[]{:S(2)}, u32[]{:S(2)}) collective-permute-start(bf16[400,128]{1,0:T(8,128)(2,1)S(1)} %fusion.28), channel_id=1, source_target_pairs={{0,8},{8,0},{16,24},{24,16},{1,9},{9,1},{17,25},{25,17},{2,10},{10... | collective-permute-start | bytes 307208 | tf_op jit(solution)/shard_map/ppermute | solution.py:497
  100.2 1.3 %collective-permute-start.38 = (bf16[400,128]{1,0:T(8,128)(2,1)S(1)}, bf16[400,128]{1,0:T(8,128)(2,1)S(1)}, u32[]{:S(2)}, u32[]{:S(2)}) collective-permute-start(bf16[400,128]{1,0:T(8,128)(2,1)S(1)} %fusion.31), channel_id=1, source_target_pairs={{0,16},{8,24},{16,0},{24,8},{1,17},{9,25},{17,1},{25,9},{2,18},{10... | collective-permute-start | bytes 307208 | tf_op jit(solution)/shard_map/ppermute | solution.py:497
  102.0 1.6 %collective-permute-done.31 = bf16[400,128]{1,0:T(8,128)(2,1)S(1)} collective-permute-done((bf16[400,128]{1,0:T(8,128)(2,1)S(1)}, bf16[400,128]{1,0:T(8,128)(2,1)S(1)}, u32[]{:S(2)}, u32[]{:S(2)}) %collective-permute-start.31) | collective-permute-done | bytes 102432 | tf_op jit(solution)/shard_map/ppermute | solution.py:497
  104.3 1.5 %collective-permute-start.32 = (bf16[400,128]{1,0:T(8,128)(2,1)S(1)}, bf16[400,128]{1,0:T(8,128)(2,1)S(1)}, u32[]{:S(2)}, u32[]{:S(2)}) collective-permute-start(bf16[400,128]{1,0:T(8,128)(2,1)S(1)} %select_convert_fusion.1), channel_id=1, source_target_pairs={{0,1},{1,0},{2,3},{3,2},{4,5},{5,4},{6,7},{7,6},{8,9},{9,8},{10,11... | collective-permute-start | bytes 307208 | tf_op jit(solution)/shard_map/ppermute | solution.py:497
  106.5 0.9 collective-permute-done.18
  107.4 1.4 %collective-permute-start.19 = (bf16[400,128]{1,0:T(8,128)(2,1)S(1)}, bf16[400,128]{1,0:T(8,128)(2,1)S(1)}, u32[]{:S(2)}, u32[]{:S(2)}) collective-permute-start(bf16[400,128]{1,0:T(8,128)(2,1)S(1)} %add_convert_fusion.7), channel_id=1, source_target_pairs={{0,2},{1,3},{2,0},{3,1},{4,6},{5,7},{6,4},{7,5},{8,10},{9,11},{10,... | collective-permute-start | bytes 307208 | tf_op jit(solution)/shard_map/ppermute | solution.py:497
  108.9 3.0 %collective-permute-done.25 = bf16[400,128]{1,0:T(8,128)(2,1)S(1)} collective-permute-done((bf16[400,128]{1,0:T(8,128)(2,1)S(1)}, bf16[400,128]{1,0:T(8,128)(2,1)S(1)}, u32[]{:S(2)}, u32[]{:S(2)}) %collective-permute-start.25) | collective-permute-done | bytes 102432 | tf_op jit(solution)/shard_map/ppermute | solution.py:497
  112.0 3.1 %collective-permute-done.32 = bf16[400,128]{1,0:T(8,128)(2,1)S(1)} collective-permute-done((bf16[400,128]{1,0:T(8,128)(2,1)S(1)}, bf16[400,128]{1,0:T(8,128)(2,1)S(1)}, u32[]{:S(2)}, u32[]{:S(2)}) %collective-permute-start.32) | collective-permute-done | bytes 102432 | tf_op jit(solution)/shard_map/ppermute | solution.py:497
  115.3 2.9 %collective-permute-done.39 = bf16[400,128]{1,0:T(8,128)(2,1)S(1)} collective-permute-done((bf16[400,128]{1,0:T(8,128)(2,1)S(1)}, bf16[400,128]{1,0:T(8,128)(2,1)S(1)}, u32[]{:S(2)}, u32[]{:S(2)}) %collective-permute-start.39) | collective-permute-done | bytes 102432 | tf_op jit(solution)/shard_map/ppermute | solution.py:497
  118.5 2.1 %collective-permute-start.20 = (bf16[400,128]{1,0:T(8,128)(2,1)S(1)}, bf16[400,128]{1,0:T(8,128)(2,1)S(1)}, u32[]{:S(2)}, u32[]{:S(2)}) collective-permute-start(bf16[400,128]{1,0:T(8,128)(2,1)S(1)} %add_convert_fusion.6.refs_0_), channel_id=1, source_target_pairs={{0,1},{1,0},{2,3},{3,2},{4,5},{5,4},{6,7},{7,6},{8,9},{9,8},{10,11... | collective-permute-start | bytes 307208 | tf_op jit(solution)/shard_map/ppermute | solution.py:497
  121.7 1.1 collective-permute-start.34
  122.8 1.7 %collective-permute-done.40 = bf16[400,128]{1,0:T(8,128)(2,1)S(1)} collective-permute-done((bf16[400,128]{1,0:T(8,128)(2,1)S(1)}, bf16[400,128]{1,0:T(8,128)(2,1)S(1)}, u32[]{:S(2)}, u32[]{:S(2)}) %collective-permute-start.40) | collective-permute-done | bytes 102432 | tf_op jit(solution)/shard_map/ppermute | solution.py:497
  125.6 1.1 collective-permute-done.34.refs_5_
  126.7 2.6 %collective-permute-done.41.refs_7_ = bf16[400,128]{1,0:T(8,128)(2,1)S(1)} collective-permute-done((bf16[400,128]{1,0:T(8,128)(2,1)S(1)}, bf16[400,128]{1,0:T(8,128)(2,1)S(1)}, u32[]{:S(2)}, u32[]{:S(2)}) %collective-permute-start.41) | collective-permute-done | bytes 102432 | tf_op jit(solution)/shard_map/ppermute | solution.py:497
  130.0 2.5 %unpack.1 = (f32[1,256,512]{2,1,0:T(8,128)}, f32[1,128,1536]{2,1,0:T(8,128)}, f32[1,128,512]{2,1,0:T(8,128)}, f32[1,128]{1,0:T(1,128)}) custom-call(bf16[400,128]{1,0:T(8,128)(2,1)} %copy-done.20, bf16[400,128]{1,0:T(8,128)(2,1)} %copy-done.31, bf16[400,128]{1,0:T(8,128)(2,1)} %copy-done.21, bf16[400,128]{1,0:T(8,128)(2,1)} %copy-done.32, ...), custom_call_target="tpu_custom_call" | custom-call | tf_op jit(solution)/shard_map/unpack/pallas_call | solution.py:635
  (150 shorter events, 17.6 us)
Async XLA Ops:
  0.6 14.7 %copy-start = (bf16[1,128,1536]{2,1,0:T(8,128)(2,1)S(1)}, bf16[1,128,1536]{2,1,0:T(8,128)(2,1)}, u32[]{:S(2)}) copy-start(bf16[1,128,1536]{2,1,0:T(8,128)(2,1)} %param.10) | copy-start | bytes 1179652
  0.6 15.3 %collective-permute-start.6 = (bf16[128,1536]{1,0:T(8,128)(2,1)}, bf16[128,1536]{1,0:T(8,128)(2,1)S(1)}, u32[]{:S(2)}, u32[]{:S(2)}) collective-permute-start(bf16[128,1536]{1,0:T(8,128)(2,1)} %bitcast.96), channel_id=1, source_target_pairs={{0,16},{8,24},{16,0},{24,8},{1,17},{9,25},{17,1},{25,9},{2,18},{10... | collective-permute-start | bytes 1179656 | tf_op jit(solution)/shard_map/ppermute | solution.py:497
  4.7 12.7 %collective-permute-start.1 = (bf16[2,4,16,512]{3,2,1,0:T(8,128)(2,1)S(1)}, bf16[2,4,16,512]{3,2,1,0:T(8,128)(2,1)S(1)}, u32[]{:S(2)}, u32[]{:S(2)}) collective-permute-start(bf16[2,4,16,512]{3,2,1,0:T(8,128)(2,1)S(1)} %select_bitcast_fusion), channel_id=1, source_target_pairs={{0,1},{1,2},{2,3},{3,0},{4,5},{5,6},{6,7},{7,4},{8,9},{9,10},{10,1... | collective-permute-start | bytes 393224 | tf_op jit(solution)/shard_map/ppermute | solution.py:546
  8.0 10.0 %collective-permute-start.9 = (bf16[144,512]{1,0:T(8,128)(2,1)}, bf16[144,512]{1,0:T(8,128)(2,1)S(1)}, u32[]{:S(2)}, u32[]{:S(2)}) collective-permute-start(bf16[144,512]{1,0:T(8,128)(2,1)} %pack.1.refs_11_.refs_12_), channel_id=1, source_target_pairs={{0,16},{8,24},{16,0},{24,8},{1,17},{9,25},{17,1},{25,9},{2,18},{10... | collective-permute-start | bytes 442376 | tf_op jit(solution)/shard_map/ppermute | solution.py:497
  8.5 11.0 %collective-permute-start.2 = (bf16[256,512]{1,0:T(8,128)(2,1)S(1)}, bf16[256,512]{1,0:T(8,128)(2,1)S(1)}, u32[]{:S(2)}, u32[]{:S(2)}) collective-permute-start(bf16[256,512]{1,0:T(8,128)(2,1)S(1)} %bitcast.104), channel_id=1, source_target_pairs={{0,8},{8,0},{16,24},{24,16},{1,9},{9,1},{17,25},{25,17},{2,10},{10... | collective-permute-start | bytes 786440 | tf_op jit(solution)/shard_map/ppermute | solution.py:497
  10.0 5.4 %collective-permute-start = (s32[2,4,16]{2,1,0:T(4,128)S(1)}, s32[2,4,16]{2,1,0:T(4,128)S(1)}, u32[]{:S(2)}, u32[]{:S(2)}) collective-permute-start(s32[2,4,16]{2,1,0:T(4,128)S(1)} %get-tuple-element.109), channel_id=1, source_target_pairs={{0,1},{1,2},{2,3},{3,0},{4,5},{5,6},{6,7},{7,4},{8,9},{9,10},{10,1... | collective-permute-start | bytes 1544 | tf_op jit(solution)/shard_map/ppermute | solution.py:548
  15.4 25.5 %collective-permute-start.5 = (bf16[128,1536]{1,0:T(8,128)(2,1)S(1)}, bf16[128,1536]{1,0:T(8,128)(2,1)S(1)}, u32[]{:S(2)}, u32[]{:S(2)}) collective-permute-start(bf16[128,1536]{1,0:T(8,128)(2,1)S(1)} %bitcast.100), channel_id=1, source_target_pairs={{0,8},{8,0},{16,24},{24,16},{1,9},{9,1},{17,25},{25,17},{2,10},{10... | collective-permute-start | bytes 1179656 | tf_op jit(solution)/shard_map/ppermute | solution.py:497
  15.9 25.0 %copy-start.1 = (bf16[128,1536]{1,0:T(8,128)(2,1)}, bf16[128,1536]{1,0:T(8,128)(2,1)S(1)}, u32[]{:S(2)}) copy-start(bf16[128,1536]{1,0:T(8,128)(2,1)S(1)} %collective-permute-done.6.refs_9_.refs_10_) | copy-start | bytes 1179652
  15.9 24.9 %collective-permute-start.7 = (bf16[128,1536]{1,0:T(8,128)(2,1)S(1)}, bf16[128,1536]{1,0:T(8,128)(2,1)S(1)}, u32[]{:S(2)}, u32[]{:S(2)}) collective-permute-start(bf16[128,1536]{1,0:T(8,128)(2,1)S(1)} %collective-permute-done.6.refs_9_.refs_10_), channel_id=1, source_target_pairs={{0,8},{8,0},{16,24},{24,16},{1,9},{9,1},{17,25},{25,17},{2,10},{10... | collective-permute-start | bytes 1179656 | tf_op jit(solution)/shard_map/ppermute | solution.py:497
  17.4 23.5 %copy-start.19 = (bf16[2,4,16,512]{3,2,1,0:T(8,128)(2,1)}, bf16[2,4,16,512]{3,2,1,0:T(8,128)(2,1)S(1)}, u32[]{:S(2)}) copy-start(bf16[2,4,16,512]{3,2,1,0:T(8,128)(2,1)S(1)} %collective-permute-done.1) | copy-start | bytes 393220
  17.4 18.3 %collective-permute-start.8 = (bf16[144,512]{1,0:T(8,128)(2,1)}, bf16[144,512]{1,0:T(8,128)(2,1)S(1)}, u32[]{:S(2)}, u32[]{:S(2)}) collective-permute-start(bf16[144,512]{1,0:T(8,128)(2,1)} %pack.1.refs_11_.refs_12_), channel_id=1, source_target_pairs={{0,8},{8,0},{16,24},{24,16},{1,9},{9,1},{17,25},{25,17},{2,10},{10... | collective-permute-start | bytes 442376 | tf_op jit(solution)/shard_map/ppermute | solution.py:497
  17.9 22.9 %copy-start.16 = (bf16[144,512]{1,0:T(8,128)(2,1)}, bf16[144,512]{1,0:T(8,128)(2,1)S(1)}, u32[]{:S(2)}) copy-start(bf16[144,512]{1,0:T(8,128)(2,1)S(1)} %collective-permute-done.9.refs_13_.refs_14_) | copy-start | bytes 442372
  17.9 19.9 %collective-permute-start.3 = (bf16[256,512]{1,0:T(8,128)(2,1)S(1)}, bf16[256,512]{1,0:T(8,128)(2,1)S(1)}, u32[]{:S(2)}, u32[]{:S(2)}) collective-permute-start(bf16[256,512]{1,0:T(8,128)(2,1)S(1)} %bitcast.105), channel_id=1, source_target_pairs={{0,16},{8,24},{16,0},{24,8},{1,17},{9,25},{17,1},{25,9},{2,18},{10... | collective-permute-start | bytes 786440 | tf_op jit(solution)/shard_map/ppermute | solution.py:497
  19.5 21.4 %copy-start.13 = (bf16[256,512]{1,0:T(8,128)(2,1)}, bf16[256,512]{1,0:T(8,128)(2,1)S(1)}, u32[]{:S(2)}) copy-start(bf16[256,512]{1,0:T(8,128)(2,1)S(1)} %collective-permute-done.2.refs_4_.refs_5_) | copy-start | bytes 786436
  19.5 21.4 %collective-permute-start.4 = (bf16[256,512]{1,0:T(8,128)(2,1)S(1)}, bf16[256,512]{1,0:T(8,128)(2,1)S(1)}, u32[]{:S(2)}, u32[]{:S(2)}) collective-permute-start(bf16[256,512]{1,0:T(8,128)(2,1)S(1)} %collective-permute-done.2.refs_4_.refs_5_), channel_id=1, source_target_pairs={{0,16},{8,24},{16,0},{24,8},{1,17},{9,25},{17,1},{25,9},{2,18},{10... | collective-permute-start | bytes 786440 | tf_op jit(solution)/shard_map/ppermute | solution.py:497
  35.7 5.1 %collective-permute-start.10 = (bf16[144,512]{1,0:T(8,128)(2,1)S(1)}, bf16[144,512]{1,0:T(8,128)(2,1)S(1)}, u32[]{:S(2)}, u32[]{:S(2)}) collective-permute-start(bf16[144,512]{1,0:T(8,128)(2,1)S(1)} %collective-permute-done.8.refs_12_.refs_13_), channel_id=1, source_target_pairs={{0,16},{8,24},{16,0},{24,8},{1,17},{9,25},{17,1},{25,9},{2,18},{10... | collective-permute-start | bytes 442376 | tf_op jit(solution)/shard_map/ppermute | solution.py:497
  48.0 2.7 %collective-permute-start.11 = (bf16[256,512]{1,0:T(8,128)(2,1)}, bf16[256,512]{1,0:T(8,128)(2,1)S(1)}, u32[]{:S(2)}, u32[]{:S(2)}) collective-permute-start(bf16[256,512]{1,0:T(8,128)(2,1)} %get-tuple-element.56.refs_16_), channel_id=1, source_target_pairs={{0,4},{1,5},{2,6},{3,7},{8,12},{9,13},{10,14},{11,15},{16,20},{17,... | collective-permute-start | bytes 786440 | tf_op jit(solution)/shard_map/ppermute | solution.py:576
  52.5 10.1 %collective-permute-start.13 = (bf16[256,512]{1,0:T(8,128)(2,1)}, bf16[256,512]{1,0:T(8,128)(2,1)S(1)}, u32[]{:S(2)}, u32[]{:S(2)}) collective-permute-start(bf16[256,512]{1,0:T(8,128)(2,1)} %get-tuple-element.58), channel_id=1, source_target_pairs={{4,0},{5,1},{6,2},{7,3},{12,8},{13,9},{14,10},{15,11},{20,16},{21,... | collective-permute-start | bytes 786440 | tf_op jit(solution)/shard_map/ppermute | solution.py:587
  63.3 9.3 %copy-start.25 = (bf16[256,512]{1,0:T(8,128)(2,1)S(1)}, bf16[256,512]{1,0:T(8,128)(2,1)}, u32[]{:S(2)}) copy-start(bf16[256,512]{1,0:T(8,128)(2,1)} %get-tuple-element.57) | copy-start | bytes 786436
  71.0 7.5 %collective-permute-start.14 = (bf16[2,400,128]{2,1,0:T(8,128)(2,1)}, bf16[2,400,128]{2,1,0:T(8,128)(2,1)S(1)}, u32[]{:S(2)}, u32[]{:S(2)}) collective-permute-start(bf16[2,400,128]{2,1,0:T(8,128)(2,1)} %get-tuple-element.88), channel_id=1, source_target_pairs={{0,16},{8,24},{16,0},{24,8},{1,17},{9,25},{17,1},{25,9},{2,18},{10... | collective-permute-start | bytes 614408 | tf_op jit(solution)/shard_map/ppermute | solution.py:497
  72.7 52.0 %collective-permute-start.12 = (bf16[2,64,512]{2,1,0:T(8,128)(2,1)S(1)}, bf16[2,64,512]{2,1,0:T(8,128)(2,1)S(1)}, u32[]{:S(2)}, u32[]{:S(2)}) collective-permute-start(bf16[2,64,512]{2,1,0:T(8,128)(2,1)S(1)} %get-tuple-element.108), channel_id=1, source_target_pairs={{1,0},{2,1},{3,2},{0,3},{5,4},{6,5},{7,6},{4,7},{9,8},{10,9},{11,1... | collective-permute-start | bytes 393224 | tf_op jit(solution)/shard_map/ppermute | solution.py:599
  75.0 7.6 %collective-permute-start.16 = (bf16[2,400,128]{2,1,0:T(8,128)(2,1)S(1)}, bf16[2,400,128]{2,1,0:T(8,128)(2,1)S(1)}, u32[]{:S(2)}, u32[]{:S(2)}) collective-permute-start(bf16[2,400,128]{2,1,0:T(8,128)(2,1)S(1)} %copy-done.26), channel_id=1, source_target_pairs={{0,8},{8,0},{16,24},{24,16},{1,9},{9,1},{17,25},{25,17},{2,10},{10... | collective-permute-start | bytes 614408 | tf_op jit(solution)/shard_map/ppermute | solution.py:497
  76.5 7.9 %collective-permute-start.21 = (bf16[2,400,128]{2,1,0:T(8,128)(2,1)S(1)}, bf16[2,400,128]{2,1,0:T(8,128)(2,1)S(1)}, u32[]{:S(2)}, u32[]{:S(2)}) collective-permute-start(bf16[2,400,128]{2,1,0:T(8,128)(2,1)S(1)} %copy-done.27), channel_id=1, source_target_pairs={{0,16},{8,24},{16,0},{24,8},{1,17},{9,25},{17,1},{25,9},{2,18},{10... | collective-permute-start | bytes 614408 | tf_op jit(solution)/shard_map/ppermute | solution.py:497
  77.1 9.8 %collective-permute-start.23 = (bf16[2,400,128]{2,1,0:T(8,128)(2,1)}, bf16[2,400,128]{2,1,0:T(8,128)(2,1)S(1)}, u32[]{:S(2)}, u32[]{:S(2)}) collective-permute-start(bf16[2,400,128]{2,1,0:T(8,128)(2,1)} %get-tuple-element.94), channel_id=1, source_target_pairs={{0,8},{8,0},{16,24},{24,16},{1,9},{9,1},{17,25},{25,17},{2,10},{10... | collective-permute-start | bytes 614408 | tf_op jit(solution)/shard_map/ppermute | solution.py:497
  78.5 10.3 %collective-permute-start.28 = (bf16[2,400,128]{2,1,0:T(8,128)(2,1)}, bf16[2,400,128]{2,1,0:T(8,128)(2,1)S(1)}, u32[]{:S(2)}, u32[]{:S(2)}) collective-permute-start(bf16[2,400,128]{2,1,0:T(8,128)(2,1)} %get-tuple-element.96), channel_id=1, source_target_pairs={{0,16},{8,24},{16,0},{24,8},{1,17},{9,25},{17,1},{25,9},{2,18},{10... | collective-permute-start | bytes 614408 | tf_op jit(solution)/shard_map/ppermute | solution.py:497
  82.7 8.6 %collective-permute-start.30 = (bf16[2,400,128]{2,1,0:T(8,128)(2,1)S(1)}, bf16[2,400,128]{2,1,0:T(8,128)(2,1)S(1)}, u32[]{:S(2)}, u32[]{:S(2)}) collective-permute-start(bf16[2,400,128]{2,1,0:T(8,128)(2,1)S(1)} %copy-done.28), channel_id=1, source_target_pairs={{0,8},{8,0},{16,24},{24,16},{1,9},{9,1},{17,25},{25,17},{2,10},{10... | collective-permute-start | bytes 614408 | tf_op jit(solution)/shard_map/ppermute | solution.py:497
  85.1 6.9 %collective-permute-start.35 = (bf16[2,400,128]{2,1,0:T(8,128)(2,1)S(1)}, bf16[2,400,128]{2,1,0:T(8,128)(2,1)S(1)}, u32[]{:S(2)}, u32[]{:S(2)}) collective-permute-start(bf16[2,400,128]{2,1,0:T(8,128)(2,1)S(1)} %copy-done.29), channel_id=1, source_target_pairs={{0,16},{8,24},{16,0},{24,8},{1,17},{9,25},{17,1},{25,9},{2,18},{10... | collective-permute-start | bytes 614408 | tf_op jit(solution)/shard_map/ppermute | solution.py:497
  87.0 8.2 %collective-permute-start.37 = (bf16[2,400,128]{2,1,0:T(8,128)(2,1)S(1)}, bf16[2,400,128]{2,1,0:T(8,128)(2,1)S(1)}, u32[]{:S(2)}, u32[]{:S(2)}) collective-permute-start(bf16[2,400,128]{2,1,0:T(8,128)(2,1)S(1)} %copy-done.30), channel_id=1, source_target_pairs={{0,8},{8,0},{16,24},{24,16},{1,9},{9,1},{17,25},{25,17},{2,10},{10... | collective-permute-start | bytes 614408 | tf_op jit(solution)/shard_map/ppermute | solution.py:497
  88.8 8.5 %collective-permute-start.15 = (bf16[400,128]{1,0:T(8,128)(2,1)S(1)}, bf16[400,128]{1,0:T(8,128)(2,1)S(1)}, u32[]{:S(2)}, u32[]{:S(2)}) collective-permute-start(bf16[400,128]{1,0:T(8,128)(2,1)S(1)} %fusion.24), channel_id=1, source_target_pairs={{0,8},{8,0},{16,24},{24,16},{1,9},{9,1},{17,25},{25,17},{2,10},{10... | collective-permute-start | bytes 307208 | tf_op jit(solution)/shard_map/ppermute | solution.py:497
  91.3 7.7 %collective-permute-start.17 = (bf16[400,128]{1,0:T(8,128)(2,1)S(1)}, bf16[400,128]{1,0:T(8,128)(2,1)S(1)}, u32[]{:S(2)}, u32[]{:S(2)}) collective-permute-start(bf16[400,128]{1,0:T(8,128)(2,1)S(1)} %fusion.25), channel_id=1, source_target_pairs={{0,16},{8,24},{16,0},{24,8},{1,17},{9,25},{17,1},{25,9},{2,18},{10... | collective-permute-start | bytes 307208 | tf_op jit(solution)/shard_map/ppermute | solution.py:497
  92.1 7.5 %collective-permute-start.22 = (bf16[400,128]{1,0:T(8,128)(2,1)S(1)}, bf16[400,128]{1,0:T(8,128)(2,1)S(1)}, u32[]{:S(2)}, u32[]{:S(2)}) collective-permute-start(bf16[400,128]{1,0:T(8,128)(2,1)S(1)} %fusion.26), channel_id=1, source_target_pairs={{0,8},{8,0},{16,24},{24,16},{1,9},{9,1},{17,25},{25,17},{2,10},{10... | collective-permute-start | bytes 307208 | tf_op jit(solution)/shard_map/ppermute | solution.py:497
  95.1 5.1 %collective-permute-start.24 = (bf16[400,128]{1,0:T(8,128)(2,1)S(1)}, bf16[400,128]{1,0:T(8,128)(2,1)S(1)}, u32[]{:S(2)}, u32[]{:S(2)}) collective-permute-start(bf16[400,128]{1,0:T(8,128)(2,1)S(1)} %fusion.27), channel_id=1, source_target_pairs={{0,16},{8,24},{16,0},{24,8},{1,17},{9,25},{17,1},{25,9},{2,18},{10... | collective-permute-start | bytes 307208 | tf_op jit(solution)/shard_map/ppermute | solution.py:497
  97.3 4.7 %collective-permute-start.29 = (bf16[400,128]{1,0:T(8,128)(2,1)S(1)}, bf16[400,128]{1,0:T(8,128)(2,1)S(1)}, u32[]{:S(2)}, u32[]{:S(2)}) collective-permute-start(bf16[400,128]{1,0:T(8,128)(2,1)S(1)} %fusion.28), channel_id=1, source_target_pairs={{0,8},{8,0},{16,24},{24,16},{1,9},{9,1},{17,25},{25,17},{2,10},{10... | collective-permute-start | bytes 307208 | tf_op jit(solution)/shard_map/ppermute | solution.py:497
  98.9 4.7 %collective-permute-start.31 = (bf16[400,128]{1,0:T(8,128)(2,1)S(1)}, bf16[400,128]{1,0:T(8,128)(2,1)S(1)}, u32[]{:S(2)}, u32[]{:S(2)}) collective-permute-start(bf16[400,128]{1,0:T(8,128)(2,1)S(1)} %fusion.29), channel_id=1, source_target_pairs={{0,16},{8,24},{16,0},{24,8},{1,17},{9,25},{17,1},{25,9},{2,18},{10... | collective-permute-start | bytes 307208 | tf_op jit(solution)/shard_map/ppermute | solution.py:497
  99.5 4.7 %collective-permute-start.36 = (bf16[400,128]{1,0:T(8,128)(2,1)S(1)}, bf16[400,128]{1,0:T(8,128)(2,1)S(1)}, u32[]{:S(2)}, u32[]{:S(2)}) collective-permute-start(bf16[400,128]{1,0:T(8,128)(2,1)S(1)} %fusion.30), channel_id=1, source_target_pairs={{0,8},{8,0},{16,24},{24,16},{1,9},{9,1},{17,25},{25,17},{2,10},{10... | collective-permute-start | bytes 307208 | tf_op jit(solution)/shard_map/ppermute | solution.py:497
  100.2 5.6 %collective-permute-start.38 = (bf16[400,128]{1,0:T(8,128)(2,1)S(1)}, bf16[400,128]{1,0:T(8,128)(2,1)S(1)}, u32[]{:S(2)}, u32[]{:S(2)}) collective-permute-start(bf16[400,128]{1,0:T(8,128)(2,1)S(1)} %fusion.31), channel_id=1, source_target_pairs={{0,16},{8,24},{16,0},{24,8},{1,17},{9,25},{17,1},{25,9},{2,18},{10... | collective-permute-start | bytes 307208 | tf_op jit(solution)/shard_map/ppermute | solution.py:497
  102.0 5.3 %collective-permute-start.18 = (bf16[400,128]{1,0:T(8,128)(2,1)S(1)}, bf16[400,128]{1,0:T(8,128)(2,1)S(1)}, u32[]{:S(2)}, u32[]{:S(2)}) collective-permute-start(bf16[400,128]{1,0:T(8,128)(2,1)S(1)} %select_convert_fusion.3), channel_id=1, source_target_pairs={{0,1},{1,0},{2,3},{3,2},{4,5},{5,4},{6,7},{7,6},{8,9},{9,8},{10,11... | collective-permute-start | bytes 307208 | tf_op jit(solution)/shard_map/ppermute | solution.py:497
  103.6 8.3 %collective-permute-start.25 = (bf16[400,128]{1,0:T(8,128)(2,1)S(1)}, bf16[400,128]{1,0:T(8,128)(2,1)S(1)}, u32[]{:S(2)}, u32[]{:S(2)}) collective-permute-start(bf16[400,128]{1,0:T(8,128)(2,1)S(1)} %select_convert_fusion.2), channel_id=1, source_target_pairs={{0,1},{1,0},{2,3},{3,2},{4,5},{5,4},{6,7},{7,6},{8,9},{9,8},{10,11... | collective-permute-start | bytes 307208 | tf_op jit(solution)/shard_map/ppermute | solution.py:497
  104.3 10.9 %collective-permute-start.32 = (bf16[400,128]{1,0:T(8,128)(2,1)S(1)}, bf16[400,128]{1,0:T(8,128)(2,1)S(1)}, u32[]{:S(2)}, u32[]{:S(2)}) collective-permute-start(bf16[400,128]{1,0:T(8,128)(2,1)S(1)} %select_convert_fusion.1), channel_id=1, source_target_pairs={{0,1},{1,0},{2,3},{3,2},{4,5},{5,4},{6,7},{7,6},{8,9},{9,8},{10,11... | collective-permute-start | bytes 307208 | tf_op jit(solution)/shard_map/ppermute | solution.py:497
  105.9 12.3 %collective-permute-start.39 = (bf16[400,128]{1,0:T(8,128)(2,1)S(1)}, bf16[400,128]{1,0:T(8,128)(2,1)S(1)}, u32[]{:S(2)}, u32[]{:S(2)}) collective-permute-start(bf16[400,128]{1,0:T(8,128)(2,1)S(1)} %select_convert_fusion), channel_id=1, source_target_pairs={{0,1},{1,0},{2,3},{3,2},{4,5},{5,4},{6,7},{7,6},{8,9},{9,8},{10,11... | collective-permute-start | bytes 307208 | tf_op jit(solution)/shard_map/ppermute | solution.py:497
  107.4 11.0 %collective-permute-start.19 = (bf16[400,128]{1,0:T(8,128)(2,1)S(1)}, bf16[400,128]{1,0:T(8,128)(2,1)S(1)}, u32[]{:S(2)}, u32[]{:S(2)}) collective-permute-start(bf16[400,128]{1,0:T(8,128)(2,1)S(1)} %add_convert_fusion.7), channel_id=1, source_target_pairs={{0,2},{1,3},{2,0},{3,1},{4,6},{5,7},{6,4},{7,5},{8,10},{9,11},{10,... | collective-permute-start | bytes 307208 | tf_op jit(solution)/shard_map/ppermute | solution.py:497
  112.0 8.6 %collective-permute-start.26 = (bf16[400,128]{1,0:T(8,128)(2,1)S(1)}, bf16[400,128]{1,0:T(8,128)(2,1)S(1)}, u32[]{:S(2)}, u32[]{:S(2)}) collective-permute-start(bf16[400,128]{1,0:T(8,128)(2,1)S(1)} %add_convert_fusion.5), channel_id=1, source_target_pairs={{0,2},{1,3},{2,0},{3,1},{4,6},{5,7},{6,4},{7,5},{8,10},{9,11},{10,... | collective-permute-start | bytes 307208 | tf_op jit(solution)/shard_map/ppermute | solution.py:497
  115.3 6.4 %collective-permute-start.33 = (bf16[400,128]{1,0:T(8,128)(2,1)S(1)}, bf16[400,128]{1,0:T(8,128)(2,1)S(1)}, u32[]{:S(2)}, u32[]{:S(2)}) collective-permute-start(bf16[400,128]{1,0:T(8,128)(2,1)S(1)} %add_convert_fusion.3), channel_id=1, source_target_pairs={{0,2},{1,3},{2,0},{3,1},{4,6},{5,7},{6,4},{7,5},{8,10},{9,11},{10,... | collective-permute-start | bytes 307208 | tf_op jit(solution)/shard_map/ppermute | solution.py:497
  118.3 6.2 %collective-permute-start.40 = (bf16[400,128]{1,0:T(8,128)(2,1)S(1)}, bf16[400,128]{1,0:T(8,128)(2,1)S(1)}, u32[]{:S(2)}, u32[]{:S(2)}) collective-permute-start(bf16[400,128]{1,0:T(8,128)(2,1)S(1)} %add_convert_fusion.1), channel_id=1, source_target_pairs={{0,2},{1,3},{2,0},{3,1},{4,6},{5,7},{6,4},{7,5},{8,10},{9,11},{10,... | collective-permute-start | bytes 307208 | tf_op jit(solution)/shard_map/ppermute | solution.py:497
  118.5 6.9 %collective-permute-start.20 = (bf16[400,128]{1,0:T(8,128)(2,1)S(1)}, bf16[400,128]{1,0:T(8,128)(2,1)S(1)}, u32[]{:S(2)}, u32[]{:S(2)}) collective-permute-start(bf16[400,128]{1,0:T(8,128)(2,1)S(1)} %add_convert_fusion.6.refs_0_), channel_id=1, source_target_pairs={{0,1},{1,0},{2,3},{3,2},{4,5},{5,4},{6,7},{7,6},{8,9},{9,8},{10,11... | collective-permute-start | bytes 307208 | tf_op jit(solution)/shard_map/ppermute | solution.py:497
  120.6 5.0 %collective-permute-start.27 = (bf16[400,128]{1,0:T(8,128)(2,1)S(1)}, bf16[400,128]{1,0:T(8,128)(2,1)S(1)}, u32[]{:S(2)}, u32[]{:S(2)}) collective-permute-start(bf16[400,128]{1,0:T(8,128)(2,1)S(1)} %add_convert_fusion.4.refs_2_), channel_id=1, source_target_pairs={{0,1},{1,0},{2,3},{3,2},{4,5},{5,4},{6,7},{7,6},{8,9},{9,8},{10,11... | collective-permute-start | bytes 307208 | tf_op jit(solution)/shard_map/ppermute | solution.py:497
  121.7 4.9 %collective-permute-start.34 = (bf16[400,128]{1,0:T(8,128)(2,1)S(1)}, bf16[400,128]{1,0:T(8,128)(2,1)S(1)}, u32[]{:S(2)}, u32[]{:S(2)}) collective-permute-start(bf16[400,128]{1,0:T(8,128)(2,1)S(1)} %add_convert_fusion.2.refs_4_), channel_id=1, source_target_pairs={{0,1},{1,0},{2,3},{3,2},{4,5},{5,4},{6,7},{7,6},{8,9},{9,8},{10,11... | collective-permute-start | bytes 307208 | tf_op jit(solution)/shard_map/ppermute | solution.py:497
  124.6 4.7 %collective-permute-start.41 = (bf16[400,128]{1,0:T(8,128)(2,1)S(1)}, bf16[400,128]{1,0:T(8,128)(2,1)S(1)}, u32[]{:S(2)}, u32[]{:S(2)}) collective-permute-start(bf16[400,128]{1,0:T(8,128)(2,1)S(1)} %add_convert_fusion.refs_6_), channel_id=1, source_target_pairs={{0,1},{1,0},{2,3},{3,2},{4,5},{5,4},{6,7},{7,6},{8,9},{9,8},{10,11... | collective-permute-start | bytes 307208 | tf_op jit(solution)/shard_map/ppermute | solution.py:497
  (31 other events, 63.0 us)

commit v5 on v4

--- a/solution.py
+++ b/solution.py
@@ -12,7 +12,7 @@
 SH = 4
 SW = 8
 PAD = 16
-CHUNKS = 4
+CHUNKS = 2
 
 EPSILON = 1e-05
 MASKED = -1e30
@@ -52,10 +52,11 @@
 
 
 def layout(feature, shards):
-    merge, rows = 2 * feature // shards, feature // shards
-    first = {"merge": (0, merge), "q": (merge, rows), "gain": (merge + rows, PAD)}
-    second = {"k": (0, rows), "v": (rows, rows), "out": (2 * rows, rows), "pad": (3 * rows, PAD)}
-    return (first, second, merge + rows + PAD)
+    rows = feature // shards
+    part = rows // 2
+    first = {"merge": (0, rows), "q": (rows, rows), "gain": (2 * rows, PAD), "k0": (2 * rows + PAD, part)}
+    second = {"k1": (0, part), "v": (part, rows), "out": (part + rows, rows), "pad": (part + 2 * rows, PAD)}
+    return (first, second, 2 * rows + part + PAD)
 
 
 def load_weights(copies, pieces, names, dst):
@@ -269,13 +270,11 @@
     dw_first, dw_second = dw
     started = []
 
-    def put(name, value):
+    def put(name, value, row_of):
         block = dw_first if name in first else dw_second
         start, size = first[name] if name in first else second[name]
-        value = value.astype(BF16)
         for i in range(shards):
-            at = (i * size) % feature
-            block[i, start : start + size, :] = value[at : at + size]
+            block[i, start : start + size, :] = value[row_of(i) : row_of(i) + size]
 
     def emit(which, start, size):
         block = (dw_first, dw_second)[which]
@@ -291,19 +290,26 @@
                     part = block.at[owner, pl.ds(start, size), pl.ds(chunk * width, width)]
                     started.append(copies.start(part, ref.at[pl.ds(start, size)]))
 
-    put("out", dot_tn(mix[...], grad_out[...]))
-    for i, name in ((1, "k"), (2, "v")):
-        put(name, dot_tn(hidden[...], grad_proj[:, i * feature : (i + 1) * feature]))
-    dw_second[:, 3 * rows :, :] = jnp.zeros((shards, PAD, feature), BF16)
+    def of_projection(i):
+        part = grad_proj[:, i * feature : (i + 1) * feature]
+        return dot_tn(hidden[...], part).astype(BF16)
+
+    put("out", dot_tn(mix[...], grad_out[...]).astype(BF16), lambda i: i * rows)
+    grad_k = of_projection(1)
+    put("k1", grad_k, lambda i: i * rows + rows // 2)
+    put("v", of_projection(2), lambda i: i * rows)
+    dw_second[:, second["pad"][0] :, :] = jnp.zeros((shards, PAD, feature), BF16)
     emit(1, 0, half)
-    put("q", dot_tn(hidden[...], grad_proj[:, :feature]))
+    put("k0", grad_k, lambda i: i * rows)
+    put("q", of_projection(0), lambda i: i * rows)
     start = first["gain"][0]
     for i in range(shards):
         part = grad_gain[:, i * rows : (i + 1) * rows].astype(BF16)
-        dw_first[i, start:, :] = jnp.zeros((PAD, feature), BF16)
-        dw_first[i, start:, :rows] = jnp.broadcast_to(part, (PAD, rows))
+        dw_first[i, start : start + PAD, :] = jnp.zeros((PAD, feature), BF16)
+        dw_first[i, start : start + PAD, :rows] = jnp.broadcast_to(part, (PAD, rows))
     emit(0, first["q"][0], half - first["q"][0])
-    put("merge", dot_tn(x[...], grad_update[...]))
+    put("merge", dot_tn(x[...], grad_update[...]).astype(BF16),
+        lambda i: (i % 2) * 2 * rows + (i // 2) * rows)
     emit(0, 0, first["merge"][1])
     return started
 
@@ -451,28 +457,39 @@
 
 
 def final_kernel(*refs):
-    halves, (merge, qkv, out, gain) = refs[: 2 * CHUNKS], refs[2 * CHUNKS :]
+    halves, (near, far), (merge, qkv, out, gain) = refs[: 4 * CHUNKS], refs[4 * CHUNKS : -4], refs[-4:]
     feature = merge.shape[2]
-    shards = 2 * feature // merge.shape[1]
-    first, second, _ = layout(feature, shards)
+    size = qkv.shape[1]
+    first, second, _ = layout(feature, feature // size)
     even = lax.axis_index("band") % 2 == 0
+    upper = lax.axis_index("dp") >= feature // size // 2
     width = feature // CHUNKS
 
-    def rows(name, chunk):
-        own, other = halves[2 * chunk], halves[2 * chunk + 1]
-        table, flip = (first, False) if name in first else (second, True)
-        start, size = table[name]
-        mine, theirs = own[start : start + size, :], other[start : start + size, :]
-        a, b = (theirs, mine) if flip else (mine, theirs)
+    def chosen(mine, theirs, side):
+        a, b = (theirs, mine) if side else (mine, theirs)
         return jnp.where(even, a.astype(F32), b.astype(F32))
 
+    def rows(name, chunk, side):
+        which = 0 if name in first else 1
+        own, other = halves[4 * chunk + 2 * which : 4 * chunk + 2 * which + 2]
+        start, count = (second if which else first)[name]
+        return chosen(own[start : start + count, :], other[start : start + count, :], side)
+
     for chunk in range(CHUNKS):
-        at = chunk * width
-        merge[0, :, at : at + width] = rows("merge", chunk)
-        for i, name in enumerate(("q", "k", "v")):
-            qkv[0, :, i * feature + at : i * feature + at + width] = rows(name, chunk)
-        out[0, :, at : at + width] = rows("out", chunk)
-    gain[...] = rows("gain", 0)[:1, : gain.shape[1]]
+        for side in range(2):
+            low = chunk * width + side * (width // 2)
+            high = low + width // 2
+            piece = slice(chunk * width // 2, (chunk + 1) * width // 2)
+            here, there = rows("merge", chunk, side), chosen(near[:, piece], far[:, piece], side)
+            merge[0, :size, low:high] = jnp.where(upper, there, here)
+            merge[0, size:, low:high] = jnp.where(upper, here, there)
+            for i, (name, begin, count) in enumerate(
+                (("q", 0, size), ("k0", 0, size // 2), ("k1", size // 2, size // 2), ("v", 0, size))
+            ):
+                at = (0, 1, 1, 2)[i] * feature
+                qkv[0, begin : begin + count, at + low : at + high] = rows(name, chunk, side)
+            out[0, :, low:high] = rows("out", chunk, side)
+    gain[...] = rows("gain", 0, 0)[:1, : gain.shape[1]]
 
 
 ANY = pl.BlockSpec(memory_space=pl.ANY)
@@ -611,27 +628,33 @@
 
     high = shards // 2
     even = band % 2 == 0
+    side = feature // CHUNKS // 2
     halves = []
 
     def named(value, axis, bit):
         return flip(value, axis, bit).astype(F32)
 
     for chunk in range(CHUNKS):
-        p_keep, p_send, q_keep, q_send = grads[4 * chunk : 4 * chunk + 4]
-        p_in = named(p_send, "dp", high)
-        q_in = named(q_send, "dp", 1)
-        p_pass = (p_keep[1].astype(F32) + p_in[1]).astype(BF16)
-        q_pass = (q_keep[1].astype(F32) + q_in[1]).astype(BF16)
-        p_sum = p_keep[0].astype(F32) + p_in[0] + named(p_pass, "dp", 1)
-        q_sum = q_keep[0].astype(F32) + q_in[0] + named(q_pass, "dp", high)
-        mine = jnp.where(even, p_sum, q_sum)
-        theirs = jnp.where(even, q_sum, p_sum).astype(BF16)
-        mine = (mine + named(theirs, "band", 1)).astype(BF16)
-        bit = 2
-        while bit < bands:
-            mine = (mine.astype(F32) + named(mine, "band", bit)).astype(BF16)
-            bit *= 2
-        halves += [mine, flip(mine, "band", 1)]
+        for which, bits in (("p", (high, 1)), ("q", (1, high))):
+            keep, send = grads[4 * chunk + 2 * (which == "q") :][:2]
+            got = named(send, "dp", bits[0])
+            on = (keep[1].astype(F32) + got[1]).astype(BF16)
+            total_here = keep[0].astype(F32) + got[0] + named(on, "dp", bits[1])
+            left, right = total_here[:, :side], total_here[:, side:]
+            mine = jnp.where(even, left, right)
+            theirs = jnp.where(even, right, left).astype(BF16)
+            mine = (mine + named(theirs, "band", 1)).astype(BF16)
+            bit = 2
+            while bit < bands:
+                mine = (mine.astype(F32) + named(mine, "band", bit)).astype(BF16)
+                bit *= 2
+            halves += [mine, flip(mine, "band", 1)]
+    pieces = jnp.concatenate([halves[4 * chunk][:rows] for chunk in range(CHUNKS)], axis=1)
+    pairs_far = [
+        (i * bands + j, (i ^ high) * bands + (j ^ 1)) for i in range(shards) for j in range(bands)
+    ]
+    halves.append(flip(pieces, "dp", high))
+    halves.append(lax.ppermute(pieces, ("dp", "band"), pairs_far))
     merge_grad, qkv_grad, out_grad, gain_grad = pl.pallas_call(
         final_kernel,
         out_shape=(

time: 133 us -> 123 us (0.925)
  waiting for transfers between devices: 57.8 us -> 42.9 us
  starting transfers between devices: 45.4 us -> 52.6 us
    ppermute x37 -> x30, waiting for transfers between devices: 44.9 us -> 29.6 us  [flip(): return lax.ppermute(value, axis, [(i, i ^ bit) for i in range(size)])]
    ppermute x37 -> x30, starting transfers between devices: 37.2 us -> 43.5 us  [flip(): return lax.ppermute(value, axis, [(i, i ^ bit) for i in range(size)])]
    unnamed x74 -> x62, local copies, waits for them, and re-layouts: 4.24 us -> 3.08 us
  transfers between devices with their start and end apart: 42 -> 36, of which waited for: 25 -> 11; matrix products, arithmetic and copies ran while one was open for 3% -> 3% of each run, Pallas kernels for 2% -> 2%
where the time goes in v5:
time: 123 us
  starting transfers between devices  52.6 us (43%)
  waiting for transfers between devices  42.9 us (35%)
  Pallas kernels  20 us (16%)
  local copies, waits for them, and re-layouts  3.74 us (3%)
  other arithmetic  2.66 us (2%)
    ppermute x30, starting transfers between devices, flip(): return lax.ppermute(value, axis, [(i, i ^ bit) for i in range(size)])  43.5 us
    ppermute x30, waiting for transfers between devices, flip(): return lax.ppermute(value, axis, [(i, i ^ bit) for i in range(size)])  29.6 us
    pallas_call x4, Pallas kernels, call(): pl.pallas_call(kernel, out_shape=tuple(outs), in_specs=[ANY] * len(ins),...  15.9 us
    ppermute x1, waiting for transfers between devices, body(): g0 = lax.ppermute(g_out, 'segment', [(1, 0)])  7.63 us
    ppermute x1, waiting for transfers between devices, body(): mask_moved = lax.ppermute(cell_mask[0, :, row_count - SH:], 'band', down)  3.83 us
    unnamed x62, local copies, waits for them, and re-layouts  3.08 us
  transfers between devices with their start and end apart: 36, of which 11 were waited for; matrix products, arithmetic and copies ran while one was open for 3% of the time, Pallas kernels for 2%

profile of v5, /device:TPU:0, one launch (start us, length us, event | category | flops | bytes accessed | tf_op | source)
XLA Modules:
  0.0 123.0 jit_solution(12952940916376428035)
XLA Ops:
  0.6 3.1 %collective-permute-start.6 = (bf16[128,1536]{1,0:T(8,128)(2,1)}, bf16[128,1536]{1,0:T(8,128)(2,1)S(1)}, u32[]{:S(2)}, u32[]{:S(2)}) collective-permute-start(bf16[128,1536]{1,0:T(8,128)(2,1)} %bitcast.40), channel_id=1, source_target_pairs={{0,16},{8,24},{16,0},{24,8},{1,17},{9,25},{17,1},{25,9},{2,18},{10... | collective-permute-start | bytes 1179656 | tf_op jit(solution)/shard_map/ppermute | solution.py:514
  3.7 1.0 select_bitcast_fusion
  4.7 1.6 %collective-permute-start.1 = (bf16[2,4,16,512]{3,2,1,0:T(8,128)(2,1)S(1)}, bf16[2,4,16,512]{3,2,1,0:T(8,128)(2,1)S(1)}, u32[]{:S(2)}, u32[]{:S(2)}) collective-permute-start(bf16[2,4,16,512]{3,2,1,0:T(8,128)(2,1)S(1)} %select_bitcast_fusion), channel_id=1, source_target_pairs={{0,1},{1,2},{2,3},{3,0},{4,5},{5,6},{6,7},{7,4},{8,9},{9,10},{10,1... | collective-permute-start | bytes 393224 | tf_op jit(solution)/shard_map/ppermute | solution.py:563
  6.4 1.6 %pack.1.refs_11_.refs_12_ = bf16[144,512]{1,0:T(8,128)(2,1)} custom-call(bf16[128,512]{1,0:T(8,128)(2,1)} %bitcast.55, bf16[1,128]{1,0:T(2,128)(2,1)} %gain.1), custom_call_target="tpu_custom_call" | custom-call | tf_op jit(solution)/shard_map/pack/pallas_call | solution.py:550
  8.5 1.5 %collective-permute-start.2 = (bf16[256,512]{1,0:T(8,128)(2,1)S(1)}, bf16[256,512]{1,0:T(8,128)(2,1)S(1)}, u32[]{:S(2)}, u32[]{:S(2)}) collective-permute-start(bf16[256,512]{1,0:T(8,128)(2,1)S(1)} %bitcast.48), channel_id=1, source_target_pairs={{0,8},{8,0},{16,24},{24,16},{1,9},{9,1},{17,25},{25,17},{2,10},{10... | collective-permute-start | bytes 786440 | tf_op jit(solution)/shard_map/ppermute | solution.py:514
  10.0 1.6 %collective-permute-start = (s32[2,4,16]{2,1,0:T(4,128)S(1)}, s32[2,4,16]{2,1,0:T(4,128)S(1)}, u32[]{:S(2)}, u32[]{:S(2)}) collective-permute-start(s32[2,4,16]{2,1,0:T(4,128)S(1)} %get-tuple-element.77), channel_id=1, source_target_pairs={{0,1},{1,2},{2,3},{3,0},{4,5},{5,6},{6,7},{7,4},{8,9},{9,10},{10,1... | collective-permute-start | bytes 1544 | tf_op jit(solution)/shard_map/ppermute | solution.py:565
  11.5 3.8 %collective-permute-done = s32[2,4,16]{2,1,0:T(4,128)S(1)} collective-permute-done((s32[2,4,16]{2,1,0:T(4,128)S(1)}, s32[2,4,16]{2,1,0:T(4,128)S(1)}, u32[]{:S(2)}, u32[]{:S(2)}) %collective-permute-start) | collective-permute-done | bytes 544 | tf_op jit(solution)/shard_map/ppermute | solution.py:565
  15.9 1.5 %collective-permute-start.7 = (bf16[128,1536]{1,0:T(8,128)(2,1)S(1)}, bf16[128,1536]{1,0:T(8,128)(2,1)S(1)}, u32[]{:S(2)}, u32[]{:S(2)}) collective-permute-start(bf16[128,1536]{1,0:T(8,128)(2,1)S(1)} %collective-permute-done.6.refs_9_.refs_10_), channel_id=1, source_target_pairs={{0,8},{8,0},{16,24},{24,16},{1,9},{9,1},{17,25},{25,17},{2,10},{10... | collective-permute-start | bytes 1179656 | tf_op jit(solution)/shard_map/ppermute | solution.py:514
  18.0 1.5 %collective-permute-start.3 = (bf16[256,512]{1,0:T(8,128)(2,1)S(1)}, bf16[256,512]{1,0:T(8,128)(2,1)S(1)}, u32[]{:S(2)}, u32[]{:S(2)}) collective-permute-start(bf16[256,512]{1,0:T(8,128)(2,1)S(1)} %bitcast.49), channel_id=1, source_target_pairs={{0,16},{8,24},{16,0},{24,8},{1,17},{9,25},{17,1},{25,9},{2,18},{10... | collective-permute-start | bytes 786440 | tf_op jit(solution)/shard_map/ppermute | solution.py:514
  20.0 15.7 %collective-permute-done.8.refs_12_.refs_13_ = bf16[144,512]{1,0:T(8,128)(2,1)S(1)} collective-permute-done((bf16[144,512]{1,0:T(8,128)(2,1)}, bf16[144,512]{1,0:T(8,128)(2,1)S(1)}, u32[]{:S(2)}, u32[]{:S(2)}) %collective-permute-start.8) | collective-permute-done | bytes 147488 | tf_op jit(solution)/shard_map/ppermute | solution.py:514
  35.7 1.5 %collective-permute-start.10 = (bf16[144,512]{1,0:T(8,128)(2,1)S(1)}, bf16[144,512]{1,0:T(8,128)(2,1)S(1)}, u32[]{:S(2)}, u32[]{:S(2)}) collective-permute-start(bf16[144,512]{1,0:T(8,128)(2,1)S(1)} %collective-permute-done.8.refs_12_.refs_13_), channel_id=1, source_target_pairs={{0,16},{8,24},{16,0},{24,8},{1,17},{9,25},{17,1},{25,9},{2,18},{10... | collective-permute-start | bytes 442376 | tf_op jit(solution)/shard_map/ppermute | solution.py:514
  37.9 3.0 %collective-permute-done.10.refs_14_.refs_15_ = bf16[144,512]{1,0:T(8,128)(2,1)S(1)} collective-permute-done((bf16[144,512]{1,0:T(8,128)(2,1)S(1)}, bf16[144,512]{1,0:T(8,128)(2,1)S(1)}, u32[]{:S(2)}, u32[]{:S(2)}) %collective-permute-start.10) | collective-permute-done | bytes 147488 | tf_op jit(solution)/shard_map/ppermute | solution.py:514
  41.9 6.1 %shard_map.110 = (bf16[256,512]{1,0:T(8,128)(2,1)}, f32[256,512]{1,0:T(8,128)}, f32[256,128]{1,0:T(8,128)}, bf16[256,512]{1,0:T(8,128)(2,1)}, bf16[256,1536]{1,0...) custom-call(s32[2,128]{1,0:T(2,128)} %reshape.50.refs_0_, bf16[2,64,512]{2,1,0:T(8,128)(2,1)} %bitcast.50, ...), custom_call_target="tpu_custom_call" | custom-call | flops 805306368 | bytes 6358016 | tf_op jit(solution)/shard_map/pallas_call | solution.py:501
  48.0 1.3 %collective-permute-start.11 = (bf16[256,512]{1,0:T(8,128)(2,1)}, bf16[256,512]{1,0:T(8,128)(2,1)S(1)}, u32[]{:S(2)}, u32[]{:S(2)}) collective-permute-start(bf16[256,512]{1,0:T(8,128)(2,1)} %get-tuple-element.40.refs_16_), channel_id=1, source_target_pairs={{0,4},{1,5},{2,6},{3,7},{8,12},{9,13},{10,14},{11,15},{16,20},{17,... | collective-permute-start | bytes 786440 | tf_op jit(solution)/shard_map/ppermute | solution.py:593
  49.3 1.3 %collective-permute-done.11.refs_3_.refs_0_ = bf16[256,512]{1,0:T(8,128)(2,1)S(1)} collective-permute-done((bf16[256,512]{1,0:T(8,128)(2,1)}, bf16[256,512]{1,0:T(8,128)(2,1)S(1)}, u32[]{:S(2)}, u32[]{:S(2)}) %collective-permute-start.11) | collective-permute-done | bytes 262176 | tf_op jit(solution)/shard_map/ppermute | solution.py:593
  50.7 0.7 copy-done.30
  51.4 1.1 shard_map.111
  52.5 1.3 %collective-permute-start.13 = (bf16[256,512]{1,0:T(8,128)(2,1)}, bf16[256,512]{1,0:T(8,128)(2,1)S(1)}, u32[]{:S(2)}, u32[]{:S(2)}) collective-permute-start(bf16[256,512]{1,0:T(8,128)(2,1)} %get-tuple-element.42), channel_id=1, source_target_pairs={{4,0},{5,1},{6,2},{7,3},{12,8},{13,9},{14,10},{15,11},{20,16},{21,... | collective-permute-start | bytes 786440 | tf_op jit(solution)/shard_map/ppermute | solution.py:604
  53.8 1.2 shard_map.112
  55.0 7.6 %collective-permute-done.13.refs_3_ = bf16[256,512]{1,0:T(8,128)(2,1)S(1)} collective-permute-done((bf16[256,512]{1,0:T(8,128)(2,1)}, bf16[256,512]{1,0:T(8,128)(2,1)S(1)}, u32[]{:S(2)}, u32[]{:S(2)}) %collective-permute-start.13) | collective-permute-done | bytes 262176 | tf_op jit(solution)/shard_map/ppermute | solution.py:604
  63.3 7.5 %shard_map.113 = (bf16[2,336,256]{2,1,0:T(8,128)(2,1)}, bf16[2,336,256]{2,1,0:T(8,128)(2,1)}, bf16[2,336,256]{2,1,0:T(8,128)(2,1)}, bf16[2,336,256]{2,1,0:T(8,12...) custom-call(s32[2,128]{1,0:T(2,128)} %reshape.50.refs_0_, ...), custom_call_target="tpu_custom_call", output_to_operand_aliasing={{0}: (22, {}), {1}: (23, {}), {2}: (24, {}), {3}: (25, {}),... | custom-call | flops 1610612736 | bytes 11863040 | tf_op jit(solution)/shard_map/pallas_call | solution.py:501
  70.9 1.6 %collective-permute-start.14 = (bf16[2,336,256]{2,1,0:T(8,128)(2,1)}, bf16[2,336,256]{2,1,0:T(8,128)(2,1)S(1)}, u32[]{:S(2)}, u32[]{:S(2)}) collective-permute-start(bf16[2,336,256]{2,1,0:T(8,128)(2,1)} %get-tuple-element.64), channel_id=1, source_target_pairs={{0,16},{8,24},{16,0},{24,8},{1,17},{9,25},{17,1},{25,9},{2,18},{10... | collective-permute-start | bytes 1032200 | tf_op jit(solution)/shard_map/ppermute | solution.py:514
  72.5 1.5 %collective-permute-start.19 = (bf16[2,336,256]{2,1,0:T(8,128)(2,1)}, bf16[2,336,256]{2,1,0:T(8,128)(2,1)S(1)}, u32[]{:S(2)}, u32[]{:S(2)}) collective-permute-start(bf16[2,336,256]{2,1,0:T(8,128)(2,1)} %get-tuple-element.66), channel_id=1, source_target_pairs={{0,8},{8,0},{16,24},{24,16},{1,9},{9,1},{17,25},{25,17},{2,10},{10... | collective-permute-start | bytes 1032200 | tf_op jit(solution)/shard_map/ppermute | solution.py:514
  74.0 2.4 %collective-permute-start.12 = (bf16[2,64,512]{2,1,0:T(8,128)(2,1)S(1)}, bf16[2,64,512]{2,1,0:T(8,128)(2,1)S(1)}, u32[]{:S(2)}, u32[]{:S(2)}) collective-permute-start(bf16[2,64,512]{2,1,0:T(8,128)(2,1)S(1)} %get-tuple-element.76), channel_id=1, source_target_pairs={{1,0},{2,1},{3,2},{0,3},{5,4},{6,5},{7,6},{4,7},{9,8},{10,9},{11,1... | collective-permute-start | bytes 393224 | tf_op jit(solution)/shard_map/ppermute | solution.py:616
  77.4 4.0 %collective-permute-done.14 = bf16[2,336,256]{2,1,0:T(8,128)(2,1)S(1)} collective-permute-done((bf16[2,336,256]{2,1,0:T(8,128)(2,1)}, bf16[2,336,256]{2,1,0:T(8,128)(2,1)S(1)}, u32[]{:S(2)}, u32[]{:S(2)}) %collective-permute-start.14) | collective-permute-done | bytes 344096 | tf_op jit(solution)/shard_map/ppermute | solution.py:514
  81.6 2.2 %collective-permute-start.15 = (bf16[336,256]{1,0:T(8,128)(2,1)S(1)}, bf16[336,256]{1,0:T(8,128)(2,1)S(1)}, u32[]{:S(2)}, u32[]{:S(2)}) collective-permute-start(bf16[336,256]{1,0:T(8,128)(2,1)S(1)} %fusion.12), channel_id=1, source_target_pairs={{0,8},{8,0},{16,24},{24,16},{1,9},{9,1},{17,25},{25,17},{2,10},{10... | collective-permute-start | bytes 516104 | tf_op jit(solution)/shard_map/ppermute | solution.py:514
  83.9 1.6 %collective-permute-start.20 = (bf16[336,256]{1,0:T(8,128)(2,1)S(1)}, bf16[336,256]{1,0:T(8,128)(2,1)S(1)}, u32[]{:S(2)}, u32[]{:S(2)}) collective-permute-start(bf16[336,256]{1,0:T(8,128)(2,1)S(1)} %fusion.13), channel_id=1, source_target_pairs={{0,16},{8,24},{16,0},{24,8},{1,17},{9,25},{17,1},{25,9},{2,18},{10... | collective-permute-start | bytes 516104 | tf_op jit(solution)/shard_map/ppermute | solution.py:514
  85.5 3.1 %collective-permute-done.24 = bf16[2,336,256]{2,1,0:T(8,128)(2,1)S(1)} collective-permute-done((bf16[2,336,256]{2,1,0:T(8,128)(2,1)S(1)}, bf16[2,336,256]{2,1,0:T(8,128)(2,1)S(1)}, u32[]{:S(2)}, u32[]{:S(2)}) %collective-permute-start.24) | collective-permute-done | bytes 344096 | tf_op jit(solution)/shard_map/ppermute | solution.py:514
  88.7 2.1 %collective-permute-start.25 = (bf16[336,256]{1,0:T(8,128)(2,1)S(1)}, bf16[336,256]{1,0:T(8,128)(2,1)S(1)}, u32[]{:S(2)}, u32[]{:S(2)}) collective-permute-start(bf16[336,256]{1,0:T(8,128)(2,1)S(1)} %fusion.14), channel_id=1, source_target_pairs={{0,8},{8,0},{16,24},{24,16},{1,9},{9,1},{17,25},{25,17},{2,10},{10... | collective-permute-start | bytes 516104 | tf_op jit(solution)/shard_map/ppermute | solution.py:514
  91.0 1.6 %collective-permute-start.30 = (bf16[336,256]{1,0:T(8,128)(2,1)S(1)}, bf16[336,256]{1,0:T(8,128)(2,1)S(1)}, u32[]{:S(2)}, u32[]{:S(2)}) collective-permute-start(bf16[336,256]{1,0:T(8,128)(2,1)S(1)} %fusion.15), channel_id=1, source_target_pairs={{0,16},{8,24},{16,0},{24,8},{1,17},{9,25},{17,1},{25,9},{2,18},{10... | collective-permute-start | bytes 516104 | tf_op jit(solution)/shard_map/ppermute | solution.py:514
  92.7 1.6 %collective-permute-start.16 = (bf16[336,128]{1,0:T(8,128)(2,1)S(1)}, bf16[336,128]{1,0:T(8,128)(2,1)S(1)}, u32[]{:S(2)}, u32[]{:S(2)}) collective-permute-start(bf16[336,128]{1,0:T(8,128)(2,1)S(1)} %select_convert_fusion.3), channel_id=1, source_target_pairs={{0,1},{1,0},{2,3},{3,2},{4,5},{5,4},{6,7},{7,6},{8,9},{9,8},{10,11... | collective-permute-start | bytes 258056 | tf_op jit(solution)/shard_map/ppermute | solution.py:514
  95.0 1.6 %collective-permute-start.26 = (bf16[336,128]{1,0:T(8,128)(2,1)S(1)}, bf16[336,128]{1,0:T(8,128)(2,1)S(1)}, u32[]{:S(2)}, u32[]{:S(2)}) collective-permute-start(bf16[336,128]{1,0:T(8,128)(2,1)S(1)} %select_convert_fusion.1), channel_id=1, source_target_pairs={{0,1},{1,0},{2,3},{3,2},{4,5},{5,4},{6,7},{7,6},{8,9},{9,8},{10,11... | collective-permute-start | bytes 258056 | tf_op jit(solution)/shard_map/ppermute | solution.py:514
  96.8 1.5 %collective-permute-start.31 = (bf16[336,128]{1,0:T(8,128)(2,1)S(1)}, bf16[336,128]{1,0:T(8,128)(2,1)S(1)}, u32[]{:S(2)}, u32[]{:S(2)}) collective-permute-start(bf16[336,128]{1,0:T(8,128)(2,1)S(1)} %select_convert_fusion), channel_id=1, source_target_pairs={{0,1},{1,0},{2,3},{3,2},{4,5},{5,4},{6,7},{7,6},{8,9},{9,8},{10,11... | collective-permute-start | bytes 258056 | tf_op jit(solution)/shard_map/ppermute | solution.py:514
  98.3 2.6 %collective-permute-start.17 = (bf16[336,128]{1,0:T(8,128)(2,1)S(1)}, bf16[336,128]{1,0:T(8,128)(2,1)S(1)}, u32[]{:S(2)}, u32[]{:S(2)}) collective-permute-start(bf16[336,128]{1,0:T(8,128)(2,1)S(1)} %add_convert_fusion.7), channel_id=1, source_target_pairs={{0,2},{1,3},{2,0},{3,1},{4,6},{5,7},{6,4},{7,5},{8,10},{9,11},{10,... | collective-permute-start | bytes 258056 | tf_op jit(solution)/shard_map/ppermute | solution.py:514
  100.9 1.8 %collective-permute-start.22 = (bf16[336,128]{1,0:T(8,128)(2,1)S(1)}, bf16[336,128]{1,0:T(8,128)(2,1)S(1)}, u32[]{:S(2)}, u32[]{:S(2)}) collective-permute-start(bf16[336,128]{1,0:T(8,128)(2,1)S(1)} %add_convert_fusion.5), channel_id=1, source_target_pairs={{0,2},{1,3},{2,0},{3,1},{4,6},{5,7},{6,4},{7,5},{8,10},{9,11},{10,... | collective-permute-start | bytes 258056 | tf_op jit(solution)/shard_map/ppermute | solution.py:514
  102.8 1.8 %collective-permute-start.27 = (bf16[336,128]{1,0:T(8,128)(2,1)S(1)}, bf16[336,128]{1,0:T(8,128)(2,1)S(1)}, u32[]{:S(2)}, u32[]{:S(2)}) collective-permute-start(bf16[336,128]{1,0:T(8,128)(2,1)S(1)} %add_convert_fusion.3), channel_id=1, source_target_pairs={{0,2},{1,3},{2,0},{3,1},{4,6},{5,7},{6,4},{7,5},{8,10},{9,11},{10,... | collective-permute-start | bytes 258056 | tf_op jit(solution)/shard_map/ppermute | solution.py:514
  104.6 0.9 collective-permute-done.31
  105.5 1.7 %collective-permute-start.32 = (bf16[336,128]{1,0:T(8,128)(2,1)S(1)}, bf16[336,128]{1,0:T(8,128)(2,1)S(1)}, u32[]{:S(2)}, u32[]{:S(2)}) collective-permute-start(bf16[336,128]{1,0:T(8,128)(2,1)S(1)} %add_convert_fusion.1), channel_id=1, source_target_pairs={{0,2},{1,3},{2,0},{3,1},{4,6},{5,7},{6,4},{7,5},{8,10},{9,11},{10,... | collective-permute-start | bytes 258056 | tf_op jit(solution)/shard_map/ppermute | solution.py:514
  107.3 2.7 %collective-permute-start.18 = (bf16[336,128]{1,0:T(8,128)(2,1)S(1)}, bf16[336,128]{1,0:T(8,128)(2,1)S(1)}, u32[]{:S(2)}, u32[]{:S(2)}) collective-permute-start(bf16[336,128]{1,0:T(8,128)(2,1)S(1)} %add_convert_fusion.6.refs_0_), channel_id=1, source_target_pairs={{0,1},{1,0},{2,3},{3,2},{4,5},{5,4},{6,7},{7,6},{8,9},{9,8},{10,11... | collective-permute-start | bytes 258056 | tf_op jit(solution)/shard_map/ppermute | solution.py:514
  110.0 0.9 collective-permute-start.35
  110.9 1.7 %collective-permute-start.34 = (bf16[128,256]{1,0:T(8,128)(2,1)S(1)}, bf16[128,256]{1,0:T(8,128)(2,1)S(1)}, u32[]{:S(2)}, u32[]{:S(2)}) collective-permute-start(bf16[128,256]{1,0:T(8,128)(2,1)S(1)} %pad_maximum_fusion.1), channel_id=1, source_target_pairs={{0,16},{8,24},{16,0},{24,8},{1,17},{9,25},{17,1},{25,9},{2,18},{10... | collective-permute-start | bytes 196616 | tf_op jit(solution)/shard_map/ppermute | solution.py:514
  112.7 1.1 collective-permute-start.28
  113.8 1.1 collective-permute-start.23
  115.4 1.0 collective-permute-start.33
  116.3 0.7 pad_maximum_fusion
  117.1 1.2 %collective-permute-done.23.refs_3_ = bf16[336,128]{1,0:T(8,128)(2,1)S(1)} collective-permute-done((bf16[336,128]{1,0:T(8,128)(2,1)S(1)}, bf16[336,128]{1,0:T(8,128)(2,1)S(1)}, u32[]{:S(2)}, u32[]{:S(2)}) %collective-permute-start.23) | collective-permute-done | bytes 86048 | tf_op jit(solution)/shard_map/ppermute | solution.py:514
  118.3 1.5 %collective-permute-done.33.refs_7_ = bf16[336,128]{1,0:T(8,128)(2,1)S(1)} collective-permute-done((bf16[336,128]{1,0:T(8,128)(2,1)S(1)}, bf16[336,128]{1,0:T(8,128)(2,1)S(1)}, u32[]{:S(2)}, u32[]{:S(2)}) %collective-permute-start.33) | collective-permute-done | bytes 86048 | tf_op jit(solution)/shard_map/ppermute | solution.py:514
  120.5 2.4 %unpack.1 = (f32[1,256,512]{2,1,0:T(8,128)}, f32[1,128,1536]{2,1,0:T(8,128)}, f32[1,128,512]{2,1,0:T(8,128)}, f32[1,128]{1,0:T(1,128)}) custom-call(bf16[336,128]{1,0:T(8,128)(2,1)} %copy-done.16, bf16[336,128]{1,0:T(8,128)(2,1)} %copy-done.23, bf16[336,128]{1,0:T(8,128)(2,1)} %copy-done.19, bf16[336,128]{1,0:T(8,128)(2,1)} %copy-done.25, ...), custom_call_target="tpu_custom_call" | custom-call | tf_op jit(solution)/shard_map/unpack/pallas_call | solution.py:658
  (125 shorter events, 8.1 us)
Async XLA Ops:
  0.6 14.7 %copy-start = (bf16[1,128,1536]{2,1,0:T(8,128)(2,1)S(1)}, bf16[1,128,1536]{2,1,0:T(8,128)(2,1)}, u32[]{:S(2)}) copy-start(bf16[1,128,1536]{2,1,0:T(8,128)(2,1)} %param.10) | copy-start | bytes 1179652
  0.6 15.3 %collective-permute-start.6 = (bf16[128,1536]{1,0:T(8,128)(2,1)}, bf16[128,1536]{1,0:T(8,128)(2,1)S(1)}, u32[]{:S(2)}, u32[]{:S(2)}) collective-permute-start(bf16[128,1536]{1,0:T(8,128)(2,1)} %bitcast.40), channel_id=1, source_target_pairs={{0,16},{8,24},{16,0},{24,8},{1,17},{9,25},{17,1},{25,9},{2,18},{10... | collective-permute-start | bytes 1179656 | tf_op jit(solution)/shard_map/ppermute | solution.py:514
  3.7 4.8 %copy-start.8 = (bf16[1,256,512]{2,1,0:T(8,128)(2,1)S(1)}, bf16[1,256,512]{2,1,0:T(8,128)(2,1)}, u32[]{:S(2)}) copy-start(bf16[1,256,512]{2,1,0:T(8,128)(2,1)} %param.9) | copy-start | bytes 786436
  4.7 12.7 %collective-permute-start.1 = (bf16[2,4,16,512]{3,2,1,0:T(8,128)(2,1)S(1)}, bf16[2,4,16,512]{3,2,1,0:T(8,128)(2,1)S(1)}, u32[]{:S(2)}, u32[]{:S(2)}) collective-permute-start(bf16[2,4,16,512]{3,2,1,0:T(8,128)(2,1)S(1)} %select_bitcast_fusion), channel_id=1, source_target_pairs={{0,1},{1,2},{2,3},{3,0},{4,5},{5,6},{6,7},{7,4},{8,9},{9,10},{10,1... | collective-permute-start | bytes 393224 | tf_op jit(solution)/shard_map/ppermute | solution.py:563
  6.4 3.6 %copy-start.29 = (s32[1,2,8,16]{3,2,1,0:T(8,128)S(1)}, s32[1,2,8,16]{3,2,1,0:T(8,128)}, u32[]{:S(2)}) copy-start(s32[1,2,8,16]{3,2,1,0:T(8,128)} %param.8) | copy-start | bytes 3076
  8.0 10.0 %collective-permute-start.9 = (bf16[144,512]{1,0:T(8,128)(2,1)}, bf16[144,512]{1,0:T(8,128)(2,1)S(1)}, u32[]{:S(2)}, u32[]{:S(2)}) collective-permute-start(bf16[144,512]{1,0:T(8,128)(2,1)} %pack.1.refs_11_.refs_12_), channel_id=1, source_target_pairs={{0,16},{8,24},{16,0},{24,8},{1,17},{9,25},{17,1},{25,9},{2,18},{10... | collective-permute-start | bytes 442376 | tf_op jit(solution)/shard_map/ppermute | solution.py:514
  8.5 11.0 %collective-permute-start.2 = (bf16[256,512]{1,0:T(8,128)(2,1)S(1)}, bf16[256,512]{1,0:T(8,128)(2,1)S(1)}, u32[]{:S(2)}, u32[]{:S(2)}) collective-permute-start(bf16[256,512]{1,0:T(8,128)(2,1)S(1)} %bitcast.48), channel_id=1, source_target_pairs={{0,8},{8,0},{16,24},{24,16},{1,9},{9,1},{17,25},{25,17},{2,10},{10... | collective-permute-start | bytes 786440 | tf_op jit(solution)/shard_map/ppermute | solution.py:514
  10.0 5.4 %collective-permute-start = (s32[2,4,16]{2,1,0:T(4,128)S(1)}, s32[2,4,16]{2,1,0:T(4,128)S(1)}, u32[]{:S(2)}, u32[]{:S(2)}) collective-permute-start(s32[2,4,16]{2,1,0:T(4,128)S(1)} %get-tuple-element.77), channel_id=1, source_target_pairs={{0,1},{1,2},{2,3},{3,0},{4,5},{5,6},{6,7},{7,4},{8,9},{9,10},{10,1... | collective-permute-start | bytes 1544 | tf_op jit(solution)/shard_map/ppermute | solution.py:565
  15.4 25.5 %collective-permute-start.5 = (bf16[128,1536]{1,0:T(8,128)(2,1)S(1)}, bf16[128,1536]{1,0:T(8,128)(2,1)S(1)}, u32[]{:S(2)}, u32[]{:S(2)}) collective-permute-start(bf16[128,1536]{1,0:T(8,128)(2,1)S(1)} %bitcast.44), channel_id=1, source_target_pairs={{0,8},{8,0},{16,24},{24,16},{1,9},{9,1},{17,25},{25,17},{2,10},{10... | collective-permute-start | bytes 1179656 | tf_op jit(solution)/shard_map/ppermute | solution.py:514
  15.9 25.0 %copy-start.1 = (bf16[128,1536]{1,0:T(8,128)(2,1)}, bf16[128,1536]{1,0:T(8,128)(2,1)S(1)}, u32[]{:S(2)}) copy-start(bf16[128,1536]{1,0:T(8,128)(2,1)S(1)} %collective-permute-done.6.refs_9_.refs_10_) | copy-start | bytes 1179652
  15.9 24.9 %collective-permute-start.7 = (bf16[128,1536]{1,0:T(8,128)(2,1)S(1)}, bf16[128,1536]{1,0:T(8,128)(2,1)S(1)}, u32[]{:S(2)}, u32[]{:S(2)}) collective-permute-start(bf16[128,1536]{1,0:T(8,128)(2,1)S(1)} %collective-permute-done.6.refs_9_.refs_10_), channel_id=1, source_target_pairs={{0,8},{8,0},{16,24},{24,16},{1,9},{9,1},{17,25},{25,17},{2,10},{10... | collective-permute-start | bytes 1179656 | tf_op jit(solution)/shard_map/ppermute | solution.py:514
  17.4 23.5 %copy-start.15 = (bf16[2,4,16,512]{3,2,1,0:T(8,128)(2,1)}, bf16[2,4,16,512]{3,2,1,0:T(8,128)(2,1)S(1)}, u32[]{:S(2)}) copy-start(bf16[2,4,16,512]{3,2,1,0:T(8,128)(2,1)S(1)} %collective-permute-done.1) | copy-start | bytes 393220
  17.4 18.3 %collective-permute-start.8 = (bf16[144,512]{1,0:T(8,128)(2,1)}, bf16[144,512]{1,0:T(8,128)(2,1)S(1)}, u32[]{:S(2)}, u32[]{:S(2)}) collective-permute-start(bf16[144,512]{1,0:T(8,128)(2,1)} %pack.1.refs_11_.refs_12_), channel_id=1, source_target_pairs={{0,8},{8,0},{16,24},{24,16},{1,9},{9,1},{17,25},{25,17},{2,10},{10... | collective-permute-start | bytes 442376 | tf_op jit(solution)/shard_map/ppermute | solution.py:514
  18.0 22.9 %copy-start.12 = (bf16[144,512]{1,0:T(8,128)(2,1)}, bf16[144,512]{1,0:T(8,128)(2,1)S(1)}, u32[]{:S(2)}) copy-start(bf16[144,512]{1,0:T(8,128)(2,1)S(1)} %collective-permute-done.9.refs_13_.refs_14_) | copy-start | bytes 442372
  18.0 19.9 %collective-permute-start.3 = (bf16[256,512]{1,0:T(8,128)(2,1)S(1)}, bf16[256,512]{1,0:T(8,128)(2,1)S(1)}, u32[]{:S(2)}, u32[]{:S(2)}) collective-permute-start(bf16[256,512]{1,0:T(8,128)(2,1)S(1)} %bitcast.49), channel_id=1, source_target_pairs={{0,16},{8,24},{16,0},{24,8},{1,17},{9,25},{17,1},{25,9},{2,18},{10... | collective-permute-start | bytes 786440 | tf_op jit(solution)/shard_map/ppermute | solution.py:514
  19.5 21.4 %copy-start.9 = (bf16[256,512]{1,0:T(8,128)(2,1)}, bf16[256,512]{1,0:T(8,128)(2,1)S(1)}, u32[]{:S(2)}) copy-start(bf16[256,512]{1,0:T(8,128)(2,1)S(1)} %collective-permute-done.2.refs_4_.refs_5_) | copy-start | bytes 786436
  19.5 21.4 %collective-permute-start.4 = (bf16[256,512]{1,0:T(8,128)(2,1)S(1)}, bf16[256,512]{1,0:T(8,128)(2,1)S(1)}, u32[]{:S(2)}, u32[]{:S(2)}) collective-permute-start(bf16[256,512]{1,0:T(8,128)(2,1)S(1)} %collective-permute-done.2.refs_4_.refs_5_), channel_id=1, source_target_pairs={{0,16},{8,24},{16,0},{24,8},{1,17},{9,25},{17,1},{25,9},{2,18},{10... | collective-permute-start | bytes 786440 | tf_op jit(solution)/shard_map/ppermute | solution.py:514
  35.7 5.2 %copy-start.13 = (bf16[144,512]{1,0:T(8,128)(2,1)}, bf16[144,512]{1,0:T(8,128)(2,1)S(1)}, u32[]{:S(2)}) copy-start(bf16[144,512]{1,0:T(8,128)(2,1)S(1)} %collective-permute-done.8.refs_12_.refs_13_) | copy-start | bytes 442372
  35.7 5.1 %collective-permute-start.10 = (bf16[144,512]{1,0:T(8,128)(2,1)S(1)}, bf16[144,512]{1,0:T(8,128)(2,1)S(1)}, u32[]{:S(2)}, u32[]{:S(2)}) collective-permute-start(bf16[144,512]{1,0:T(8,128)(2,1)S(1)} %collective-permute-done.8.refs_12_.refs_13_), channel_id=1, source_target_pairs={{0,16},{8,24},{16,0},{24,8},{1,17},{9,25},{17,1},{25,9},{2,18},{10... | collective-permute-start | bytes 442376 | tf_op jit(solution)/shard_map/ppermute | solution.py:514
  48.0 2.7 %collective-permute-start.11 = (bf16[256,512]{1,0:T(8,128)(2,1)}, bf16[256,512]{1,0:T(8,128)(2,1)S(1)}, u32[]{:S(2)}, u32[]{:S(2)}) collective-permute-start(bf16[256,512]{1,0:T(8,128)(2,1)} %get-tuple-element.40.refs_16_), channel_id=1, source_target_pairs={{0,4},{1,5},{2,6},{3,7},{8,12},{9,13},{10,14},{11,15},{16,20},{17,... | collective-permute-start | bytes 786440 | tf_op jit(solution)/shard_map/ppermute | solution.py:593
  52.5 10.1 %collective-permute-start.13 = (bf16[256,512]{1,0:T(8,128)(2,1)}, bf16[256,512]{1,0:T(8,128)(2,1)S(1)}, u32[]{:S(2)}, u32[]{:S(2)}) collective-permute-start(bf16[256,512]{1,0:T(8,128)(2,1)} %get-tuple-element.42), channel_id=1, source_target_pairs={{4,0},{5,1},{6,2},{7,3},{12,8},{13,9},{14,10},{15,11},{20,16},{21,... | collective-permute-start | bytes 786440 | tf_op jit(solution)/shard_map/ppermute | solution.py:604
  63.3 10.6 %copy-start.22 = (bf16[256,512]{1,0:T(8,128)(2,1)S(1)}, bf16[256,512]{1,0:T(8,128)(2,1)}, u32[]{:S(2)}) copy-start(bf16[256,512]{1,0:T(8,128)(2,1)} %get-tuple-element.41) | copy-start | bytes 786436
  70.9 5.5 %copy-start.18 = (bf16[2,336,256]{2,1,0:T(8,128)(2,1)S(1)}, bf16[2,336,256]{2,1,0:T(8,128)(2,1)}, u32[]{:S(2)}) copy-start(bf16[2,336,256]{2,1,0:T(8,128)(2,1)} %get-tuple-element.68) | copy-start | bytes 1032196
  70.9 10.6 %collective-permute-start.14 = (bf16[2,336,256]{2,1,0:T(8,128)(2,1)}, bf16[2,336,256]{2,1,0:T(8,128)(2,1)S(1)}, u32[]{:S(2)}, u32[]{:S(2)}) collective-permute-start(bf16[2,336,256]{2,1,0:T(8,128)(2,1)} %get-tuple-element.64), channel_id=1, source_target_pairs={{0,16},{8,24},{16,0},{24,8},{1,17},{9,25},{17,1},{25,9},{2,18},{10... | collective-permute-start | bytes 1032200 | tf_op jit(solution)/shard_map/ppermute | solution.py:514
  72.5 11.3 %collective-permute-start.19 = (bf16[2,336,256]{2,1,0:T(8,128)(2,1)}, bf16[2,336,256]{2,1,0:T(8,128)(2,1)S(1)}, u32[]{:S(2)}, u32[]{:S(2)}) collective-permute-start(bf16[2,336,256]{2,1,0:T(8,128)(2,1)} %get-tuple-element.66), channel_id=1, source_target_pairs={{0,8},{8,0},{16,24},{24,16},{1,9},{9,1},{17,25},{25,17},{2,10},{10... | collective-permute-start | bytes 1032200 | tf_op jit(solution)/shard_map/ppermute | solution.py:514
  74.0 39.8 %collective-permute-start.12 = (bf16[2,64,512]{2,1,0:T(8,128)(2,1)S(1)}, bf16[2,64,512]{2,1,0:T(8,128)(2,1)S(1)}, u32[]{:S(2)}, u32[]{:S(2)}) collective-permute-start(bf16[2,64,512]{2,1,0:T(8,128)(2,1)S(1)} %get-tuple-element.76), channel_id=1, source_target_pairs={{1,0},{2,1},{3,2},{0,3},{5,4},{6,5},{7,6},{4,7},{9,8},{10,9},{11,1... | collective-permute-start | bytes 393224 | tf_op jit(solution)/shard_map/ppermute | solution.py:616
  76.3 12.3 %collective-permute-start.24 = (bf16[2,336,256]{2,1,0:T(8,128)(2,1)S(1)}, bf16[2,336,256]{2,1,0:T(8,128)(2,1)S(1)}, u32[]{:S(2)}, u32[]{:S(2)}) collective-permute-start(bf16[2,336,256]{2,1,0:T(8,128)(2,1)S(1)} %copy-done.18), channel_id=1, source_target_pairs={{0,16},{8,24},{16,0},{24,8},{1,17},{9,25},{17,1},{25,9},{2,18},{10... | collective-permute-start | bytes 1032200 | tf_op jit(solution)/shard_map/ppermute | solution.py:514
  76.8 4.7 %copy-start.4 = (bf16[2,336,256]{2,1,0:T(8,128)(2,1)S(1)}, bf16[2,336,256]{2,1,0:T(8,128)(2,1)}, u32[]{:S(2)}) copy-start(bf16[2,336,256]{2,1,0:T(8,128)(2,1)} %get-tuple-element.63) | copy-start | bytes 1032196
  76.9 14.0 %collective-permute-start.29 = (bf16[2,336,256]{2,1,0:T(8,128)(2,1)}, bf16[2,336,256]{2,1,0:T(8,128)(2,1)S(1)}, u32[]{:S(2)}, u32[]{:S(2)}) collective-permute-start(bf16[2,336,256]{2,1,0:T(8,128)(2,1)} %get-tuple-element.70), channel_id=1, source_target_pairs={{0,8},{8,0},{16,24},{24,16},{1,9},{9,1},{17,25},{25,17},{2,10},{10... | collective-permute-start | bytes 1032200 | tf_op jit(solution)/shard_map/ppermute | solution.py:514
  81.6 11.0 %collective-permute-start.15 = (bf16[336,256]{1,0:T(8,128)(2,1)S(1)}, bf16[336,256]{1,0:T(8,128)(2,1)S(1)}, u32[]{:S(2)}, u32[]{:S(2)}) collective-permute-start(bf16[336,256]{1,0:T(8,128)(2,1)S(1)} %fusion.12), channel_id=1, source_target_pairs={{0,8},{8,0},{16,24},{24,16},{1,9},{9,1},{17,25},{25,17},{2,10},{10... | collective-permute-start | bytes 516104 | tf_op jit(solution)/shard_map/ppermute | solution.py:514
  83.9 4.8 %copy-start.6 = (bf16[2,336,256]{2,1,0:T(8,128)(2,1)S(1)}, bf16[2,336,256]{2,1,0:T(8,128)(2,1)}, u32[]{:S(2)}) copy-start(bf16[2,336,256]{2,1,0:T(8,128)(2,1)} %get-tuple-element.67) | copy-start | bytes 1032196
  83.9 10.5 %collective-permute-start.20 = (bf16[336,256]{1,0:T(8,128)(2,1)S(1)}, bf16[336,256]{1,0:T(8,128)(2,1)S(1)}, u32[]{:S(2)}, u32[]{:S(2)}) collective-permute-start(bf16[336,256]{1,0:T(8,128)(2,1)S(1)} %fusion.13), channel_id=1, source_target_pairs={{0,16},{8,24},{16,0},{24,8},{1,17},{9,25},{17,1},{25,9},{2,18},{10... | collective-permute-start | bytes 516104 | tf_op jit(solution)/shard_map/ppermute | solution.py:514
  88.7 6.2 %collective-permute-start.25 = (bf16[336,256]{1,0:T(8,128)(2,1)S(1)}, bf16[336,256]{1,0:T(8,128)(2,1)S(1)}, u32[]{:S(2)}, u32[]{:S(2)}) collective-permute-start(bf16[336,256]{1,0:T(8,128)(2,1)S(1)} %fusion.14), channel_id=1, source_target_pairs={{0,8},{8,0},{16,24},{24,16},{1,9},{9,1},{17,25},{25,17},{2,10},{10... | collective-permute-start | bytes 516104 | tf_op jit(solution)/shard_map/ppermute | solution.py:514
  91.0 5.7 %collective-permute-start.30 = (bf16[336,256]{1,0:T(8,128)(2,1)S(1)}, bf16[336,256]{1,0:T(8,128)(2,1)S(1)}, u32[]{:S(2)}, u32[]{:S(2)}) collective-permute-start(bf16[336,256]{1,0:T(8,128)(2,1)S(1)} %fusion.15), channel_id=1, source_target_pairs={{0,16},{8,24},{16,0},{24,8},{1,17},{9,25},{17,1},{25,9},{2,18},{10... | collective-permute-start | bytes 516104 | tf_op jit(solution)/shard_map/ppermute | solution.py:514
  92.7 5.5 %collective-permute-start.16 = (bf16[336,128]{1,0:T(8,128)(2,1)S(1)}, bf16[336,128]{1,0:T(8,128)(2,1)S(1)}, u32[]{:S(2)}, u32[]{:S(2)}) collective-permute-start(bf16[336,128]{1,0:T(8,128)(2,1)S(1)} %select_convert_fusion.3), channel_id=1, source_target_pairs={{0,1},{1,0},{2,3},{3,2},{4,5},{5,4},{6,7},{7,6},{8,9},{9,8},{10,11... | collective-permute-start | bytes 258056 | tf_op jit(solution)/shard_map/ppermute | solution.py:514
  94.4 6.4 %collective-permute-start.21 = (bf16[336,128]{1,0:T(8,128)(2,1)S(1)}, bf16[336,128]{1,0:T(8,128)(2,1)S(1)}, u32[]{:S(2)}, u32[]{:S(2)}) collective-permute-start(bf16[336,128]{1,0:T(8,128)(2,1)S(1)} %select_convert_fusion.2), channel_id=1, source_target_pairs={{0,1},{1,0},{2,3},{3,2},{4,5},{5,4},{6,7},{7,6},{8,9},{9,8},{10,11... | collective-permute-start | bytes 258056 | tf_op jit(solution)/shard_map/ppermute | solution.py:514
  95.0 7.7 %collective-permute-start.26 = (bf16[336,128]{1,0:T(8,128)(2,1)S(1)}, bf16[336,128]{1,0:T(8,128)(2,1)S(1)}, u32[]{:S(2)}, u32[]{:S(2)}) collective-permute-start(bf16[336,128]{1,0:T(8,128)(2,1)S(1)} %select_convert_fusion.1), channel_id=1, source_target_pairs={{0,1},{1,0},{2,3},{3,2},{4,5},{5,4},{6,7},{7,6},{8,9},{9,8},{10,11... | collective-permute-start | bytes 258056 | tf_op jit(solution)/shard_map/ppermute | solution.py:514
  96.8 8.7 %collective-permute-start.31 = (bf16[336,128]{1,0:T(8,128)(2,1)S(1)}, bf16[336,128]{1,0:T(8,128)(2,1)S(1)}, u32[]{:S(2)}, u32[]{:S(2)}) collective-permute-start(bf16[336,128]{1,0:T(8,128)(2,1)S(1)} %select_convert_fusion), channel_id=1, source_target_pairs={{0,1},{1,0},{2,3},{3,2},{4,5},{5,4},{6,7},{7,6},{8,9},{9,8},{10,11... | collective-permute-start | bytes 258056 | tf_op jit(solution)/shard_map/ppermute | solution.py:514
  98.3 8.9 %collective-permute-start.17 = (bf16[336,128]{1,0:T(8,128)(2,1)S(1)}, bf16[336,128]{1,0:T(8,128)(2,1)S(1)}, u32[]{:S(2)}, u32[]{:S(2)}) collective-permute-start(bf16[336,128]{1,0:T(8,128)(2,1)S(1)} %add_convert_fusion.7), channel_id=1, source_target_pairs={{0,2},{1,3},{2,0},{3,1},{4,6},{5,7},{6,4},{7,5},{8,10},{9,11},{10,... | collective-permute-start | bytes 258056 | tf_op jit(solution)/shard_map/ppermute | solution.py:514
  100.9 10.0 %collective-permute-start.22 = (bf16[336,128]{1,0:T(8,128)(2,1)S(1)}, bf16[336,128]{1,0:T(8,128)(2,1)S(1)}, u32[]{:S(2)}, u32[]{:S(2)}) collective-permute-start(bf16[336,128]{1,0:T(8,128)(2,1)S(1)} %add_convert_fusion.5), channel_id=1, source_target_pairs={{0,2},{1,3},{2,0},{3,1},{4,6},{5,7},{6,4},{7,5},{8,10},{9,11},{10,... | collective-permute-start | bytes 258056 | tf_op jit(solution)/shard_map/ppermute | solution.py:514
  102.8 7.2 %collective-permute-start.27 = (bf16[336,128]{1,0:T(8,128)(2,1)S(1)}, bf16[336,128]{1,0:T(8,128)(2,1)S(1)}, u32[]{:S(2)}, u32[]{:S(2)}) collective-permute-start(bf16[336,128]{1,0:T(8,128)(2,1)S(1)} %add_convert_fusion.3), channel_id=1, source_target_pairs={{0,2},{1,3},{2,0},{3,1},{4,6},{5,7},{6,4},{7,5},{8,10},{9,11},{10,... | collective-permute-start | bytes 258056 | tf_op jit(solution)/shard_map/ppermute | solution.py:514
  105.5 7.2 %collective-permute-start.32 = (bf16[336,128]{1,0:T(8,128)(2,1)S(1)}, bf16[336,128]{1,0:T(8,128)(2,1)S(1)}, u32[]{:S(2)}, u32[]{:S(2)}) collective-permute-start(bf16[336,128]{1,0:T(8,128)(2,1)S(1)} %add_convert_fusion.1), channel_id=1, source_target_pairs={{0,2},{1,3},{2,0},{3,1},{4,6},{5,7},{6,4},{7,5},{8,10},{9,11},{10,... | collective-permute-start | bytes 258056 | tf_op jit(solution)/shard_map/ppermute | solution.py:514
  107.3 9.8 %collective-permute-start.18 = (bf16[336,128]{1,0:T(8,128)(2,1)S(1)}, bf16[336,128]{1,0:T(8,128)(2,1)S(1)}, u32[]{:S(2)}, u32[]{:S(2)}) collective-permute-start(bf16[336,128]{1,0:T(8,128)(2,1)S(1)} %add_convert_fusion.6.refs_0_), channel_id=1, source_target_pairs={{0,1},{1,0},{2,3},{3,2},{4,5},{5,4},{6,7},{7,6},{8,9},{9,8},{10,11... | collective-permute-start | bytes 258056 | tf_op jit(solution)/shard_map/ppermute | solution.py:514
  110.0 5.3 %collective-permute-start.35 = (bf16[128,256]{1,0:T(8,128)(2,1)S(1)}, bf16[128,256]{1,0:T(8,128)(2,1)S(1)}, u32[]{:S(2)}, u32[]{:S(2)}) collective-permute-start(bf16[128,256]{1,0:T(8,128)(2,1)S(1)} %pad_maximum_fusion.1), channel_id=1, source_target_pairs={{0,17},{1,16},{2,19},{3,18},{8,25},{9,24},{10,27},{11,26},{16,1},{... | collective-permute-start | bytes 196616 | tf_op jit(solution)/shard_map/ppermute | solution.py:657
  110.9 6.1 %collective-permute-start.34 = (bf16[128,256]{1,0:T(8,128)(2,1)S(1)}, bf16[128,256]{1,0:T(8,128)(2,1)S(1)}, u32[]{:S(2)}, u32[]{:S(2)}) collective-permute-start(bf16[128,256]{1,0:T(8,128)(2,1)S(1)} %pad_maximum_fusion.1), channel_id=1, source_target_pairs={{0,16},{8,24},{16,0},{24,8},{1,17},{9,25},{17,1},{25,9},{2,18},{10... | collective-permute-start | bytes 196616 | tf_op jit(solution)/shard_map/ppermute | solution.py:514
  112.7 5.7 %collective-permute-start.28 = (bf16[336,128]{1,0:T(8,128)(2,1)S(1)}, bf16[336,128]{1,0:T(8,128)(2,1)S(1)}, u32[]{:S(2)}, u32[]{:S(2)}) collective-permute-start(bf16[336,128]{1,0:T(8,128)(2,1)S(1)} %add_convert_fusion.2.refs_4_), channel_id=1, source_target_pairs={{0,1},{1,0},{2,3},{3,2},{4,5},{5,4},{6,7},{7,6},{8,9},{9,8},{10,11... | collective-permute-start | bytes 258056 | tf_op jit(solution)/shard_map/ppermute | solution.py:514
  113.8 4.6 %collective-permute-start.23 = (bf16[336,128]{1,0:T(8,128)(2,1)S(1)}, bf16[336,128]{1,0:T(8,128)(2,1)S(1)}, u32[]{:S(2)}, u32[]{:S(2)}) collective-permute-start(bf16[336,128]{1,0:T(8,128)(2,1)S(1)} %add_convert_fusion.4.refs_2_), channel_id=1, source_target_pairs={{0,1},{1,0},{2,3},{3,2},{4,5},{5,4},{6,7},{7,6},{8,9},{9,8},{10,11... | collective-permute-start | bytes 258056 | tf_op jit(solution)/shard_map/ppermute | solution.py:514
  115.4 4.5 %collective-permute-start.33 = (bf16[336,128]{1,0:T(8,128)(2,1)S(1)}, bf16[336,128]{1,0:T(8,128)(2,1)S(1)}, u32[]{:S(2)}, u32[]{:S(2)}) collective-permute-start(bf16[336,128]{1,0:T(8,128)(2,1)S(1)} %add_convert_fusion.refs_6_), channel_id=1, source_target_pairs={{0,1},{1,0},{2,3},{3,2},{4,5},{5,4},{6,7},{7,6},{8,9},{9,8},{10,11... | collective-permute-start | bytes 258056 | tf_op jit(solution)/shard_map/ppermute | solution.py:514
  (19 other events, 33.1 us)

commit v6 on v5

--- a/solution.py
+++ b/solution.py
@@ -61,35 +61,31 @@
 
 def load_weights(copies, pieces, names, dst):
     me = lax.axis_index("dp")
-    shards = 4
+    shards = len(pieces) // 2
     started = {}
     for name in names:
         kind, column = WHERE[name]
-        arrays = pieces[kind]
+        arrays = pieces[:shards] if kind == "qkv" else pieces[shards:]
         started[name] = []
         for flip, ref in zip((0, 1, shards // 2, shards - 1), arrays):
+            owner = me ^ flip
             rows = dst[name].shape[0] // shards
-            at = pl.multiple_of((me ^ flip) * rows, rows)
+            if name == "merge":
+                owner = (owner % 2) * (shards // 2) + owner // 2
+            at = pl.multiple_of(owner * rows, rows)
             if kind == "rest":
-                base = 0 if name == "out" else ref.shape[0] - PAD
-                source = ref.at[pl.ds(base, rows)]
-            elif kind == "qkv":
+                source = ref.at[pl.ds(column * ((ref.shape[0] - PAD) // 2), rows)]
+            else:
                 width = dst[name].shape[1]
                 source = ref.at[:, pl.ds(column * width, width)]
-            else:
-                source = ref
             started[name].append(copies.start(source, dst[name].at[pl.ds(at, rows)]))
     return started
 
 
 WHERE = {
-    "merge": ("merge", 0), "q": ("qkv", 0), "k": ("qkv", 1), "v": ("qkv", 2),
-    "out": ("rest", 0), "gain": ("rest", 1),
+    "q": ("qkv", 0), "k": ("qkv", 1), "v": ("qkv", 2),
+    "merge": ("rest", 0), "out": ("rest", 1), "gain": ("rest", 2),
 }
-
-
-def pieces_of(refs):
-    return {"merge": refs[0:4], "qkv": refs[4:8], "rest": refs[8:12]}
 
 
 def load_tokens(copies, moved, own, dst):
@@ -215,8 +211,7 @@
 def forward(x, w, waits, gain_of, allowed, mask_shape, room, kept):
     feature = x.shape[1]
     wait_all(waits["merge"])
-    tokens = x[...]
-    update = dot(tokens, w["merge"][:feature]) + dot(tokens, w["merge"][feature:])
+    update = dot(x[...], w["merge"][...])
     normed, inverse = normalize(update)
     room["normed"][...] = normed
     kept("normed")
@@ -324,7 +319,7 @@
 
 def forward_kernel(*refs):
     mask_in, moved, own, *rest = refs
-    pieces, rest = rest[:12], rest[12:]
+    pieces, rest = rest[:8], rest[8:]
     y, rest = rest[0], rest[1:]
     saved, rest = dict(zip(RECORDS, rest)), rest[len(RECORDS) :]
     mask, x, wm, wq, wk, wv, wo, wg, y_s, *rest = rest
@@ -338,7 +333,7 @@
         mask_copy = copies.start(mask_in, mask)
         tokens = load_tokens(copies, moved, own, x)
         names = ("merge", "gain", "q", "k", "v", "out")
-        waits = load_weights(copies, pieces_of(pieces), names, w)
+        waits = load_weights(copies, pieces, names, w)
         mask_copy.wait()
         allowed = masks(mask, lax.axis_index("band") == 0, lon_of(mask.shape[1]))
         wait_all(tokens)
@@ -360,7 +355,7 @@
 
 def last_kernel(*refs):
     mask_in, moved, own, y0, *rest = refs
-    pieces, rest = rest[:12], rest[13:]
+    pieces, rest = rest[:8], rest[9:]
     y, g0, gain_out, g_out, hidden, mix, proj_out, update_out, *rest = rest
     mask, x, g, wm, wq, wk, wv, wo, wg, y_s, g_s, *rest = rest
     room, rest = dict(zip(RECORDS, rest)), rest[len(RECORDS) :]
@@ -369,13 +364,12 @@
     @role(1)
     def run():
         shards = wg.shape[0] // PAD
-        feature = x.shape[1]
         copies = Copies(sems)
         w = {"merge": wm, "q": wq, "k": wk, "v": wv, "out": wo, "gain": wg}
         mask_copy = copies.start(mask_in, mask)
         x_in = copies.start(y0, x)
         names = ("merge", "gain", "q", "k", "v", "out")
-        waits = load_weights(copies, pieces_of(pieces), names, w)
+        waits = load_weights(copies, pieces, names, w)
         tokens = load_tokens(copies, moved, own, g)
         mask_copy.wait()
         allowed = masks(mask, lax.axis_index("band") == 0, lon_of(mask.shape[1]))
@@ -400,9 +394,7 @@
         gain_s[...] = jnp.broadcast_to(grad_gain, gain_s.shape)
         update_s[...] = grad_update
         done += [copies.start(gain_s, gain_out), copies.start(update_s, update_out)]
-        chain = dot_nt(grad_update, wm[:feature]).astype(BF16).astype(F32)
-        side = dot_nt(grad_update, wm[feature:]).astype(BF16).astype(F32)
-        g_s[...] = (chain + side).astype(BF16)
+        g_s[...] = dot_nt(grad_update, wm[...]).astype(BF16)
         done.append(copies.start(g_s, g0))
         wait_all(done)
 
@@ -421,7 +413,7 @@
 
 def first_kernel(*refs):
     cells, moved, own, g0, *rest = refs
-    pieces, rest = rest[:12], rest[12:]
+    pieces, rest = rest[:8], rest[8:]
     saved, rest = rest[: len(RECORDS)], rest[len(RECORDS) :]
     skip = count = 4 * CHUNKS
     outs, rest = rest[skip : skip + count], rest[skip + count :]
@@ -437,7 +429,7 @@
         w = {"q": wq, "k": wk, "v": wv, "out": wo, "gain": wg}
         early = [copies.start(g0, g)]
         names = ("out", "q", "k", "v", "gain")
-        waits = load_weights(copies, pieces_of(pieces), names, w)
+        waits = load_weights(copies, pieces, names, w)
         early += [copies.start(a, b) for a, b in zip(saved, rooms)]
         early += load_tokens(copies, moved, own, x)
         wait_all(early)
@@ -449,11 +441,15 @@
                             (dw_first, dw_second), outs))
 
 
-def rest_kernel(out, gain, packed):
-    rows, width = gain.shape[1], out.shape[1]
-    packed[: out.shape[0], :] = out[...]
-    packed[out.shape[0] :, :] = jnp.zeros((PAD, width), BF16)
-    packed[out.shape[0] :, :rows] = jnp.broadcast_to(gain[...], (PAD, rows))
+def rest_kernel(merge, got, out, gain, packed):
+    size, width = out.shape
+    rows = gain.shape[1]
+    upper = lax.axis_index("dp") >= lax.axis_size("dp") // 2
+    kept = jnp.where(upper, merge[size:, :].astype(F32), merge[:size, :].astype(F32))
+    packed[:size, :] = (kept + got[...].astype(F32)).astype(BF16)
+    packed[size : 2 * size, :] = out[...]
+    packed[2 * size :, :] = jnp.zeros((PAD, width), BF16)
+    packed[2 * size :, :rows] = jnp.broadcast_to(gain[...], (PAD, rows))
 
 
 def final_kernel(*refs):
@@ -514,20 +510,17 @@
     return lax.ppermute(value, axis, [(i, i ^ bit) for i in range(size)])
 
 
-def gather(merge, qkv, rest):
+def gather(qkv, rest):
     high = lax.axis_size("dp") // 2
 
     def named(value, bit):
         return flip(value, "dp", bit)
 
-    merge_low, merge_high = named(merge, 1), named(merge, high)
     qkv_low, qkv_high = named(qkv, 1), named(qkv, high)
     rest_low, rest_high = named(rest, 1), named(rest, high)
-    merge_both = named(merge_low, high)
     qkv_both = named(qkv_high, 1)
     rest_both = named(rest_low, high)
-    return (merge, merge_low, merge_high, merge_both, qkv, qkv_low, qkv_high, qkv_both,
-            rest, rest_low, rest_high, rest_both)
+    return (qkv, qkv_low, qkv_high, qkv_both, rest, rest_low, rest_high, rest_both)
 
 
 def body(fields, cell_mask, merge_weight, qkv_weight, out_weight, norm_gain, out_cotangent):
@@ -547,14 +540,16 @@
         return pltpu.VMEM(dims, dtype)
 
     merge, qkv, out = merge_weight[0], qkv_weight[0], out_weight[0]
+    upper = lax.axis_index("dp") >= shards // 2
+    got = flip(jnp.where(upper, merge[:rows], merge[rows:]), "dp", shards // 2)
     rest = pl.pallas_call(
         rest_kernel,
-        out_shape=shape(rows + PAD, feature),
-        in_specs=[VMEM, VMEM],
+        out_shape=shape(2 * rows + PAD, feature),
+        in_specs=[VMEM] * 4,
         out_specs=VMEM,
         name="pack",
-    )(out, norm_gain)
-    pieces = gather(merge, qkv, rest)
+    )(merge, got, out, norm_gain)
+    pieces = gather(qkv, rest)
 
     down = [(i, (i + 1) % bands) for i in range(bands)]
     up = [(j, i) for i, j in down]
@@ -572,7 +567,7 @@
     wide = room(total, 3 * feature)
     mask_room = pltpu.VMEM((micro, cells), jnp.int32)
     weights = [square] * 4 + [room(shards * PAD, feature)]
-    merge_room = room(2 * feature, feature)
+    merge_room = square
     record_rooms = [
         room(total, feature, dtype=F32), room(total, 128, dtype=F32), tokens, wide, tokens,
         room(micro * HEADS // 2, 2 * cells, cells),
@@ -599,7 +594,7 @@
          wide_shape, token_shape],
         [mask_room, tokens, tokens, merge_room] + weights + [tokens, tokens] + record_rooms
         + [tokens, wide, gain_room, tokens] + sems,
-        {16: 0}, 13 * unit,
+        {12: 0}, 13 * unit,
     )
     g0 = lax.ppermute(g_out, "segment", [(1, 0)])
     shard_shapes = [shape(2, half, feature // CHUNKS)] * (4 * CHUNKS)

time: 123 us -> 126 us (1.024)
  starting transfers between devices: 52.6 us -> 55.2 us
    ppermute x1, waiting for transfers between devices: 0.01 us -> 4.52 us  [body(): moved = lax.ppermute(source, 'band', down)]
    ppermute x1, waiting for transfers between devices: 3.83 us -> 0.01 us  [body(): mask_moved = lax.ppermute(cell_mask[0, :, row_count - SH:], 'band', down)]
    ppermute x30 -> x28, starting transfers between devices: 43.5 us -> 45.5 us  [flip(): return lax.ppermute(value, axis, [(i, i ^ bit) for i in range(size)])]
    ppermute x1, starting transfers between devices: 2.37 us -> 3.83 us  [body(): back = lax.ppermute(y[:, :part], 'band', up)]
    ppermute x30 -> x28, waiting for transfers between devices: 29.6 us -> 28.3 us  [flip(): return lax.ppermute(value, axis, [(i, i ^ bit) for i in range(size)])]
    unnamed x62 -> x60, local copies, waits for them, and re-layouts: 3.08 us -> 3.48 us
  transfers between devices with their start and end apart: 36 -> 34, of which waited for: 11 -> 13; matrix products, arithmetic and copies ran while one was open for 3% -> 3% of each run, Pallas kernels for 2% -> 2%
where the time goes in v6:
time: 126 us; the launch traced here: 125 us
  starting transfers between devices  55.2 us (44%)
  waiting for transfers between devices  42.3 us (34%)
  Pallas kernels  20 us (16%)
  local copies, waits for them, and re-layouts  4.17 us (3%)
  other arithmetic  2.68 us (2%)
    ppermute x28, starting transfers between devices, flip(): return lax.ppermute(value, axis, [(i, i ^ bit) for i in range(size)])  45.5 us
    ppermute x28, waiting for transfers between devices, flip(): return lax.ppermute(value, axis, [(i, i ^ bit) for i in range(size)])  28.3 us
    pallas_call x4, Pallas kernels, call(): pl.pallas_call(kernel, out_shape=tuple(outs), in_specs=[ANY] * len(ins),...  15.7 us
    ppermute x1, waiting for transfers between devices, body(): g0 = lax.ppermute(g_out, 'segment', [(1, 0)])  7.24 us
    ppermute x1, waiting for transfers between devices, body(): moved = lax.ppermute(source, 'band', down)  4.52 us
    ppermute x1, starting transfers between devices, body(): back = lax.ppermute(y[:, :part], 'band', up)  3.83 us
    unnamed x60, local copies, waits for them, and re-layouts  3.48 us
  transfers between devices with their start and end apart: 34, of which 13 were waited for; matrix products, arithmetic and copies ran while one was open for 3% of the time, Pallas kernels for 2%

profile of v6, /device:TPU:0, one launch (start us, length us, event | category | flops | bytes accessed | tf_op | source)
XLA Modules:
  0.0 125.5 jit_solution(3402783511580753105)
XLA Ops:
  0.6 3.1 %collective-permute-start.3 = (bf16[128,1536]{1,0:T(8,128)(2,1)}, bf16[128,1536]{1,0:T(8,128)(2,1)S(1)}, u32[]{:S(2)}, u32[]{:S(2)}) collective-permute-start(bf16[128,1536]{1,0:T(8,128)(2,1)} %bitcast.42), channel_id=1, source_target_pairs={{0,16},{8,24},{16,0},{24,8},{1,17},{9,25},{17,1},{25,9},{2,18},{10... | collective-permute-start | bytes 1179656 | tf_op jit(solution)/shard_map/ppermute | solution.py:510
  3.7 1.0 select_bitcast_fusion
  4.8 11.0 %collective-permute-done.5.got = bf16[128,512]{1,0:T(8,128)(2,1)S(1)} collective-permute-done((bf16[128,512]{1,0:T(8,128)(2,1)S(1)}, bf16[128,512]{1,0:T(8,128)(2,1)S(1)}, u32[]{:S(2)}, u32[]{:S(2)}) %collective-permute-start.5) | collective-permute-done | bytes 131104 | tf_op jit(solution)/shard_map/ppermute | solution.py:510
  16.5 1.9 %pack.1.refs_7_.refs_8_ = bf16[272,512]{1,0:T(8,128)(2,1)} custom-call(bf16[256,512]{1,0:T(8,128)(2,1)} %bitcast.47, bf16[128,512]{1,0:T(8,128)(2,1)} %copy-done.20, bf16[128,512]{1,0:T(8,128)(2,1)} %bitcast.53, bf16[1,128]{1,0:T(2,128)(2,1)} %gain.1), custom_call_target="tpu_custom_call" | custom-call | tf_op jit(solution)/shard_map/pack/pallas_call | solution.py:545
  18.4 1.7 %collective-permute-start.6 = (bf16[272,512]{1,0:T(8,128)(2,1)}, bf16[272,512]{1,0:T(8,128)(2,1)S(1)}, u32[]{:S(2)}, u32[]{:S(2)}) collective-permute-start(bf16[272,512]{1,0:T(8,128)(2,1)} %pack.1.refs_7_.refs_8_), channel_id=1, source_target_pairs={{0,8},{8,0},{16,24},{24,16},{1,9},{9,1},{17,25},{25,17},{2,10},{10... | collective-permute-start | bytes 835592 | tf_op jit(solution)/shard_map/ppermute | solution.py:510
  20.4 1.7 %collective-permute-start.4 = (bf16[128,1536]{1,0:T(8,128)(2,1)S(1)}, bf16[128,1536]{1,0:T(8,128)(2,1)S(1)}, u32[]{:S(2)}, u32[]{:S(2)}) collective-permute-start(bf16[128,1536]{1,0:T(8,128)(2,1)S(1)} %collective-permute-done.3.refs_5_.refs_6_), channel_id=1, source_target_pairs={{0,8},{8,0},{16,24},{24,16},{1,9},{9,1},{17,25},{25,17},{2,10},{10... | collective-permute-start | bytes 1179656 | tf_op jit(solution)/shard_map/ppermute | solution.py:510
  22.1 1.6 %collective-permute-start = (s32[2,4,16]{2,1,0:T(4,128)S(1)}, s32[2,4,16]{2,1,0:T(4,128)S(1)}, u32[]{:S(2)}, u32[]{:S(2)}) collective-permute-start(s32[2,4,16]{2,1,0:T(4,128)S(1)} %get-tuple-element.77), channel_id=1, source_target_pairs={{0,1},{1,2},{2,3},{3,0},{4,5},{5,6},{6,7},{7,4},{8,9},{9,10},{10,1... | collective-permute-start | bytes 1544 | tf_op jit(solution)/shard_map/ppermute | solution.py:560
  23.7 1.5 %collective-permute-start.7 = (bf16[272,512]{1,0:T(8,128)(2,1)}, bf16[272,512]{1,0:T(8,128)(2,1)S(1)}, u32[]{:S(2)}, u32[]{:S(2)}) collective-permute-start(bf16[272,512]{1,0:T(8,128)(2,1)} %pack.1.refs_7_.refs_8_), channel_id=1, source_target_pairs={{0,16},{8,24},{16,0},{24,8},{1,17},{9,25},{17,1},{25,9},{2,18},{10... | collective-permute-start | bytes 835592 | tf_op jit(solution)/shard_map/ppermute | solution.py:510
  25.2 2.9 %collective-permute-done.6.refs_8_.refs_9_ = bf16[272,512]{1,0:T(8,128)(2,1)S(1)} collective-permute-done((bf16[272,512]{1,0:T(8,128)(2,1)}, bf16[272,512]{1,0:T(8,128)(2,1)S(1)}, u32[]{:S(2)}, u32[]{:S(2)}) %collective-permute-start.6) | collective-permute-done | bytes 278560 | tf_op jit(solution)/shard_map/ppermute | solution.py:510
  28.1 1.7 %collective-permute-start.8 = (bf16[272,512]{1,0:T(8,128)(2,1)S(1)}, bf16[272,512]{1,0:T(8,128)(2,1)S(1)}, u32[]{:S(2)}, u32[]{:S(2)}) collective-permute-start(bf16[272,512]{1,0:T(8,128)(2,1)S(1)} %collective-permute-done.6.refs_8_.refs_9_), channel_id=1, source_target_pairs={{0,16},{8,24},{16,0},{24,8},{1,17},{9,25},{17,1},{25,9},{2,18},{10... | collective-permute-start | bytes 835592 | tf_op jit(solution)/shard_map/ppermute | solution.py:510
  29.9 1.6 %collective-permute-start.1 = (bf16[2,4,16,512]{3,2,1,0:T(8,128)(2,1)S(1)}, bf16[2,4,16,512]{3,2,1,0:T(8,128)(2,1)S(1)}, u32[]{:S(2)}, u32[]{:S(2)}) collective-permute-start(bf16[2,4,16,512]{3,2,1,0:T(8,128)(2,1)S(1)} %select_bitcast_fusion.1), channel_id=1, source_target_pairs={{0,1},{1,2},{2,3},{3,0},{4,5},{5,6},{6,7},{7,4},{8,9},{9,10},{10,1... | collective-permute-start | bytes 393224 | tf_op jit(solution)/shard_map/ppermute | solution.py:558
  32.2 4.5 %collective-permute-done.1 = bf16[2,4,16,512]{3,2,1,0:T(8,128)(2,1)S(1)} collective-permute-done((bf16[2,4,16,512]{3,2,1,0:T(8,128)(2,1)S(1)}, bf16[2,4,16,512]{3,2,1,0:T(8,128)(2,1)S(1)}, u32[]{:S(2)}, u32[]{:S(2)}) %collective-permute-start.1) | collective-permute-done | bytes 131104 | tf_op jit(solution)/shard_map/ppermute | solution.py:558
  36.7 6.5 %collective-permute-done.4.refs_6_.refs_7_ = bf16[128,1536]{1,0:T(8,128)(2,1)S(1)} collective-permute-done((bf16[128,1536]{1,0:T(8,128)(2,1)S(1)}, bf16[128,1536]{1,0:T(8,128)(2,1)S(1)}, u32[]{:S(2)}, u32[]{:S(2)}) %collective-permute-start.4) | collective-permute-done | bytes 393248 | tf_op jit(solution)/shard_map/ppermute | solution.py:510
  44.0 5.9 %shard_map.110 = (bf16[256,512]{1,0:T(8,128)(2,1)}, f32[256,512]{1,0:T(8,128)}, f32[256,128]{1,0:T(8,128)}, bf16[256,512]{1,0:T(8,128)(2,1)}, bf16[256,1536]{1,0...) custom-call(s32[2,128]{1,0:T(2,128)} %reshape.54.refs_0_, bf16[2,64,512]{2,1,0:T(8,128)(2,1)} %bitcast.48, ...), custom_call_target="tpu_custom_call" | custom-call | flops 805306368 | bytes 5833728 | tf_op jit(solution)/shard_map/pallas_call | solution.py:497
  49.9 1.3 %collective-permute-start.9 = (bf16[256,512]{1,0:T(8,128)(2,1)}, bf16[256,512]{1,0:T(8,128)(2,1)S(1)}, u32[]{:S(2)}, u32[]{:S(2)}) collective-permute-start(bf16[256,512]{1,0:T(8,128)(2,1)} %get-tuple-element.40.refs_12_), channel_id=1, source_target_pairs={{0,4},{1,5},{2,6},{3,7},{8,12},{9,13},{10,14},{11,15},{16,20},{17,... | collective-permute-start | bytes 786440 | tf_op jit(solution)/shard_map/ppermute | solution.py:588
  51.2 1.3 %collective-permute-done.9.refs_3_.refs_0_ = bf16[256,512]{1,0:T(8,128)(2,1)S(1)} collective-permute-done((bf16[256,512]{1,0:T(8,128)(2,1)}, bf16[256,512]{1,0:T(8,128)(2,1)S(1)}, u32[]{:S(2)}, u32[]{:S(2)}) %collective-permute-start.9) | collective-permute-done | bytes 262176 | tf_op jit(solution)/shard_map/ppermute | solution.py:588
  53.2 1.1 shard_map.111
  54.4 1.3 %collective-permute-start.11 = (bf16[256,512]{1,0:T(8,128)(2,1)}, bf16[256,512]{1,0:T(8,128)(2,1)S(1)}, u32[]{:S(2)}, u32[]{:S(2)}) collective-permute-start(bf16[256,512]{1,0:T(8,128)(2,1)} %get-tuple-element.42), channel_id=1, source_target_pairs={{4,0},{5,1},{6,2},{7,3},{12,8},{13,9},{14,10},{15,11},{20,16},{21,... | collective-permute-start | bytes 786440 | tf_op jit(solution)/shard_map/ppermute | solution.py:599
  55.7 1.2 shard_map.112
  56.8 7.2 %collective-permute-done.11.refs_3_ = bf16[256,512]{1,0:T(8,128)(2,1)S(1)} collective-permute-done((bf16[256,512]{1,0:T(8,128)(2,1)}, bf16[256,512]{1,0:T(8,128)(2,1)S(1)}, u32[]{:S(2)}, u32[]{:S(2)}) %collective-permute-start.11) | collective-permute-done | bytes 262176 | tf_op jit(solution)/shard_map/ppermute | solution.py:599
  64.1 0.7 copy-done.18
  64.8 7.5 %shard_map.113 = (bf16[2,336,256]{2,1,0:T(8,128)(2,1)}, bf16[2,336,256]{2,1,0:T(8,128)(2,1)}, bf16[2,336,256]{2,1,0:T(8,128)(2,1)}, bf16[2,336,256]{2,1,0:T(8,12...) custom-call(s32[2,128]{1,0:T(2,128)} %reshape.54.refs_0_, ...), custom_call_target="tpu_custom_call", output_to_operand_aliasing={{0}: (18, {}), {1}: (19, {}), {2}: (20, {}), {3}: (21, {}),... | custom-call | flops 1610612736 | bytes 11338752 | tf_op jit(solution)/shard_map/pallas_call | solution.py:497
  72.3 1.5 %collective-permute-start.12 = (bf16[2,336,256]{2,1,0:T(8,128)(2,1)}, bf16[2,336,256]{2,1,0:T(8,128)(2,1)S(1)}, u32[]{:S(2)}, u32[]{:S(2)}) collective-permute-start(bf16[2,336,256]{2,1,0:T(8,128)(2,1)} %get-tuple-element.64), channel_id=1, source_target_pairs={{0,16},{8,24},{16,0},{24,8},{1,17},{9,25},{17,1},{25,9},{2,18},{10... | collective-permute-start | bytes 1032200 | tf_op jit(solution)/shard_map/ppermute | solution.py:510
  73.9 1.5 %collective-permute-start.17 = (bf16[2,336,256]{2,1,0:T(8,128)(2,1)}, bf16[2,336,256]{2,1,0:T(8,128)(2,1)S(1)}, u32[]{:S(2)}, u32[]{:S(2)}) collective-permute-start(bf16[2,336,256]{2,1,0:T(8,128)(2,1)} %get-tuple-element.66), channel_id=1, source_target_pairs={{0,8},{8,0},{16,24},{24,16},{1,9},{9,1},{17,25},{25,17},{2,10},{10... | collective-permute-start | bytes 1032200 | tf_op jit(solution)/shard_map/ppermute | solution.py:510
  75.4 3.8 %collective-permute-start.10 = (bf16[2,64,512]{2,1,0:T(8,128)(2,1)S(1)}, bf16[2,64,512]{2,1,0:T(8,128)(2,1)S(1)}, u32[]{:S(2)}, u32[]{:S(2)}) collective-permute-start(bf16[2,64,512]{2,1,0:T(8,128)(2,1)S(1)} %get-tuple-element.76), channel_id=1, source_target_pairs={{1,0},{2,1},{3,2},{0,3},{5,4},{6,5},{7,6},{4,7},{9,8},{10,9},{11,1... | collective-permute-start | bytes 393224 | tf_op jit(solution)/shard_map/ppermute | solution.py:611
  80.2 1.3 %collective-permute-done.12 = bf16[2,336,256]{2,1,0:T(8,128)(2,1)S(1)} collective-permute-done((bf16[2,336,256]{2,1,0:T(8,128)(2,1)}, bf16[2,336,256]{2,1,0:T(8,128)(2,1)S(1)}, u32[]{:S(2)}, u32[]{:S(2)}) %collective-permute-start.12) | collective-permute-done | bytes 344096 | tf_op jit(solution)/shard_map/ppermute | solution.py:510
  81.7 2.5 %collective-permute-start.13 = (bf16[336,256]{1,0:T(8,128)(2,1)S(1)}, bf16[336,256]{1,0:T(8,128)(2,1)S(1)}, u32[]{:S(2)}, u32[]{:S(2)}) collective-permute-start(bf16[336,256]{1,0:T(8,128)(2,1)S(1)} %fusion.12), channel_id=1, source_target_pairs={{0,8},{8,0},{16,24},{24,16},{1,9},{9,1},{17,25},{25,17},{2,10},{10... | collective-permute-start | bytes 516104 | tf_op jit(solution)/shard_map/ppermute | solution.py:510
  84.3 2.4 %collective-permute-start.18 = (bf16[336,256]{1,0:T(8,128)(2,1)S(1)}, bf16[336,256]{1,0:T(8,128)(2,1)S(1)}, u32[]{:S(2)}, u32[]{:S(2)}) collective-permute-start(bf16[336,256]{1,0:T(8,128)(2,1)S(1)} %fusion.13), channel_id=1, source_target_pairs={{0,16},{8,24},{16,0},{24,8},{1,17},{9,25},{17,1},{25,9},{2,18},{10... | collective-permute-start | bytes 516104 | tf_op jit(solution)/shard_map/ppermute | solution.py:510
  86.8 2.5 %collective-permute-done.22 = bf16[2,336,256]{2,1,0:T(8,128)(2,1)S(1)} collective-permute-done((bf16[2,336,256]{2,1,0:T(8,128)(2,1)S(1)}, bf16[2,336,256]{2,1,0:T(8,128)(2,1)S(1)}, u32[]{:S(2)}, u32[]{:S(2)}) %collective-permute-start.22) | collective-permute-done | bytes 344096 | tf_op jit(solution)/shard_map/ppermute | solution.py:510
  89.4 1.8 %collective-permute-start.23 = (bf16[336,256]{1,0:T(8,128)(2,1)S(1)}, bf16[336,256]{1,0:T(8,128)(2,1)S(1)}, u32[]{:S(2)}, u32[]{:S(2)}) collective-permute-start(bf16[336,256]{1,0:T(8,128)(2,1)S(1)} %fusion.14), channel_id=1, source_target_pairs={{0,8},{8,0},{16,24},{24,16},{1,9},{9,1},{17,25},{25,17},{2,10},{10... | collective-permute-start | bytes 516104 | tf_op jit(solution)/shard_map/ppermute | solution.py:510
  91.4 2.0 %collective-permute-start.28 = (bf16[336,256]{1,0:T(8,128)(2,1)S(1)}, bf16[336,256]{1,0:T(8,128)(2,1)S(1)}, u32[]{:S(2)}, u32[]{:S(2)}) collective-permute-start(bf16[336,256]{1,0:T(8,128)(2,1)S(1)} %fusion.15), channel_id=1, source_target_pairs={{0,16},{8,24},{16,0},{24,8},{1,17},{9,25},{17,1},{25,9},{2,18},{10... | collective-permute-start | bytes 516104 | tf_op jit(solution)/shard_map/ppermute | solution.py:510
  93.5 0.7 collective-permute-done.13
  94.3 1.4 %collective-permute-start.14 = (bf16[336,128]{1,0:T(8,128)(2,1)S(1)}, bf16[336,128]{1,0:T(8,128)(2,1)S(1)}, u32[]{:S(2)}, u32[]{:S(2)}) collective-permute-start(bf16[336,128]{1,0:T(8,128)(2,1)S(1)} %select_convert_fusion.3), channel_id=1, source_target_pairs={{0,1},{1,0},{2,3},{3,2},{4,5},{5,4},{6,7},{7,6},{8,9},{9,8},{10,11... | collective-permute-start | bytes 258056 | tf_op jit(solution)/shard_map/ppermute | solution.py:510
  95.8 0.7 collective-permute-start.19
  96.6 1.4 %collective-permute-start.24 = (bf16[336,128]{1,0:T(8,128)(2,1)S(1)}, bf16[336,128]{1,0:T(8,128)(2,1)S(1)}, u32[]{:S(2)}, u32[]{:S(2)}) collective-permute-start(bf16[336,128]{1,0:T(8,128)(2,1)S(1)} %select_convert_fusion.1), channel_id=1, source_target_pairs={{0,1},{1,0},{2,3},{3,2},{4,5},{5,4},{6,7},{7,6},{8,9},{9,8},{10,11... | collective-permute-start | bytes 258056 | tf_op jit(solution)/shard_map/ppermute | solution.py:510
  98.2 1.5 %collective-permute-start.29 = (bf16[336,128]{1,0:T(8,128)(2,1)S(1)}, bf16[336,128]{1,0:T(8,128)(2,1)S(1)}, u32[]{:S(2)}, u32[]{:S(2)}) collective-permute-start(bf16[336,128]{1,0:T(8,128)(2,1)S(1)} %select_convert_fusion), channel_id=1, source_target_pairs={{0,1},{1,0},{2,3},{3,2},{4,5},{5,4},{6,7},{7,6},{8,9},{9,8},{10,11... | collective-permute-start | bytes 258056 | tf_op jit(solution)/shard_map/ppermute | solution.py:510
  99.7 2.6 %collective-permute-start.15 = (bf16[336,128]{1,0:T(8,128)(2,1)S(1)}, bf16[336,128]{1,0:T(8,128)(2,1)S(1)}, u32[]{:S(2)}, u32[]{:S(2)}) collective-permute-start(bf16[336,128]{1,0:T(8,128)(2,1)S(1)} %add_convert_fusion.7), channel_id=1, source_target_pairs={{0,2},{1,3},{2,0},{3,1},{4,6},{5,7},{6,4},{7,5},{8,10},{9,11},{10,... | collective-permute-start | bytes 258056 | tf_op jit(solution)/shard_map/ppermute | solution.py:510
  102.3 1.6 %collective-permute-start.20 = (bf16[336,128]{1,0:T(8,128)(2,1)S(1)}, bf16[336,128]{1,0:T(8,128)(2,1)S(1)}, u32[]{:S(2)}, u32[]{:S(2)}) collective-permute-start(bf16[336,128]{1,0:T(8,128)(2,1)S(1)} %add_convert_fusion.5), channel_id=1, source_target_pairs={{0,2},{1,3},{2,0},{3,1},{4,6},{5,7},{6,4},{7,5},{8,10},{9,11},{10,... | collective-permute-start | bytes 258056 | tf_op jit(solution)/shard_map/ppermute | solution.py:510
  104.0 1.9 %collective-permute-start.25 = (bf16[336,128]{1,0:T(8,128)(2,1)S(1)}, bf16[336,128]{1,0:T(8,128)(2,1)S(1)}, u32[]{:S(2)}, u32[]{:S(2)}) collective-permute-start(bf16[336,128]{1,0:T(8,128)(2,1)S(1)} %add_convert_fusion.3), channel_id=1, source_target_pairs={{0,2},{1,3},{2,0},{3,1},{4,6},{5,7},{6,4},{7,5},{8,10},{9,11},{10,... | collective-permute-start | bytes 258056 | tf_op jit(solution)/shard_map/ppermute | solution.py:510
  106.0 3.8 %collective-permute-start.30 = (bf16[336,128]{1,0:T(8,128)(2,1)S(1)}, bf16[336,128]{1,0:T(8,128)(2,1)S(1)}, u32[]{:S(2)}, u32[]{:S(2)}) collective-permute-start(bf16[336,128]{1,0:T(8,128)(2,1)S(1)} %add_convert_fusion.1), channel_id=1, source_target_pairs={{0,2},{1,3},{2,0},{3,1},{4,6},{5,7},{6,4},{7,5},{8,10},{9,11},{10,... | collective-permute-start | bytes 258056 | tf_op jit(solution)/shard_map/ppermute | solution.py:510
  109.8 2.8 %collective-permute-start.16 = (bf16[336,128]{1,0:T(8,128)(2,1)S(1)}, bf16[336,128]{1,0:T(8,128)(2,1)S(1)}, u32[]{:S(2)}, u32[]{:S(2)}) collective-permute-start(bf16[336,128]{1,0:T(8,128)(2,1)S(1)} %add_convert_fusion.6.refs_0_), channel_id=1, source_target_pairs={{0,1},{1,0},{2,3},{3,2},{4,5},{5,4},{6,7},{7,6},{8,9},{9,8},{10,11... | collective-permute-start | bytes 258056 | tf_op jit(solution)/shard_map/ppermute | solution.py:510
  112.8 1.9 %collective-permute-start.32 = (bf16[128,256]{1,0:T(8,128)(2,1)S(1)}, bf16[128,256]{1,0:T(8,128)(2,1)S(1)}, u32[]{:S(2)}, u32[]{:S(2)}) collective-permute-start(bf16[128,256]{1,0:T(8,128)(2,1)S(1)} %pad_maximum_fusion.1), channel_id=1, source_target_pairs={{0,16},{8,24},{16,0},{24,8},{1,17},{9,25},{17,1},{25,9},{2,18},{10... | collective-permute-start | bytes 196616 | tf_op jit(solution)/shard_map/ppermute | solution.py:510
  114.8 1.6 %collective-permute-start.26 = (bf16[336,128]{1,0:T(8,128)(2,1)S(1)}, bf16[336,128]{1,0:T(8,128)(2,1)S(1)}, u32[]{:S(2)}, u32[]{:S(2)}) collective-permute-start(bf16[336,128]{1,0:T(8,128)(2,1)S(1)} %add_convert_fusion.2.refs_4_), channel_id=1, source_target_pairs={{0,1},{1,0},{2,3},{3,2},{4,5},{5,4},{6,7},{7,6},{8,9},{9,8},{10,11... | collective-permute-start | bytes 258056 | tf_op jit(solution)/shard_map/ppermute | solution.py:510
  117.0 0.9 collective-permute-done.33.refs_9_
  118.5 0.7 pad_maximum_fusion
  119.3 1.7 %collective-permute-done.21.refs_3_ = bf16[336,128]{1,0:T(8,128)(2,1)S(1)} collective-permute-done((bf16[336,128]{1,0:T(8,128)(2,1)S(1)}, bf16[336,128]{1,0:T(8,128)(2,1)S(1)}, u32[]{:S(2)}, u32[]{:S(2)}) %collective-permute-start.21) | collective-permute-done | bytes 86048 | tf_op jit(solution)/shard_map/ppermute | solution.py:510
  121.0 1.4 %collective-permute-done.31.refs_7_ = bf16[336,128]{1,0:T(8,128)(2,1)S(1)} collective-permute-done((bf16[336,128]{1,0:T(8,128)(2,1)S(1)}, bf16[336,128]{1,0:T(8,128)(2,1)S(1)}, u32[]{:S(2)}, u32[]{:S(2)}) %collective-permute-start.31) | collective-permute-done | bytes 86048 | tf_op jit(solution)/shard_map/ppermute | solution.py:510
  123.0 2.4 %unpack.1 = (f32[1,256,512]{2,1,0:T(8,128)}, f32[1,128,1536]{2,1,0:T(8,128)}, f32[1,128,512]{2,1,0:T(8,128)}, f32[1,128]{1,0:T(1,128)}) custom-call(bf16[336,128]{1,0:T(8,128)(2,1)} %copy-done.13, bf16[336,128]{1,0:T(8,128)(2,1)} %copy-done.21, bf16[336,128]{1,0:T(8,128)(2,1)} %copy-done.16, bf16[336,128]{1,0:T(8,128)(2,1)} %copy-done.23, ...), custom_call_target="tpu_custom_call" | custom-call | tf_op jit(solution)/shard_map/unpack/pallas_call | solution.py:653
  (120 shorter events, 7.3 us)
Async XLA Ops:
  0.6 19.8 %collective-permute-start.3 = (bf16[128,1536]{1,0:T(8,128)(2,1)}, bf16[128,1536]{1,0:T(8,128)(2,1)S(1)}, u32[]{:S(2)}, u32[]{:S(2)}) collective-permute-start(bf16[128,1536]{1,0:T(8,128)(2,1)} %bitcast.42), channel_id=1, source_target_pairs={{0,16},{8,24},{16,0},{24,8},{1,17},{9,25},{17,1},{25,9},{2,18},{10... | collective-permute-start | bytes 1179656 | tf_op jit(solution)/shard_map/ppermute | solution.py:510
  3.7 26.2 %copy-start.27 = (bf16[1,2,8,16,512]{4,3,2,1,0:T(8,128)(2,1)S(1)}, bf16[1,2,8,16,512]{4,3,2,1,0:T(8,128)(2,1)}, u32[]{:S(2)}) copy-start(bf16[1,2,8,16,512]{4,3,2,1,0:T(8,128)(2,1)} %param.13) | copy-start | bytes 786436
  4.7 11.1 %collective-permute-start.5 = (bf16[128,512]{1,0:T(8,128)(2,1)S(1)}, bf16[128,512]{1,0:T(8,128)(2,1)S(1)}, u32[]{:S(2)}, u32[]{:S(2)}) collective-permute-start(bf16[128,512]{1,0:T(8,128)(2,1)S(1)} %select_bitcast_fusion), channel_id=1, source_target_pairs={{0,16},{8,24},{16,0},{24,8},{1,17},{9,25},{17,1},{25,9},{2,18},{10... | collective-permute-start | bytes 393224 | tf_op jit(solution)/shard_map/ppermute | solution.py:510
  16.5 3.6 %copy-start.1 = (bf16[1,128,1536]{2,1,0:T(8,128)(2,1)S(1)}, bf16[1,128,1536]{2,1,0:T(8,128)(2,1)}, u32[]{:S(2)}) copy-start(bf16[1,128,1536]{2,1,0:T(8,128)(2,1)} %param.10) | copy-start | bytes 1179652
  16.5 5.6 %copy-start.28 = (s32[1,2,8,16]{3,2,1,0:T(8,128)S(1)}, s32[1,2,8,16]{3,2,1,0:T(8,128)}, u32[]{:S(2)}) copy-start(s32[1,2,8,16]{3,2,1,0:T(8,128)} %param.8) | copy-start | bytes 3076
  16.5 13.4 %copy-start = (bf16[1,2,8,16,512]{4,3,2,1,0:T(8,128)(2,1)S(1)}, bf16[1,2,8,16,512]{4,3,2,1,0:T(8,128)(2,1)}, u32[]{:S(2)}) copy-start(bf16[1,2,8,16,512]{4,3,2,1,0:T(8,128)(2,1)} %param.7) | copy-start | bytes 786436
  18.4 9.7 %collective-permute-start.6 = (bf16[272,512]{1,0:T(8,128)(2,1)}, bf16[272,512]{1,0:T(8,128)(2,1)S(1)}, u32[]{:S(2)}, u32[]{:S(2)}) collective-permute-start(bf16[272,512]{1,0:T(8,128)(2,1)} %pack.1.refs_7_.refs_8_), channel_id=1, source_target_pairs={{0,8},{8,0},{16,24},{24,16},{1,9},{9,1},{17,25},{25,17},{2,10},{10... | collective-permute-start | bytes 835592 | tf_op jit(solution)/shard_map/ppermute | solution.py:510
  20.1 16.6 %collective-permute-start.2 = (bf16[128,1536]{1,0:T(8,128)(2,1)S(1)}, bf16[128,1536]{1,0:T(8,128)(2,1)S(1)}, u32[]{:S(2)}, u32[]{:S(2)}) collective-permute-start(bf16[128,1536]{1,0:T(8,128)(2,1)S(1)} %bitcast.46), channel_id=1, source_target_pairs={{0,8},{8,0},{16,24},{24,16},{1,9},{9,1},{17,25},{25,17},{2,10},{10... | collective-permute-start | bytes 1179656 | tf_op jit(solution)/shard_map/ppermute | solution.py:510
  20.4 22.9 %copy-start.2 = (bf16[128,1536]{1,0:T(8,128)(2,1)}, bf16[128,1536]{1,0:T(8,128)(2,1)S(1)}, u32[]{:S(2)}) copy-start(bf16[128,1536]{1,0:T(8,128)(2,1)S(1)} %collective-permute-done.3.refs_5_.refs_6_) | copy-start | bytes 1179652
  20.4 22.9 %collective-permute-start.4 = (bf16[128,1536]{1,0:T(8,128)(2,1)S(1)}, bf16[128,1536]{1,0:T(8,128)(2,1)S(1)}, u32[]{:S(2)}, u32[]{:S(2)}) collective-permute-start(bf16[128,1536]{1,0:T(8,128)(2,1)S(1)} %collective-permute-done.3.refs_5_.refs_6_), channel_id=1, source_target_pairs={{0,8},{8,0},{16,24},{24,16},{1,9},{9,1},{17,25},{25,17},{2,10},{10... | collective-permute-start | bytes 1179656 | tf_op jit(solution)/shard_map/ppermute | solution.py:510
  22.1 7.8 %collective-permute-start = (s32[2,4,16]{2,1,0:T(4,128)S(1)}, s32[2,4,16]{2,1,0:T(4,128)S(1)}, u32[]{:S(2)}, u32[]{:S(2)}) collective-permute-start(s32[2,4,16]{2,1,0:T(4,128)S(1)} %get-tuple-element.77), channel_id=1, source_target_pairs={{0,1},{1,2},{2,3},{3,0},{4,5},{5,6},{6,7},{7,4},{8,9},{9,10},{10,1... | collective-permute-start | bytes 1544 | tf_op jit(solution)/shard_map/ppermute | solution.py:560
  23.7 13.0 %collective-permute-start.7 = (bf16[272,512]{1,0:T(8,128)(2,1)}, bf16[272,512]{1,0:T(8,128)(2,1)S(1)}, u32[]{:S(2)}, u32[]{:S(2)}) collective-permute-start(bf16[272,512]{1,0:T(8,128)(2,1)} %pack.1.refs_7_.refs_8_), channel_id=1, source_target_pairs={{0,16},{8,24},{16,0},{24,8},{1,17},{9,25},{17,1},{25,9},{2,18},{10... | collective-permute-start | bytes 835592 | tf_op jit(solution)/shard_map/ppermute | solution.py:510
  28.1 15.2 %copy-start.9 = (bf16[272,512]{1,0:T(8,128)(2,1)}, bf16[272,512]{1,0:T(8,128)(2,1)S(1)}, u32[]{:S(2)}) copy-start(bf16[272,512]{1,0:T(8,128)(2,1)S(1)} %collective-permute-done.6.refs_8_.refs_9_) | copy-start | bytes 835588
  28.1 8.6 %collective-permute-start.8 = (bf16[272,512]{1,0:T(8,128)(2,1)S(1)}, bf16[272,512]{1,0:T(8,128)(2,1)S(1)}, u32[]{:S(2)}, u32[]{:S(2)}) collective-permute-start(bf16[272,512]{1,0:T(8,128)(2,1)S(1)} %collective-permute-done.6.refs_8_.refs_9_), channel_id=1, source_target_pairs={{0,16},{8,24},{16,0},{24,8},{1,17},{9,25},{17,1},{25,9},{2,18},{10... | collective-permute-start | bytes 835592 | tf_op jit(solution)/shard_map/ppermute | solution.py:510
  29.9 6.8 %collective-permute-start.1 = (bf16[2,4,16,512]{3,2,1,0:T(8,128)(2,1)S(1)}, bf16[2,4,16,512]{3,2,1,0:T(8,128)(2,1)S(1)}, u32[]{:S(2)}, u32[]{:S(2)}) collective-permute-start(bf16[2,4,16,512]{3,2,1,0:T(8,128)(2,1)S(1)} %select_bitcast_fusion.1), channel_id=1, source_target_pairs={{0,1},{1,2},{2,3},{3,0},{4,5},{5,6},{6,7},{7,4},{8,9},{9,10},{10,1... | collective-permute-start | bytes 393224 | tf_op jit(solution)/shard_map/ppermute | solution.py:558
  36.7 6.6 %copy-start.12 = (bf16[2,4,16,512]{3,2,1,0:T(8,128)(2,1)}, bf16[2,4,16,512]{3,2,1,0:T(8,128)(2,1)S(1)}, u32[]{:S(2)}) copy-start(bf16[2,4,16,512]{3,2,1,0:T(8,128)(2,1)S(1)} %collective-permute-done.1) | copy-start | bytes 393220
  36.7 6.6 %copy-start.3 = (bf16[128,1536]{1,0:T(8,128)(2,1)}, bf16[128,1536]{1,0:T(8,128)(2,1)S(1)}, u32[]{:S(2)}) copy-start(bf16[128,1536]{1,0:T(8,128)(2,1)S(1)} %collective-permute-done.2.refs_4_.refs_5_) | copy-start | bytes 1179652
  36.7 6.6 %copy-start.10 = (bf16[272,512]{1,0:T(8,128)(2,1)}, bf16[272,512]{1,0:T(8,128)(2,1)S(1)}, u32[]{:S(2)}) copy-start(bf16[272,512]{1,0:T(8,128)(2,1)S(1)} %collective-permute-done.7.refs_9_.refs_10_) | copy-start | bytes 835588
  36.7 6.6 %copy-start.11 = (bf16[272,512]{1,0:T(8,128)(2,1)}, bf16[272,512]{1,0:T(8,128)(2,1)S(1)}, u32[]{:S(2)}) copy-start(bf16[272,512]{1,0:T(8,128)(2,1)S(1)} %collective-permute-done.8.refs_10_.refs_11_) | copy-start | bytes 835588
  49.9 2.7 %collective-permute-start.9 = (bf16[256,512]{1,0:T(8,128)(2,1)}, bf16[256,512]{1,0:T(8,128)(2,1)S(1)}, u32[]{:S(2)}, u32[]{:S(2)}) collective-permute-start(bf16[256,512]{1,0:T(8,128)(2,1)} %get-tuple-element.40.refs_12_), channel_id=1, source_target_pairs={{0,4},{1,5},{2,6},{3,7},{8,12},{9,13},{10,14},{11,15},{16,20},{17,... | collective-permute-start | bytes 786440 | tf_op jit(solution)/shard_map/ppermute | solution.py:588
  54.4 9.7 %collective-permute-start.11 = (bf16[256,512]{1,0:T(8,128)(2,1)}, bf16[256,512]{1,0:T(8,128)(2,1)S(1)}, u32[]{:S(2)}, u32[]{:S(2)}) collective-permute-start(bf16[256,512]{1,0:T(8,128)(2,1)} %get-tuple-element.42), channel_id=1, source_target_pairs={{4,0},{5,1},{6,2},{7,3},{12,8},{13,9},{14,10},{15,11},{20,16},{21,... | collective-permute-start | bytes 786440 | tf_op jit(solution)/shard_map/ppermute | solution.py:599
  64.8 10.6 %copy-start.19 = (bf16[256,512]{1,0:T(8,128)(2,1)S(1)}, bf16[256,512]{1,0:T(8,128)(2,1)}, u32[]{:S(2)}) copy-start(bf16[256,512]{1,0:T(8,128)(2,1)} %get-tuple-element.41) | copy-start | bytes 786436
  72.3 6.9 %copy-start.15 = (bf16[2,336,256]{2,1,0:T(8,128)(2,1)S(1)}, bf16[2,336,256]{2,1,0:T(8,128)(2,1)}, u32[]{:S(2)}) copy-start(bf16[2,336,256]{2,1,0:T(8,128)(2,1)} %get-tuple-element.68) | copy-start | bytes 1032196
  72.3 9.2 %collective-permute-start.12 = (bf16[2,336,256]{2,1,0:T(8,128)(2,1)}, bf16[2,336,256]{2,1,0:T(8,128)(2,1)S(1)}, u32[]{:S(2)}, u32[]{:S(2)}) collective-permute-start(bf16[2,336,256]{2,1,0:T(8,128)(2,1)} %get-tuple-element.64), channel_id=1, source_target_pairs={{0,16},{8,24},{16,0},{24,8},{1,17},{9,25},{17,1},{25,9},{2,18},{10... | collective-permute-start | bytes 1032200 | tf_op jit(solution)/shard_map/ppermute | solution.py:510
  73.9 10.3 %collective-permute-start.17 = (bf16[2,336,256]{2,1,0:T(8,128)(2,1)}, bf16[2,336,256]{2,1,0:T(8,128)(2,1)S(1)}, u32[]{:S(2)}, u32[]{:S(2)}) collective-permute-start(bf16[2,336,256]{2,1,0:T(8,128)(2,1)} %get-tuple-element.66), channel_id=1, source_target_pairs={{0,8},{8,0},{16,24},{24,16},{1,9},{9,1},{17,25},{25,17},{2,10},{10... | collective-permute-start | bytes 1032200 | tf_op jit(solution)/shard_map/ppermute | solution.py:510
  75.4 41.0 %collective-permute-start.10 = (bf16[2,64,512]{2,1,0:T(8,128)(2,1)S(1)}, bf16[2,64,512]{2,1,0:T(8,128)(2,1)S(1)}, u32[]{:S(2)}, u32[]{:S(2)}) collective-permute-start(bf16[2,64,512]{2,1,0:T(8,128)(2,1)S(1)} %get-tuple-element.76), channel_id=1, source_target_pairs={{1,0},{2,1},{3,2},{0,3},{5,4},{6,5},{7,6},{4,7},{9,8},{10,9},{11,1... | collective-permute-start | bytes 393224 | tf_op jit(solution)/shard_map/ppermute | solution.py:611
  79.2 10.1 %collective-permute-start.22 = (bf16[2,336,256]{2,1,0:T(8,128)(2,1)S(1)}, bf16[2,336,256]{2,1,0:T(8,128)(2,1)S(1)}, u32[]{:S(2)}, u32[]{:S(2)}) collective-permute-start(bf16[2,336,256]{2,1,0:T(8,128)(2,1)S(1)} %copy-done.15), channel_id=1, source_target_pairs={{0,16},{8,24},{16,0},{24,8},{1,17},{9,25},{17,1},{25,9},{2,18},{10... | collective-permute-start | bytes 1032200 | tf_op jit(solution)/shard_map/ppermute | solution.py:510
  79.7 11.6 %collective-permute-start.27 = (bf16[2,336,256]{2,1,0:T(8,128)(2,1)}, bf16[2,336,256]{2,1,0:T(8,128)(2,1)S(1)}, u32[]{:S(2)}, u32[]{:S(2)}) collective-permute-start(bf16[2,336,256]{2,1,0:T(8,128)(2,1)} %get-tuple-element.70), channel_id=1, source_target_pairs={{0,8},{8,0},{16,24},{24,16},{1,9},{9,1},{17,25},{25,17},{2,10},{10... | collective-permute-start | bytes 1032200 | tf_op jit(solution)/shard_map/ppermute | solution.py:510
  81.7 12.5 %collective-permute-start.13 = (bf16[336,256]{1,0:T(8,128)(2,1)S(1)}, bf16[336,256]{1,0:T(8,128)(2,1)S(1)}, u32[]{:S(2)}, u32[]{:S(2)}) collective-permute-start(bf16[336,256]{1,0:T(8,128)(2,1)S(1)} %fusion.12), channel_id=1, source_target_pairs={{0,8},{8,0},{16,24},{24,16},{1,9},{9,1},{17,25},{25,17},{2,10},{10... | collective-permute-start | bytes 516104 | tf_op jit(solution)/shard_map/ppermute | solution.py:510
  84.3 5.0 %copy-start.7 = (bf16[2,336,256]{2,1,0:T(8,128)(2,1)S(1)}, bf16[2,336,256]{2,1,0:T(8,128)(2,1)}, u32[]{:S(2)}) copy-start(bf16[2,336,256]{2,1,0:T(8,128)(2,1)} %get-tuple-element.67) | copy-start | bytes 1032196
  84.3 11.4 %collective-permute-start.18 = (bf16[336,256]{1,0:T(8,128)(2,1)S(1)}, bf16[336,256]{1,0:T(8,128)(2,1)S(1)}, u32[]{:S(2)}, u32[]{:S(2)}) collective-permute-start(bf16[336,256]{1,0:T(8,128)(2,1)S(1)} %fusion.13), channel_id=1, source_target_pairs={{0,16},{8,24},{16,0},{24,8},{1,17},{9,25},{17,1},{25,9},{2,18},{10... | collective-permute-start | bytes 516104 | tf_op jit(solution)/shard_map/ppermute | solution.py:510
  89.4 7.2 %collective-permute-start.23 = (bf16[336,256]{1,0:T(8,128)(2,1)S(1)}, bf16[336,256]{1,0:T(8,128)(2,1)S(1)}, u32[]{:S(2)}, u32[]{:S(2)}) collective-permute-start(bf16[336,256]{1,0:T(8,128)(2,1)S(1)} %fusion.14), channel_id=1, source_target_pairs={{0,8},{8,0},{16,24},{24,16},{1,9},{9,1},{17,25},{25,17},{2,10},{10... | collective-permute-start | bytes 516104 | tf_op jit(solution)/shard_map/ppermute | solution.py:510
  91.4 6.6 %collective-permute-start.28 = (bf16[336,256]{1,0:T(8,128)(2,1)S(1)}, bf16[336,256]{1,0:T(8,128)(2,1)S(1)}, u32[]{:S(2)}, u32[]{:S(2)}) collective-permute-start(bf16[336,256]{1,0:T(8,128)(2,1)S(1)} %fusion.15), channel_id=1, source_target_pairs={{0,16},{8,24},{16,0},{24,8},{1,17},{9,25},{17,1},{25,9},{2,18},{10... | collective-permute-start | bytes 516104 | tf_op jit(solution)/shard_map/ppermute | solution.py:510
  94.3 5.3 %collective-permute-start.14 = (bf16[336,128]{1,0:T(8,128)(2,1)S(1)}, bf16[336,128]{1,0:T(8,128)(2,1)S(1)}, u32[]{:S(2)}, u32[]{:S(2)}) collective-permute-start(bf16[336,128]{1,0:T(8,128)(2,1)S(1)} %select_convert_fusion.3), channel_id=1, source_target_pairs={{0,1},{1,0},{2,3},{3,2},{4,5},{5,4},{6,7},{7,6},{8,9},{9,8},{10,11... | collective-permute-start | bytes 258056 | tf_op jit(solution)/shard_map/ppermute | solution.py:510
  95.8 6.5 %collective-permute-start.19 = (bf16[336,128]{1,0:T(8,128)(2,1)S(1)}, bf16[336,128]{1,0:T(8,128)(2,1)S(1)}, u32[]{:S(2)}, u32[]{:S(2)}) collective-permute-start(bf16[336,128]{1,0:T(8,128)(2,1)S(1)} %select_convert_fusion.2), channel_id=1, source_target_pairs={{0,1},{1,0},{2,3},{3,2},{4,5},{5,4},{6,7},{7,6},{8,9},{9,8},{10,11... | collective-permute-start | bytes 258056 | tf_op jit(solution)/shard_map/ppermute | solution.py:510
  96.6 7.3 %collective-permute-start.24 = (bf16[336,128]{1,0:T(8,128)(2,1)S(1)}, bf16[336,128]{1,0:T(8,128)(2,1)S(1)}, u32[]{:S(2)}, u32[]{:S(2)}) collective-permute-start(bf16[336,128]{1,0:T(8,128)(2,1)S(1)} %select_convert_fusion.1), channel_id=1, source_target_pairs={{0,1},{1,0},{2,3},{3,2},{4,5},{5,4},{6,7},{7,6},{8,9},{9,8},{10,11... | collective-permute-start | bytes 258056 | tf_op jit(solution)/shard_map/ppermute | solution.py:510
  98.2 7.8 %collective-permute-start.29 = (bf16[336,128]{1,0:T(8,128)(2,1)S(1)}, bf16[336,128]{1,0:T(8,128)(2,1)S(1)}, u32[]{:S(2)}, u32[]{:S(2)}) collective-permute-start(bf16[336,128]{1,0:T(8,128)(2,1)S(1)} %select_convert_fusion), channel_id=1, source_target_pairs={{0,1},{1,0},{2,3},{3,2},{4,5},{5,4},{6,7},{7,6},{8,9},{9,8},{10,11... | collective-permute-start | bytes 258056 | tf_op jit(solution)/shard_map/ppermute | solution.py:510
  99.7 10.1 %collective-permute-start.15 = (bf16[336,128]{1,0:T(8,128)(2,1)S(1)}, bf16[336,128]{1,0:T(8,128)(2,1)S(1)}, u32[]{:S(2)}, u32[]{:S(2)}) collective-permute-start(bf16[336,128]{1,0:T(8,128)(2,1)S(1)} %add_convert_fusion.7), channel_id=1, source_target_pairs={{0,2},{1,3},{2,0},{3,1},{4,6},{5,7},{6,4},{7,5},{8,10},{9,11},{10,... | collective-permute-start | bytes 258056 | tf_op jit(solution)/shard_map/ppermute | solution.py:510
  102.3 10.4 %collective-permute-start.20 = (bf16[336,128]{1,0:T(8,128)(2,1)S(1)}, bf16[336,128]{1,0:T(8,128)(2,1)S(1)}, u32[]{:S(2)}, u32[]{:S(2)}) collective-permute-start(bf16[336,128]{1,0:T(8,128)(2,1)S(1)} %add_convert_fusion.5), channel_id=1, source_target_pairs={{0,2},{1,3},{2,0},{3,1},{4,6},{5,7},{6,4},{7,5},{8,10},{9,11},{10,... | collective-permute-start | bytes 258056 | tf_op jit(solution)/shard_map/ppermute | solution.py:510
  104.0 8.6 %collective-permute-start.25 = (bf16[336,128]{1,0:T(8,128)(2,1)S(1)}, bf16[336,128]{1,0:T(8,128)(2,1)S(1)}, u32[]{:S(2)}, u32[]{:S(2)}) collective-permute-start(bf16[336,128]{1,0:T(8,128)(2,1)S(1)} %add_convert_fusion.3), channel_id=1, source_target_pairs={{0,2},{1,3},{2,0},{3,1},{4,6},{5,7},{6,4},{7,5},{8,10},{9,11},{10,... | collective-permute-start | bytes 258056 | tf_op jit(solution)/shard_map/ppermute | solution.py:510
  106.0 8.8 %collective-permute-start.30 = (bf16[336,128]{1,0:T(8,128)(2,1)S(1)}, bf16[336,128]{1,0:T(8,128)(2,1)S(1)}, u32[]{:S(2)}, u32[]{:S(2)}) collective-permute-start(bf16[336,128]{1,0:T(8,128)(2,1)S(1)} %add_convert_fusion.1), channel_id=1, source_target_pairs={{0,2},{1,3},{2,0},{3,1},{4,6},{5,7},{6,4},{7,5},{8,10},{9,11},{10,... | collective-permute-start | bytes 258056 | tf_op jit(solution)/shard_map/ppermute | solution.py:510
  109.8 9.5 %collective-permute-start.16 = (bf16[336,128]{1,0:T(8,128)(2,1)S(1)}, bf16[336,128]{1,0:T(8,128)(2,1)S(1)}, u32[]{:S(2)}, u32[]{:S(2)}) collective-permute-start(bf16[336,128]{1,0:T(8,128)(2,1)S(1)} %add_convert_fusion.6.refs_0_), channel_id=1, source_target_pairs={{0,1},{1,0},{2,3},{3,2},{4,5},{5,4},{6,7},{7,6},{8,9},{9,8},{10,11... | collective-permute-start | bytes 258056 | tf_op jit(solution)/shard_map/ppermute | solution.py:510
  112.7 5.2 %collective-permute-start.33 = (bf16[128,256]{1,0:T(8,128)(2,1)S(1)}, bf16[128,256]{1,0:T(8,128)(2,1)S(1)}, u32[]{:S(2)}, u32[]{:S(2)}) collective-permute-start(bf16[128,256]{1,0:T(8,128)(2,1)S(1)} %pad_maximum_fusion.1), channel_id=1, source_target_pairs={{0,17},{1,16},{2,19},{3,18},{8,25},{9,24},{10,27},{11,26},{16,1},{... | collective-permute-start | bytes 196616 | tf_op jit(solution)/shard_map/ppermute | solution.py:652
  112.8 6.5 %collective-permute-start.32 = (bf16[128,256]{1,0:T(8,128)(2,1)S(1)}, bf16[128,256]{1,0:T(8,128)(2,1)S(1)}, u32[]{:S(2)}, u32[]{:S(2)}) collective-permute-start(bf16[128,256]{1,0:T(8,128)(2,1)S(1)} %pad_maximum_fusion.1), channel_id=1, source_target_pairs={{0,16},{8,24},{16,0},{24,8},{1,17},{9,25},{17,1},{25,9},{2,18},{10... | collective-permute-start | bytes 196616 | tf_op jit(solution)/shard_map/ppermute | solution.py:510
  114.8 6.2 %collective-permute-start.26 = (bf16[336,128]{1,0:T(8,128)(2,1)S(1)}, bf16[336,128]{1,0:T(8,128)(2,1)S(1)}, u32[]{:S(2)}, u32[]{:S(2)}) collective-permute-start(bf16[336,128]{1,0:T(8,128)(2,1)S(1)} %add_convert_fusion.2.refs_4_), channel_id=1, source_target_pairs={{0,1},{1,0},{2,3},{3,2},{4,5},{5,4},{6,7},{7,6},{8,9},{9,8},{10,11... | collective-permute-start | bytes 258056 | tf_op jit(solution)/shard_map/ppermute | solution.py:510
  116.4 4.6 %collective-permute-start.21 = (bf16[336,128]{1,0:T(8,128)(2,1)S(1)}, bf16[336,128]{1,0:T(8,128)(2,1)S(1)}, u32[]{:S(2)}, u32[]{:S(2)}) collective-permute-start(bf16[336,128]{1,0:T(8,128)(2,1)S(1)} %add_convert_fusion.4.refs_2_), channel_id=1, source_target_pairs={{0,1},{1,0},{2,3},{3,2},{4,5},{5,4},{6,7},{7,6},{8,9},{9,8},{10,11... | collective-permute-start | bytes 258056 | tf_op jit(solution)/shard_map/ppermute | solution.py:510
  117.9 4.5 %collective-permute-start.31 = (bf16[336,128]{1,0:T(8,128)(2,1)S(1)}, bf16[336,128]{1,0:T(8,128)(2,1)S(1)}, u32[]{:S(2)}, u32[]{:S(2)}) collective-permute-start(bf16[336,128]{1,0:T(8,128)(2,1)S(1)} %add_convert_fusion.refs_6_), channel_id=1, source_target_pairs={{0,1},{1,0},{2,3},{3,2},{4,5},{5,4},{6,7},{7,6},{8,9},{9,8},{10,11... | collective-permute-start | bytes 258056 | tf_op jit(solution)/shard_map/ppermute | solution.py:510
  119.3 3.1 %copy-start.26 = (bf16[128,256]{1,0:T(8,128)(2,1)}, bf16[128,256]{1,0:T(8,128)(2,1)S(1)}, u32[]{:S(2)}) copy-start(bf16[128,256]{1,0:T(8,128)(2,1)S(1)} %collective-permute-done.32.refs_8_) | copy-start | bytes 196612
  (16 other events, 26.8 us)

commit v7 on v6

--- a/solution.py
+++ b/solution.py
@@ -44,6 +44,14 @@
         self.used += 1
         copy.start()
         return copy
+
+
+def waiter(started):
+    def need(*names):
+        for name in names:
+            wait_all(started.pop(name, ()))
+
+    return need
 
 
 def wait_all(copies):
@@ -234,10 +242,14 @@
 RECORDS = ("normed", "inverse", "hidden", "qkv", "mix", "probs")
 
 
-def backward(grad_out, w, gain, mask_shape, room, grad_mix, grad_proj):
+def backward(grad_out, w, gain_of, mask_shape, room, grad_mix, grad_proj, need):
     feature = grad_out.shape[1]
+    need("grad_out", "out")
     grad_mix[...] = dot_nt(grad_out[...], w["out"][...]).astype(BF16)
+    need("qkv", "probs")
     attend_back(room["qkv"], room["probs"], grad_mix, grad_proj, mask_shape, feature)
+    need("q", "k", "v", "normed", "inverse", "gain")
+    gain = gain_of()
     grad_hidden = sum(
         dot_nt(grad_proj[:, i * feature : (i + 1) * feature], w[name][...])
         for i, name in enumerate(("q", "k", "v"))
@@ -254,7 +266,7 @@
     return (grad_update.astype(BF16), grad_gain)
 
 
-def send_grads(copies, x, hidden, mix, grad_out, grad_proj, grad_update, grad_gain, dw, outs):
+def send_grads(copies, x, hidden, mix, grad_out, grad_proj, grad_update, gain_of, dw, outs, need):
     feature = x.shape[1]
     shards = 2 * outs[0].shape[0]
     first, second, half = layout(feature, shards)
@@ -289,7 +301,9 @@
         part = grad_proj[:, i * feature : (i + 1) * feature]
         return dot_tn(hidden[...], part).astype(BF16)
 
+    need("mix", "grad_out")
     put("out", dot_tn(mix[...], grad_out[...]).astype(BF16), lambda i: i * rows)
+    need("hidden", "grad_proj")
     grad_k = of_projection(1)
     put("k1", grad_k, lambda i: i * rows + rows // 2)
     put("v", of_projection(2), lambda i: i * rows)
@@ -298,11 +312,14 @@
     put("k0", grad_k, lambda i: i * rows)
     put("q", of_projection(0), lambda i: i * rows)
     start = first["gain"][0]
+    need("grad_gain")
+    grad_gain = gain_of()
     for i in range(shards):
         part = grad_gain[:, i * rows : (i + 1) * rows].astype(BF16)
         dw_first[i, start : start + PAD, :] = jnp.zeros((PAD, feature), BF16)
         dw_first[i, start : start + PAD, :rows] = jnp.broadcast_to(part, (PAD, rows))
     emit(0, first["q"][0], half - first["q"][0])
+    need("x", "grad_update")
     put("merge", dot_tn(x[...], grad_update[...]).astype(BF16),
         lambda i: (i % 2) * 2 * rows + (i // 2) * rows)
     emit(0, 0, first["merge"][1])
@@ -389,7 +406,8 @@
         y_s[...] = result.astype(BF16)
         wait_all(tokens)
         done += [copies.start(y_s, y), copies.start(g, g_out)]
-        grad_update, grad_gain = backward(g, w, full_gain(wg, shards), mask.shape, room, gmix, gproj)
+        grad_update, grad_gain = backward(g, w, lambda: full_gain(wg, shards), mask.shape, room, gmix, gproj,
+                                          waiter({}))
         done.append(copies.start(gproj, proj_out))
         gain_s[...] = jnp.broadcast_to(grad_gain, gain_s.shape)
         update_s[...] = grad_update
@@ -406,9 +424,12 @@
     @role(1)
     def run():
         copies = Copies(sems)
-        wait_all([copies.start(a, b) for a, b in zip(ins, scratch)])
+        names = ("x", "grad_gain", "grad_out", "hidden", "mix", "grad_proj", "grad_update")
+        arrays = dict(zip(names, zip(ins, scratch)))
+        order = ("mix", "grad_out", "hidden", "grad_proj", "grad_gain", "x", "grad_update")
+        need = waiter({name: [copies.start(*arrays[name])] for name in order})
         x, gain, g, hidden, mix, gproj, update = scratch
-        wait_all(send_grads(copies, x, hidden, mix, g, gproj, update, gain[:1, :], dw, outs))
+        wait_all(send_grads(copies, x, hidden, mix, g, gproj, update, lambda: gain[:1, :], dw, outs, need))
 
 
 def first_kernel(*refs):
@@ -427,18 +448,23 @@
         micro, size = own.shape[:2]
         copies = Copies(sems)
         w = {"q": wq, "k": wk, "v": wv, "out": wo, "gain": wg}
-        early = [copies.start(g0, g)]
-        names = ("out", "q", "k", "v", "gain")
-        waits = load_weights(copies, pieces, names, w)
-        early += [copies.start(a, b) for a, b in zip(saved, rooms)]
-        early += load_tokens(copies, moved, own, x)
-        wait_all(early)
-        for name in names:
-            wait_all(waits[name])
         room = dict(zip(RECORDS, rooms))
-        grad_update, grad_gain = backward(g, w, full_gain(wg, shards), (micro, size), room, gmix, gproj)
-        wait_all(send_grads(copies, x, room["hidden"], room["mix"], g, gproj, grad_update, grad_gain,
-                            (dw_first, dw_second), outs))
+        started = {"grad_out": [copies.start(g0, g)]}
+
+        def fetch(*names):
+            for name in names:
+                if name in w:
+                    started.update(load_weights(copies, pieces, (name,), w))
+                else:
+                    started[name] = [copies.start(saved[RECORDS.index(name)], room[name])]
+
+        fetch("out", "qkv", "probs", "q", "k", "v", "normed", "inverse", "gain", "mix", "hidden")
+        started["x"] = load_tokens(copies, moved, own, x)
+        need = waiter(started)
+        grad_update, grad_gain = backward(g, w, lambda: full_gain(wg, shards), (micro, size), room,
+                                          gmix, gproj, need)
+        wait_all(send_grads(copies, x, room["hidden"], room["mix"], g, gproj, grad_update,
+                            lambda: grad_gain, (dw_first, dw_second), outs, need))
 
 
 def rest_kernel(merge, got, out, gain, packed):
@@ -547,6 +573,7 @@
         out_shape=shape(2 * rows + PAD, feature),
         in_specs=[VMEM] * 4,
         out_specs=VMEM,
+        compiler_params=pltpu.CompilerParams(vmem_limit_bytes=16 << 20),
         name="pack",
     )(merge, got, out, norm_gain)
     pieces = gather(qkv, rest)
@@ -658,6 +685,7 @@
         ),
         in_specs=[VMEM] * len(halves),
         out_specs=(VMEM,) * 4,
+        compiler_params=pltpu.CompilerParams(vmem_limit_bytes=16 << 20),
         name="unpack",
     )(*halves)
     return (section_out, merge_grad, qkv_grad, out_grad, gain_grad)

time: 126 us -> 122 us (0.968)
  Pallas kernels: 20 us -> 16.5 us
  starting transfers between devices: 55.2 us -> 52.6 us
  waiting for transfers between devices: 42.3 us -> 44.1 us
    ppermute x28, starting transfers between devices: 45.5 us -> 43 us  [flip(): return lax.ppermute(value, axis, [(i, i ^ bit) for i in range(size)])]
    pallas_call x1, Pallas kernels: 1.87 us -> 0.06 us  [body(): pl.pallas_call(rest_kernel, out_shape=shape(2 * rows + PAD, feature), in_...]
    unnamed x60 -> x44, local copies, waits for them, and re-layouts: 3.48 us -> 2.83 us
  transfers between devices with their start and end apart: 34 -> 34, of which waited for: 13 -> 14; matrix products, arithmetic and copies ran while one was open for 3% -> 3% of each run, Pallas kernels for 2% -> 1%
where the time goes in v7:
time: 122 us; the launch traced here: 121 us
  starting transfers between devices  52.6 us (43%)
  waiting for transfers between devices  44.1 us (36%)
  Pallas kernels  16.5 us (14%)
  other arithmetic  3.56 us (3%)
  local copies, waits for them, and re-layouts  3.51 us (3%)
    ppermute x28, starting transfers between devices, flip(): return lax.ppermute(value, axis, [(i, i ^ bit) for i in range(size)])  43 us
    ppermute x28, waiting for transfers between devices, flip(): return lax.ppermute(value, axis, [(i, i ^ bit) for i in range(size)])  29.5 us
    pallas_call x4, Pallas kernels, call(): pl.pallas_call(kernel, out_shape=tuple(outs), in_specs=[ANY] * len(ins),...  15.2 us
    ppermute x1, waiting for transfers between devices, body(): g0 = lax.ppermute(g_out, 'segment', [(1, 0)])  7.25 us
    ppermute x1, waiting for transfers between devices, body(): moved = lax.ppermute(source, 'band', down)  4.53 us
    ppermute x1, starting transfers between devices, body(): back = lax.ppermute(y[:, :part], 'band', up)  3.66 us
    unnamed x44, local copies, waits for them, and re-layouts  2.83 us
  transfers between devices with their start and end apart: 34, of which 14 were waited for; matrix products, arithmetic and copies ran while one was open for 3% of the time, Pallas kernels for 1%

profile of v7, /device:TPU:0, one launch (start us, length us, event | category | flops | bytes accessed | tf_op | source)
XLA Modules:
  0.0 121.3 jit_solution(6332417682105328402)
XLA Ops:
  0.6 3.1 %collective-permute-start.3 = (bf16[128,1536]{1,0:T(8,128)(2,1)}, bf16[128,1536]{1,0:T(8,128)(2,1)S(1)}, u32[]{:S(2)}, u32[]{:S(2)}) collective-permute-start(bf16[128,1536]{1,0:T(8,128)(2,1)} %bitcast.44), channel_id=1, source_target_pairs={{0,16},{8,24},{16,0},{24,8},{1,17},{9,25},{17,1},{25,9},{2,18},{10... | collective-permute-start | bytes 1179656 | tf_op jit(solution)/shard_map/ppermute | solution.py:536
  3.7 1.0 select_bitcast_fusion
  4.8 11.0 %collective-permute-done.5.got = bf16[128,512]{1,0:T(8,128)(2,1)S(1)} collective-permute-done((bf16[128,512]{1,0:T(8,128)(2,1)S(1)}, bf16[128,512]{1,0:T(8,128)(2,1)S(1)}, u32[]{:S(2)}, u32[]{:S(2)}) %collective-permute-start.5) | collective-permute-done | bytes 131104 | tf_op jit(solution)/shard_map/ppermute | solution.py:536
  16.6 1.8 %collective-permute-start.6 = (bf16[272,512]{1,0:T(8,128)(2,1)S(1)}, bf16[272,512]{1,0:T(8,128)(2,1)S(1)}, u32[]{:S(2)}, u32[]{:S(2)}) collective-permute-start(bf16[272,512]{1,0:T(8,128)(2,1)S(1)} %pack.1.refs_7_.refs_8_), channel_id=1, source_target_pairs={{0,8},{8,0},{16,24},{24,16},{1,9},{9,1},{17,25},{25,17},{2,10},{10... | collective-permute-start | bytes 835592 | tf_op jit(solution)/shard_map/ppermute | solution.py:536
  18.4 0.9 collective-permute-start.2
  19.3 1.1 collective-permute-start.4
  20.4 1.6 %collective-permute-start = (s32[2,4,16]{2,1,0:T(4,128)S(1)}, s32[2,4,16]{2,1,0:T(4,128)S(1)}, u32[]{:S(2)}, u32[]{:S(2)}) collective-permute-start(s32[2,4,16]{2,1,0:T(4,128)S(1)} %get-tuple-element.77), channel_id=1, source_target_pairs={{0,1},{1,2},{2,3},{3,0},{4,5},{5,6},{6,7},{7,4},{8,9},{9,10},{10,1... | collective-permute-start | bytes 1544 | tf_op jit(solution)/shard_map/ppermute | solution.py:587
  22.0 1.5 %collective-permute-start.7 = (bf16[272,512]{1,0:T(8,128)(2,1)S(1)}, bf16[272,512]{1,0:T(8,128)(2,1)S(1)}, u32[]{:S(2)}, u32[]{:S(2)}) collective-permute-start(bf16[272,512]{1,0:T(8,128)(2,1)S(1)} %pack.1.refs_7_.refs_8_), channel_id=1, source_target_pairs={{0,16},{8,24},{16,0},{24,8},{1,17},{9,25},{17,1},{25,9},{2,18},{10... | collective-permute-start | bytes 835592 | tf_op jit(solution)/shard_map/ppermute | solution.py:536
  23.5 2.7 %collective-permute-done.6.refs_8_.refs_9_ = bf16[272,512]{1,0:T(8,128)(2,1)S(1)} collective-permute-done((bf16[272,512]{1,0:T(8,128)(2,1)S(1)}, bf16[272,512]{1,0:T(8,128)(2,1)S(1)}, u32[]{:S(2)}, u32[]{:S(2)}) %collective-permute-start.6) | collective-permute-done | bytes 278560 | tf_op jit(solution)/shard_map/ppermute | solution.py:536
  26.2 1.7 %collective-permute-start.8 = (bf16[272,512]{1,0:T(8,128)(2,1)S(1)}, bf16[272,512]{1,0:T(8,128)(2,1)S(1)}, u32[]{:S(2)}, u32[]{:S(2)}) collective-permute-start(bf16[272,512]{1,0:T(8,128)(2,1)S(1)} %collective-permute-done.6.refs_8_.refs_9_), channel_id=1, source_target_pairs={{0,16},{8,24},{16,0},{24,8},{1,17},{9,25},{17,1},{25,9},{2,18},{10... | collective-permute-start | bytes 835592 | tf_op jit(solution)/shard_map/ppermute | solution.py:536
  27.9 0.9 select_bitcast_fusion.1
  28.8 1.6 %collective-permute-start.1 = (bf16[2,4,16,512]{3,2,1,0:T(8,128)(2,1)S(1)}, bf16[2,4,16,512]{3,2,1,0:T(8,128)(2,1)S(1)}, u32[]{:S(2)}, u32[]{:S(2)}) collective-permute-start(bf16[2,4,16,512]{3,2,1,0:T(8,128)(2,1)S(1)} %select_bitcast_fusion.1), channel_id=1, source_target_pairs={{0,1},{1,2},{2,3},{3,0},{4,5},{5,6},{6,7},{7,4},{8,9},{9,10},{10,1... | collective-permute-start | bytes 393224 | tf_op jit(solution)/shard_map/ppermute | solution.py:585
  31.1 4.5 %collective-permute-done.1 = bf16[2,4,16,512]{3,2,1,0:T(8,128)(2,1)S(1)} collective-permute-done((bf16[2,4,16,512]{3,2,1,0:T(8,128)(2,1)S(1)}, bf16[2,4,16,512]{3,2,1,0:T(8,128)(2,1)S(1)}, u32[]{:S(2)}, u32[]{:S(2)}) %collective-permute-start.1) | collective-permute-done | bytes 131104 | tf_op jit(solution)/shard_map/ppermute | solution.py:585
  35.7 5.6 %collective-permute-done.4.refs_6_.refs_7_ = bf16[128,1536]{1,0:T(8,128)(2,1)S(1)} collective-permute-done((bf16[128,1536]{1,0:T(8,128)(2,1)S(1)}, bf16[128,1536]{1,0:T(8,128)(2,1)S(1)}, u32[]{:S(2)}, u32[]{:S(2)}) %collective-permute-start.4) | collective-permute-done | bytes 393248 | tf_op jit(solution)/shard_map/ppermute | solution.py:536
  42.1 5.9 %shard_map.110 = (bf16[256,512]{1,0:T(8,128)(2,1)}, f32[256,512]{1,0:T(8,128)}, f32[256,128]{1,0:T(8,128)}, bf16[256,512]{1,0:T(8,128)(2,1)}, bf16[256,1536]{1,0...) custom-call(s32[2,128]{1,0:T(2,128)} %reshape.54.refs_0_, bf16[2,64,512]{2,1,0:T(8,128)(2,1)} %bitcast.49, ...), custom_call_target="tpu_custom_call" | custom-call | flops 805306368 | bytes 5833728 | tf_op jit(solution)/shard_map/pallas_call | solution.py:523
  47.9 1.3 %collective-permute-start.9 = (bf16[256,512]{1,0:T(8,128)(2,1)}, bf16[256,512]{1,0:T(8,128)(2,1)S(1)}, u32[]{:S(2)}, u32[]{:S(2)}) collective-permute-start(bf16[256,512]{1,0:T(8,128)(2,1)} %get-tuple-element.40.refs_12_), channel_id=1, source_target_pairs={{0,4},{1,5},{2,6},{3,7},{8,12},{9,13},{10,14},{11,15},{16,20},{17,... | collective-permute-start | bytes 786440 | tf_op jit(solution)/shard_map/ppermute | solution.py:615
  49.2 1.3 %collective-permute-done.9.refs_3_.refs_0_ = bf16[256,512]{1,0:T(8,128)(2,1)S(1)} collective-permute-done((bf16[256,512]{1,0:T(8,128)(2,1)}, bf16[256,512]{1,0:T(8,128)(2,1)S(1)}, u32[]{:S(2)}, u32[]{:S(2)}) %collective-permute-start.9) | collective-permute-done | bytes 262176 | tf_op jit(solution)/shard_map/ppermute | solution.py:615
  51.3 1.1 shard_map.111
  52.4 1.3 %collective-permute-start.11 = (bf16[256,512]{1,0:T(8,128)(2,1)}, bf16[256,512]{1,0:T(8,128)(2,1)S(1)}, u32[]{:S(2)}, u32[]{:S(2)}) collective-permute-start(bf16[256,512]{1,0:T(8,128)(2,1)} %get-tuple-element.42), channel_id=1, source_target_pairs={{4,0},{5,1},{6,2},{7,3},{12,8},{13,9},{14,10},{15,11},{20,16},{21,... | collective-permute-start | bytes 786440 | tf_op jit(solution)/shard_map/ppermute | solution.py:626
  53.7 1.2 shard_map.112
  54.9 7.2 %collective-permute-done.11.refs_3_ = bf16[256,512]{1,0:T(8,128)(2,1)S(1)} collective-permute-done((bf16[256,512]{1,0:T(8,128)(2,1)}, bf16[256,512]{1,0:T(8,128)(2,1)S(1)}, u32[]{:S(2)}, u32[]{:S(2)}) %collective-permute-start.11) | collective-permute-done | bytes 262176 | tf_op jit(solution)/shard_map/ppermute | solution.py:626
  62.1 0.7 copy-done.18
  62.9 7.0 %shard_map.113 = (bf16[2,336,256]{2,1,0:T(8,128)(2,1)}, bf16[2,336,256]{2,1,0:T(8,128)(2,1)}, bf16[2,336,256]{2,1,0:T(8,128)(2,1)}, bf16[2,336,256]{2,1,0:T(8,12...) custom-call(s32[2,128]{1,0:T(2,128)} %reshape.54.refs_0_, ...), custom_call_target="tpu_custom_call", output_to_operand_aliasing={{0}: (18, {}), {1}: (19, {}), {2}: (20, {}), {3}: (21, {}),... | custom-call | flops 1610612736 | bytes 11338752 | tf_op jit(solution)/shard_map/pallas_call | solution.py:523
  69.9 1.5 %collective-permute-start.12 = (bf16[2,336,256]{2,1,0:T(8,128)(2,1)}, bf16[2,336,256]{2,1,0:T(8,128)(2,1)S(1)}, u32[]{:S(2)}, u32[]{:S(2)}) collective-permute-start(bf16[2,336,256]{2,1,0:T(8,128)(2,1)} %get-tuple-element.64), channel_id=1, source_target_pairs={{0,16},{8,24},{16,0},{24,8},{1,17},{9,25},{17,1},{25,9},{2,18},{10... | collective-permute-start | bytes 1032200 | tf_op jit(solution)/shard_map/ppermute | solution.py:536
  71.4 1.5 %collective-permute-start.17 = (bf16[2,336,256]{2,1,0:T(8,128)(2,1)}, bf16[2,336,256]{2,1,0:T(8,128)(2,1)S(1)}, u32[]{:S(2)}, u32[]{:S(2)}) collective-permute-start(bf16[2,336,256]{2,1,0:T(8,128)(2,1)} %get-tuple-element.66), channel_id=1, source_target_pairs={{0,8},{8,0},{16,24},{24,16},{1,9},{9,1},{17,25},{25,17},{2,10},{10... | collective-permute-start | bytes 1032200 | tf_op jit(solution)/shard_map/ppermute | solution.py:536
  72.9 3.7 %collective-permute-start.10 = (bf16[2,64,512]{2,1,0:T(8,128)(2,1)S(1)}, bf16[2,64,512]{2,1,0:T(8,128)(2,1)S(1)}, u32[]{:S(2)}, u32[]{:S(2)}) collective-permute-start(bf16[2,64,512]{2,1,0:T(8,128)(2,1)S(1)} %get-tuple-element.76), channel_id=1, source_target_pairs={{1,0},{2,1},{3,2},{0,3},{5,4},{6,5},{7,6},{4,7},{9,8},{10,9},{11,1... | collective-permute-start | bytes 393224 | tf_op jit(solution)/shard_map/ppermute | solution.py:638
  77.6 1.9 %collective-permute-done.12 = bf16[2,336,256]{2,1,0:T(8,128)(2,1)S(1)} collective-permute-done((bf16[2,336,256]{2,1,0:T(8,128)(2,1)}, bf16[2,336,256]{2,1,0:T(8,128)(2,1)S(1)}, u32[]{:S(2)}, u32[]{:S(2)}) %collective-permute-start.12) | collective-permute-done | bytes 344096 | tf_op jit(solution)/shard_map/ppermute | solution.py:536
  79.6 2.4 %collective-permute-start.13 = (bf16[336,256]{1,0:T(8,128)(2,1)S(1)}, bf16[336,256]{1,0:T(8,128)(2,1)S(1)}, u32[]{:S(2)}, u32[]{:S(2)}) collective-permute-start(bf16[336,256]{1,0:T(8,128)(2,1)S(1)} %fusion.12), channel_id=1, source_target_pairs={{0,8},{8,0},{16,24},{24,16},{1,9},{9,1},{17,25},{25,17},{2,10},{10... | collective-permute-start | bytes 516104 | tf_op jit(solution)/shard_map/ppermute | solution.py:536
  82.1 2.3 %collective-permute-start.18 = (bf16[336,256]{1,0:T(8,128)(2,1)S(1)}, bf16[336,256]{1,0:T(8,128)(2,1)S(1)}, u32[]{:S(2)}, u32[]{:S(2)}) collective-permute-start(bf16[336,256]{1,0:T(8,128)(2,1)S(1)} %fusion.13), channel_id=1, source_target_pairs={{0,16},{8,24},{16,0},{24,8},{1,17},{9,25},{17,1},{25,9},{2,18},{10... | collective-permute-start | bytes 516104 | tf_op jit(solution)/shard_map/ppermute | solution.py:536
  84.4 2.8 %collective-permute-done.22 = bf16[2,336,256]{2,1,0:T(8,128)(2,1)S(1)} collective-permute-done((bf16[2,336,256]{2,1,0:T(8,128)(2,1)S(1)}, bf16[2,336,256]{2,1,0:T(8,128)(2,1)S(1)}, u32[]{:S(2)}, u32[]{:S(2)}) %collective-permute-start.22) | collective-permute-done | bytes 344096 | tf_op jit(solution)/shard_map/ppermute | solution.py:536
  87.4 1.8 %collective-permute-start.23 = (bf16[336,256]{1,0:T(8,128)(2,1)S(1)}, bf16[336,256]{1,0:T(8,128)(2,1)S(1)}, u32[]{:S(2)}, u32[]{:S(2)}) collective-permute-start(bf16[336,256]{1,0:T(8,128)(2,1)S(1)} %fusion.14), channel_id=1, source_target_pairs={{0,8},{8,0},{16,24},{24,16},{1,9},{9,1},{17,25},{25,17},{2,10},{10... | collective-permute-start | bytes 516104 | tf_op jit(solution)/shard_map/ppermute | solution.py:536
  89.3 2.2 %collective-permute-start.28 = (bf16[336,256]{1,0:T(8,128)(2,1)S(1)}, bf16[336,256]{1,0:T(8,128)(2,1)S(1)}, u32[]{:S(2)}, u32[]{:S(2)}) collective-permute-start(bf16[336,256]{1,0:T(8,128)(2,1)S(1)} %fusion.15), channel_id=1, source_target_pairs={{0,16},{8,24},{16,0},{24,8},{1,17},{9,25},{17,1},{25,9},{2,18},{10... | collective-permute-start | bytes 516104 | tf_op jit(solution)/shard_map/ppermute | solution.py:536
  91.9 1.6 %collective-permute-start.14 = (bf16[336,128]{1,0:T(8,128)(2,1)S(1)}, bf16[336,128]{1,0:T(8,128)(2,1)S(1)}, u32[]{:S(2)}, u32[]{:S(2)}) collective-permute-start(bf16[336,128]{1,0:T(8,128)(2,1)S(1)} %select_convert_fusion.3), channel_id=1, source_target_pairs={{0,1},{1,0},{2,3},{3,2},{4,5},{5,4},{6,7},{7,6},{8,9},{9,8},{10,11... | collective-permute-start | bytes 258056 | tf_op jit(solution)/shard_map/ppermute | solution.py:536
  94.2 1.6 %collective-permute-start.24 = (bf16[336,128]{1,0:T(8,128)(2,1)S(1)}, bf16[336,128]{1,0:T(8,128)(2,1)S(1)}, u32[]{:S(2)}, u32[]{:S(2)}) collective-permute-start(bf16[336,128]{1,0:T(8,128)(2,1)S(1)} %select_convert_fusion.1), channel_id=1, source_target_pairs={{0,1},{1,0},{2,3},{3,2},{4,5},{5,4},{6,7},{7,6},{8,9},{9,8},{10,11... | collective-permute-start | bytes 258056 | tf_op jit(solution)/shard_map/ppermute | solution.py:536
  95.9 1.3 %collective-permute-start.29 = (bf16[336,128]{1,0:T(8,128)(2,1)S(1)}, bf16[336,128]{1,0:T(8,128)(2,1)S(1)}, u32[]{:S(2)}, u32[]{:S(2)}) collective-permute-start(bf16[336,128]{1,0:T(8,128)(2,1)S(1)} %select_convert_fusion), channel_id=1, source_target_pairs={{0,1},{1,0},{2,3},{3,2},{4,5},{5,4},{6,7},{7,6},{8,9},{9,8},{10,11... | collective-permute-start | bytes 258056 | tf_op jit(solution)/shard_map/ppermute | solution.py:536
  97.5 2.4 %collective-permute-start.15 = (bf16[336,128]{1,0:T(8,128)(2,1)S(1)}, bf16[336,128]{1,0:T(8,128)(2,1)S(1)}, u32[]{:S(2)}, u32[]{:S(2)}) collective-permute-start(bf16[336,128]{1,0:T(8,128)(2,1)S(1)} %add_convert_fusion.7), channel_id=1, source_target_pairs={{0,2},{1,3},{2,0},{3,1},{4,6},{5,7},{6,4},{7,5},{8,10},{9,11},{10,... | collective-permute-start | bytes 258056 | tf_op jit(solution)/shard_map/ppermute | solution.py:536
  100.0 1.8 %collective-permute-start.20 = (bf16[336,128]{1,0:T(8,128)(2,1)S(1)}, bf16[336,128]{1,0:T(8,128)(2,1)S(1)}, u32[]{:S(2)}, u32[]{:S(2)}) collective-permute-start(bf16[336,128]{1,0:T(8,128)(2,1)S(1)} %add_convert_fusion.5), channel_id=1, source_target_pairs={{0,2},{1,3},{2,0},{3,1},{4,6},{5,7},{6,4},{7,5},{8,10},{9,11},{10,... | collective-permute-start | bytes 258056 | tf_op jit(solution)/shard_map/ppermute | solution.py:536
  101.8 1.8 %collective-permute-start.25 = (bf16[336,128]{1,0:T(8,128)(2,1)S(1)}, bf16[336,128]{1,0:T(8,128)(2,1)S(1)}, u32[]{:S(2)}, u32[]{:S(2)}) collective-permute-start(bf16[336,128]{1,0:T(8,128)(2,1)S(1)} %add_convert_fusion.3), channel_id=1, source_target_pairs={{0,2},{1,3},{2,0},{3,1},{4,6},{5,7},{6,4},{7,5},{8,10},{9,11},{10,... | collective-permute-start | bytes 258056 | tf_op jit(solution)/shard_map/ppermute | solution.py:536
  103.6 1.7 %collective-permute-done.29 = bf16[336,128]{1,0:T(8,128)(2,1)S(1)} collective-permute-done((bf16[336,128]{1,0:T(8,128)(2,1)S(1)}, bf16[336,128]{1,0:T(8,128)(2,1)S(1)}, u32[]{:S(2)}, u32[]{:S(2)}) %collective-permute-start.29) | collective-permute-done | bytes 86048 | tf_op jit(solution)/shard_map/ppermute | solution.py:536
  105.3 1.8 %collective-permute-start.30 = (bf16[336,128]{1,0:T(8,128)(2,1)S(1)}, bf16[336,128]{1,0:T(8,128)(2,1)S(1)}, u32[]{:S(2)}, u32[]{:S(2)}) collective-permute-start(bf16[336,128]{1,0:T(8,128)(2,1)S(1)} %add_convert_fusion.1), channel_id=1, source_target_pairs={{0,2},{1,3},{2,0},{3,1},{4,6},{5,7},{6,4},{7,5},{8,10},{9,11},{10,... | collective-permute-start | bytes 258056 | tf_op jit(solution)/shard_map/ppermute | solution.py:536
  107.2 3.0 %collective-permute-start.16 = (bf16[336,128]{1,0:T(8,128)(2,1)S(1)}, bf16[336,128]{1,0:T(8,128)(2,1)S(1)}, u32[]{:S(2)}, u32[]{:S(2)}) collective-permute-start(bf16[336,128]{1,0:T(8,128)(2,1)S(1)} %add_convert_fusion.6.refs_0_), channel_id=1, source_target_pairs={{0,1},{1,0},{2,3},{3,2},{4,5},{5,4},{6,7},{7,6},{8,9},{9,8},{10,11... | collective-permute-start | bytes 258056 | tf_op jit(solution)/shard_map/ppermute | solution.py:536
  110.5 1.3 %collective-permute-start.32 = (bf16[128,256]{1,0:T(8,128)(2,1)S(1)}, bf16[128,256]{1,0:T(8,128)(2,1)S(1)}, u32[]{:S(2)}, u32[]{:S(2)}) collective-permute-start(bf16[128,256]{1,0:T(8,128)(2,1)S(1)} %pad_maximum_fusion.1), channel_id=1, source_target_pairs={{0,16},{8,24},{16,0},{24,8},{1,17},{9,25},{17,1},{25,9},{2,18},{10... | collective-permute-start | bytes 196616 | tf_op jit(solution)/shard_map/ppermute | solution.py:536
  111.9 2.1 %collective-permute-start.26 = (bf16[336,128]{1,0:T(8,128)(2,1)S(1)}, bf16[336,128]{1,0:T(8,128)(2,1)S(1)}, u32[]{:S(2)}, u32[]{:S(2)}) collective-permute-start(bf16[336,128]{1,0:T(8,128)(2,1)S(1)} %add_convert_fusion.2.refs_4_), channel_id=1, source_target_pairs={{0,1},{1,0},{2,3},{3,2},{4,5},{5,4},{6,7},{7,6},{8,9},{9,8},{10,11... | collective-permute-start | bytes 258056 | tf_op jit(solution)/shard_map/ppermute | solution.py:536
  114.1 1.4 %collective-permute-done.33.refs_9_ = bf16[128,256]{1,0:T(8,128)(2,1)S(1)} collective-permute-done((bf16[128,256]{1,0:T(8,128)(2,1)S(1)}, bf16[128,256]{1,0:T(8,128)(2,1)S(1)}, u32[]{:S(2)}, u32[]{:S(2)}) %collective-permute-start.33) | collective-permute-done | bytes 65568 | tf_op jit(solution)/shard_map/ppermute | solution.py:679
  116.1 0.7 pad_maximum_fusion
  116.8 1.7 %collective-permute-done.21.refs_3_ = bf16[336,128]{1,0:T(8,128)(2,1)S(1)} collective-permute-done((bf16[336,128]{1,0:T(8,128)(2,1)S(1)}, bf16[336,128]{1,0:T(8,128)(2,1)S(1)}, u32[]{:S(2)}, u32[]{:S(2)}) %collective-permute-start.21) | collective-permute-done | bytes 86048 | tf_op jit(solution)/shard_map/ppermute | solution.py:536
  118.5 1.5 %collective-permute-done.31.refs_7_ = bf16[336,128]{1,0:T(8,128)(2,1)S(1)} collective-permute-done((bf16[336,128]{1,0:T(8,128)(2,1)S(1)}, bf16[336,128]{1,0:T(8,128)(2,1)S(1)}, u32[]{:S(2)}, u32[]{:S(2)}) %collective-permute-start.31) | collective-permute-done | bytes 86048 | tf_op jit(solution)/shard_map/ppermute | solution.py:536
  120.0 1.3 %unpack.1 = (f32[1,256,512]{2,1,0:T(8,128)}, f32[1,128,1536]{2,1,0:T(8,128)}, f32[1,128,512]{2,1,0:T(8,128)}, f32[1,128]{1,0:T(1,128)}) custom-call(bf16[336,128]{1,0:T(8,128)(2,1)S(1)} %add_convert_fusion.6.refs_0_, bf16[336,128]{1,0:T(8,128)(2,1)S(1)} %collective-permute-done.16.refs_1_, bf16[336,128]{1,0:T(8,128)(2,1)S(1)} %add_convert_fusion.4.refs_2_, ...), custom_call_target="tpu_custom_call" | custom-call | tf_op jit(solution)/shard_map/unpack/pallas_call | solution.py:680
  (104 shorter events, 6.9 us)
Async XLA Ops:
  0.6 15.2 %copy-start.1 = (bf16[1,256,512]{2,1,0:T(8,128)(2,1)S(1)}, bf16[1,256,512]{2,1,0:T(8,128)(2,1)}, u32[]{:S(2)}) copy-start(bf16[1,256,512]{2,1,0:T(8,128)(2,1)} %param.9) | copy-start | bytes 786436
  0.6 18.6 %collective-permute-start.3 = (bf16[128,1536]{1,0:T(8,128)(2,1)}, bf16[128,1536]{1,0:T(8,128)(2,1)S(1)}, u32[]{:S(2)}, u32[]{:S(2)}) collective-permute-start(bf16[128,1536]{1,0:T(8,128)(2,1)} %bitcast.44), channel_id=1, source_target_pairs={{0,16},{8,24},{16,0},{24,8},{1,17},{9,25},{17,1},{25,9},{2,18},{10... | collective-permute-start | bytes 1179656 | tf_op jit(solution)/shard_map/ppermute | solution.py:536
  3.7 12.1 %copy-start.2 = (bf16[1,128,512]{2,1,0:T(8,128)(2,1)S(1)}, bf16[1,128,512]{2,1,0:T(8,128)(2,1)}, u32[]{:S(2)}) copy-start(bf16[1,128,512]{2,1,0:T(8,128)(2,1)} %param.11) | copy-start | bytes 393220
  4.7 11.1 %collective-permute-start.5 = (bf16[128,512]{1,0:T(8,128)(2,1)S(1)}, bf16[128,512]{1,0:T(8,128)(2,1)S(1)}, u32[]{:S(2)}, u32[]{:S(2)}) collective-permute-start(bf16[128,512]{1,0:T(8,128)(2,1)S(1)} %select_bitcast_fusion), channel_id=1, source_target_pairs={{0,16},{8,24},{16,0},{24,8},{1,17},{9,25},{17,1},{25,9},{2,18},{10... | collective-permute-start | bytes 393224 | tf_op jit(solution)/shard_map/ppermute | solution.py:536
  16.5 3.9 %copy-start.20 = (s32[1,2,8,16]{3,2,1,0:T(8,128)S(1)}, s32[1,2,8,16]{3,2,1,0:T(8,128)}, u32[]{:S(2)}) copy-start(s32[1,2,8,16]{3,2,1,0:T(8,128)} %param.8) | copy-start | bytes 3076
  16.5 11.4 %copy-start.4 = (bf16[1,2,8,16,512]{4,3,2,1,0:T(8,128)(2,1)S(1)}, bf16[1,2,8,16,512]{4,3,2,1,0:T(8,128)(2,1)}, u32[]{:S(2)}) copy-start(bf16[1,2,8,16,512]{4,3,2,1,0:T(8,128)(2,1)} %param.7) | copy-start | bytes 786436
  16.6 24.8 %copy-start = (bf16[272,512]{1,0:T(8,128)(2,1)}, bf16[272,512]{1,0:T(8,128)(2,1)S(1)}, u32[]{:S(2)}) copy-start(bf16[272,512]{1,0:T(8,128)(2,1)S(1)} %pack.1.refs_7_.refs_8_) | copy-start | bytes 835588
  16.6 9.6 %collective-permute-start.6 = (bf16[272,512]{1,0:T(8,128)(2,1)S(1)}, bf16[272,512]{1,0:T(8,128)(2,1)S(1)}, u32[]{:S(2)}, u32[]{:S(2)}) collective-permute-start(bf16[272,512]{1,0:T(8,128)(2,1)S(1)} %pack.1.refs_7_.refs_8_), channel_id=1, source_target_pairs={{0,8},{8,0},{16,24},{24,16},{1,9},{9,1},{17,25},{25,17},{2,10},{10... | collective-permute-start | bytes 835592 | tf_op jit(solution)/shard_map/ppermute | solution.py:536
  18.4 17.3 %collective-permute-start.2 = (bf16[128,1536]{1,0:T(8,128)(2,1)S(1)}, bf16[128,1536]{1,0:T(8,128)(2,1)S(1)}, u32[]{:S(2)}, u32[]{:S(2)}) collective-permute-start(bf16[128,1536]{1,0:T(8,128)(2,1)S(1)} %bitcast.48), channel_id=1, source_target_pairs={{0,8},{8,0},{16,24},{24,16},{1,9},{9,1},{17,25},{25,17},{2,10},{10... | collective-permute-start | bytes 1179656 | tf_op jit(solution)/shard_map/ppermute | solution.py:536
  19.3 22.0 %copy-start.6 = (bf16[128,1536]{1,0:T(8,128)(2,1)}, bf16[128,1536]{1,0:T(8,128)(2,1)S(1)}, u32[]{:S(2)}) copy-start(bf16[128,1536]{1,0:T(8,128)(2,1)S(1)} %collective-permute-done.3.refs_5_.refs_6_) | copy-start | bytes 1179652
  19.3 22.0 %collective-permute-start.4 = (bf16[128,1536]{1,0:T(8,128)(2,1)S(1)}, bf16[128,1536]{1,0:T(8,128)(2,1)S(1)}, u32[]{:S(2)}, u32[]{:S(2)}) collective-permute-start(bf16[128,1536]{1,0:T(8,128)(2,1)S(1)} %collective-permute-done.3.refs_5_.refs_6_), channel_id=1, source_target_pairs={{0,8},{8,0},{16,24},{24,16},{1,9},{9,1},{17,25},{25,17},{2,10},{10... | collective-permute-start | bytes 1179656 | tf_op jit(solution)/shard_map/ppermute | solution.py:536
  20.4 8.4 %collective-permute-start = (s32[2,4,16]{2,1,0:T(4,128)S(1)}, s32[2,4,16]{2,1,0:T(4,128)S(1)}, u32[]{:S(2)}, u32[]{:S(2)}) collective-permute-start(s32[2,4,16]{2,1,0:T(4,128)S(1)} %get-tuple-element.77), channel_id=1, source_target_pairs={{0,1},{1,2},{2,3},{3,0},{4,5},{5,6},{6,7},{7,4},{8,9},{9,10},{10,1... | collective-permute-start | bytes 1544 | tf_op jit(solution)/shard_map/ppermute | solution.py:587
  22.0 13.7 %collective-permute-start.7 = (bf16[272,512]{1,0:T(8,128)(2,1)S(1)}, bf16[272,512]{1,0:T(8,128)(2,1)S(1)}, u32[]{:S(2)}, u32[]{:S(2)}) collective-permute-start(bf16[272,512]{1,0:T(8,128)(2,1)S(1)} %pack.1.refs_7_.refs_8_), channel_id=1, source_target_pairs={{0,16},{8,24},{16,0},{24,8},{1,17},{9,25},{17,1},{25,9},{2,18},{10... | collective-permute-start | bytes 835592 | tf_op jit(solution)/shard_map/ppermute | solution.py:536
  26.2 15.2 %copy-start.13 = (bf16[272,512]{1,0:T(8,128)(2,1)}, bf16[272,512]{1,0:T(8,128)(2,1)S(1)}, u32[]{:S(2)}) copy-start(bf16[272,512]{1,0:T(8,128)(2,1)S(1)} %collective-permute-done.6.refs_8_.refs_9_) | copy-start | bytes 835588
  26.2 9.5 %collective-permute-start.8 = (bf16[272,512]{1,0:T(8,128)(2,1)S(1)}, bf16[272,512]{1,0:T(8,128)(2,1)S(1)}, u32[]{:S(2)}, u32[]{:S(2)}) collective-permute-start(bf16[272,512]{1,0:T(8,128)(2,1)S(1)} %collective-permute-done.6.refs_8_.refs_9_), channel_id=1, source_target_pairs={{0,16},{8,24},{16,0},{24,8},{1,17},{9,25},{17,1},{25,9},{2,18},{10... | collective-permute-start | bytes 835592 | tf_op jit(solution)/shard_map/ppermute | solution.py:536
  28.8 6.8 %collective-permute-start.1 = (bf16[2,4,16,512]{3,2,1,0:T(8,128)(2,1)S(1)}, bf16[2,4,16,512]{3,2,1,0:T(8,128)(2,1)S(1)}, u32[]{:S(2)}, u32[]{:S(2)}) collective-permute-start(bf16[2,4,16,512]{3,2,1,0:T(8,128)(2,1)S(1)} %select_bitcast_fusion.1), channel_id=1, source_target_pairs={{0,1},{1,2},{2,3},{3,0},{4,5},{5,6},{6,7},{7,4},{8,9},{9,10},{10,1... | collective-permute-start | bytes 393224 | tf_op jit(solution)/shard_map/ppermute | solution.py:585
  35.7 5.7 %copy-start.16 = (bf16[2,4,16,512]{3,2,1,0:T(8,128)(2,1)}, bf16[2,4,16,512]{3,2,1,0:T(8,128)(2,1)S(1)}, u32[]{:S(2)}) copy-start(bf16[2,4,16,512]{3,2,1,0:T(8,128)(2,1)S(1)} %collective-permute-done.1) | copy-start | bytes 393220
  35.7 5.7 %copy-start.7 = (bf16[128,1536]{1,0:T(8,128)(2,1)}, bf16[128,1536]{1,0:T(8,128)(2,1)S(1)}, u32[]{:S(2)}) copy-start(bf16[128,1536]{1,0:T(8,128)(2,1)S(1)} %collective-permute-done.2.refs_4_.refs_5_) | copy-start | bytes 1179652
  35.7 5.7 %copy-start.14 = (bf16[272,512]{1,0:T(8,128)(2,1)}, bf16[272,512]{1,0:T(8,128)(2,1)S(1)}, u32[]{:S(2)}) copy-start(bf16[272,512]{1,0:T(8,128)(2,1)S(1)} %collective-permute-done.7.refs_9_.refs_10_) | copy-start | bytes 835588
  35.7 5.7 %copy-start.15 = (bf16[272,512]{1,0:T(8,128)(2,1)}, bf16[272,512]{1,0:T(8,128)(2,1)S(1)}, u32[]{:S(2)}) copy-start(bf16[272,512]{1,0:T(8,128)(2,1)S(1)} %collective-permute-done.8.refs_10_.refs_11_) | copy-start | bytes 835588
  47.9 2.7 %collective-permute-start.9 = (bf16[256,512]{1,0:T(8,128)(2,1)}, bf16[256,512]{1,0:T(8,128)(2,1)S(1)}, u32[]{:S(2)}, u32[]{:S(2)}) collective-permute-start(bf16[256,512]{1,0:T(8,128)(2,1)} %get-tuple-element.40.refs_12_), channel_id=1, source_target_pairs={{0,4},{1,5},{2,6},{3,7},{8,12},{9,13},{10,14},{11,15},{16,20},{17,... | collective-permute-start | bytes 786440 | tf_op jit(solution)/shard_map/ppermute | solution.py:615
  52.4 9.7 %collective-permute-start.11 = (bf16[256,512]{1,0:T(8,128)(2,1)}, bf16[256,512]{1,0:T(8,128)(2,1)S(1)}, u32[]{:S(2)}, u32[]{:S(2)}) collective-permute-start(bf16[256,512]{1,0:T(8,128)(2,1)} %get-tuple-element.42), channel_id=1, source_target_pairs={{4,0},{5,1},{6,2},{7,3},{12,8},{13,9},{14,10},{15,11},{20,16},{21,... | collective-permute-start | bytes 786440 | tf_op jit(solution)/shard_map/ppermute | solution.py:626
  62.9 10.0 %copy-start.19 = (bf16[256,512]{1,0:T(8,128)(2,1)S(1)}, bf16[256,512]{1,0:T(8,128)(2,1)}, u32[]{:S(2)}) copy-start(bf16[256,512]{1,0:T(8,128)(2,1)} %get-tuple-element.41) | copy-start | bytes 786436
  69.9 6.7 %copy-start.17 = (bf16[2,336,256]{2,1,0:T(8,128)(2,1)S(1)}, bf16[2,336,256]{2,1,0:T(8,128)(2,1)}, u32[]{:S(2)}) copy-start(bf16[2,336,256]{2,1,0:T(8,128)(2,1)} %get-tuple-element.68) | copy-start | bytes 1032196
  69.9 9.6 %collective-permute-start.12 = (bf16[2,336,256]{2,1,0:T(8,128)(2,1)}, bf16[2,336,256]{2,1,0:T(8,128)(2,1)S(1)}, u32[]{:S(2)}, u32[]{:S(2)}) collective-permute-start(bf16[2,336,256]{2,1,0:T(8,128)(2,1)} %get-tuple-element.64), channel_id=1, source_target_pairs={{0,16},{8,24},{16,0},{24,8},{1,17},{9,25},{17,1},{25,9},{2,18},{10... | collective-permute-start | bytes 1032200 | tf_op jit(solution)/shard_map/ppermute | solution.py:536
  71.4 10.6 %collective-permute-start.17 = (bf16[2,336,256]{2,1,0:T(8,128)(2,1)}, bf16[2,336,256]{2,1,0:T(8,128)(2,1)S(1)}, u32[]{:S(2)}, u32[]{:S(2)}) collective-permute-start(bf16[2,336,256]{2,1,0:T(8,128)(2,1)} %get-tuple-element.66), channel_id=1, source_target_pairs={{0,8},{8,0},{16,24},{24,16},{1,9},{9,1},{17,25},{25,17},{2,10},{10... | collective-permute-start | bytes 1032200 | tf_op jit(solution)/shard_map/ppermute | solution.py:536
  72.9 41.1 %collective-permute-start.10 = (bf16[2,64,512]{2,1,0:T(8,128)(2,1)S(1)}, bf16[2,64,512]{2,1,0:T(8,128)(2,1)S(1)}, u32[]{:S(2)}, u32[]{:S(2)}) collective-permute-start(bf16[2,64,512]{2,1,0:T(8,128)(2,1)S(1)} %get-tuple-element.76), channel_id=1, source_target_pairs={{1,0},{2,1},{3,2},{0,3},{5,4},{6,5},{7,6},{4,7},{9,8},{10,9},{11,1... | collective-permute-start | bytes 393224 | tf_op jit(solution)/shard_map/ppermute | solution.py:638
  76.6 10.7 %collective-permute-start.22 = (bf16[2,336,256]{2,1,0:T(8,128)(2,1)S(1)}, bf16[2,336,256]{2,1,0:T(8,128)(2,1)S(1)}, u32[]{:S(2)}, u32[]{:S(2)}) collective-permute-start(bf16[2,336,256]{2,1,0:T(8,128)(2,1)S(1)} %copy-done.17), channel_id=1, source_target_pairs={{0,16},{8,24},{16,0},{24,8},{1,17},{9,25},{17,1},{25,9},{2,18},{10... | collective-permute-start | bytes 1032200 | tf_op jit(solution)/shard_map/ppermute | solution.py:536
  77.1 12.1 %collective-permute-start.27 = (bf16[2,336,256]{2,1,0:T(8,128)(2,1)}, bf16[2,336,256]{2,1,0:T(8,128)(2,1)S(1)}, u32[]{:S(2)}, u32[]{:S(2)}) collective-permute-start(bf16[2,336,256]{2,1,0:T(8,128)(2,1)} %get-tuple-element.70), channel_id=1, source_target_pairs={{0,8},{8,0},{16,24},{24,16},{1,9},{9,1},{17,25},{25,17},{2,10},{10... | collective-permute-start | bytes 1032200 | tf_op jit(solution)/shard_map/ppermute | solution.py:536
  79.6 12.1 %collective-permute-start.13 = (bf16[336,256]{1,0:T(8,128)(2,1)S(1)}, bf16[336,256]{1,0:T(8,128)(2,1)S(1)}, u32[]{:S(2)}, u32[]{:S(2)}) collective-permute-start(bf16[336,256]{1,0:T(8,128)(2,1)S(1)} %fusion.12), channel_id=1, source_target_pairs={{0,8},{8,0},{16,24},{24,16},{1,9},{9,1},{17,25},{25,17},{2,10},{10... | collective-permute-start | bytes 516104 | tf_op jit(solution)/shard_map/ppermute | solution.py:536
  82.1 5.2 %copy-start.11 = (bf16[2,336,256]{2,1,0:T(8,128)(2,1)S(1)}, bf16[2,336,256]{2,1,0:T(8,128)(2,1)}, u32[]{:S(2)}) copy-start(bf16[2,336,256]{2,1,0:T(8,128)(2,1)} %get-tuple-element.67) | copy-start | bytes 1032196
  82.1 11.4 %collective-permute-start.18 = (bf16[336,256]{1,0:T(8,128)(2,1)S(1)}, bf16[336,256]{1,0:T(8,128)(2,1)S(1)}, u32[]{:S(2)}, u32[]{:S(2)}) collective-permute-start(bf16[336,256]{1,0:T(8,128)(2,1)S(1)} %fusion.13), channel_id=1, source_target_pairs={{0,16},{8,24},{16,0},{24,8},{1,17},{9,25},{17,1},{25,9},{2,18},{10... | collective-permute-start | bytes 516104 | tf_op jit(solution)/shard_map/ppermute | solution.py:536
  87.4 6.8 %collective-permute-start.23 = (bf16[336,256]{1,0:T(8,128)(2,1)S(1)}, bf16[336,256]{1,0:T(8,128)(2,1)S(1)}, u32[]{:S(2)}, u32[]{:S(2)}) collective-permute-start(bf16[336,256]{1,0:T(8,128)(2,1)S(1)} %fusion.14), channel_id=1, source_target_pairs={{0,8},{8,0},{16,24},{24,16},{1,9},{9,1},{17,25},{25,17},{2,10},{10... | collective-permute-start | bytes 516104 | tf_op jit(solution)/shard_map/ppermute | solution.py:536
  89.3 6.6 %collective-permute-start.28 = (bf16[336,256]{1,0:T(8,128)(2,1)S(1)}, bf16[336,256]{1,0:T(8,128)(2,1)S(1)}, u32[]{:S(2)}, u32[]{:S(2)}) collective-permute-start(bf16[336,256]{1,0:T(8,128)(2,1)S(1)} %fusion.15), channel_id=1, source_target_pairs={{0,16},{8,24},{16,0},{24,8},{1,17},{9,25},{17,1},{25,9},{2,18},{10... | collective-permute-start | bytes 516104 | tf_op jit(solution)/shard_map/ppermute | solution.py:536
  91.9 5.6 %collective-permute-start.14 = (bf16[336,128]{1,0:T(8,128)(2,1)S(1)}, bf16[336,128]{1,0:T(8,128)(2,1)S(1)}, u32[]{:S(2)}, u32[]{:S(2)}) collective-permute-start(bf16[336,128]{1,0:T(8,128)(2,1)S(1)} %select_convert_fusion.3), channel_id=1, source_target_pairs={{0,1},{1,0},{2,3},{3,2},{4,5},{5,4},{6,7},{7,6},{8,9},{9,8},{10,11... | collective-permute-start | bytes 258056 | tf_op jit(solution)/shard_map/ppermute | solution.py:536
  93.6 6.3 %collective-permute-start.19 = (bf16[336,128]{1,0:T(8,128)(2,1)S(1)}, bf16[336,128]{1,0:T(8,128)(2,1)S(1)}, u32[]{:S(2)}, u32[]{:S(2)}) collective-permute-start(bf16[336,128]{1,0:T(8,128)(2,1)S(1)} %select_convert_fusion.2), channel_id=1, source_target_pairs={{0,1},{1,0},{2,3},{3,2},{4,5},{5,4},{6,7},{7,6},{8,9},{9,8},{10,11... | collective-permute-start | bytes 258056 | tf_op jit(solution)/shard_map/ppermute | solution.py:536
  94.2 7.6 %collective-permute-start.24 = (bf16[336,128]{1,0:T(8,128)(2,1)S(1)}, bf16[336,128]{1,0:T(8,128)(2,1)S(1)}, u32[]{:S(2)}, u32[]{:S(2)}) collective-permute-start(bf16[336,128]{1,0:T(8,128)(2,1)S(1)} %select_convert_fusion.1), channel_id=1, source_target_pairs={{0,1},{1,0},{2,3},{3,2},{4,5},{5,4},{6,7},{7,6},{8,9},{9,8},{10,11... | collective-permute-start | bytes 258056 | tf_op jit(solution)/shard_map/ppermute | solution.py:536
  95.9 9.3 %collective-permute-start.29 = (bf16[336,128]{1,0:T(8,128)(2,1)S(1)}, bf16[336,128]{1,0:T(8,128)(2,1)S(1)}, u32[]{:S(2)}, u32[]{:S(2)}) collective-permute-start(bf16[336,128]{1,0:T(8,128)(2,1)S(1)} %select_convert_fusion), channel_id=1, source_target_pairs={{0,1},{1,0},{2,3},{3,2},{4,5},{5,4},{6,7},{7,6},{8,9},{9,8},{10,11... | collective-permute-start | bytes 258056 | tf_op jit(solution)/shard_map/ppermute | solution.py:536
  97.5 9.6 %collective-permute-start.15 = (bf16[336,128]{1,0:T(8,128)(2,1)S(1)}, bf16[336,128]{1,0:T(8,128)(2,1)S(1)}, u32[]{:S(2)}, u32[]{:S(2)}) collective-permute-start(bf16[336,128]{1,0:T(8,128)(2,1)S(1)} %add_convert_fusion.7), channel_id=1, source_target_pairs={{0,2},{1,3},{2,0},{3,1},{4,6},{5,7},{6,4},{7,5},{8,10},{9,11},{10,... | collective-permute-start | bytes 258056 | tf_op jit(solution)/shard_map/ppermute | solution.py:536
  100.0 10.5 %collective-permute-start.20 = (bf16[336,128]{1,0:T(8,128)(2,1)S(1)}, bf16[336,128]{1,0:T(8,128)(2,1)S(1)}, u32[]{:S(2)}, u32[]{:S(2)}) collective-permute-start(bf16[336,128]{1,0:T(8,128)(2,1)S(1)} %add_convert_fusion.5), channel_id=1, source_target_pairs={{0,2},{1,3},{2,0},{3,1},{4,6},{5,7},{6,4},{7,5},{8,10},{9,11},{10,... | collective-permute-start | bytes 258056 | tf_op jit(solution)/shard_map/ppermute | solution.py:536
  101.8 8.4 %collective-permute-start.25 = (bf16[336,128]{1,0:T(8,128)(2,1)S(1)}, bf16[336,128]{1,0:T(8,128)(2,1)S(1)}, u32[]{:S(2)}, u32[]{:S(2)}) collective-permute-start(bf16[336,128]{1,0:T(8,128)(2,1)S(1)} %add_convert_fusion.3), channel_id=1, source_target_pairs={{0,2},{1,3},{2,0},{3,1},{4,6},{5,7},{6,4},{7,5},{8,10},{9,11},{10,... | collective-permute-start | bytes 258056 | tf_op jit(solution)/shard_map/ppermute | solution.py:536
  105.3 6.6 %collective-permute-start.30 = (bf16[336,128]{1,0:T(8,128)(2,1)S(1)}, bf16[336,128]{1,0:T(8,128)(2,1)S(1)}, u32[]{:S(2)}, u32[]{:S(2)}) collective-permute-start(bf16[336,128]{1,0:T(8,128)(2,1)S(1)} %add_convert_fusion.1), channel_id=1, source_target_pairs={{0,2},{1,3},{2,0},{3,1},{4,6},{5,7},{6,4},{7,5},{8,10},{9,11},{10,... | collective-permute-start | bytes 258056 | tf_op jit(solution)/shard_map/ppermute | solution.py:536
  107.2 9.6 %collective-permute-start.16 = (bf16[336,128]{1,0:T(8,128)(2,1)S(1)}, bf16[336,128]{1,0:T(8,128)(2,1)S(1)}, u32[]{:S(2)}, u32[]{:S(2)}) collective-permute-start(bf16[336,128]{1,0:T(8,128)(2,1)S(1)} %add_convert_fusion.6.refs_0_), channel_id=1, source_target_pairs={{0,1},{1,0},{2,3},{3,2},{4,5},{5,4},{6,7},{7,6},{8,9},{9,8},{10,11... | collective-permute-start | bytes 258056 | tf_op jit(solution)/shard_map/ppermute | solution.py:536
  110.3 5.2 %collective-permute-start.33 = (bf16[128,256]{1,0:T(8,128)(2,1)S(1)}, bf16[128,256]{1,0:T(8,128)(2,1)S(1)}, u32[]{:S(2)}, u32[]{:S(2)}) collective-permute-start(bf16[128,256]{1,0:T(8,128)(2,1)S(1)} %pad_maximum_fusion.1), channel_id=1, source_target_pairs={{0,17},{1,16},{2,19},{3,18},{8,25},{9,24},{10,27},{11,26},{16,1},{... | collective-permute-start | bytes 196616 | tf_op jit(solution)/shard_map/ppermute | solution.py:679
  110.5 6.3 %collective-permute-start.32 = (bf16[128,256]{1,0:T(8,128)(2,1)S(1)}, bf16[128,256]{1,0:T(8,128)(2,1)S(1)}, u32[]{:S(2)}, u32[]{:S(2)}) collective-permute-start(bf16[128,256]{1,0:T(8,128)(2,1)S(1)} %pad_maximum_fusion.1), channel_id=1, source_target_pairs={{0,16},{8,24},{16,0},{24,8},{1,17},{9,25},{17,1},{25,9},{2,18},{10... | collective-permute-start | bytes 196616 | tf_op jit(solution)/shard_map/ppermute | solution.py:536
  111.9 6.7 %collective-permute-start.26 = (bf16[336,128]{1,0:T(8,128)(2,1)S(1)}, bf16[336,128]{1,0:T(8,128)(2,1)S(1)}, u32[]{:S(2)}, u32[]{:S(2)}) collective-permute-start(bf16[336,128]{1,0:T(8,128)(2,1)S(1)} %add_convert_fusion.2.refs_4_), channel_id=1, source_target_pairs={{0,1},{1,0},{2,3},{3,2},{4,5},{5,4},{6,7},{7,6},{8,9},{9,8},{10,11... | collective-permute-start | bytes 258056 | tf_op jit(solution)/shard_map/ppermute | solution.py:536
  114.0 4.6 %collective-permute-start.21 = (bf16[336,128]{1,0:T(8,128)(2,1)S(1)}, bf16[336,128]{1,0:T(8,128)(2,1)S(1)}, u32[]{:S(2)}, u32[]{:S(2)}) collective-permute-start(bf16[336,128]{1,0:T(8,128)(2,1)S(1)} %add_convert_fusion.4.refs_2_), channel_id=1, source_target_pairs={{0,1},{1,0},{2,3},{3,2},{4,5},{5,4},{6,7},{7,6},{8,9},{9,8},{10,11... | collective-permute-start | bytes 258056 | tf_op jit(solution)/shard_map/ppermute | solution.py:536
  115.5 4.5 %collective-permute-start.31 = (bf16[336,128]{1,0:T(8,128)(2,1)S(1)}, bf16[336,128]{1,0:T(8,128)(2,1)S(1)}, u32[]{:S(2)}, u32[]{:S(2)}) collective-permute-start(bf16[336,128]{1,0:T(8,128)(2,1)S(1)} %add_convert_fusion.refs_6_), channel_id=1, source_target_pairs={{0,1},{1,0},{2,3},{3,2},{4,5},{5,4},{6,7},{7,6},{8,9},{9,8},{10,11... | collective-permute-start | bytes 258056 | tf_op jit(solution)/shard_map/ppermute | solution.py:536
  (8 other events, 11.5 us)
